TPU v7x, 32 devices: a whole 2x2x4 slice. The times are simulated.
32 devices in a mesh: blade: 4 (over y, x), dp: 8 (over z, core).
Axes of the slice: x: 2, y: 2, z: 4, core: 2. Of those that a mesh axis runs over, the one named last changes fastest.
Arguments:
- inputs: bfloat16 [64, 4, 48, 4096], P('dp', 'blade'), may hold values from -6 to 6
- cotangent: bfloat16 [64, 4, 48, 4096], P('dp', 'blade'), may hold values from -6 to 6
- norm_table: float32 [16], replicated, may hold values from 0.5 to 2
- sample_index: int32 [64], P('dp'), may hold values from 0 to 15
- spec_weight: float32 [4, 256, 2, 48, 48], P('blade', 'dp'), may hold values from -0.875 to 0.875
- spec_first: float32 [4, 256, 2, 48, 48], P('blade', 'dp'), may hold values from -6 to 6
- spec_second: float32 [4, 256, 2, 48, 48], P('blade', 'dp'), may hold values from 0.32 to 1.344
- lin_weight: float32 [4, 48, 48], P('blade'), may hold values from -0.4375 to 0.4375
- lin_first: float32 [4, 48, 48], P('blade'), may hold values from -640 to 640
- lin_second: float32 [4, 48, 48], P('blade'), may hold values from 786.432 to 3145.728
Outputs:
- output: bfloat16 [64, 4, 48, 4096], P('dp', 'blade')
- input_grad: float32 [64, 4, 48, 4096], P('dp', 'blade')
- spec_new: float32 [4, 256, 2, 48, 48], P('blade', 'dp')
- spec_first_new: float32 [4, 256, 2, 48, 48], P('blade', 'dp')
- spec_second_new: float32 [4, 256, 2, 48, 48], P('blade', 'dp')
- lin_new: float32 [4, 48, 48], P('blade')
- lin_first_new: float32 [4, 48, 48], P('blade')
- lin_second_new: float32 [4, 48, 48], P('blade')
All inputs are finite; a program needn't handle non-finite values.
Results may differ from a plain program's by a relative error of at most 0.014.
Values may be sent and summed in bfloat16 or wider, within the bound.
No kernel may reach another device: no remote copies, remote signals or barrier semaphores. Data moves between devices by JAX's collectives and lax.ppermute only.
A program may use at most 192 MiB of HBM per device.

v0:
```python
from functools import partial
import math

import jax
import jax.numpy as jnp
from jax import lax
from jax.sharding import PartitionSpec as P

GRID = 64
MSIDE = 16
NTAB = 16
STEP_COUNT = 5
NPIX = 4096
MODES = 256


BETA_ONE = 0.9
BETA_TWO = 0.999
EPSILON = 1e-08
RATE = 0.1
DECAY = 0.01


def blade_sign(left_blade, right_blade):
    return 1 - 2 * (left_blade // 2 % 2) * (right_blade % 2)


def tables():
    pix_ids = jnp.arange(NPIX, dtype=jnp.int32)
    pix_row = pix_ids // GRID
    pix_col = pix_ids % GRID
    mode_ids = jnp.arange(MODES, dtype=jnp.int32)
    row_index = mode_ids // MSIDE
    col_freq = mode_ids % MSIDE
    row_freq = jnp.where(row_index < MSIDE // 2, row_index, GRID - MSIDE + row_index)
    phase_int = (pix_row[:, None] * row_freq[None, :] + pix_col[:, None] * col_freq[None, :]) % GRID
    angles = phase_int.astype(jnp.float32) * (2.0 * math.pi / GRID)
    forward = jnp.concatenate([jnp.cos(angles), -jnp.sin(angles)], axis=1) / GRID
    factor = jnp.where(col_freq == 0, 1.0, 2.0).astype(jnp.float32)
    factor = jnp.concatenate([factor, factor])
    return (forward.astype(jnp.bfloat16), (forward * factor[None, :]).astype(jnp.bfloat16))


def sign_matrix(own_blade, first_side):
    lane_ids = jnp.arange(4, dtype=jnp.int32)
    row_ids = lane_ids[:, None]
    col_ids = lane_ids[None, :]
    matches = jnp.bitwise_xor(row_ids, col_ids) == own_blade
    if first_side == "col":
        values = blade_sign(col_ids, own_blade)
    elif first_side == "row":
        values = blade_sign(row_ids, col_ids)
    else:
        values = blade_sign(own_blade, col_ids)
    return jnp.where(matches, values, 0).astype(jnp.bfloat16)


def adamw(weight, first, second, grad):
    first_new = BETA_ONE * first + (1.0 - BETA_ONE) * grad
    second_new = BETA_TWO * second + (1.0 - BETA_TWO) * grad * grad
    corr_one = 1.0 - BETA_ONE**STEP_COUNT
    corr_two = 1.0 - BETA_TWO**STEP_COUNT
    update = first_new / corr_one / (jnp.sqrt(second_new / corr_two) + EPSILON)
    return (weight - RATE * (update + DECAY * weight), first_new, second_new)


def body(
    inputs,
    cotangent,
    norm_table,
    sample_index,
    spec_weight,
    spec_first,
    spec_second,
    lin_weight,
    lin_first,
    lin_second,
):
    own_blade = lax.axis_index("blade")
    num_samples = inputs.shape[0]
    num_chans = inputs.shape[2]
    forward_table, inverse_table = tables()
    matches = sample_index[:, None] == jnp.arange(NTAB, dtype=jnp.int32)[None, :]
    normalizer = jnp.sum(jnp.where(matches, norm_table[None, :], 0.0), axis=1)[:, None, None, None]
    normed = inputs.astype(jnp.float32) / normalizer
    normed_low = normed.astype(jnp.bfloat16)
    lin_low = lin_weight.astype(jnp.bfloat16)
    spec_low = spec_weight.astype(jnp.bfloat16)
    own_modes = jnp.einsum(
        "sjcp,pn->sjcn", normed_low, forward_table, preferred_element_type=jnp.float32
    ).astype(jnp.bfloat16)
    normed_all, lin_all, modes_all = (
        lax.all_gather(normed_low, "blade", axis=1, tiled=True),
        lax.all_gather(lin_low, "blade", axis=0, tiled=True),
        lax.all_gather(own_modes, "blade", axis=1, tiled=True),
    )
    modes_real = modes_all[..., :MODES]
    modes_imag = modes_all[..., MODES:]
    block_in = lax.all_gather(spec_low, "dp", axis=1, tiled=True)
    w_real = block_in[0, :, 0]
    w_imag = block_in[0, :, 1]
    form = partial(jnp.einsum, "sjcm,mco->sjom", preferred_element_type=jnp.float32)
    out_real = form(modes_real, w_real) - form(modes_imag, w_imag)
    out_imag = form(modes_real, w_imag) + form(modes_imag, w_real)
    products = jnp.stack([out_real, out_imag], axis=3)
    blade_mix = sign_matrix(own_blade, "col")
    partial_spec = jnp.einsum("ij,sjcrm->sicrm", blade_mix.astype(jnp.float32), products)
    spec_sum = lax.psum_scatter(partial_spec, "blade", scatter_dimension=1, tiled=True)
    spec_out = spec_sum.reshape(num_samples, 1, num_chans, 2 * MODES).astype(jnp.bfloat16)
    spatial = jnp.einsum(
        "sjcn,pn->sjcp", spec_out, inverse_table, preferred_element_type=jnp.float32
    )
    forward_lin = sign_matrix(own_blade, "row")
    lin_cat = jnp.einsum(
        "jk,kco->jco", forward_lin, lin_all, preferred_element_type=jnp.float32
    ).astype(jnp.bfloat16)
    linear = jnp.einsum("sjcp,jco->sop", normed_all, lin_cat, preferred_element_type=jnp.float32)[
        :, None
    ]
    pre = spatial + linear
    activated, gelu_pullback = jax.vjp(partial(jax.nn.gelu, approximate=False), pre)
    output = (normed + activated).astype(jnp.bfloat16)
    cot_float = cotangent.astype(jnp.float32)
    grad_pre = gelu_pullback(cot_float)[0].astype(jnp.bfloat16)
    grad_spec = jnp.einsum(
        "sjcp,pn->sjcn", grad_pre, inverse_table, preferred_element_type=jnp.float32
    ).astype(jnp.bfloat16)
    pre_all, spec_grad_all = (
        lax.all_gather(grad_pre, "blade", axis=1, tiled=True),
        lax.all_gather(grad_spec, "blade", axis=1, tiled=True),
    )
    mixed_spec = jnp.einsum(
        "ij,sicn->sjcn", blade_mix, spec_grad_all, preferred_element_type=jnp.float32
    ).astype(jnp.bfloat16)
    mixed_pre = jnp.einsum(
        "ij,sicp->sjcp", blade_mix, pre_all, preferred_element_type=jnp.float32
    ).astype(jnp.bfloat16)
    grad_real = mixed_spec[..., :MODES]
    grad_imag = mixed_spec[..., MODES:]
    d_real = grad_real
    d_imag = grad_imag
    form = partial(jnp.einsum, "sjcm,sjom->mco", preferred_element_type=jnp.float32)
    term_real = form(modes_real, d_real) + form(modes_imag, d_imag)
    term_imag = form(modes_real, d_imag) - form(modes_imag, d_real)
    spec_grad = lax.psum_scatter(
        jnp.stack([term_real, term_imag], axis=1).astype(jnp.bfloat16),
        "dp",
        scatter_dimension=0,
        tiled=True,
    ).astype(jnp.float32)[None]
    block_in = lax.all_gather(spec_low, "dp", axis=1, tiled=True)
    d_real = grad_real
    d_imag = grad_imag
    w_real = block_in[0, :, 0]
    w_imag = block_in[0, :, 1]
    form = partial(jnp.einsum, "sjom,mco->sjcm", preferred_element_type=jnp.float32)
    back_real = form(d_real, w_real) + form(d_imag, w_imag)
    back_imag = form(d_imag, w_real) - form(d_real, w_imag)
    back_all = jnp.stack([back_real, back_imag], axis=3)
    grad_modes = lax.psum_scatter(
        back_all.astype(jnp.bfloat16), "blade", scatter_dimension=1, tiled=True
    ).astype(jnp.float32)
    grad_modes = grad_modes.reshape(num_samples, 1, num_chans, 2 * MODES).astype(jnp.bfloat16)
    from_spec = jnp.einsum(
        "sjcn,pn->sjcp", grad_modes, forward_table, preferred_element_type=jnp.float32
    )
    lin_grad = jnp.einsum(
        "sjcp,sjop->co", normed_all, mixed_pre, preferred_element_type=jnp.float32
    )[None]
    lin_grad = lax.psum(lin_grad, "dp")
    back_lin = sign_matrix(own_blade, "own")
    lin_sel = jnp.einsum(
        "ik,kco->ico", back_lin, lin_all, preferred_element_type=jnp.float32
    ).astype(jnp.bfloat16)
    from_lin = jnp.einsum("siop,ico->scp", pre_all, lin_sel, preferred_element_type=jnp.float32)[
        :, None
    ]
    input_grad = (cot_float + from_lin + from_spec) / normalizer
    spec_new, spec_first_new, spec_second_new = adamw(
        spec_weight, spec_first, spec_second, spec_grad
    )
    lin_new, lin_first_new, lin_second_new = adamw(lin_weight, lin_first, lin_second, lin_grad)
    return (
        output,
        input_grad,
        spec_new,
        spec_first_new,
        spec_second_new,
        lin_new,
        lin_first_new,
        lin_second_new,
    )


def solution(mesh):
    return jax.shard_map(
        body,
        mesh=mesh,
        in_specs=(
            P("dp", "blade", None, None),
            P("dp", "blade", None, None),
            P(),
            P("dp"),
            P("blade", "dp", None, None, None),
            P("blade", "dp", None, None, None),
            P("blade", "dp", None, None, None),
            P("blade", None, None),
            P("blade", None, None),
            P("blade", None, None),
        ),
        out_specs=(
            P("dp", "blade", None, None),
            P("dp", "blade", None, None),
            P("blade", "dp", None, None, None),
            P("blade", "dp", None, None, None),
            P("blade", "dp", None, None, None),
            P("blade", None, None),
            P("blade", None, None),
            P("blade", None, None),
        ),
        check_vma=False,
    )
```

profile of v0, /device:TPU:0, one launch (start us, length us, event | category | flops | bytes accessed | tf_op | source)
XLA Modules:
  0.0 696.2 jit_solution(13028528623821768969)
XLA Ops:
  10.8 16.9 %fusion.38 = (f32[4096,256]{1,0:T(8,128)S(1)}, f32[4096,256]{1,0:T(8,128)S(1)}) fusion(s32[256]{0:T(256)S(1)} %get-tuple-element.66, s32[4096]{0:T(1024)S(1)} %get-tuple-element.63, s32[256]{0:T(256)S(1)} %get-tuple-element.65, s32[4096]{0:T(1024)S(1)} %get-tuple-element.64), kind=kLoop, calls=%fused_computation.71 | loop fusion | flops 17825792 | bytes 8423424 | tf_op jit(solution)/shard_map/cos | solution.py:38
  36.4 31.1 %all-gather.14.cloned.1.call-done = bf16[8,192,512]{2,1,0:T(8,128)(2,1)} async-done(((bf16[8,48,512]{2,1,0:T(8,128)(2,1)}), bf16[8,192,512]{2,1,0:T(8,128)(2,1)}) %all-gather.14.cloned.1.call-update) | async-done | bytes 1572880 | tf_op jit(solution)/shard_map/all_gather | solution.py:95
  77.5 56.9 %all-gather.8.cloned.1.call-done = bf16[1,256,2,48,48]{4,3,1,2,0:T(8,128)(2,1)} async-done(((bf16[1,32,2,48,48]{4,3,1,2,0:T(8,128)(2,1)}), bf16[1,256,2,48,48]{4,3,1,2,0:T(8,128)(2,1)}) %all-gather.8.cloned.1.call-update) | async-done | bytes 2359312 | tf_op jit(solution)/shard_map/all_gather | solution.py:99
  144.5 6.7 copy.169
  155.7 8.8 %all_gather.21 = bf16[4,48,48]{2,1,0:T(8,128)(2,1)S(1)} all-gather(bf16[1,48,48]{2,1,0:T(8,128)(2,1)S(1)} %convert_element_type.106), channel_id=1, replica_groups=mesh['blade'=4,'dp'=8] {'blade'}, dimensions={0}, use_global_device_ids=true | all-gather | bytes 23040 | tf_op jit(solution)/shard_map/all_gather | solution.py:94
  165.0 32.8 %reduce-scatter.12.cloned.1.call-done = f32[8,1,48,2,256]{4,2,3,0,1:T(8,128)} async-done(((f32[8,4,48,2,256]{4,2,3,0,1:T(8,128)}), f32[8,1,48,2,256]{4,2,3,0,1:T(8,128)}) %reduce-scatter.12.cloned.1.call-update) | async-done | bytes 786448
  199.5 8.9 %fusion.66 = f32[8,48,4096]{2,1,0:T(8,128)} fusion(bf16[8,48,512]{2,1,0:T(8,128)(2,1)S(1)} %convert_element_type.103, f32[4096,256]{1,0:T(8,128)} %copy-done.10, f32[4096,256]{1,0:T(8,128)} %copy-done.9, f32[512]{0:T(512)S(1)} %maximum_multiply_fusion), kind=kOutput, calls=%fused_computation.97 | convolution fusion | flops 1616904192 | bytes 15075328 | tf_op jit(solution)/shard_map/sjcn,pn->sjcp/dot_general | solution.py:110
  208.4 113.6 %all-gather.10.cloned.1.call-done = bf16[8,4,48,4096]{3,2,0,1:T(8,128)(2,1)} async-done(((bf16[8,1,48,4096]{3,2,0,1:T(8,128)(2,1)}), bf16[8,4,48,4096]{3,2,0,1:T(8,128)(2,1)}) %all-gather.10.cloned.1.call-update) | async-done | bytes 12582928 | tf_op jit(solution)/shard_map/all_gather | solution.py:93
  322.0 21.2 %fusion.12 = (bf16[8,1,48,4096]{3,2,0,1:T(8,128)(2,1)S(1)}, f32[8,48,4096]{2,1,0:T(8,128)}, f32[8,48,4096]{2,1,0:T(8,128)}) fusion(bf16[8,1,48,4096]{3,2,1,0:T(8,128)(2,1)} %param.11, f32[8,48,4096]{2,1,0:T(8,128)} %fusion.66, bf16[8,4,48,4096]{3,2,0,1:T(8,128)(2,1)} %all-gather.10.cloned.1.call-done, bf16[4,48,48]{1,2,0:T(8,128)(2,1)S(1)} %copy.175), kind=kOutput, calls=%fused_computation.19 | convolution fusion | flops 720371712 | bytes 37767168 | tf_op jit(solution)/shard_map/sjcp,jco->sop/dot_general | solution.py:117
  343.2 7.1 %fusion.56 = bf16[8,48,512]{2,1,0:T(8,128)(2,1)} fusion(bf16[8,1,48,4096]{3,2,0,1:T(8,128)(2,1)S(1)} %get-tuple-element.54, f32[4096,256]{1,0:T(8,128)} %copy-done.10, f32[4096,256]{1,0:T(8,128)} %copy-done.9, f32[512]{0:T(512)S(1)} %maximum_multiply_fusion), kind=kOutput, calls=%fused_computation.92 | convolution fusion | flops 1617100800 | bytes 11929600 | tf_op jit(solution)/shard_map/sjcp,pn->sjcn/dot_general | solution.py:125
  350.6 30.9 %all-gather.16.cloned.1.call-done = bf16[8,192,512]{2,1,0:T(8,128)(2,1)} async-done(((bf16[8,48,512]{2,1,0:T(8,128)(2,1)}), bf16[8,192,512]{2,1,0:T(8,128)(2,1)}) %all-gather.16.cloned.1.call-update) | async-done | bytes 1572880 | tf_op jit(solution)/shard_map/all_gather | solution.py:130
  385.9 5.4 copy.184
  391.2 4.0 copy.183
  395.2 4.4 fusion.39
  407.8 5.5 copy.187
  425.9 12.8 %reshape.319 = bf16[256,4608]{1,0:T(8,128)(2,1)} reshape(bf16[256,2,48,48]{3,2,1,0:T(8,128)(2,1)} %copy.220) | data formatting | bytes 4718592
  440.6 8.3 %fusion.37 = bf16[8,1,48,4096]{3,2,1,0:T(8,128)(2,1)} fusion(f32[8,48,4096]{2,1,0:T(8,128)} %get-tuple-element.55, f32[8,48,4096]{2,1,0:T(8,128)} %get-tuple-element.62, f32[8]{0:T(128)S(1)} %select_reduce_fusion, bf16[8,1,48,4096]{3,2,1,0:T(8,128)(2,1)S(1)} %copy-done.12), kind=kLoop, calls=%fused_computation.69 | loop fusion | flops 9437184 | bytes 18874400
  450.5 8.3 %fusion.62 = f32[8,48,4096]{2,1,0:T(8,128)} fusion(bf16[8,48,512]{2,1,0:T(8,128)(2,1)S(1)} %convert_element_type.117, f32[4096,256]{1,0:T(8,128)} %copy-done.10, f32[4096,256]{1,0:T(8,128)} %copy-done.9), kind=kOutput, calls=%fused_computation.96 | convolution fusion | flops 1616904192 | bytes 15073280 | tf_op jit(solution)/shard_map/sjcn,pn->sjcp/dot_general | solution.py:164
  458.8 24.2 %reduce-scatter.10.cloned.1.call-done = bf16[32,4608]{1,0:T(8,128)(2,1)} async-done(((bf16[256,4608]{1,0:T(8,128)(2,1)}), bf16[32,4608]{1,0:T(8,128)(2,1)}) %reduce-scatter.10.cloned.1.call-update) | async-done | bytes 294928
  491.8 114.7 %all-gather.12.cloned.1.call-done = bf16[8,4,48,4096]{3,2,0,1:T(8,128)(2,1)} async-done(((bf16[8,1,48,4096]{3,2,0,1:T(8,128)(2,1)}), bf16[8,4,48,4096]{3,2,0,1:T(8,128)(2,1)}) %all-gather.12.cloned.1.call-update) | async-done | bytes 12582928 | tf_op jit(solution)/shard_map/all_gather | solution.py:129
  606.6 17.3 %convert_bitcast_fusion = bf16[8,4,48,4096]{3,1,2,0:T(4,128)(2,1)} fusion(bf16[8,4,48,4096]{3,2,0,1:T(8,128)(2,1)} %all-gather.12.cloned.1.call-done, s32[4]{0:T(128)S(1)} %multiply_subtract_fusion.3, s32[]{:T(128)S(6)} %axis_index.15), kind=kOutput, calls=%fused_computation.4 | convolution fusion | flops 56623168 | bytes 25165844 | tf_op jit(solution)/shard_map/ij,sicp->sjcp/dot_general | solution.py:135
  624.0 23.2 %fusion.59 = f32[1,48,48]{2,1,0:T(8,128)S(1)} fusion(bf16[8,4,48,4096]{3,2,0,1:T(8,128)(2,1)} %all-gather.10.cloned.1.call-done, bf16[8,4,48,4096]{3,1,2,0:T(4,128)(2,1)} %convert_bitcast_fusion), kind=kOutput, calls=%fused_computation.95 | convolution fusion | flops 603979776 | bytes 25175040 | tf_op jit(solution)/shard_map/sjcp,sjop->co/dot_general | solution.py:167
  647.1 28.5 %psum.7 = f32[1,48,48]{2,1,0:T(8,128)S(1)} all-reduce(f32[1,48,48]{2,1,0:T(8,128)S(1)} %fusion.59), channel_id=1, replica_groups=mesh['blade'=4,'dp'=8] {'dp'}, use_global_device_ids=true, to_apply=%region_4.5 | all-reduce | flops 2304 | bytes 18432 | tf_op jit(solution)/shard_map/psum | solution.py:170
  676.3 12.8 %fusion.16 = f32[8,1,48,4096]{3,2,1,0:T(8,128)} fusion(f32[8,48,4096]{2,1,0:T(8,128)} %fusion.62, bf16[8,4,48,4096]{3,2,0,1:T(8,128)(2,1)} %all-gather.12.cloned.1.call-done, bf16[8,1,48,4096]{3,2,1,0:T(8,128)(2,1)} %param.11, f32[8]{0:T(128)S(1)} %select_reduce_fusion, bf16[4,48,48]{2,0,1:T(4,128)(2,1)S(1)} %convolution_convert_fusion.1), kind=kOutput, calls=%fused_computation.23 | convolution fusion | flops 610271232 | bytes 28330016 | tf_op jit(solution)/shard_map/siop,ico->scp/dot_general | solution.py:175
  (106 shorter events, 77.0 us)
Async XLA Ops:
  7.2 60.3 %all-gather.14.cloned.1.call-start = ((), (), s32[]{:S(2)}) async-start(), calls=%async_computation.6 | async-start | bytes 1966080 | tf_op jit(solution)/shard_map/all_gather | solution.py:95
  10.8 16.9 %copy-start.11 = (bf16[8,1,48,4096]{3,2,0,1:T(8,128)(2,1)}, bf16[8,1,48,4096]{3,2,0,1:T(8,128)(2,1)S(1)}, u32[]{:S(2)}) copy-start(bf16[8,1,48,4096]{3,2,0,1:T(8,128)(2,1)S(1)} %fusion.30) | copy-start | bytes 9437188
  27.7 2.0 copy-start.9
  27.7 3.2 copy-start.10
  33.6 100.8 %all-gather.8.cloned.1.call-start = ((), (), s32[]{:S(2)}) async-start(), calls=%async_computation.3 | async-start | bytes 7077888 | tf_op jit(solution)/shard_map/all_gather | solution.py:99
  36.1 161.7 %reduce-scatter.12.cloned.1.call-start = ((), (), s32[]{:S(2)}) async-start(), calls=%async_computation.9 | async-start | bytes 3932160
  73.7 63.6 %copy-start.1 = (bf16[8,4,48,256]{2,0,1,3:T(8,128)(2,1)}, bf16[8,4,48,256]{2,0,1,3:T(8,128)(2,1)S(1)}, u32[]{:S(2)}) copy-start(bf16[8,4,48,256]{2,0,1,3:T(8,128)(2,1)S(1)} %copy.222) | copy-start | bytes 2359300
  134.4 3.7 copy-start
  155.0 167.0 %all-gather.10.cloned.1.call-start = ((), (), s32[]{:S(2)}) async-start(), calls=%async_computation.4 | async-start | bytes 15728640 | tf_op jit(solution)/shard_map/all_gather | solution.py:93
  155.6 225.9 %all-gather.16.cloned.1.call-start = ((), (), s32[]{:S(2)}) async-start(), calls=%async_computation.7 | async-start | bytes 1966080 | tf_op jit(solution)/shard_map/all_gather | solution.py:130
  343.2 7.1 %copy-start.14 = (bf16[8,1,48,4096]{3,2,0,1:T(8,128)(2,1)}, bf16[8,1,48,4096]{3,2,0,1:T(8,128)(2,1)S(1)}, u32[]{:S(2)}) copy-start(bf16[8,1,48,4096]{3,2,0,1:T(8,128)(2,1)S(1)} %get-tuple-element.54) | copy-start | bytes 9437188
  350.3 98.5 %reduce-scatter.14.cloned.1.call-start = ((), (), s32[]{:S(2)}) async-start(), calls=%async_computation.10 | async-start | bytes 1966080
  385.9 13.8 %slice-start = ((s8[6291456]{0:T(1024)(128)(4,1)}), s8[2097152]{0:T(1024)(128)(4,1)S(1)}, s32[]{:S(2)}) async-start(s8[6291456]{0:T(1024)(128)(4,1)} %bitcast.210), calls=%async_computation.11 | async-start | bytes 4194304
  395.2 4.4 slice-start.1
  395.2 4.4 copy-start.7
  401.4 1.8 copy-start.5
  407.8 5.8 copy-start.2
  413.4 69.7 %reduce-scatter.10.cloned.1.call-start = ((), (), s32[]{:S(2)}) async-start(), calls=%async_computation.8 | async-start | bytes 2654208
  413.6 2.8 copy-start.8
  438.7 1.9 copy-start.12
  438.7 167.8 %all-gather.12.cloned.1.call-start = ((), (), s32[]{:S(2)}) async-start(), calls=%async_computation.5 | async-start | bytes 15728640 | tf_op jit(solution)/shard_map/all_gather | solution.py:129
  450.4 34.3 %copy-start.13 = (f32[1,32,2,48,48]{4,3,2,1,0:T(8,128)S(1)}, f32[1,32,2,48,48]{4,3,2,1,0:T(8,128)}, u32[]{:S(2)}) copy-start(f32[1,32,2,48,48]{4,3,2,1,0:T(8,128)} %param.14) | copy-start | bytes 1769476
  623.9 51.8 %copy-start.16 = (f32[1,48,48]{2,1,0:T(8,128)S(1)}, f32[1,48,48]{2,1,0:T(8,128)}, u32[]{:S(2)}) copy-start(f32[1,48,48]{2,1,0:T(8,128)} %param.18) | copy-start | bytes 27652
  623.9 51.7 %copy-start.17 = (f32[1,48,48]{2,1,0:T(8,128)S(1)}, f32[1,48,48]{2,1,0:T(8,128)}, u32[]{:S(2)}) copy-start(f32[1,48,48]{2,1,0:T(8,128)} %param.19) | copy-start | bytes 27652
  (4 other events, 5.5 us)
Sparse Core Ops, SparseCore 0:
  33.7 33.6 all-gather.13
  69.6 64.7 all-gather.7
  155.1 42.6 reduce-scatter.11
  199.5 122.4 all-gather.9
  350.5 30.9 all-gather.15
  413.5 30.9 reduce-scatter.13
  446.8 36.2 reduce-scatter.9
  484.9 121.6 all-gather.11
where the time goes:
time: 705 us; the launch traced here: 696 us
  waiting for transfers between devices  405 us (57%)
  matrix products  128 us (18%)
  local copies, waits for them, and re-layouts  69 us (10%)
  other arithmetic  41 us (6%)
  blocking collectives  37.4 us (5%)
  between operations  14.8 us (2%)
    all_gather x1, waiting for transfers between devices, body(): lax.all_gather(grad_pre, 'blade', axis=1, tiled=True)  115 us
    all_gather x1, waiting for transfers between devices, body(): lax.all_gather(normed_low, 'blade', axis=1, tiled=True)  114 us
    unnamed x11, waiting for transfers between devices  58 us
    all_gather x1, waiting for transfers between devices, body(): block_in = lax.all_gather(spec_low, 'dp', axis=1, tiled=True)  56.9 us
    unnamed x49, local copies, waits for them, and re-layouts  38.6 us
    all_gather x1, waiting for transfers between devices, body(): lax.all_gather(own_modes, 'blade', axis=1, tiled=True)  31.1 us
    all_gather x1, waiting for transfers between devices, body(): lax.all_gather(grad_spec, 'blade', axis=1, tiled=True)  30.9 us
    psum x1, blocking collectives, body(): lin_grad = lax.psum(lin_grad, 'dp')  28.5 us
  transfers between devices with their start and end apart: 8, of which 7 were waited for; matrix products, arithmetic and copies ran while one was open for 11% of the time, Pallas kernels for 0%

commit v1 on v0

v1 whole, which is shorter than its diff:
```python
from functools import partial
import math

import jax
import jax.numpy as jnp
from jax import lax
from jax.experimental import pallas as pl
from jax.experimental.pallas import tpu as pltpu
from jax.sharding import PartitionSpec as P

GRID = 64
MSIDE = 16
NTAB = 16
STEP_COUNT = 5
NPIX = 4096
MODES = 256
C = 48
LANES = 2 * C
QUAD = 4
TILE = 1024
ROWS = 16

BETA_ONE = 0.9
BETA_TWO = 0.999
EPSILON = 1e-08
RATE = 0.1
DECAY = 0.01

F32 = jnp.float32
BF16 = jnp.bfloat16
SMEM = pltpu.MemorySpace.SMEM


def sgn(left, right):
    return -1.0 if (left & 2) and (right & 1) else 1.0


def flip_of(own, k):
    if k & 1:
        return (1 - 2 * ((own // 2) % 2)).astype(F32)
    return jnp.float32(1.0)


def mode_factor(mode):
    return jnp.where(mode % MSIDE == 0, 1.0, 2.0).astype(F32)


def dot(left, right, dims=((1,), (0,))):
    return lax.dot_general(left, right, (dims, ((), ())), preferred_element_type=F32)


def whole(shape):
    zeros = (0,) * len(shape)
    return pl.BlockSpec(tuple(shape), lambda *_: zeros)


def params(**kw):
    return pltpu.CompilerParams(vmem_limit_bytes=60 * 1024 * 1024, **kw)


def small_tables():
    mode_ids = jnp.arange(2 * MODES, dtype=jnp.int32)
    imag = mode_ids >= MODES
    mode_ids = mode_ids % MODES
    row_index = mode_ids // MSIDE
    col_freq = mode_ids % MSIDE
    row_freq = jnp.where(row_index < MSIDE // 2, row_index, GRID - MSIDE + row_index)
    place = jnp.arange(GRID, dtype=jnp.int32)[:, None]
    row_angle = ((place * row_freq[None, :]) % GRID).astype(F32) * (2.0 * math.pi / GRID)
    col_angle = ((place * col_freq[None, :]) % GRID).astype(F32) * (2.0 * math.pi / GRID)
    row_cos, row_sin = jnp.cos(row_angle) / GRID, jnp.sin(row_angle) / GRID
    first = jnp.where(imag[None, :], -row_sin, row_cos)
    second = jnp.where(imag[None, :], -row_cos, -row_sin)
    return first, second, jnp.cos(col_angle), jnp.sin(col_angle)


def table_kernel(first_ref, second_ref, cos_ref, sin_ref, f_ref, ft_ref):
    for h in range(first_ref.shape[0]):
        tile = first_ref[h : h + 1, :] * cos_ref[...] + second_ref[h : h + 1, :] * sin_ref[...]
        f_ref[h * GRID : (h + 1) * GRID, :] = tile.astype(BF16)
    for h in range(0, first_ref.shape[0], 2):
        tile = f_ref[h * GRID : (h + 2) * GRID, :].astype(F32)
        ft_ref[:, h * GRID : (h + 2) * GRID] = tile.T.astype(BF16)


def make_tables():
    first, second, cosine, sine = lax.optimization_barrier(small_tables())
    rows = 8
    n = 2 * MODES
    return pl.pallas_call(
        table_kernel,
        grid=(GRID // rows,),
        in_specs=[
            pl.BlockSpec((rows, n), lambda i: (i, 0)),
            pl.BlockSpec((rows, n), lambda i: (i, 0)),
            whole((GRID, n)),
            whole((GRID, n)),
        ],
        out_specs=[
            pl.BlockSpec((rows * GRID, n), lambda i: (i, 0)),
            pl.BlockSpec((n, rows * GRID), lambda i: (0, i)),
        ],
        out_shape=[
            jax.ShapeDtypeStruct((NPIX, n), BF16),
            jax.ShapeDtypeStruct((n, NPIX), BF16),
        ],
        compiler_params=params(),
        cost_estimate=pl.CostEstimate(
            flops=4 * NPIX * n, bytes_accessed=4 * NPIX * n, transcendentals=0
        ),
        name="tables",
    )(first, second, cosine, sine)


def pack_kernel(w_ref, o_ref):
    for q in range(QUAD):
        for r in range(2):
            lane = q * LANES + r * C
            o_ref[0, :, lane : lane + C] = w_ref[0, q, r].astype(BF16)


def pack_weights(spec_weight):
    modes = spec_weight.shape[1]
    return pl.pallas_call(
        pack_kernel,
        grid=(modes // QUAD,),
        in_specs=[pl.BlockSpec((1, QUAD, 2, C, C), lambda g: (0, g, 0, 0, 0))],
        out_specs=pl.BlockSpec((1, C, QUAD * LANES), lambda g: (g, 0, 0)),
        out_shape=jax.ShapeDtypeStruct((modes // QUAD, C, QUAD * LANES), BF16),
        compiler_params=params(),
        cost_estimate=pl.CostEstimate(
            flops=modes * 4608, bytes_accessed=modes * 4608 * 6, transcendentals=0
        ),
        name="pack",
    )(spec_weight)


def build_kernel(ids_ref, w0, w1, w2, w3, l0, l1, l2, l3, pq_ref, lt_ref, lb_ref, wsc, lsc):
    own = ids_ref[0]
    shard = ids_ref[1]
    quads = w0.shape[0]
    for t, (w, line) in enumerate(((w0, l0), (w1, l1), (w2, l2), (w3, l3))):
        slot = jnp.bitwise_xor(own, t)
        wsc[slot] = w[...]
        lsc[slot] = line[...]

    for k in range(4):
        flip = flip_of(own, k)

        def step(g, carry):
            for q in range(QUAD):
                mode = shard * (quads * QUAD) + g * QUAD + q
                scale = mode_factor(mode) * flip
                p = wsc[k, g, :, q * LANES : (q + 1) * LANES].astype(F32) * scale
                low = jnp.concatenate([-p[:, C:], p[:, :C]], axis=1)
                pq_ref[k, g * QUAD + q] = jnp.concatenate([p, low], axis=0).astype(BF16)
            return carry

        lax.fori_loop(0, quads, step, 0)

    for t in range(4):
        for u in range(4):
            k = t ^ u
            block = lsc[k].astype(F32) * (flip_of(own, k) * sgn(t, k))
            lb_ref[t * C : (t + 1) * C, u * C : (u + 1) * C] = block.astype(BF16)
            lt_ref[u * C : (u + 1) * C, t * C : (t + 1) * C] = block.T.astype(BF16)


def build_weights(ids, packs, lines):
    quads = packs[0].shape[0]
    modes = quads * QUAD
    return pl.pallas_call(
        build_kernel,
        in_specs=[pl.BlockSpec(memory_space=SMEM)]
        + [pl.BlockSpec(memory_space=pltpu.MemorySpace.VMEM)] * 8,
        out_shape=[
            jax.ShapeDtypeStruct((4, modes, LANES, LANES), BF16),
            jax.ShapeDtypeStruct((4 * C, 4 * C), BF16),
            jax.ShapeDtypeStruct((4 * C, 4 * C), BF16),
        ],
        scratch_shapes=[
            pltpu.VMEM((4, quads, C, QUAD * LANES), BF16),
            pltpu.VMEM((4, C, C), BF16),
        ],
        compiler_params=params(),
        cost_estimate=pl.CostEstimate(
            flops=modes * 4 * 40000, bytes_accessed=modes * 4 * 30000, transcendentals=0
        ),
        name="build",
    )(ids, *packs, *lines)


def spread(acc, rsc, outs, shard):
    samples = acc.shape[0]
    modes = rsc.shape[1]
    rows = []
    for s in range(samples):
        for t in range(4):
            for r in range(2):
                rows.append(acc[s, t * C : (t + 1) * C, r * MODES : (r + 1) * MODES])
    turned = jnp.concatenate(rows, axis=0).T
    rsc[...] = turned.reshape(rsc.shape)
    for x, out in enumerate(outs):
        out[...] = rsc[jnp.bitwise_xor(shard, x)].astype(BF16)


def collect(blocks, rsc, ysc, shard):
    samples = ysc.shape[0]
    for x, block in enumerate(blocks):
        rsc[jnp.bitwise_xor(shard, x)] = block[...].astype(F32)
    turned = rsc[...].reshape(MODES, rsc.shape[2]).T
    for s in range(samples):
        for t in range(4):
            for r in range(2):
                row = ((s * 4 + t) * 2 + r) * C
                ysc[s, t * C : (t + 1) * C, r * MODES : (r + 1) * MODES] = turned[
                    row : row + C
                ].astype(BF16)


def forward_kernel(shards, ids_ref, inv_ref, *refs):
    x = refs[:4]
    f_ref = refs[4]
    outs = refs[5 : 5 + shards]
    acc, rsc = refs[5 + shards :]
    i = pl.program_id(0)
    for s in range(acc.shape[0]):
        low = [(x[t][s, 0].astype(F32) * inv_ref[s]).astype(BF16) for t in range(4)]
        part = dot(jnp.concatenate(low, axis=0), f_ref[...])

        @pl.when(i == 0)
        def _():
            acc[s] = part

        @pl.when(i > 0)
        def _():
            acc[s] += part

    @pl.when(i == pl.num_programs(0) - 1)
    def _():
        spread(acc, rsc, outs, ids_ref[1])


def forward_spectrum(ids, inv, x, table, shards):
    samples = x[0].shape[0]
    modes = MODES // shards
    width = samples * 4 * LANES
    n = 2 * MODES
    return pl.pallas_call(
        partial(forward_kernel, shards),
        grid=(NPIX // TILE,),
        in_specs=[pl.BlockSpec(memory_space=SMEM)] * 2
        + [pl.BlockSpec((samples, 1, C, TILE), lambda i: (0, 0, 0, i))] * 4
        + [pl.BlockSpec((TILE, n), lambda i: (i, 0))],
        out_specs=[whole((modes, width))] * shards,
        out_shape=[jax.ShapeDtypeStruct((modes, width), BF16)] * shards,
        scratch_shapes=[
            pltpu.VMEM((samples, 4 * C, n), F32),
            pltpu.VMEM((shards, modes, width), F32),
        ],
        compiler_params=params(),
        cost_estimate=pl.CostEstimate(
            flops=2 * samples * 4 * C * NPIX * n, bytes_accessed=8_000_000, transcendentals=0
        ),
        name="forward",
    )(ids, inv, *x, table)


def rows_of(sc, mode, samples, shards):
    at = pl.ds(pl.multiple_of(mode * shards, shards), shards)
    line = jnp.concatenate([sc[n, at, :] for n in range(sc.shape[0])], axis=1)
    parts = []
    for t in range(4):
        for s in range(samples):
            lane = (s * 4 + t) * LANES
            parts.append(line[:, lane : lane + LANES])
    return jnp.concatenate(parts, axis=0)


def gather_rows(blocks, sc):
    shards = len(blocks)
    modes = blocks[0].shape[0]
    for x, block in enumerate(blocks):
        for n in range(sc.shape[0]):
            sc[n, pl.ds(x, modes, stride=shards), :] = block[:, n * 128 : (n + 1) * 128].astype(F32)


def row_scratch(modes, shards, width):
    return pltpu.VMEM((width // 128, modes * shards, 128), F32)


def mix_kernel(shards, samples, back, *refs):
    blocks = refs[:shards]
    pq_ref = refs[shards]
    outs = refs[shards + 1 : 2 * shards + 1]
    xsc, ysc = refs[2 * shards + 1 :]
    modes = xsc.shape[1] // shards
    group = samples * shards
    gather_rows(blocks, xsc)

    def step(m, carry):
        low = rows_of(xsc, m, samples, shards).astype(BF16)
        total = [None] * 4
        for k in range(4):
            part = dot(low, pq_ref[k, m], ((1,), (1,)) if back else ((1,), (0,)))
            for t in range(4):
                u = t ^ k
                piece = part[t * group : (t + 1) * group]
                sign = sgn(u, k) if back else sgn(t, k)
                if total[u] is None:
                    total[u] = piece if sign > 0 else -piece
                else:
                    total[u] = total[u] + piece if sign > 0 else total[u] - piece
        lanes = []
        for s in range(samples):
            for u in range(4):
                lanes.append(total[u][s * shards : (s + 1) * shards])
        line = jnp.concatenate(lanes, axis=1)
        at = pl.ds(pl.multiple_of(m * shards, shards), shards)
        for n in range(ysc.shape[0]):
            ysc[n, at, :] = line[:, n * 128 : (n + 1) * 128]
        return carry

    lax.fori_loop(0, modes, step, 0, unroll=2)
    for x, out in enumerate(outs):
        for n in range(ysc.shape[0]):
            piece = ysc[n, pl.ds(x, modes, stride=shards), :]
            out[:, n * 128 : (n + 1) * 128] = piece.astype(BF16)


def mix(blocks, pq, samples, back):
    shards = len(blocks)
    modes, width = blocks[0].shape
    vmem = pl.BlockSpec(memory_space=pltpu.MemorySpace.VMEM)
    return pl.pallas_call(
        partial(mix_kernel, shards, samples, back),
        in_specs=[vmem] * (shards + 1),
        out_specs=[vmem] * shards,
        out_shape=[jax.ShapeDtypeStruct((modes, width), BF16)] * shards,
        scratch_shapes=[row_scratch(modes, shards, width)] * 2,
        compiler_params=params(),
        cost_estimate=pl.CostEstimate(
            flops=modes * 4 * 2 * 64 * 96 * 96, bytes_accessed=4_000_000, transcendentals=0
        ),
        name="mix_back" if back else "mix",
    )(*blocks, pq)


def grad_kernel(shards, samples, ids_ref, *refs):
    x_blocks = refs[:shards]
    g_blocks = refs[shards : 2 * shards]
    outs = refs[2 * shards : 2 * shards + 4]
    xsc, gsc, osc = refs[2 * shards + 4 :]
    modes = xsc.shape[1] // shards
    group = samples * shards
    own = ids_ref[0]
    first_mode = ids_ref[1] * modes
    gather_rows(x_blocks, xsc)
    gather_rows(g_blocks, gsc)

    def step(quad, carry):
        for q in range(QUAD):
            m = quad * QUAD + q
            x = rows_of(xsc, m, samples, shards)
            g = rows_of(gsc, m, samples, shards)
            turned = jnp.concatenate([g[:, C:], -g[:, :C]], axis=1)
            left = jnp.concatenate([x[:, :C], x[:, C:]], axis=0).astype(BF16)
            factor = mode_factor(first_mode + m)
            for k in range(4):
                rows = []
                for source in (g, turned):
                    for t in range(4):
                        u = t ^ k
                        piece = source[u * group : (u + 1) * group]
                        rows.append(piece if sgn(t, k) > 0 else -piece)
                right = jnp.concatenate(rows, axis=0).astype(BF16)
                grad = dot(left, right, ((0,), (0,))) * (factor * flip_of(own, k))
                osc[k, quad, :, q * LANES : (q + 1) * LANES] = grad.astype(BF16)
        return carry

    lax.fori_loop(0, modes // QUAD, step, 0)
    for t, out in enumerate(outs):
        out[...] = osc[jnp.bitwise_xor(own, t)]


def weight_grads(ids, x_blocks, g_blocks, samples):
    shards = len(x_blocks)
    modes, width = x_blocks[0].shape
    vmem = pl.BlockSpec(memory_space=pltpu.MemorySpace.VMEM)
    shape = (modes // QUAD, C, QUAD * LANES)
    return pl.pallas_call(
        partial(grad_kernel, shards, samples),
        in_specs=[pl.BlockSpec(memory_space=SMEM)] + [vmem] * (2 * shards),
        out_specs=[vmem] * 4,
        out_shape=[jax.ShapeDtypeStruct(shape, BF16)] * 4,
        scratch_shapes=[row_scratch(modes, shards, width)] * 2
        + [pltpu.VMEM((4,) + shape, BF16)],
        compiler_params=params(),
        cost_estimate=pl.CostEstimate(
            flops=modes * 4 * 2 * 128 * 96 * 96, bytes_accessed=4_000_000, transcendentals=0
        ),
        name="weight_grads",
    )(ids, *x_blocks, *g_blocks)


def pixel_kernel(shards, ids_ref, inv_ref, *refs):
    x = refs[:4]
    cot = refs[4:8]
    y = refs[8 : 8 + shards]
    f_ref, ft_ref, lt_ref = refs[8 + shards : 11 + shards]
    refs = refs[11 + shards :]
    outs = refs[:4]
    g_ref = refs[4]
    g_outs = refs[5 : 5 + shards]
    lin_ref = refs[5 + shards]
    ysc, rsc, pre, low, gacc, lacc = refs[6 + shards :]
    i = pl.program_id(0)
    s = pl.program_id(1)
    own = ids_ref[0]
    shard = ids_ref[1]
    inv = inv_ref[s]
    start = jnp.logical_and(i == 0, s == 0)

    @pl.when(start)
    def _():
        collect(y, rsc, ysc, shard)

    for t in range(4):
        low[t * C : (t + 1) * C] = (x[t][0, 0].astype(F32) * inv).astype(BF16)
    pre[...] = dot(ysc[s], ft_ref[...]) + dot(lt_ref[...], low[...])

    for t in range(4):
        for c in range(0, C, ROWS):
            v = pre[t * C + c : t * C + c + ROWS]
            phi = jnp.exp(v * v * -0.5) * (1.0 / math.sqrt(2.0 * math.pi))
            cdf = 0.5 + 0.5 * lax.erf(v * (1.0 / math.sqrt(2.0)))
            normed = x[t][0, 0, c : c + ROWS].astype(F32) * inv
            outs[t][0, 0, c : c + ROWS] = (normed + v * cdf).astype(BF16)
            grad = cot[t][0, 0, c : c + ROWS].astype(F32) * (cdf + v * phi)
            g_ref[0, t * C + c : t * C + c + ROWS] = grad.astype(BF16)

    g = g_ref[0]
    part = dot(g, f_ref[...])
    lin = dot(low[...], g, ((1,), (1,)))

    @pl.when(i == 0)
    def _():
        gacc[s] = part

    @pl.when(i > 0)
    def _():
        gacc[s] += part

    @pl.when(start)
    def _():
        lacc[...] = lin

    @pl.when(jnp.logical_not(start))
    def _():
        lacc[...] += lin

    @pl.when(jnp.logical_and(i == pl.num_programs(0) - 1, s == pl.num_programs(1) - 1))
    def _():
        spread(gacc, rsc, g_outs, shard)
        for k in range(4):
            total = None
            for t in range(4):
                u = t ^ k
                piece = lacc[t * C : (t + 1) * C, u * C : (u + 1) * C] * sgn(t, k)
                total = piece if total is None else total + piece
            lin_ref[k] = total * flip_of(own, k)


def pixels(ids, inv, x, cot, y, table, turned, lt):
    samples = x[0].shape[0]
    shards = len(y)
    modes, width = y[0].shape
    n = 2 * MODES
    tile = TILE // 2
    block = pl.BlockSpec((1, 1, C, tile), lambda i, s: (s, 0, 0, i))
    block_shape = jax.ShapeDtypeStruct((samples, 1, C, NPIX), BF16)
    return pl.pallas_call(
        partial(pixel_kernel, shards),
        grid=(NPIX // tile, samples),
        in_specs=[pl.BlockSpec(memory_space=SMEM)] * 2
        + [block] * 8
        + [whole((modes, width))] * shards
        + [
            pl.BlockSpec((tile, n), lambda i, s: (i, 0)),
            pl.BlockSpec((n, tile), lambda i, s: (0, i)),
            whole((4 * C, 4 * C)),
        ],
        out_specs=[block] * 4
        + [pl.BlockSpec((1, 4 * C, tile), lambda i, s: (s, 0, i))]
        + [whole((modes, width))] * shards
        + [whole((4, C, C))],
        out_shape=[block_shape] * 4
        + [jax.ShapeDtypeStruct((samples, 4 * C, NPIX), BF16)]
        + [jax.ShapeDtypeStruct((modes, width), BF16)] * shards
        + [jax.ShapeDtypeStruct((4, C, C), F32)],
        scratch_shapes=[
            pltpu.VMEM((samples, 4 * C, n), BF16),
            pltpu.VMEM((shards, modes, width), F32),
            pltpu.VMEM((4 * C, tile), F32),
            pltpu.VMEM((4 * C, tile), BF16),
            pltpu.VMEM((samples, 4 * C, n), F32),
            pltpu.VMEM((4 * C, 4 * C), F32),
        ],
        compiler_params=params(),
        cost_estimate=pl.CostEstimate(
            flops=4 * samples * 4 * C * NPIX * n,
            bytes_accessed=20_000_000,
            transcendentals=2 * samples * 4 * C * NPIX,
        ),
        name="pixels",
    )(ids, inv, *x, *cot, *y, table, turned, lt)


def inner_kernel(shards, ids_ref, *refs):
    blocks = refs[:shards]
    g_ref, ft_ref, lb_ref = refs[shards : shards + 3]
    outs = refs[shards + 3 : shards + 7]
    ysc, rsc = refs[shards + 7 :]
    i = pl.program_id(0)
    s = pl.program_id(1)

    @pl.when(jnp.logical_and(i == 0, s == 0))
    def _():
        collect(blocks, rsc, ysc, ids_ref[1])

    total = dot(ysc[s], ft_ref[...]) + dot(lb_ref[...], g_ref[0])
    for t in range(4):
        outs[t][0, 0] = total[t * C : (t + 1) * C].astype(BF16)


def inner_grads(ids, blocks, g, turned, lb):
    samples = g.shape[0]
    shards = len(blocks)
    modes, width = blocks[0].shape
    n = 2 * MODES
    tile = TILE
    block = pl.BlockSpec((1, 1, C, tile), lambda i, s: (s, 0, 0, i))
    return pl.pallas_call(
        partial(inner_kernel, shards),
        grid=(NPIX // tile, samples),
        in_specs=[pl.BlockSpec(memory_space=SMEM)]
        + [whole((modes, width))] * shards
        + [
            pl.BlockSpec((1, 4 * C, tile), lambda i, s: (s, 0, i)),
            pl.BlockSpec((n, tile), lambda i, s: (0, i)),
            whole((4 * C, 4 * C)),
        ],
        out_specs=[block] * 4,
        out_shape=[jax.ShapeDtypeStruct((samples, 1, C, NPIX), BF16)] * 4,
        scratch_shapes=[
            pltpu.VMEM((samples, 4 * C, n), BF16),
            pltpu.VMEM((shards, modes, width), F32),
        ],
        compiler_params=params(),
        cost_estimate=pl.CostEstimate(
            flops=3 * samples * 4 * C * NPIX * n, bytes_accessed=10_000_000, transcendentals=0
        ),
        name="inner_grads",
    )(ids, *blocks, g, turned, lb)


def place_kernel(ids_ref, part_ref, *refs):
    refs[-1][...] = part_ref[...]


def place_output(own, parts, total):
    samples = parts[0].shape[0]
    result = None
    for t, part in enumerate(parts):
        slot = jnp.bitwise_xor(own, t).reshape(1)
        extra = [] if result is None else [result]
        result = pl.pallas_call(
            place_kernel,
            grid_spec=pltpu.PrefetchScalarGridSpec(
                num_scalar_prefetch=1,
                grid=(samples,),
                in_specs=[pl.BlockSpec((1, 1, C, NPIX), lambda s, ids: (s, 0, 0, 0))]
                + [pl.BlockSpec(memory_space=pl.ANY)] * len(extra),
                out_specs=pl.BlockSpec(
                    (1, 1, C, NPIX), lambda s, ids: (ids[0] * samples + s, 0, 0, 0)
                ),
            ),
            out_shape=jax.ShapeDtypeStruct((total, 1, C, NPIX), BF16),
            input_output_aliases={2: 0} if extra else {},
            compiler_params=params(),
            cost_estimate=pl.CostEstimate(
                flops=0, bytes_accessed=4 * samples * C * NPIX, transcendentals=0
            ),
            name="place",
        )(slot, part, *extra)
    return result


def final_kernel(ids_ref, inv_ref, cot_ref, part_ref, *refs):
    inv = inv_ref[ids_ref[0] * pl.num_programs(0) + pl.program_id(0)]
    refs[-1][...] = (cot_ref[...].astype(F32) + part_ref[...].astype(F32)) * inv


def final_grads(own, inv, cotangent, parts):
    samples = parts[0].shape[0]
    result = None
    for t, part in enumerate(parts):
        slot = jnp.bitwise_xor(own, t).reshape(1)
        extra = [] if result is None else [result]
        place = pl.BlockSpec(
            (1, 1, C, NPIX // 2), lambda s, i, ids, inv: (ids[0] * samples + s, 0, 0, i)
        )
        result = pl.pallas_call(
            final_kernel,
            grid_spec=pltpu.PrefetchScalarGridSpec(
                num_scalar_prefetch=2,
                grid=(samples, 2),
                in_specs=[
                    place,
                    pl.BlockSpec((1, 1, C, NPIX // 2), lambda s, i, ids, inv: (s, 0, 0, i)),
                ]
                + [pl.BlockSpec(memory_space=pl.ANY)] * len(extra),
                out_specs=place,
            ),
            out_shape=jax.ShapeDtypeStruct(cotangent.shape, F32),
            input_output_aliases={4: 0} if extra else {},
            compiler_params=params(),
            cost_estimate=pl.CostEstimate(
                flops=0, bytes_accessed=8 * samples * C * NPIX, transcendentals=0
            ),
            name="final",
        )(slot, inv, cotangent, part, *extra)
    return result


def adamw(weight, first, second, grad):
    first_new = BETA_ONE * first + (1.0 - BETA_ONE) * grad
    second_new = BETA_TWO * second + (1.0 - BETA_TWO) * grad * grad
    corr_one = 1.0 - BETA_ONE**STEP_COUNT
    corr_two = 1.0 - BETA_TWO**STEP_COUNT
    update = first_new / corr_one / (jnp.sqrt(second_new / corr_two) + EPSILON)
    return (weight - RATE * (update + DECAY * weight), first_new, second_new)


def adam_kernel(d0, d1, d2, d3, w_ref, first_ref, second_ref, w_out, first_out, second_out):
    grad = d0[0].astype(F32) + d1[0].astype(F32) + d2[0].astype(F32) + d3[0].astype(F32)
    for q in range(QUAD):
        for r in range(2):
            lane = q * LANES + r * C
            at = (0, q, r)
            new = adamw(w_ref[at], first_ref[at], second_ref[at], grad[:, lane : lane + C])
            w_out[at], first_out[at], second_out[at] = new


def adam_spec(grads, weight, first, second):
    modes = weight.shape[1]
    packed = pl.BlockSpec((1, C, QUAD * LANES), lambda g: (g, 0, 0))
    block = pl.BlockSpec((1, QUAD, 2, C, C), lambda g: (0, g, 0, 0, 0))
    return pl.pallas_call(
        adam_kernel,
        grid=(modes // QUAD,),
        in_specs=[packed] * 4 + [block] * 3,
        out_specs=[block] * 3,
        out_shape=[jax.ShapeDtypeStruct(weight.shape, F32)] * 3,
        compiler_params=params(),
        cost_estimate=pl.CostEstimate(
            flops=modes * 4608 * 20, bytes_accessed=modes * 4608 * 72, transcendentals=modes * 4608
        ),
        name="adam",
    )(*grads, weight, first, second)


def swap(value, axis, size, x):
    return lax.ppermute(value, axis, [(i, i ^ x) for i in range(size)])


def exchange(values, axis):
    size = len(values)
    return [values[0]] + [swap(values[x], axis, size, x) for x in range(1, size)]


def after(values, first):
    values, _ = lax.optimization_barrier((values, first))
    return values


def body(
    shards,
    inputs,
    cotangent,
    norm_table,
    sample_index,
    spec_weight,
    spec_first,
    spec_second,
    lin_weight,
    lin_first,
    lin_second,
):
    own = lax.axis_index("blade")
    shard = lax.axis_index("dp")
    ids = jnp.stack([own, shard]).astype(jnp.int32)
    total = inputs.shape[0]
    samples = total // 4

    def cut(array):
        return [
            lax.dynamic_slice_in_dim(array, jnp.bitwise_xor(own, t) * samples, samples, 0)
            for t in range(4)
        ]

    x = exchange(cut(inputs), "blade")

    matches = sample_index[:, None] == jnp.arange(NTAB, dtype=jnp.int32)[None, :]
    normalizer = jnp.sum(jnp.where(matches, norm_table[None, :], 0.0), axis=1)
    inv_all = 1.0 / normalizer
    inv = lax.dynamic_slice_in_dim(inv_all, own * samples, samples, 0)

    table, turned = make_tables()
    packed = pack_weights(spec_weight)
    line = lin_weight[0].astype(BF16)
    packed, line = after((packed, line), x)
    packs = [packed] + [swap(packed, "blade", 4, t) for t in range(1, 4)]
    lines = [line] + [swap(line, "blade", 4, t) for t in range(1, 4)]
    cot = exchange(after(cut(cotangent), packs), "blade")

    modes_sent = forward_spectrum(ids, inv, x, table, shards)
    modes_got = exchange(modes_sent, "dp")
    pq, lt, lb = build_weights(ids, packs, lines)
    y = exchange(mix(modes_got, pq, samples, False), "dp")

    result = pixels(ids, inv, x, cot, y, table, turned, lt)
    out_parts, grad_pre = result[:4], result[4]
    grads_sent, lin_parts = result[5 : 5 + shards], result[5 + shards]

    grads_got = exchange(grads_sent, "dp")
    out_parts = exchange(out_parts, "blade")
    back = exchange(mix(grads_got, pq, samples, True), "dp")
    spec_grads = weight_grads(ids, modes_got, grads_got, samples)
    spec_grads = exchange(spec_grads, "blade")

    lin_grads = [
        lax.dynamic_index_in_dim(lin_parts, jnp.bitwise_xor(own, t), 0, keepdims=False)
        for t in range(4)
    ]
    lin_grads = exchange(lin_grads, "blade")
    lin_grad = lin_grads[0] + lin_grads[1] + lin_grads[2] + lin_grads[3]
    step = 1
    while step < shards:
        lin_grad = lin_grad + swap(lin_grad, "dp", shards, step)
        step *= 2

    inner = exchange(inner_grads(ids, back, grad_pre, turned, lb), "blade")

    output = place_output(own, out_parts, total)
    spec_out = adam_spec(spec_grads, spec_weight, spec_first, spec_second)
    lin_out = adamw(lin_weight, lin_first, lin_second, lin_grad[None])
    input_grad = final_grads(own, inv_all, cotangent, inner)
    return (output, input_grad, *spec_out, *lin_out)


def solution(mesh):
    fields = P("dp", "blade", None, None)
    spec = P("blade", "dp", None, None, None)
    lin = P("blade", None, None)
    return jax.shard_map(
        partial(body, mesh.shape["dp"]),
        mesh=mesh,
        in_specs=(fields, fields, P(), P("dp"), spec, spec, spec, lin, lin, lin),
        out_specs=(fields, fields, spec, spec, spec, lin, lin, lin),
        check_vma=False,
    )
```

time: 705 us -> 322 us (0.46)
  waiting for transfers between devices: 405 us -> 110 us
  matrix products: 128 us -> 0 us
  Pallas kernels: 0 us -> 119 us
  starting transfers between devices: 1.33 us -> 70.8 us
  local copies, waits for them, and re-layouts: 69 us -> 14.3 us
  blocking collectives: 37.4 us -> 0 us
  other arithmetic: 41 us -> 4.72 us
  between operations: 14.8 us -> 1.13 us
    all_gather x5 -> x0, waiting for transfers between devices: 347 us -> none  [the longest x1 115 us: body(): lax.all_gather(grad_pre, 'blade', axis=1, tiled=True)]
    dot_general x24 -> x0, matrix products: 128 us -> none  [the longest x1 23.2 us: body(): jnp.einsum('sjcp,sjop->co', normed_all, mixed_pre, preferred_element_type...]
    pallas_call x0 -> x18, Pallas kernels: none -> 119 us  [the longest x1 21.6 us: pixels(): pl.pallas_call(partial(pixel_kernel, shards), grid=(NPIX // tile, samples...]
    ppermute x0 -> x55, waiting for transfers between devices: none -> 110 us  [swap(): return lax.ppermute(value, axis, [(i, i ^ x) for i in range(size)])]
    ppermute x0 -> x55, starting transfers between devices: none -> 70.8 us  [swap(): return lax.ppermute(value, axis, [(i, i ^ x) for i in range(size)])]
    unnamed x11 -> x0, waiting for transfers between devices: 58 us -> none
    unnamed x49 -> x108, local copies, waits for them, and re-layouts: 38.6 us -> 7.48 us
    psum x1 -> x0, blocking collectives: 28.5 us -> none  [body(): lin_grad = lax.psum(lin_grad, 'dp')]
  transfers between devices with their start and end apart: 8 -> 55, of which waited for: 7 -> 22; matrix products, arithmetic and copies ran while one was open for 11% -> 2% of each run, Pallas kernels for 0% -> 29%
where the time goes in v1:
time: 322 us; the launch traced here: 320 us
  Pallas kernels  119 us (37%)
  waiting for transfers between devices  110 us (34%)
  starting transfers between devices  70.8 us (22%)
  local copies, waits for them, and re-layouts  14.3 us (4%)
  other arithmetic  4.72 us (1%)
    ppermute x55, waiting for transfers between devices, swap(): return lax.ppermute(value, axis, [(i, i ^ x) for i in range(size)])  110 us
    ppermute x55, starting transfers between devices, swap(): return lax.ppermute(value, axis, [(i, i ^ x) for i in range(size)])  70.8 us
    pallas_call x1, Pallas kernels, pixels(): pl.pallas_call(partial(pixel_kernel, shards), grid=(NPIX // tile, samples...  21.6 us
    pallas_call x4, Pallas kernels, final_grads(): pl.pallas_call(final_kernel, grid_spec=pltpu.PrefetchScalarGridSpec(num_s...  17.4 us
    pallas_call x2, Pallas kernels, mix(): pl.pallas_call(partial(mix_kernel, shards, samples, back), in_specs=[vmem...  17.3 us
    pallas_call x1, Pallas kernels, build_weights(): pl.pallas_call(build_kernel, in_specs=[pl.BlockSpec(memory_space=SMEM)] +...  11.2 us
    pallas_call x1, Pallas kernels, inner_grads(): pl.pallas_call(partial(inner_kernel, shards), grid=(NPIX // tile, samples...  9.52 us
    pallas_call x1, Pallas kernels, adam_spec(): pl.pallas_call(adam_kernel, grid=(modes // QUAD,), in_specs=[packed] * 4...  8.17 us
  transfers between devices with their start and end apart: 55, of which 22 were waited for; matrix products, arithmetic and copies ran while one was open for 2% of the time, Pallas kernels for 29%

profile of v1, /device:TPU:0, one launch (start us, length us, event | category | flops | bytes accessed | tf_op | source)
XLA Modules:
  0.0 319.9 jit_solution(13295541375197762508)
XLA Ops:
  0.7 3.7 %constant_dynamic-slice_fusion.4 = (bf16[2,1,48,4096]{3,2,1,0:T(8,128)(2,1)}, bf16[2,1,48,4096]{3,2,1,0:T(8,128)(2,1)}, bf16[2,1,48,4096]{3,2,1,0:T(8,128)(2,1)}, bf16[2,1,48,4096]{3,2,1,0:T(8,128)(2,1)}) fusion(bf16[8,1,48,4096]{3,2,1,0:T(8,128)(2,1)} %param.10, s32[]{:T(128)S(6)} %select_n.109, s32[]{:T(128)S(6)} %select_n.107, s32[]{:T(128)S(6)} %select_n.106, ...), kind=kLoop, calls=%fused_computation.49 | loop fusion | bytes 6291472 | tf_op jit(solution)/shard_map/dynamic_slice | solution.py:708
  8.9 5.5 %pack.1.w0 = bf16[8,48,384]{2,1,0:T(8,128)(2,1)} custom-call(f32[1,32,2,48,48]{4,3,2,1,0:T(8,128)} %w_ref.3), custom_call_target="tpu_custom_call" | custom-call | flops 147456 | bytes 884736 | tf_op jit(solution)/shard_map/pack/pallas_call | solution.py:124
  17.4 8.6 %collective-permute-done.refs_1_ = bf16[2,1,48,4096]{3,2,1,0:T(8,128)(2,1)} collective-permute-done((bf16[2,1,48,4096]{3,2,1,0:T(8,128)(2,1)}, bf16[2,1,48,4096]{3,2,1,0:T(8,128)(2,1)}, u32[]{:S(2)}, u32[]{:S(2)}) %collective-permute-start) | collective-permute-done | bytes 786464 | tf_op jit(solution)/shard_map/ppermute | solution.py:674
  26.0 17.5 %collective-permute-done.1.refs_2_ = bf16[2,1,48,4096]{3,2,1,0:T(8,128)(2,1)} collective-permute-done((bf16[2,1,48,4096]{3,2,1,0:T(8,128)(2,1)}, bf16[2,1,48,4096]{3,2,1,0:T(8,128)(2,1)}, u32[]{:S(2)}, u32[]{:S(2)}) %collective-permute-start.1) | collective-permute-done | bytes 786464 | tf_op jit(solution)/shard_map/ppermute | solution.py:674
  48.4 5.0 %collective-permute-done.3.w1 = bf16[8,48,384]{2,1,0:T(8,128)(2,1)S(1)} collective-permute-done((bf16[8,48,384]{2,1,0:T(8,128)(2,1)S(1)}, bf16[8,48,384]{2,1,0:T(8,128)(2,1)S(1)}, u32[]{:S(2)}, u32[]{:S(2)}) %collective-permute-start.3) | collective-permute-done | bytes 294944 | tf_op jit(solution)/shard_map/ppermute | solution.py:674
  53.5 5.2 %collective-permute-done.4.w2 = bf16[8,48,384]{2,1,0:T(8,128)(2,1)S(1)} collective-permute-done((bf16[8,48,384]{2,1,0:T(8,128)(2,1)S(1)}, bf16[8,48,384]{2,1,0:T(8,128)(2,1)S(1)}, u32[]{:S(2)}, u32[]{:S(2)}) %collective-permute-start.4) | collective-permute-done | bytes 294944 | tf_op jit(solution)/shard_map/ppermute | solution.py:674
  62.9 6.7 %tables.1 = (bf16[4096,512]{1,0:T(8,128)(2,1)}, bf16[512,4096]{1,0:T(8,128)(2,1)}) custom-call(f32[64,512]{1,0:T(8,128)} %get-tuple-element.77.first_ref, f32[64,512]{1,0:T(8,128)} %get-tuple-element.78.second_ref, f32[64,512]{1,0:T(8,128)} %get-tuple-element.79.cos_ref, f32[64,512]{1,0:T(8,128)} %get-tuple-element.80.sin_ref), custom_call_target="tpu_custom_call" | custom-call | flops 8388608 | bytes 8388608 | tf_op jit(solution)/shard_map/tables/pallas_call | solution.py:90
  70.1 6.8 %forward.1 = (bf16[32,768]{1,0:T(8,128)(2,1)}, bf16[32,768]{1,0:T(8,128)(2,1)}, bf16[32,768]{1,0:T(8,128)(2,1)}, bf16[32,768]{1,0:T(8,128)(2,1)}, bf16[32,768]{1...) custom-call(s32[2]{0:T(128)} %pad_add_fusion.ids_ref, ...), custom_call_target="tpu_custom_call" | custom-call | flops 1610612736 | bytes 8000000 | tf_op jit(solution)/shard_map/forward/pallas_call | solution.py:249
  79.2 12.6 %collective-permute-done.16.l1 = bf16[48,48]{1,0:T(8,128)(2,1)S(1)} collective-permute-done((bf16[48,48]{1,0:T(8,128)(2,1)S(1)}, bf16[48,48]{1,0:T(8,128)(2,1)S(1)}, u32[]{:S(2)}, u32[]{:S(2)}) %collective-permute-start.16) | collective-permute-done | bytes 4640 | tf_op jit(solution)/shard_map/ppermute | solution.py:674
  106.6 3.5 %collective-permute-start.14 = (bf16[32,768]{1,0:T(8,128)(2,1)}, bf16[32,768]{1,0:T(8,128)(2,1)S(1)}, u32[]{:S(2)}, u32[]{:S(2)}) collective-permute-start(bf16[32,768]{1,0:T(8,128)(2,1)} %get-tuple-element.88), channel_id=1, source_target_pairs={{0,6},{1,7},{2,4},{3,5},{4,2},{5,3},{6,0},{7,1},{8,14},{9,15},{10,... | collective-permute-start | bytes 147464 | tf_op jit(solution)/shard_map/ppermute | solution.py:674
  113.4 11.2 %build.1 = (bf16[4,32,96,96]{3,2,1,0:T(8,128)(2,1)}, bf16[192,192]{1,0:T(8,128)(2,1)}, bf16[192,192]{1,0:T(8,128)(2,1)}) custom-call(s32[2]{0:T(128)} %pad_add_fusion.ids_ref, bf16[8,48,384]{2,1,0:T(8,128)(2,1)} %pack.1.w0, bf16[8,48,384]{2,1,0:T(8,128)(2,1)} %copy-done.13, bf16[8,48,384]{2,1,0:T(8,128)(2,1)} %copy-done.14, bf16[8,48,384]{2,1,0:T(8,128)(2,1)} %copy-done.15, ...), custom_call_target="tpu_custom_call" | custom-call | flops 5120000 | bytes 3840000 | tf_op jit(solution)/shard_map/build/pallas_call | solution.py:172
  125.2 8.3 %mix.1 = (bf16[32,768]{1,0:T(8,128)(2,1)}, bf16[32,768]{1,0:T(8,128)(2,1)}, bf16[32,768]{1,0:T(8,128)(2,1)}, bf16[32,768]{1,0:T(8,128)(2,1)}, bf16[32,768]{1,0:T...) custom-call(bf16[32,768]{1,0:T(8,128)(2,1)} %get-tuple-element.82.refs_0_, ...), custom_call_target="tpu_custom_call" | custom-call | flops 150994944 | bytes 4000000 | tf_op jit(solution)/shard_map/mix/pallas_call | solution.py:335
  143.2 4.9 %collective-permute-start.24 = (bf16[32,768]{1,0:T(8,128)(2,1)}, bf16[32,768]{1,0:T(8,128)(2,1)S(1)}, u32[]{:S(2)}, u32[]{:S(2)}) collective-permute-start(bf16[32,768]{1,0:T(8,128)(2,1)} %get-tuple-element.98), channel_id=1, source_target_pairs={{0,6},{1,7},{2,4},{3,5},{4,2},{5,3},{6,0},{7,1},{8,14},{9,15},{10,... | collective-permute-start | bytes 147464 | tf_op jit(solution)/shard_map/ppermute | solution.py:674
  155.1 21.6 %pixels.1 = (bf16[2,1,48,4096]{3,2,1,0:T(8,128)(2,1)}, bf16[2,1,48,4096]{3,2,1,0:T(8,128)(2,1)}, bf16[2,1,48,4096]{3,2,1,0:T(8,128)(2,1)}, bf16[2,1,48,4096]{3,2...) custom-call(s32[2]{0:T(128)} %pad_add_fusion.ids_ref, ...), custom_call_target="tpu_custom_call" | custom-call | flops 3221225472 | bytes 20000000 | tf_op jit(solution)/shard_map/pixels/pallas_call | solution.py:482
  192.0 9.0 %mix_back.1 = (bf16[32,768]{1,0:T(8,128)(2,1)}, bf16[32,768]{1,0:T(8,128)(2,1)}, bf16[32,768]{1,0:T(8,128)(2,1)}, bf16[32,768]{1,0:T(8,128)(2,1)}, bf16[32,768]{...) custom-call(bf16[32,768]{1,0:T(8,128)(2,1)} %get-tuple-element.106.refs_0_.refs_8_, ...), custom_call_target="tpu_custom_call" | custom-call | flops 150994944 | bytes 4000000 | tf_op jit(solution)/shard_map/mix_back/pallas_call | solution.py:335
  211.8 7.7 %weight_grads.1 = (bf16[8,48,384]{2,1,0:T(8,128)(2,1)}, bf16[8,48,384]{2,1,0:T(8,128)(2,1)}, bf16[8,48,384]{2,1,0:T(8,128)(2,1)}, bf16[8,48,384]{2,1,0:T(8,128)(2,1)}) custom-call(s32[2]{0:T(128)} %pad_add_fusion.ids_ref, bf16[32,768]{1,0:T(8,128)(2,1)} %get-tuple-element.82.refs_0_, bf16[32,768]{1,0:T(8,128)(2,1)} %copy-done.23, ...), custom_call_target="tpu_custom_call" | custom-call | flops 301989888 | bytes 4000000 | tf_op jit(solution)/shard_map/weight_grads/pallas_call | solution.py:391
  229.4 9.5 %inner_grads.1 = (bf16[2,1,48,4096]{3,2,1,0:T(8,128)(2,1)}, bf16[2,1,48,4096]{3,2,1,0:T(8,128)(2,1)}, bf16[2,1,48,4096]{3,2,1,0:T(8,128)(2,1)}, bf16[2,1,48,4096]{3,2,1,0:T(8,128)(2,1)}) custom-call(s32[2]{0:T(128)} %pad_add_fusion.ids_ref, bf16[32,768]{1,0:T(8,128)(2,1)} %get-tuple-element.114.refs_0_, bf16[32,768]{1,0:T(8,128)(2,1)} %copy-done.45, ...), custom_call_target="tpu_custom_call" | custom-call | flops 2415919104 | bytes 10000000 | tf_op jit(solution)/shard_map/inner_grads/pallas_call | solution.py:543
  249.0 4.4 %final.4.refs_0_ = f32[8,1,48,4096]{3,2,1,0:T(8,128)} custom-call(s32[1]{0:T(128)} %bitcast.1.ids_ref, f32[8]{0:T(128)} %copy-done.44, bf16[8,1,48,4096]{3,2,1,0:T(8,128)(2,1)} %cot_ref.7, bf16[2,1,48,4096]{3,2,1,0:T(8,128)(2,1)} %get-tuple-element.127.part_ref), custom_call_target="tpu_custom_call" | custom-call | bytes 3145728 | tf_op jit(solution)/shard_map/final/pallas_call | solution.py:613
  253.3 8.2 %adam.1 = (f32[1,32,2,48,48]{4,3,2,1,0:T(8,128)}, f32[1,32,2,48,48]{4,3,2,1,0:T(8,128)}, f32[1,32,2,48,48]{4,3,2,1,0:T(8,128)}) custom-call(bf16[8,48,384]{2,1,0:T(8,128)(2,1)} %get-tuple-element.128.d0, bf16[8,48,384]{2,1,0:T(8,128)(2,1)} %copy-done.10, bf16[8,48,384]{2,1,0:T(8,128)(2,1)} %copy-done.11, bf16[8,48,384]{2,1,0:T(8,128)(2,1)} %copy-done.12, ...), custom_call_target="tpu_custom_call" | custom-call | flops 2949120 | bytes 10616832 | tf_op jit(solution)/shard_map/adam/pallas_call | solution.py:659
  263.4 13.1 %collective-permute-done.27.part_ref = bf16[2,1,48,4096]{3,2,1,0:T(8,128)(2,1)S(1)} collective-permute-done((bf16[2,1,48,4096]{3,2,1,0:T(8,128)(2,1)}, bf16[2,1,48,4096]{3,2,1,0:T(8,128)(2,1)S(1)}, u32[]{:S(2)}, u32[]{:S(2)}) %collective-permute-start.27) | collective-permute-done | bytes 786464 | tf_op jit(solution)/shard_map/ppermute | solution.py:674
  282.1 4.4 %final.5.refs_0_ = f32[8,1,48,4096]{3,2,1,0:T(8,128)} custom-call(s32[1]{0:T(128)} %bitcast.5.ids_ref, f32[8]{0:T(128)} %copy-done.44, bf16[8,1,48,4096]{3,2,1,0:T(8,128)(2,1)} %cot_ref.7, bf16[2,1,48,4096]{3,2,1,0:T(8,128)(2,1)} %copy-done.3, f32[8,1,48,4096]{3,2,1,0:T(8,128)} %final.4.refs_0_), custom_call_target="tpu_custom_call", output_to_operand_aliasing={{}: (4, {})} | custom-call | bytes 3145728 | tf_op jit(solution)/shard_map/final/pallas_call | solution.py:613
  286.4 23.0 %collective-permute-done.44.part_ref = bf16[2,1,48,4096]{3,2,1,0:T(8,128)(2,1)S(1)} collective-permute-done((bf16[2,1,48,4096]{3,2,1,0:T(8,128)(2,1)}, bf16[2,1,48,4096]{3,2,1,0:T(8,128)(2,1)S(1)}, u32[]{:S(2)}, u32[]{:S(2)}) %collective-permute-start.44) | collective-permute-done | bytes 786464 | tf_op jit(solution)/shard_map/ppermute | solution.py:674
  310.3 4.4 %final.6.refs_0_ = f32[8,1,48,4096]{3,2,1,0:T(8,128)} custom-call(s32[1]{0:T(128)} %bitcast.4.ids_ref, f32[8]{0:T(128)} %copy-done.44, bf16[8,1,48,4096]{3,2,1,0:T(8,128)(2,1)} %cot_ref.7, bf16[2,1,48,4096]{3,2,1,0:T(8,128)(2,1)} %copy-done.4, f32[8,1,48,4096]{3,2,1,0:T(8,128)} %final.5.refs_0_), custom_call_target="tpu_custom_call", output_to_operand_aliasing={{}: (4, {})} | custom-call | bytes 3145728 | tf_op jit(solution)/shard_map/final/pallas_call | solution.py:613
  315.5 4.4 %final.7 = f32[8,1,48,4096]{3,2,1,0:T(8,128)} custom-call(s32[1]{0:T(128)} %bitcast.ids_ref, f32[8]{0:T(128)} %copy-done.44, bf16[8,1,48,4096]{3,2,1,0:T(8,128)(2,1)} %cot_ref.7, bf16[2,1,48,4096]{3,2,1,0:T(8,128)(2,1)} %copy-done.2, f32[8,1,48,4096]{3,2,1,0:T(8,128)} %final.6.refs_0_), custom_call_target="tpu_custom_call", output_to_operand_aliasing={{}: (4, {})} | custom-call | bytes 3145728 | tf_op jit(solution)/shard_map/final/pallas_call | solution.py:613
  (228 shorter events, 109.8 us)
Async XLA Ops:
  4.4 21.6 %collective-permute-start = (bf16[2,1,48,4096]{3,2,1,0:T(8,128)(2,1)}, bf16[2,1,48,4096]{3,2,1,0:T(8,128)(2,1)}, u32[]{:S(2)}, u32[]{:S(2)}) collective-permute-start(bf16[2,1,48,4096]{3,2,1,0:T(8,128)(2,1)} %get-tuple-element.144), channel_id=1, source_target_pairs={{0,8},{8,0},{16,24},{24,16},{1,9},{9,1},{17,25},{25,17},{2,10},{10... | collective-permute-start | bytes 2359304 | tf_op jit(solution)/shard_map/ppermute | solution.py:674
  7.3 36.2 %collective-permute-start.1 = (bf16[2,1,48,4096]{3,2,1,0:T(8,128)(2,1)}, bf16[2,1,48,4096]{3,2,1,0:T(8,128)(2,1)}, u32[]{:S(2)}, u32[]{:S(2)}) collective-permute-start(bf16[2,1,48,4096]{3,2,1,0:T(8,128)(2,1)} %get-tuple-element.146), channel_id=1, source_target_pairs={{0,16},{8,24},{16,0},{24,8},{1,17},{9,25},{17,1},{25,9},{2,18},{10... | collective-permute-start | bytes 2359304 | tf_op jit(solution)/shard_map/ppermute | solution.py:674
  8.9 34.7 %collective-permute-start.2 = (bf16[2,1,48,4096]{3,2,1,0:T(8,128)(2,1)}, bf16[2,1,48,4096]{3,2,1,0:T(8,128)(2,1)}, u32[]{:S(2)}, u32[]{:S(2)}) collective-permute-start(bf16[2,1,48,4096]{3,2,1,0:T(8,128)(2,1)} %get-tuple-element.143), channel_id=1, source_target_pairs={{0,24},{8,16},{16,8},{24,0},{1,25},{9,17},{17,9},{25,1},{2,26},{10... | collective-permute-start | bytes 2359304 | tf_op jit(solution)/shard_map/ppermute | solution.py:674
  44.7 13.9 %collective-permute-start.4 = (bf16[8,48,384]{2,1,0:T(8,128)(2,1)S(1)}, bf16[8,48,384]{2,1,0:T(8,128)(2,1)S(1)}, u32[]{:S(2)}, u32[]{:S(2)}) collective-permute-start(bf16[8,48,384]{2,1,0:T(8,128)(2,1)S(1)} %copy-done.1), channel_id=1, source_target_pairs={{0,16},{8,24},{16,0},{24,8},{1,17},{9,25},{17,1},{25,9},{2,18},{10... | collective-permute-start | bytes 884744 | tf_op jit(solution)/shard_map/ppermute | solution.py:674
  45.6 13.1 %collective-permute-start.5 = (bf16[8,48,384]{2,1,0:T(8,128)(2,1)S(1)}, bf16[8,48,384]{2,1,0:T(8,128)(2,1)S(1)}, u32[]{:S(2)}, u32[]{:S(2)}) collective-permute-start(bf16[8,48,384]{2,1,0:T(8,128)(2,1)S(1)} %copy-done.1), channel_id=1, source_target_pairs={{0,24},{8,16},{16,8},{24,0},{1,25},{9,17},{17,9},{25,1},{2,26},{10... | collective-permute-start | bytes 884744 | tf_op jit(solution)/shard_map/ppermute | solution.py:674
  58.7 95.0 %collective-permute-start.6 = (bf16[2,1,48,4096]{3,2,1,0:T(8,128)(2,1)}, bf16[2,1,48,4096]{3,2,1,0:T(8,128)(2,1)S(1)}, u32[]{:S(2)}, u32[]{:S(2)}) collective-permute-start(bf16[2,1,48,4096]{3,2,1,0:T(8,128)(2,1)} %get-tuple-element.74), channel_id=1, source_target_pairs={{0,8},{8,0},{16,24},{24,16},{1,9},{9,1},{17,25},{25,17},{2,10},{10... | collective-permute-start | bytes 2359304 | tf_op jit(solution)/shard_map/ppermute | solution.py:674
  59.3 94.4 %collective-permute-start.7 = (bf16[2,1,48,4096]{3,2,1,0:T(8,128)(2,1)}, bf16[2,1,48,4096]{3,2,1,0:T(8,128)(2,1)S(1)}, u32[]{:S(2)}, u32[]{:S(2)}) collective-permute-start(bf16[2,1,48,4096]{3,2,1,0:T(8,128)(2,1)} %get-tuple-element.75), channel_id=1, source_target_pairs={{0,16},{8,24},{16,0},{24,8},{1,17},{9,25},{17,1},{25,9},{2,18},{10... | collective-permute-start | bytes 2359304 | tf_op jit(solution)/shard_map/ppermute | solution.py:674
  60.4 93.3 %collective-permute-start.8 = (bf16[2,1,48,4096]{3,2,1,0:T(8,128)(2,1)}, bf16[2,1,48,4096]{3,2,1,0:T(8,128)(2,1)S(1)}, u32[]{:S(2)}, u32[]{:S(2)}) collective-permute-start(bf16[2,1,48,4096]{3,2,1,0:T(8,128)(2,1)} %get-tuple-element.76), channel_id=1, source_target_pairs={{0,24},{8,16},{16,8},{24,0},{1,25},{9,17},{17,9},{25,1},{2,26},{10... | collective-permute-start | bytes 2359304 | tf_op jit(solution)/shard_map/ppermute | solution.py:674
  77.0 23.2 %collective-permute-start.10 = (bf16[32,768]{1,0:T(8,128)(2,1)}, bf16[32,768]{1,0:T(8,128)(2,1)S(1)}, u32[]{:S(2)}, u32[]{:S(2)}) collective-permute-start(bf16[32,768]{1,0:T(8,128)(2,1)} %get-tuple-element.84), channel_id=1, source_target_pairs={{0,2},{1,3},{2,0},{3,1},{4,6},{5,7},{6,4},{7,5},{8,10},{9,11},{10,... | collective-permute-start | bytes 147464 | tf_op jit(solution)/shard_map/ppermute | solution.py:674
  78.6 13.2 %collective-permute-start.16 = (bf16[48,48]{1,0:T(8,128)(2,1)S(1)}, bf16[48,48]{1,0:T(8,128)(2,1)S(1)}, u32[]{:S(2)}, u32[]{:S(2)}) collective-permute-start(bf16[48,48]{1,0:T(8,128)(2,1)S(1)} %convert_bitcast_fusion.l0), channel_id=1, source_target_pairs={{0,8},{8,0},{16,24},{24,16},{1,9},{9,1},{17,25},{25,17},{2,10},{10... | collective-permute-start | bytes 13832 | tf_op jit(solution)/shard_map/ppermute | solution.py:674
  110.2 14.4 %collective-permute-start.15 = (bf16[32,768]{1,0:T(8,128)(2,1)}, bf16[32,768]{1,0:T(8,128)(2,1)S(1)}, u32[]{:S(2)}, u32[]{:S(2)}) collective-permute-start(bf16[32,768]{1,0:T(8,128)(2,1)} %get-tuple-element.89), channel_id=1, source_target_pairs={{0,7},{1,6},{2,5},{3,4},{4,3},{5,2},{6,1},{7,0},{8,15},{9,14},{10,... | collective-permute-start | bytes 147464 | tf_op jit(solution)/shard_map/ppermute | solution.py:674
  176.7 68.0 %collective-permute-start.28 = (bf16[2,1,48,4096]{3,2,1,0:T(8,128)(2,1)}, bf16[2,1,48,4096]{3,2,1,0:T(8,128)(2,1)S(1)}, u32[]{:S(2)}, u32[]{:S(2)}) collective-permute-start(bf16[2,1,48,4096]{3,2,1,0:T(8,128)(2,1)} %get-tuple-element.104), channel_id=1, source_target_pairs={{0,8},{8,0},{16,24},{24,16},{1,9},{9,1},{17,25},{25,17},{2,10},{10... | collective-permute-start | bytes 2359304 | tf_op jit(solution)/shard_map/ppermute | solution.py:674
  187.4 14.0 %collective-permute-start.49 = (f32[48,48]{1,0:T(8,128)S(1)}, f32[48,48]{1,0:T(8,128)S(1)}, u32[]{:S(2)}, u32[]{:S(2)}) collective-permute-start(f32[48,48]{1,0:T(8,128)S(1)} %get-tuple-element.147), channel_id=1, source_target_pairs={{0,8},{8,0},{16,24},{24,16},{1,9},{9,1},{17,25},{25,17},{2,10},{10... | collective-permute-start | bytes 27656 | tf_op jit(solution)/shard_map/ppermute | solution.py:674
  187.8 15.7 %collective-permute-start.50 = (f32[48,48]{1,0:T(8,128)S(1)}, f32[48,48]{1,0:T(8,128)S(1)}, u32[]{:S(2)}, u32[]{:S(2)}) collective-permute-start(f32[48,48]{1,0:T(8,128)S(1)} %get-tuple-element.149), channel_id=1, source_target_pairs={{0,16},{8,24},{16,0},{24,8},{1,17},{9,25},{17,1},{25,9},{2,18},{10... | collective-permute-start | bytes 27656 | tf_op jit(solution)/shard_map/ppermute | solution.py:674
  189.8 13.7 %collective-permute-start.51 = (f32[48,48]{1,0:T(8,128)S(1)}, f32[48,48]{1,0:T(8,128)S(1)}, u32[]{:S(2)}, u32[]{:S(2)}) collective-permute-start(f32[48,48]{1,0:T(8,128)S(1)} %get-tuple-element.148), channel_id=1, source_target_pairs={{0,24},{8,16},{16,8},{24,0},{1,25},{9,17},{17,9},{25,1},{2,26},{10... | collective-permute-start | bytes 27656 | tf_op jit(solution)/shard_map/ppermute | solution.py:674
  205.5 14.0 %collective-permute-start.38 = (bf16[32,768]{1,0:T(8,128)(2,1)}, bf16[32,768]{1,0:T(8,128)(2,1)S(1)}, u32[]{:S(2)}, u32[]{:S(2)}) collective-permute-start(bf16[32,768]{1,0:T(8,128)(2,1)} %get-tuple-element.117), channel_id=1, source_target_pairs={{0,3},{1,2},{2,1},{3,0},{4,7},{5,6},{6,5},{7,4},{8,11},{9,10},{10,... | collective-permute-start | bytes 147464 | tf_op jit(solution)/shard_map/ppermute | solution.py:674
  219.5 21.0 %collective-permute-start.46 = (bf16[8,48,384]{2,1,0:T(8,128)(2,1)}, bf16[8,48,384]{2,1,0:T(8,128)(2,1)S(1)}, u32[]{:S(2)}, u32[]{:S(2)}) collective-permute-start(bf16[8,48,384]{2,1,0:T(8,128)(2,1)} %get-tuple-element.129), channel_id=1, source_target_pairs={{0,8},{8,0},{16,24},{24,16},{1,9},{9,1},{17,25},{25,17},{2,10},{10... | collective-permute-start | bytes 884744 | tf_op jit(solution)/shard_map/ppermute | solution.py:674
  221.1 21.0 %collective-permute-start.47 = (bf16[8,48,384]{2,1,0:T(8,128)(2,1)}, bf16[8,48,384]{2,1,0:T(8,128)(2,1)S(1)}, u32[]{:S(2)}, u32[]{:S(2)}) collective-permute-start(bf16[8,48,384]{2,1,0:T(8,128)(2,1)} %get-tuple-element.130), channel_id=1, source_target_pairs={{0,16},{8,24},{16,0},{24,8},{1,17},{9,25},{17,1},{25,9},{2,18},{10... | collective-permute-start | bytes 884744 | tf_op jit(solution)/shard_map/ppermute | solution.py:674
  222.6 19.9 %collective-permute-start.48 = (bf16[8,48,384]{2,1,0:T(8,128)(2,1)}, bf16[8,48,384]{2,1,0:T(8,128)(2,1)S(1)}, u32[]{:S(2)}, u32[]{:S(2)}) collective-permute-start(bf16[8,48,384]{2,1,0:T(8,128)(2,1)} %get-tuple-element.131), channel_id=1, source_target_pairs={{0,24},{8,16},{16,8},{24,0},{1,25},{9,17},{17,9},{25,1},{2,26},{10... | collective-permute-start | bytes 884744 | tf_op jit(solution)/shard_map/ppermute | solution.py:674
  239.0 37.5 %collective-permute-start.27 = (bf16[2,1,48,4096]{3,2,1,0:T(8,128)(2,1)}, bf16[2,1,48,4096]{3,2,1,0:T(8,128)(2,1)S(1)}, u32[]{:S(2)}, u32[]{:S(2)}) collective-permute-start(bf16[2,1,48,4096]{3,2,1,0:T(8,128)(2,1)} %get-tuple-element.103), channel_id=1, source_target_pairs={{0,16},{8,24},{16,0},{24,8},{1,17},{9,25},{17,1},{25,9},{2,18},{10... | collective-permute-start | bytes 2359304 | tf_op jit(solution)/shard_map/ppermute | solution.py:674
  240.5 38.8 %collective-permute-start.26 = (bf16[2,1,48,4096]{3,2,1,0:T(8,128)(2,1)}, bf16[2,1,48,4096]{3,2,1,0:T(8,128)(2,1)}, u32[]{:S(2)}, u32[]{:S(2)}) collective-permute-start(bf16[2,1,48,4096]{3,2,1,0:T(8,128)(2,1)} %get-tuple-element.102), channel_id=1, source_target_pairs={{0,24},{8,16},{16,8},{24,0},{1,25},{9,17},{17,9},{25,1},{2,26},{10... | collective-permute-start | bytes 2359304 | tf_op jit(solution)/shard_map/ppermute | solution.py:674
  242.1 39.1 %collective-permute-start.45 = (bf16[2,1,48,4096]{3,2,1,0:T(8,128)(2,1)}, bf16[2,1,48,4096]{3,2,1,0:T(8,128)(2,1)S(1)}, u32[]{:S(2)}, u32[]{:S(2)}) collective-permute-start(bf16[2,1,48,4096]{3,2,1,0:T(8,128)(2,1)} %get-tuple-element.126), channel_id=1, source_target_pairs={{0,8},{8,0},{16,24},{24,16},{1,9},{9,1},{17,25},{25,17},{2,10},{10... | collective-permute-start | bytes 2359304 | tf_op jit(solution)/shard_map/ppermute | solution.py:674
  243.3 66.1 %collective-permute-start.44 = (bf16[2,1,48,4096]{3,2,1,0:T(8,128)(2,1)}, bf16[2,1,48,4096]{3,2,1,0:T(8,128)(2,1)S(1)}, u32[]{:S(2)}, u32[]{:S(2)}) collective-permute-start(bf16[2,1,48,4096]{3,2,1,0:T(8,128)(2,1)} %get-tuple-element.125), channel_id=1, source_target_pairs={{0,16},{8,24},{16,0},{24,8},{1,17},{9,25},{17,1},{25,9},{2,18},{10... | collective-permute-start | bytes 2359304 | tf_op jit(solution)/shard_map/ppermute | solution.py:674
  244.7 69.9 %collective-permute-start.43 = (bf16[2,1,48,4096]{3,2,1,0:T(8,128)(2,1)}, bf16[2,1,48,4096]{3,2,1,0:T(8,128)(2,1)S(1)}, u32[]{:S(2)}, u32[]{:S(2)}) collective-permute-start(bf16[2,1,48,4096]{3,2,1,0:T(8,128)(2,1)} %get-tuple-element.124), channel_id=1, source_target_pairs={{0,24},{8,16},{16,8},{24,0},{1,25},{9,17},{17,9},{25,1},{2,26},{10... | collective-permute-start | bytes 2359304 | tf_op jit(solution)/shard_map/ppermute | solution.py:674
  (85 other events, 840.9 us)

commit v2 on v0

v2 whole, which is shorter than its diff:
```python
from functools import partial
import math

import jax
import jax.numpy as jnp
from jax import lax
from jax.experimental import pallas as pl
from jax.experimental.pallas import tpu as pltpu
from jax.sharding import PartitionSpec as P

GRID = 64
MSIDE = 16
NTAB = 16
STEP_COUNT = 5
NPIX = 4096
MODES = 256
C = 48
LANES = 2 * C
QUAD = 4
PACK = 128
ROWS = 16

BETA_ONE = 0.9
BETA_TWO = 0.999
EPSILON = 1e-08
RATE = 0.1
DECAY = 0.01

F32 = jnp.float32
BF16 = jnp.bfloat16
SMEM = pltpu.MemorySpace.SMEM


def sgn(left, right):
    return -1.0 if (left & 2) and (right & 1) else 1.0


def flip_of(own, k):
    if k & 1:
        return (1 - 2 * ((own // 2) % 2)).astype(F32)
    return jnp.float32(1.0)


def mode_factor(mode):
    return jnp.where(mode % MSIDE == 0, 1.0, 2.0).astype(F32)


def dot(left, right, dims=((1,), (0,))):
    return lax.dot_general(left, right, (dims, ((), ())), preferred_element_type=F32)


def whole(shape):
    zeros = (0,) * len(shape)
    return pl.BlockSpec(tuple(shape), lambda *_: zeros)


def params(mib):
    return pltpu.CompilerParams(vmem_limit_bytes=60 * 1024 * 1024)


def in_vmem(count):
    return [pl.BlockSpec(memory_space=pltpu.MemorySpace.VMEM)] * count


def cost(flops, size, hard=0):
    return pl.CostEstimate(flops=flops, bytes_accessed=size, transcendentals=hard)


def small_tables():
    mode_ids = jnp.arange(2 * MODES, dtype=jnp.int32)
    imag = mode_ids >= MODES
    mode_ids = mode_ids % MODES
    row_index = mode_ids // MSIDE
    col_freq = mode_ids % MSIDE
    row_freq = jnp.where(row_index < MSIDE // 2, row_index, GRID - MSIDE + row_index)
    place = jnp.arange(GRID, dtype=jnp.int32)[:, None]
    row_angle = ((place * row_freq[None, :]) % GRID).astype(F32) * (2.0 * math.pi / GRID)
    col_angle = ((place * col_freq[None, :]) % GRID).astype(F32) * (2.0 * math.pi / GRID)
    row_cos, row_sin = jnp.cos(row_angle) / GRID, jnp.sin(row_angle) / GRID
    first = jnp.where(imag[None, :], -row_sin, row_cos)
    second = jnp.where(imag[None, :], -row_cos, -row_sin)
    return first, second, jnp.cos(col_angle), jnp.sin(col_angle)


def table_kernel(first_ref, second_ref, cos_ref, sin_ref, f_ref, ft_ref):
    for h in range(first_ref.shape[0]):
        tile = first_ref[h : h + 1, :] * cos_ref[...] + second_ref[h : h + 1, :] * sin_ref[...]
        f_ref[h * GRID : (h + 1) * GRID, :] = tile.astype(BF16)
    for h in range(0, first_ref.shape[0], 2):
        tile = f_ref[h * GRID : (h + 2) * GRID, :].astype(F32)
        ft_ref[:, h * GRID : (h + 2) * GRID] = tile.T.astype(BF16)


def make_tables():
    first, second, cosine, sine = lax.optimization_barrier(small_tables())
    rows = 8
    n = 2 * MODES
    return pl.pallas_call(
        table_kernel,
        grid=(GRID // rows,),
        in_specs=[
            pl.BlockSpec((rows, n), lambda i: (i, 0)),
            pl.BlockSpec((rows, n), lambda i: (i, 0)),
            whole((GRID, n)),
            whole((GRID, n)),
        ],
        out_specs=[
            pl.BlockSpec((rows * GRID, n), lambda i: (i, 0)),
            pl.BlockSpec((n, rows * GRID), lambda i: (0, i)),
        ],
        out_shape=[
            jax.ShapeDtypeStruct((NPIX, n), BF16),
            jax.ShapeDtypeStruct((n, NPIX), BF16),
        ],
        compiler_params=params(16),
        cost_estimate=cost(4 * NPIX * n, 4 * NPIX * n),
        name="tables",
    )(first, second, cosine, sine)


def pack_kernel(w_ref, l_ref, o_ref):
    def step(g, carry):
        parts = [w_ref[0, g * QUAD + q, r] for q in range(QUAD) for r in range(2)]
        at = pl.ds(pl.multiple_of(g * QUAD * LANES, PACK), QUAD * LANES)
        o_ref[:, at] = jnp.concatenate(parts, axis=1).astype(BF16)
        return carry

    modes = w_ref.shape[1]
    lax.fori_loop(0, modes // QUAD, step, 0)
    line = jnp.concatenate([l_ref[0], jnp.zeros((C, PACK - C), F32)], axis=1)
    o_ref[:, modes * LANES :] = line.astype(BF16)


def pack_weights(spec_weight, lin_weight):
    modes = spec_weight.shape[1]
    return pl.pallas_call(
        pack_kernel,
        in_specs=in_vmem(2),
        out_specs=in_vmem(1)[0],
        out_shape=jax.ShapeDtypeStruct((C, modes * LANES + PACK), BF16),
        compiler_params=params(8),
        cost_estimate=cost(modes * 4608, modes * 4608 * 12),
        name="pack",
    )(spec_weight, lin_weight)


def spread(acc, out_ref):
    rows = []
    for n in range(acc.shape[0] // C):
        for r in range(2):
            rows.append(acc[n * C : (n + 1) * C, r * MODES : (r + 1) * MODES])
    turned = jnp.concatenate(rows, axis=0).T
    out_ref[...] = turned.reshape(out_ref.shape).astype(BF16)


def collect(block, ysc):
    turned = block[...].astype(F32).reshape(MODES, block.shape[2]).T
    for n in range(ysc.shape[0] // C):
        for r in range(2):
            row = (n * 2 + r) * C
            piece = turned[row : row + C].astype(BF16)
            ysc[n * C : (n + 1) * C, r * MODES : (r + 1) * MODES] = piece


def forward_kernel(ids_ref, inv_ref, x0, x1, f_ref, out_ref, acc):
    i = pl.program_id(0)
    samples = x0.shape[0]
    first = inv_ref.shape[0] - samples
    low = []
    for s in range(samples):
        for x in (x0, x1):
            low.append((x[s, 0].astype(F32) * inv_ref[s]).astype(BF16))
    part = dot(jnp.concatenate(low, axis=0), f_ref[...])

    @pl.when(i == 0)
    def _():
        acc[...] = part

    @pl.when(i > 0)
    def _():
        acc[...] += part

    @pl.when(i == pl.num_programs(0) - 1)
    def _():
        spread(acc, out_ref)


def forward_spectrum(ids, inv, x, table, shards):
    samples = inv.shape[0]
    modes = MODES // shards
    width = samples * 2 * LANES
    n = 2 * MODES
    tile = 1024

    def spec(array):
        if array.shape[0] == samples:
            return pl.BlockSpec((samples, 1, C, tile), lambda i, ids, inv: (0, 0, 0, i))
        return pl.BlockSpec((samples, 1, C, tile), lambda i, ids, inv: (ids[0], 0, 0, i))

    return pl.pallas_call(
        forward_kernel,
        grid_spec=pltpu.PrefetchScalarGridSpec(
            num_scalar_prefetch=2,
            grid=(NPIX // tile,),
            in_specs=[spec(x[0]), spec(x[1]), pl.BlockSpec((tile, n), lambda i, ids, inv: (i, 0))],
            out_specs=whole((shards, modes, width)),
            scratch_shapes=[pltpu.VMEM((samples * 2 * C, n), F32)],
        ),
        out_shape=jax.ShapeDtypeStruct((shards, modes, width), BF16),
        compiler_params=params(16),
        cost_estimate=cost(4 * samples * C * NPIX * n, 6_000_000),
        name="forward",
    )(ids, inv, *x, table)


def row_scratch(modes, shards, width):
    return pltpu.VMEM((width // 128, modes * shards, 128), F32)


def gather_rows(blocks, sc):
    shards, modes = blocks[0].shape[:2]
    first = 0
    for block in blocks:
        for n in range(block.shape[2] // 128):
            for x in range(shards):
                rows = block[x, :, n * 128 : (n + 1) * 128].astype(F32)
                sc[first + n, pl.ds(x, modes, stride=shards), :] = rows
        first += block.shape[2] // 128


def line_of(sc, mode, shards):
    at = pl.ds(pl.multiple_of(mode * shards, shards), shards)
    return [sc[n, at, :] for n in range(sc.shape[0])]


def blade_rows(tiles, order):
    samples = len(tiles) * 128 // (4 * LANES)
    line = jnp.concatenate(tiles, axis=1)
    found = [[] for _ in range(4)]
    for n, (s, t) in enumerate(order):
        found[t].append(line[:, n * LANES : (n + 1) * LANES])
    return [jnp.concatenate(found[t], axis=0) for t in range(4)]


def split_order(samples):
    return [(s, t) for pair in ((0, 3), (1, 2)) for s in range(samples) for t in pair]


def plain_order(samples):
    return [(s, t) for s in range(samples) for t in range(4)]


def mode_weights(wk, g, q):
    rows = []
    at = pl.ds(pl.multiple_of(g * QUAD * LANES, PACK), QUAD * LANES)
    for k in range(4):
        p = wk[k, :, at][:, q * LANES : (q + 1) * LANES]
        low = jnp.concatenate([-p[:, C:], p[:, :C]], axis=1)
        both = jnp.concatenate([p, low], axis=0)
        rows.append(both)
    return rows


def mix_modes(xsc, ysc, wk, order, samples, shards, first_mode, back):
    modes = xsc.shape[1] // shards
    group = samples * shards

    def step(g, carry):
        for q in range(QUAD):
            m = g * QUAD + q
            low = jnp.concatenate(blade_rows(line_of(xsc, m, shards), order), axis=0).astype(BF16)
            weights = mode_weights(wk, g, q)
            total = [None] * 4
            for k in range(4):
                part = dot(low, weights[k], ((1,), (1,)) if back else ((1,), (0,)))
                for t in range(4):
                    u = t ^ k
                    piece = part[t * group : (t + 1) * group]
                    sign = sgn(u, k) if back else sgn(t, k)
                    if total[u] is None:
                        total[u] = piece if sign > 0 else -piece
                    else:
                        total[u] = total[u] + piece if sign > 0 else total[u] - piece
            lanes = []
            for s in range(samples):
                for u in range(4):
                    lanes.append(total[u][s * shards : (s + 1) * shards])
            line = jnp.concatenate(lanes, axis=1) * mode_factor(first_mode + m)
            at = pl.ds(pl.multiple_of(m * shards, shards), shards)
            for n in range(ysc.shape[0]):
                ysc[n, at, :] = line[:, n * 128 : (n + 1) * 128]
        return carry

    lax.fori_loop(0, modes // QUAD, step, 0)


def scatter_rows(ysc, out):
    shards, modes = out.shape[:2]
    for x in range(shards):
        for n in range(ysc.shape[0]):
            piece = ysc[n, pl.ds(x, modes, stride=shards), :]
            out[x, :, n * 128 : (n + 1) * 128] = piece.astype(BF16)


def mix_kernel(ids_ref, xa, xb, w0, w1, w2, w3, y_ref, wk, lt_ref, lb_ref, xsc, ysc):
    shards, modes, half = xa.shape
    samples = half // (2 * LANES)
    own = ids_ref[0]
    for t, w in enumerate((w0, w1, w2, w3)):
        slot = jnp.bitwise_xor(own, t)
        flip = jnp.where(slot % 2 == 1, flip_of(own, 1), 1.0)
        wk[slot] = (w[...].astype(F32) * flip).astype(BF16)
    gather_rows((xa, xb), xsc)
    mix_modes(xsc, ysc, wk, split_order(samples), samples, shards, ids_ref[1] * modes, False)
    scatter_rows(ysc, y_ref)
    for k in range(4):
        line = wk[k, :, modes * LANES :].astype(F32)
        turned = line.T
        for t in range(4):
            u = t ^ k
            lb_ref[t * C : (t + 1) * C, u * C : (u + 1) * C] = (line[:, :C] * sgn(t, k)).astype(BF16)
            lt_ref[u * C : (u + 1) * C, t * C : (t + 1) * C] = (turned[:C] * sgn(t, k)).astype(BF16)


def mix(ids, xa, xb, packs):
    shards, modes, half = xa.shape
    return pl.pallas_call(
        mix_kernel,
        in_specs=[pl.BlockSpec(memory_space=SMEM)] + in_vmem(6),
        out_specs=in_vmem(4),
        out_shape=[
            jax.ShapeDtypeStruct((shards, modes, 2 * half), BF16),
            jax.ShapeDtypeStruct((4,) + packs[0].shape, BF16),
            jax.ShapeDtypeStruct((4 * C, 4 * C), BF16),
            jax.ShapeDtypeStruct((4 * C, 4 * C), BF16),
        ],
        scratch_shapes=[row_scratch(modes, shards, 2 * half)] * 2,
        compiler_params=params(16),
        cost_estimate=cost(modes * 64 * 96 * 96 * 8, 4_000_000),
        name="mix",
    )(ids, xa, xb, *packs)


def mix_back_kernel(ids_ref, g_ref, wk, out_ref, gsc, ysc):
    shards, modes, width = g_ref.shape
    samples = width // (4 * LANES)
    gather_rows((g_ref,), gsc)
    mix_modes(gsc, ysc, wk, plain_order(samples), samples, shards, ids_ref[1] * modes, True)
    scatter_rows(ysc, out_ref)


def mix_back(ids, g, wk):
    shards, modes, width = g.shape
    return pl.pallas_call(
        mix_back_kernel,
        in_specs=[pl.BlockSpec(memory_space=SMEM)] + in_vmem(2),
        out_specs=in_vmem(1)[0],
        out_shape=jax.ShapeDtypeStruct(g.shape, BF16),
        scratch_shapes=[row_scratch(modes, shards, width)] * 2,
        compiler_params=params(16),
        cost_estimate=cost(modes * 64 * 96 * 96 * 8, 3_000_000),
        name="mix_back",
    )(ids, g, wk)


def grad_kernel(ids_ref, xa, xb, g_ref, lin_ref, o0, o1, o2, o3, xsc, gsc, osc):
    shards, modes, width = g_ref.shape
    samples = width // (4 * LANES)
    own = ids_ref[0]
    first_mode = ids_ref[1] * modes
    gather_rows((xa, xb), xsc)
    gather_rows((g_ref,), gsc)

    def step(g, carry):
        found = [[] for _ in range(4)]
        for q in range(QUAD):
            m = g * QUAD + q
            x = jnp.concatenate(
                blade_rows(line_of(xsc, m, shards), split_order(samples)), axis=0
            ).astype(BF16)
            left = jnp.concatenate([x[:, :C], x[:, C:]], axis=0)
            factor = mode_factor(first_mode + m)
            plain = [rows * factor for rows in blade_rows(line_of(gsc, m, shards), plain_order(samples))]
            turned = [jnp.concatenate([rows[:, C:], -rows[:, :C]], axis=1) for rows in plain]
            for k in range(4):
                rows = []
                for source in (plain, turned):
                    for t in range(4):
                        rows.append(source[t ^ k] if sgn(t, k) > 0 else -source[t ^ k])
                right = jnp.concatenate(rows, axis=0).astype(BF16)
                found[k].append(dot(left, right, ((0,), (0,))))
        at = pl.ds(pl.multiple_of(g * QUAD * LANES, PACK), QUAD * LANES)
        for k in range(4):
            osc[k, :, at] = jnp.concatenate(found[k], axis=1).astype(BF16)
        return carry

    lax.fori_loop(0, modes // QUAD, step, 0)
    for k in range(4):
        line = jnp.concatenate([lin_ref[k], jnp.zeros((C, PACK - C), F32)], axis=1)
        osc[k, :, modes * LANES :] = line.astype(BF16)
    for t, out in enumerate((o0, o1, o2, o3)):
        out[...] = osc[jnp.bitwise_xor(own, t)]


def weight_grads(ids, xa, xb, g, lin):
    shards, modes, width = g.shape
    shape = (C, modes * LANES + PACK)
    return pl.pallas_call(
        grad_kernel,
        in_specs=[pl.BlockSpec(memory_space=SMEM)] + in_vmem(4),
        out_specs=in_vmem(4),
        out_shape=[jax.ShapeDtypeStruct(shape, BF16)] * 4,
        scratch_shapes=[row_scratch(modes, shards, width)] * 2 + [pltpu.VMEM((4,) + shape, BF16)],
        compiler_params=params(16),
        cost_estimate=cost(modes * 128 * 96 * 96 * 8, 4_000_000),
        name="weight_grads",
    )(ids, xa, xb, g, lin)


CDF_AT = 0.28
CDF = (0.11652094, 0.06749571, 0.2689128, -0.23699677, 0.38987606, -0.10580875)


def gelu_parts(v):
    z = jnp.abs(v)
    t = 1.0 / (1.0 + CDF_AT * z)
    bell = jnp.exp2(v * v * (-0.5 * math.log2(math.e)))
    series = jnp.float32(CDF[-1])
    for value in CDF[-2::-1]:
        series = series * t + value
    tail = series * t * bell
    cdf = jnp.where(v < 0.0, tail, 1.0 - tail)
    return v * cdf, cdf + v * (bell * (1.0 / math.sqrt(2.0 * math.pi)))


def pixel_kernel(ids_ref, inv_ref, *refs):
    x, cot = refs[:4], refs[4:8]
    y_ref, f_ref, ft_ref, lt_ref = refs[8:12]
    outs = refs[12:16]
    g_ref, g_out, lin_ref = refs[16:19]
    ysc, pre, low, gacc, lacc = refs[19:]
    i = pl.program_id(0)
    own = ids_ref[0]
    samples = x[1].shape[0]
    rows = 4 * C

    @pl.when(i == 0)
    def _():
        collect(y_ref, ysc)

    for s in range(samples):
        for t in range(4):
            at = s * rows + t * C
            low[at : at + C] = (x[t][s, 0].astype(F32) * inv_ref[s]).astype(BF16)
    spatial = dot(ysc[...], ft_ref[...])
    for s in range(samples):
        at = slice(s * rows, (s + 1) * rows)
        pre[at] = spatial[at] + dot(lt_ref[...], low[at])

    for s in range(samples):
        for t in range(4):
            for c in range(0, C, ROWS):
                at = s * rows + t * C + c
                value, slope = gelu_parts(pre[at : at + ROWS])
                normed = x[t][s, 0, c : c + ROWS].astype(F32) * inv_ref[s]
                outs[t][s, 0, c : c + ROWS] = (normed + value).astype(BF16)
                grad = cot[t][s, 0, c : c + ROWS].astype(F32) * slope
                g_ref[at : at + ROWS] = grad.astype(BF16)

    part = dot(g_ref[...], f_ref[...])
    lin = None
    for s in range(samples):
        at = slice(s * rows, (s + 1) * rows)
        piece = dot(low[at], g_ref[at], ((1,), (1,)))
        lin = piece if lin is None else lin + piece

    @pl.when(i == 0)
    def _():
        gacc[...] = part
        lacc[...] = lin

    @pl.when(i > 0)
    def _():
        gacc[...] += part
        lacc[...] += lin

    @pl.when(i == pl.num_programs(0) - 1)
    def _():
        spread(gacc, g_out)
        for k in range(4):
            total = None
            for t in range(4):
                u = t ^ k
                piece = lacc[t * C : (t + 1) * C, u * C : (u + 1) * C] * sgn(t, k)
                total = piece if total is None else total + piece
            lin_ref[k] = total


def pixels(ids, inv, x, cot, y, table, turned, lt):
    samples = inv.shape[0]
    n = 2 * MODES
    tile = 512
    mine = pl.BlockSpec((samples, 1, C, tile), lambda i, ids, inv: (ids[0], 0, 0, i))
    block = pl.BlockSpec((samples, 1, C, tile), lambda i, ids, inv: (0, 0, 0, i))
    block_shape = jax.ShapeDtypeStruct((samples, 1, C, NPIX), BF16)
    rows = samples * 4 * C
    return pl.pallas_call(
        pixel_kernel,
        grid_spec=pltpu.PrefetchScalarGridSpec(
            num_scalar_prefetch=2,
            grid=(NPIX // tile,),
            in_specs=[mine]
            + [block] * 3
            + [mine]
            + [block] * 3
            + [
                whole(y.shape),
                pl.BlockSpec((tile, n), lambda i, ids, inv: (i, 0)),
                pl.BlockSpec((n, tile), lambda i, ids, inv: (0, i)),
                whole((4 * C, 4 * C)),
            ],
            out_specs=[mine]
            + [block] * 3
            + [
                pl.BlockSpec((rows, tile), lambda i, ids, inv: (0, i)),
                whole(y.shape),
                whole((4, C, C)),
            ],
            scratch_shapes=[
                pltpu.VMEM((rows, n), BF16),
                pltpu.VMEM((rows, tile), F32),
                pltpu.VMEM((rows, tile), BF16),
                pltpu.VMEM((rows, n), F32),
                pltpu.VMEM((4 * C, 4 * C), F32),
            ],
        ),
        out_shape=[jax.ShapeDtypeStruct(x[0].shape, BF16)]
        + [block_shape] * 3
        + [
            jax.ShapeDtypeStruct((rows, NPIX), BF16),
            jax.ShapeDtypeStruct(y.shape, BF16),
            jax.ShapeDtypeStruct((4, C, C), F32),
        ],
        compiler_params=params(24),
        cost_estimate=cost(4 * rows * NPIX * n, 20_000_000, 2 * rows * NPIX),
        name="pixels",
    )(ids, inv, *x, *cot, y, table, turned, lt)


def inner_kernel(ids_ref, inv_ref, y_ref, g_ref, ft_ref, lb_ref, cot_ref, mine_ref, o1, o2, o3, ysc):
    samples = cot_ref.shape[0]
    rows = 4 * C

    @pl.when(pl.program_id(0) == 0)
    def _():
        collect(y_ref, ysc)

    spatial = dot(ysc[...], ft_ref[...])
    for s in range(samples):
        at = slice(s * rows, (s + 1) * rows)
        total = spatial[at] + dot(lb_ref[...], g_ref[at])
        mine_ref[s, 0] = (cot_ref[s, 0].astype(F32) + total[:C]) * inv_ref[s]
        for t, out in ((1, o1), (2, o2), (3, o3)):
            out[s, 0] = total[t * C : (t + 1) * C].astype(BF16)


def inner_grads(ids, inv, y, g, turned, lb, cotangent):
    samples = inv.shape[0]
    n = 2 * MODES
    tile = 512
    rows = samples * 4 * C
    mine = pl.BlockSpec((samples, 1, C, tile), lambda i, ids, inv: (ids[0], 0, 0, i))
    block = pl.BlockSpec((samples, 1, C, tile), lambda i, ids, inv: (0, 0, 0, i))
    return pl.pallas_call(
        inner_kernel,
        grid_spec=pltpu.PrefetchScalarGridSpec(
            num_scalar_prefetch=2,
            grid=(NPIX // tile,),
            in_specs=[
                whole(y.shape),
                pl.BlockSpec((rows, tile), lambda i, ids, inv: (0, i)),
                pl.BlockSpec((n, tile), lambda i, ids, inv: (0, i)),
                whole((4 * C, 4 * C)),
                mine,
            ],
            out_specs=[mine] + [block] * 3,
            scratch_shapes=[pltpu.VMEM((rows, n), BF16)],
        ),
        out_shape=[jax.ShapeDtypeStruct(cotangent.shape, F32)]
        + [jax.ShapeDtypeStruct((samples, 1, C, NPIX), BF16)] * 3,
        compiler_params=params(16),
        cost_estimate=cost(3 * rows * NPIX * n, 10_000_000),
        name="inner_grads",
    )(ids, inv, y, g, turned, lb, cotangent)


def place_kernel(ids_ref, a_ref, b_ref, c_ref, old_ref, out_ref):
    for n, part in enumerate((a_ref, b_ref, c_ref)):

        @pl.when(pl.program_id(0) == n)
        def _():
            out_ref[...] = part[...]


def place_output(ids, parts, result):
    samples = parts[0].shape[0]
    shape = (1, 1, C, NPIX)

    def spec(n):
        def at(j, s, ids):
            return (jnp.where(j == n, s, jnp.where(j < n, 0, samples - 1)), 0, 0, 0)

        return pl.BlockSpec(shape, at)

    return pl.pallas_call(
        place_kernel,
        grid_spec=pltpu.PrefetchScalarGridSpec(
            num_scalar_prefetch=1,
            grid=(3, samples),
            in_specs=[spec(0), spec(1), spec(2), pl.BlockSpec(memory_space=pl.ANY)],
            out_specs=pl.BlockSpec(
                shape, lambda j, s, ids: (jnp.bitwise_xor(ids[0], j + 1) * samples + s, 0, 0, 0)
            ),
        ),
        out_shape=jax.ShapeDtypeStruct(result.shape, BF16),
        input_output_aliases={4: 0},
        compiler_params=params(12),
        cost_estimate=cost(0, 12 * samples * C * NPIX),
        name="place",
    )(ids, *parts, result)


def final_kernel(count, codes, ids_ref, inv_ref, cot_ref, *refs):
    samples = pl.num_programs(1)
    j = pl.program_id(0)
    for n in range(count):

        @pl.when(j == n)
        def _():
            inv = inv_ref[jnp.bitwise_xor(ids_ref[0], codes[n]) * samples + pl.program_id(1)]
            refs[-1][...] = (cot_ref[...].astype(F32) + refs[n][...].astype(F32)) * inv


def final_grads(ids, inv, cotangent, parts, codes, result):
    samples = parts[0].shape[0]
    count = len(parts)
    shape = (1, 1, C, NPIX)

    def code(j):
        value = codes[0]
        for n in range(1, count):
            value = jnp.where(j == n, codes[n], value)
        return value

    def spec(n):
        def at(j, s, ids, inv):
            return (jnp.where(j == n, s, jnp.where(j < n, 0, samples - 1)), 0, 0, 0)

        return pl.BlockSpec(shape, at)

    place = pl.BlockSpec(
        shape, lambda j, s, ids, inv: (jnp.bitwise_xor(ids[0], code(j)) * samples + s, 0, 0, 0)
    )
    return pl.pallas_call(
        partial(final_kernel, count, codes),
        grid_spec=pltpu.PrefetchScalarGridSpec(
            num_scalar_prefetch=2,
            grid=(count, samples),
            in_specs=[place]
            + [spec(n) for n in range(count)]
            + [pl.BlockSpec(memory_space=pl.ANY)],
            out_specs=place,
        ),
        out_shape=jax.ShapeDtypeStruct(cotangent.shape, F32),
        input_output_aliases={3 + count: 0},
        compiler_params=params(12),
        cost_estimate=cost(0, 8 * count * samples * C * NPIX),
        name="final",
    )(ids, inv, cotangent, *parts, result)


def adamw(weight, first, second, grad):
    first_new = BETA_ONE * first + (1.0 - BETA_ONE) * grad
    second_new = BETA_TWO * second + (1.0 - BETA_TWO) * grad * grad
    corr_one = 1.0 - BETA_ONE**STEP_COUNT
    corr_two = 1.0 - BETA_TWO**STEP_COUNT
    update = first_new / corr_one / (jnp.sqrt(second_new / corr_two) + EPSILON)
    return (weight - RATE * (update + DECAY * weight), first_new, second_new)


def adam_kernel(flips, d0, d1, d2, d3, w_ref, first_ref, second_ref, w_out, first_out, second_out):
    grad = d0[...].astype(F32) * flips[0]
    for t, d in ((1, d1), (2, d2), (3, d3)):
        grad = grad + d[...].astype(F32) * flips[t]
    for q in range(QUAD):
        for r in range(2):
            lane = q * LANES + r * C
            at = (0, q, r)
            new = adamw(w_ref[at], first_ref[at], second_ref[at], grad[:, lane : lane + C])
            w_out[at], first_out[at], second_out[at] = new


def adam_spec(flips, grads, weight, first, second):
    modes = weight.shape[1]
    packed = pl.BlockSpec((C, QUAD * LANES), lambda g: (0, g))
    block = pl.BlockSpec((1, QUAD, 2, C, C), lambda g: (0, g, 0, 0, 0))
    return pl.pallas_call(
        adam_kernel,
        grid=(modes // QUAD,),
        in_specs=[pl.BlockSpec(memory_space=SMEM)] + [packed] * 4 + [block] * 3,
        out_specs=[block] * 3,
        out_shape=[jax.ShapeDtypeStruct(weight.shape, F32)] * 3,
        compiler_params=params(12),
        cost_estimate=cost(modes * 4608 * 20, modes * 4608 * 72, modes * 4608),
        name="adam",
    )(flips, *grads, weight, first, second)


def swap(value, axis, size, x):
    return lax.ppermute(value, axis, [(i, i ^ x) for i in range(size)])


def to_modes(value):
    return lax.all_to_all(value, "dp", split_axis=0, concat_axis=0, tiled=True)


def after(values, first):
    values, _ = lax.optimization_barrier((values, first))
    return values


def body(
    shards,
    inputs,
    cotangent,
    norm_table,
    sample_index,
    spec_weight,
    spec_first,
    spec_second,
    lin_weight,
    lin_first,
    lin_second,
):
    own = lax.axis_index("blade")
    shard = lax.axis_index("dp")
    ids = jnp.stack([own, shard]).astype(jnp.int32)
    samples = inputs.shape[0] // 4

    def send(array, t):
        block = lax.dynamic_slice_in_dim(array, jnp.bitwise_xor(own, t) * samples, samples, 0)
        return block, swap(block, "blade", 4, t)

    sent, x3 = send(inputs, 3)
    rest = after(inputs, sent)
    sent, x1 = send(rest, 1)
    rest = after(rest, sent)
    _, x2 = send(rest, 2)

    matches = sample_index[:, None] == jnp.arange(NTAB, dtype=jnp.int32)[None, :]
    normalizer = jnp.sum(jnp.where(matches, norm_table[None, :], 0.0), axis=1)
    inv_all = 1.0 / normalizer
    inv = lax.dynamic_slice_in_dim(inv_all, own * samples, samples, 0)

    table, turned = make_tables()
    packed = pack_weights(spec_weight, lin_weight)
    packs = [packed] + [swap(packed, "blade", 4, t) for t in (1, 2, 3)]

    xa = to_modes(forward_spectrum(ids, inv, (inputs, x3), table, shards))
    late = after(cotangent, (x1, x2))
    cot = (cotangent,) + tuple(send(late, t)[1] for t in (1, 2, 3))
    xb = to_modes(forward_spectrum(ids, inv, (x1, x2), table, shards))
    sent, wk, lt, lb = mix(ids, xa, xb, packs)
    y = to_modes(sent)

    result = pixels(ids, inv, (inputs, x1, x2, x3), cot, y, table, turned, lt)
    output, grad_pre, sent, lin = result[0], result[4], result[5], result[6]
    out_parts = [swap(result[t], "blade", 4, t) for t in (1, 2, 3)]

    g = to_modes(sent)
    back = to_modes(mix_back(ids, g, wk))
    spec_grads = weight_grads(ids, xa, xb, g, lin)
    spec_grads = [spec_grads[0]] + [swap(spec_grads[t], "blade", 4, t) for t in (1, 2, 3)]

    flips = jnp.stack(
        [jnp.where(own % 2 == 1, flip_of(jnp.bitwise_xor(own, t), 1), 1.0) for t in range(4)]
    )
    lin_grad = 0.0
    first = spec_weight.shape[1] * LANES
    for t in range(4):
        lin_grad = lin_grad + spec_grads[t][:, first : first + C].astype(F32) * flips[t]
    step = 1
    while step < shards:
        lin_grad = lin_grad + swap(lin_grad, "dp", shards, step)
        step *= 2

    inner = inner_grads(ids, inv, back, grad_pre, turned, lb, cotangent)
    grad_parts = [swap(inner[t], "blade", 4, t) for t in (1, 2, 3)]

    output = place_output(ids, out_parts, output)
    spec_out = adam_spec(flips, spec_grads, spec_weight, spec_first, spec_second)
    lin_out = adamw(lin_weight, lin_first, lin_second, lin_grad[None])
    input_grad = final_grads(ids, inv_all, cotangent, grad_parts[2:], (3,), inner[0])
    input_grad = final_grads(ids, inv_all, cotangent, grad_parts[:2], (1, 2), input_grad)
    return (output, input_grad, *spec_out, *lin_out)


def solution(mesh):
    fields = P("dp", "blade", None, None)
    spec = P("blade", "dp", None, None, None)
    lin = P("blade", None, None)
    return jax.shard_map(
        partial(body, mesh.shape["dp"]),
        mesh=mesh,
        in_specs=(fields, fields, P(), P("dp"), spec, spec, spec, lin, lin, lin),
        out_specs=(fields, fields, spec, spec, spec, lin, lin, lin),
        check_vma=False,
    )
```

time: 705 us -> 256 us (0.36)
  waiting for transfers between devices: 405 us -> 72.2 us
  matrix products: 128 us -> 0 us
  Pallas kernels: 0 us -> 100 us
  local copies, waits for them, and re-layouts: 69 us -> 13.7 us
  starting transfers between devices: 1.33 us -> 43.6 us
  other arithmetic: 41 us -> 5.27 us
  blocking collectives: 37.4 us -> 17.5 us
  between operations: 14.8 us -> 0.86 us
    all_gather x5 -> x0, waiting for transfers between devices: 347 us -> none  [the longest x1 115 us: body(): lax.all_gather(grad_pre, 'blade', axis=1, tiled=True)]
    dot_general x24 -> x0, matrix products: 128 us -> none  [the longest x1 23.2 us: body(): jnp.einsum('sjcp,sjop->co', normed_all, mixed_pre, preferred_element_type...]
    pallas_call x0 -> x13, Pallas kernels: none -> 100 us  [the longest x1 17.8 us: pixels(): pl.pallas_call(pixel_kernel, grid_spec=pltpu.PrefetchScalarGridSpec(num_s...]
    ppermute x0 -> x21, waiting for transfers between devices: none -> 68.8 us  [swap(): return lax.ppermute(value, axis, [(i, i ^ x) for i in range(size)])]
    unnamed x11 -> x0, waiting for transfers between devices: 58 us -> none
    unnamed x49 -> x46, local copies, waits for them, and re-layouts: 38.6 us -> 6.3 us
    psum x1 -> x0, blocking collectives: 28.5 us -> none  [body(): lin_grad = lax.psum(lin_grad, 'dp')]
    ppermute x0 -> x21, starting transfers between devices: none -> 26 us  [swap(): return lax.ppermute(value, axis, [(i, i ^ x) for i in range(size)])]
  transfers between devices with their start and end apart: 8 -> 25, of which waited for: 7 -> 8; matrix products, arithmetic and copies ran while one was open for 11% -> 5% of each run, Pallas kernels for 0% -> 27%
where the time goes in v2:
time: 256 us; the launch traced here: 253 us
  Pallas kernels  100 us (39%)
  waiting for transfers between devices  72.2 us (28%)
  starting transfers between devices  43.6 us (17%)
  blocking collectives  17.5 us (7%)
  local copies, waits for them, and re-layouts  13.7 us (5%)
  other arithmetic  5.27 us (2%)
    ppermute x21, waiting for transfers between devices, swap(): return lax.ppermute(value, axis, [(i, i ^ x) for i in range(size)])  68.8 us
    ppermute x21, starting transfers between devices, swap(): return lax.ppermute(value, axis, [(i, i ^ x) for i in range(size)])  26 us
    pallas_call x1, Pallas kernels, pixels(): pl.pallas_call(pixel_kernel, grid_spec=pltpu.PrefetchScalarGridSpec(num_s...  17.8 us
    all_to_all x4, starting transfers between devices, to_modes(): return lax.all_to_all(value, 'dp', split_axis=0, concat_axis=0, tiled=True)  17.6 us
    all_to_all x1, blocking collectives, to_modes(): return lax.all_to_all(value, 'dp', split_axis=0, concat_axis=0, tiled=True)  17.5 us
    pallas_call x1, Pallas kernels, weight_grads(): pl.pallas_call(grad_kernel, in_specs=[pl.BlockSpec(memory_space=SMEM)] +...  13.4 us
    pallas_call x2, Pallas kernels, forward_spectrum(): pl.pallas_call(forward_kernel, grid_spec=pltpu.PrefetchScalarGridSpec(num...  11.4 us
    pallas_call x1, Pallas kernels, inner_grads(): pl.pallas_call(inner_kernel, grid_spec=pltpu.PrefetchScalarGridSpec(num_s...  9.82 us
  transfers between devices with their start and end apart: 25, of which 8 were waited for; matrix products, arithmetic and copies ran while one was open for 5% of the time, Pallas kernels for 27%

profile of v2, /device:TPU:0, one launch (start us, length us, event | category | flops | bytes accessed | tf_op | source)
XLA Modules:
  0.0 253.5 jit_solution(13361263797901002424)
XLA Ops:
  1.9 4.0 %collective-permute-start.2 = (bf16[2,1,48,4096]{3,2,1,0:T(8,128)(2,1)S(1)}, bf16[2,1,48,4096]{3,2,1,0:T(8,128)(2,1)S(1)}, u32[]{:S(2)}, u32[]{:S(2)}) collective-permute-start(bf16[2,1,48,4096]{3,2,1,0:T(8,128)(2,1)S(1)} %constant_dynamic-slice_fusion.5), channel_id=1, source_target_pairs={{0,24},{8,16},{16,8},{24,0},{1,25},{9,17},{17,9},{25,1},{2,26},{10... | collective-permute-start | bytes 2359304 | tf_op jit(solution)/shard_map/ppermute | solution.py:720
  13.8 6.6 %tables.1 = (bf16[4096,512]{1,0:T(8,128)(2,1)}, bf16[512,4096]{1,0:T(8,128)(2,1)}) custom-call(f32[64,512]{1,0:T(8,128)} %get-tuple-element.42.first_ref, f32[64,512]{1,0:T(8,128)} %get-tuple-element.43.second_ref, f32[64,512]{1,0:T(8,128)} %get-tuple-element.44.cos_ref, f32[64,512]{1,0:T(8,128)} %get-tuple-element.45.sin_ref), custom_call_target="tpu_custom_call" | custom-call | flops 8388608 | bytes 8388608 | tf_op jit(solution)/shard_map/tables/pallas_call | solution.py:98
  21.0 3.2 %collective-permute-done.2.x1.refs_3_ = bf16[2,1,48,4096]{3,2,1,0:T(8,128)(2,1)S(1)} collective-permute-done((bf16[2,1,48,4096]{3,2,1,0:T(8,128)(2,1)S(1)}, bf16[2,1,48,4096]{3,2,1,0:T(8,128)(2,1)S(1)}, u32[]{:S(2)}, u32[]{:S(2)}) %collective-permute-start.2) | collective-permute-done | bytes 786464 | tf_op jit(solution)/shard_map/ppermute | solution.py:720
  25.1 5.7 %forward.2 = bf16[8,32,384]{2,1,0:T(8,128)(2,1)} custom-call(s32[2]{0:T(128)} %pad_add_fusion.ids_ref, f32[2]{0:T(128)} %dynamic_slice.21.inv_ref, bf16[8,1,48,4096]{3,2,1,0:T(8,128)(2,1)} %refs_0_.1, bf16[2,1,48,4096]{3,2,1,0:T(8,128)(2,1)} %copy-done.1, bf16[4096,512]{1,0:T(8,128)(2,1)} %get-tuple-element.46.f_ref.refs_9_), custom_call_target="tpu_custom_call" | custom-call | flops 805306368 | bytes 6000000 | tf_op jit(solution)/shard_map/forward/pallas_call | solution.py:200
  30.8 5.4 %all-to-all-start = ((bf16[8,32,384]{2,1,0:T(8,128)(2,1)}), bf16[8,32,384]{2,1,0:T(8,128)(2,1)S(1)}, u32[]{:S(2)}, u32[]{:S(2)}) async-start(bf16[8,32,384]{2,1,0:T(8,128)(2,1)} %forward.2), calls=%async_computation | async-start | bytes 393216 | tf_op jit(solution)/shard_map/all_to_all | solution.py:724
  42.6 5.7 %forward.3 = bf16[8,32,384]{2,1,0:T(8,128)(2,1)} custom-call(s32[2]{0:T(128)} %pad_add_fusion.ids_ref, f32[2]{0:T(128)} %dynamic_slice.21.inv_ref, bf16[2,1,48,4096]{3,2,1,0:T(8,128)(2,1)} %collective-permute-done.x0.refs_1_, bf16[2,1,48,4096]{3,2,1,0:T(8,128)(2,1)} %collective-permute-done.1.x1.refs_2_, bf16[4096,512]{1,0:T(8,128)(2,1)} %get-tuple-element.46.f_ref.refs_9_), custom_call_target="tpu_custom_call" | custom-call | flops 805306368 | bytes 6000000 | tf_op jit(solution)/shard_map/forward/pallas_call | solution.py:200
  48.3 5.1 %all-to-all-start.1 = ((bf16[8,32,384]{2,1,0:T(8,128)(2,1)}), bf16[8,32,384]{2,1,0:T(8,128)(2,1)S(1)}, u32[]{:S(2)}, u32[]{:S(2)}) async-start(bf16[8,32,384]{2,1,0:T(8,128)(2,1)} %forward.3), calls=%async_computation.1 | async-start | bytes 393216 | tf_op jit(solution)/shard_map/all_to_all | solution.py:724
  58.4 3.3 %all-to-all-done.1.xb = bf16[8,32,384]{2,1,0:T(8,128)(2,1)S(1)} async-done(((bf16[8,32,384]{2,1,0:T(8,128)(2,1)}), bf16[8,32,384]{2,1,0:T(8,128)(2,1)S(1)}, u32[]{:S(2)}, u32[]{:S(2)}) %all-to-all-start.1) | async-done | bytes 196640 | tf_op jit(solution)/shard_map/all_to_all | solution.py:724
  62.4 8.2 %mix.1 = (bf16[8,32,768]{2,1,0:T(8,128)(2,1)}, bf16[4,48,3200]{2,1,0:T(8,128)(2,1)}, bf16[192,192]{1,0:T(8,128)(2,1)}, bf16[192,192]{1,0:T(8,128)(2,1)}) custom-call(s32[2]{0:T(128)} %pad_add_fusion.ids_ref, bf16[8,32,384]{2,1,0:T(8,128)(2,1)} %copy-done.11, bf16[8,32,384]{2,1,0:T(8,128)(2,1)} %copy-done.12, bf16[48,3200]{1,0:T(8,128)(2,1)} %pack.1.w0, ...), custom_call_target="tpu_custom_call" | custom-call | flops 150994944 | bytes 4000000 | tf_op jit(solution)/shard_map/mix/pallas_call | solution.py:327
  70.6 3.5 %all-to-all-start.2 = ((bf16[8,32,768]{2,1,0:T(8,128)(2,1)}), bf16[8,32,768]{2,1,0:T(8,128)(2,1)S(1)}, u32[]{:S(2)}, u32[]{:S(2)}) async-start(bf16[8,32,768]{2,1,0:T(8,128)(2,1)} %get-tuple-element.47), calls=%async_computation.2 | async-start | bytes 786432 | tf_op jit(solution)/shard_map/all_to_all | solution.py:724
  75.4 17.7 %collective-permute-done.4.refs_6_ = bf16[2,1,48,4096]{3,2,1,0:T(8,128)(2,1)S(1)} collective-permute-done((bf16[2,1,48,4096]{3,2,1,0:T(8,128)(2,1)}, bf16[2,1,48,4096]{3,2,1,0:T(8,128)(2,1)S(1)}, u32[]{:S(2)}, u32[]{:S(2)}) %collective-permute-start.4) | collective-permute-done | bytes 786464 | tf_op jit(solution)/shard_map/ppermute | solution.py:720
  94.4 17.8 %pixels.1 = (bf16[8,1,48,4096]{3,2,1,0:T(8,128)(2,1)}, bf16[2,1,48,4096]{3,2,1,0:T(8,128)(2,1)}, bf16[2,1,48,4096]{3,2,1,0:T(8,128)(2,1)}, bf16[2,1,48,4096]{3,2...) custom-call(s32[2]{0:T(128)} %pad_add_fusion.ids_ref, ...), custom_call_target="tpu_custom_call" | custom-call | flops 3221225472 | bytes 20000000 | tf_op jit(solution)/shard_map/pixels/pallas_call | solution.py:507
  112.2 17.5 %all_to_all.25.g_ref = bf16[8,32,768]{2,1,0:T(8,128)(2,1)} all-to-all(bf16[8,32,768]{2,1,0:T(8,128)(2,1)} %get-tuple-element.54), channel_id=1, replica_groups=mesh['blade'=4,'dp'=8] {'dp'}, dimensions={0} | all-to-all | bytes 786432 | tf_op jit(solution)/shard_map/all_to_all | solution.py:724
  129.7 8.1 %mix_back.1 = bf16[8,32,768]{2,1,0:T(8,128)(2,1)} custom-call(s32[2]{0:T(128)} %pad_add_fusion.ids_ref, bf16[8,32,768]{2,1,0:T(8,128)(2,1)} %all_to_all.25.g_ref, bf16[4,48,3200]{2,1,0:T(8,128)(2,1)} %get-tuple-element.55.wk), custom_call_target="tpu_custom_call" | custom-call | flops 150994944 | bytes 3000000 | tf_op jit(solution)/shard_map/mix_back/pallas_call | solution.py:354
  137.8 3.6 %all-to-all-start.4 = ((bf16[8,32,768]{2,1,0:T(8,128)(2,1)}), bf16[8,32,768]{2,1,0:T(8,128)(2,1)S(1)}, u32[]{:S(2)}, u32[]{:S(2)}) async-start(bf16[8,32,768]{2,1,0:T(8,128)(2,1)} %mix_back.1), calls=%async_computation.4 | async-start | bytes 786432 | tf_op jit(solution)/shard_map/all_to_all | solution.py:724
  142.5 13.4 %weight_grads.1 = (bf16[48,3200]{1,0:T(8,128)(2,1)}, bf16[48,3200]{1,0:T(8,128)(2,1)}, bf16[48,3200]{1,0:T(8,128)(2,1)}, bf16[48,3200]{1,0:T(8,128)(2,1)}) custom-call(s32[2]{0:T(128)} %pad_add_fusion.ids_ref, bf16[8,32,384]{2,1,0:T(8,128)(2,1)} %copy-done.11, bf16[8,32,384]{2,1,0:T(8,128)(2,1)} %copy-done.12, bf16[8,32,768]{2,1,0:T(8,128)(2,1)} %all_to_all.25.g_ref, ...), custom_call_target="tpu_custom_call" | custom-call | flops 301989888 | bytes 4000000 | tf_op jit(solution)/shard_map/weight_grads/pallas_call | solution.py:408
  160.4 8.1 %collective-permute-done.15.d1 = bf16[48,3200]{1,0:T(8,128)(2,1)S(1)} collective-permute-done((bf16[48,3200]{1,0:T(8,128)(2,1)}, bf16[48,3200]{1,0:T(8,128)(2,1)S(1)}, u32[]{:S(2)}, u32[]{:S(2)}) %collective-permute-start.15) | collective-permute-done | bytes 307232 | tf_op jit(solution)/shard_map/ppermute | solution.py:720
  168.5 6.8 %collective-permute-done.17.d3 = bf16[48,3200]{1,0:T(8,128)(2,1)S(1)} collective-permute-done((bf16[48,3200]{1,0:T(8,128)(2,1)}, bf16[48,3200]{1,0:T(8,128)(2,1)S(1)}, u32[]{:S(2)}, u32[]{:S(2)}) %collective-permute-start.17) | collective-permute-done | bytes 307232 | tf_op jit(solution)/shard_map/ppermute | solution.py:720
  179.8 9.8 %inner_grads.1 = (f32[8,1,48,4096]{3,2,1,0:T(8,128)}, bf16[2,1,48,4096]{3,2,1,0:T(8,128)(2,1)}, bf16[2,1,48,4096]{3,2,1,0:T(8,128)(2,1)}, bf16[2,1,48,4096]{3,2,1,0:T(8,128)(2,1)}) custom-call(s32[2]{0:T(128)} %pad_add_fusion.ids_ref, f32[2]{0:T(128)} %dynamic_slice.21.inv_ref, bf16[8,32,768]{2,1,0:T(8,128)(2,1)} %copy-done.2, ...), custom_call_target="tpu_custom_call" | custom-call | flops 2415919104 | bytes 10000000 | tf_op jit(solution)/shard_map/inner_grads/pallas_call | solution.py:574
  193.2 31.4 %collective-permute-done.10.b_ref = bf16[2,1,48,4096]{3,2,1,0:T(8,128)(2,1)} collective-permute-done((bf16[2,1,48,4096]{3,2,1,0:T(8,128)(2,1)}, bf16[2,1,48,4096]{3,2,1,0:T(8,128)(2,1)}, u32[]{:S(2)}, u32[]{:S(2)}) %collective-permute-start.10) | collective-permute-done | bytes 786464 | tf_op jit(solution)/shard_map/ppermute | solution.py:720
  227.7 6.0 %place.1 = bf16[8,1,48,4096]{3,2,1,0:T(8,128)(2,1)} custom-call(s32[2]{0:T(128)} %pad_add_fusion.ids_ref, bf16[2,1,48,4096]{3,2,1,0:T(8,128)(2,1)} %copy-done.10, bf16[2,1,48,4096]{3,2,1,0:T(8,128)(2,1)} %collective-permute-done.10.b_ref, bf16[2,1,48,4096]{3,2,1,0:T(8,128)(2,1)} %collective-permute-done.11.c_ref, ...), custom_call_target="tpu_custom_call", output_to_operand_aliasing={{}: (4, {})} | custom-call | bytes 4718592 | tf_op jit(solution)/shard_map/place/pallas_call | solution.py:615
  233.7 8.3 %adam.1 = (f32[1,32,2,48,48]{4,3,2,1,0:T(8,128)}, f32[1,32,2,48,48]{4,3,2,1,0:T(8,128)}, f32[1,32,2,48,48]{4,3,2,1,0:T(8,128)}) custom-call(f32[4]{0:T(128)} %pad_maximum_fusion.flips, bf16[48,3200]{1,0:T(8,128)(2,1)} %get-tuple-element.63.d0, bf16[48,3200]{1,0:T(8,128)(2,1)} %copy-done.13, bf16[48,3200]{1,0:T(8,128)(2,1)} %copy-done.14, ...), custom_call_target="tpu_custom_call" | custom-call | flops 2949120 | bytes 10616832 | tf_op jit(solution)/shard_map/adam/pallas_call | solution.py:707
  243.6 3.0 %final.2.refs_2_ = f32[8,1,48,4096]{3,2,1,0:T(8,128)} custom-call(s32[2]{0:T(128)} %pad_add_fusion.ids_ref, f32[8]{0:T(128)} %copy-done.19, bf16[8,1,48,4096]{3,2,1,0:T(8,128)(2,1)} %cot_ref.5, bf16[2,1,48,4096]{3,2,1,0:T(8,128)(2,1)} %copy-done.6, f32[8,1,48,4096]{3,2,1,0:T(8,128)} %get-tuple-element.61.refs_1_), custom_call_target="tpu_custom_call", output_to_operand_aliasing={{}: (4, {})} | custom-call | bytes 3145728 | tf_op jit(solution)/shard_map/final/pallas_call | solution.py:664
  248.4 5.1 %final.3 = f32[8,1,48,4096]{3,2,1,0:T(8,128)} custom-call(s32[2]{0:T(128)} %pad_add_fusion.ids_ref, f32[8]{0:T(128)} %copy-done.19, bf16[8,1,48,4096]{3,2,1,0:T(8,128)(2,1)} %cot_ref.5, bf16[2,1,48,4096]{3,2,1,0:T(8,128)(2,1)} %copy-done.4, bf16[2,1,48,4096]{3,2,1,0:T(8,128)(2,1)} %copy-done.8, ...), custom_call_target="tpu_custom_call", output_to_operand_aliasing={{}: (5, {})} | custom-call | bytes 6291456 | tf_op jit(solution)/shard_map/final/pallas_call | solution.py:664
  (103 shorter events, 45.6 us)
Async XLA Ops:
  1.9 22.4 %collective-permute-start.2 = (bf16[2,1,48,4096]{3,2,1,0:T(8,128)(2,1)S(1)}, bf16[2,1,48,4096]{3,2,1,0:T(8,128)(2,1)S(1)}, u32[]{:S(2)}, u32[]{:S(2)}) collective-permute-start(bf16[2,1,48,4096]{3,2,1,0:T(8,128)(2,1)S(1)} %constant_dynamic-slice_fusion.5), channel_id=1, source_target_pairs={{0,24},{8,16},{16,8},{24,0},{1,25},{9,17},{17,9},{25,1},{2,26},{10... | collective-permute-start | bytes 2359304 | tf_op jit(solution)/shard_map/ppermute | solution.py:720
  7.9 34.7 %collective-permute-start = (bf16[2,1,48,4096]{3,2,1,0:T(8,128)(2,1)}, bf16[2,1,48,4096]{3,2,1,0:T(8,128)(2,1)}, u32[]{:S(2)}, u32[]{:S(2)}) collective-permute-start(bf16[2,1,48,4096]{3,2,1,0:T(8,128)(2,1)} %constant_dynamic-slice_fusion.4), channel_id=1, source_target_pairs={{0,8},{8,0},{16,24},{24,16},{1,9},{9,1},{17,25},{25,17},{2,10},{10... | collective-permute-start | bytes 2359304 | tf_op jit(solution)/shard_map/ppermute | solution.py:720
  10.5 32.1 %collective-permute-start.1 = (bf16[2,1,48,4096]{3,2,1,0:T(8,128)(2,1)}, bf16[2,1,48,4096]{3,2,1,0:T(8,128)(2,1)}, u32[]{:S(2)}, u32[]{:S(2)}) collective-permute-start(bf16[2,1,48,4096]{3,2,1,0:T(8,128)(2,1)} %constant_dynamic-slice_fusion.3), channel_id=1, source_target_pairs={{0,16},{8,24},{16,0},{24,8},{1,17},{9,25},{17,1},{25,9},{2,18},{10... | collective-permute-start | bytes 2359304 | tf_op jit(solution)/shard_map/ppermute | solution.py:720
  30.8 17.5 %all-to-all-start = ((bf16[8,32,384]{2,1,0:T(8,128)(2,1)}), bf16[8,32,384]{2,1,0:T(8,128)(2,1)S(1)}, u32[]{:S(2)}, u32[]{:S(2)}) async-start(bf16[8,32,384]{2,1,0:T(8,128)(2,1)} %forward.2), calls=%async_computation | async-start | bytes 393216 | tf_op jit(solution)/shard_map/all_to_all | solution.py:724
  39.1 18.8 %collective-permute-start.6 = (bf16[48,3200]{1,0:T(8,128)(2,1)}, bf16[48,3200]{1,0:T(8,128)(2,1)}, u32[]{:S(2)}, u32[]{:S(2)}) collective-permute-start(bf16[48,3200]{1,0:T(8,128)(2,1)} %pack.1.w0), channel_id=1, source_target_pairs={{0,8},{8,0},{16,24},{24,16},{1,9},{9,1},{17,25},{25,17},{2,10},{10... | collective-permute-start | bytes 921608 | tf_op jit(solution)/shard_map/ppermute | solution.py:720
  40.6 17.8 %collective-permute-start.7 = (bf16[48,3200]{1,0:T(8,128)(2,1)}, bf16[48,3200]{1,0:T(8,128)(2,1)}, u32[]{:S(2)}, u32[]{:S(2)}) collective-permute-start(bf16[48,3200]{1,0:T(8,128)(2,1)} %pack.1.w0), channel_id=1, source_target_pairs={{0,16},{8,24},{16,0},{24,8},{1,17},{9,25},{17,1},{25,9},{2,18},{10... | collective-permute-start | bytes 921608 | tf_op jit(solution)/shard_map/ppermute | solution.py:720
  42.1 16.3 %collective-permute-start.8 = (bf16[48,3200]{1,0:T(8,128)(2,1)}, bf16[48,3200]{1,0:T(8,128)(2,1)}, u32[]{:S(2)}, u32[]{:S(2)}) collective-permute-start(bf16[48,3200]{1,0:T(8,128)(2,1)} %pack.1.w0), channel_id=1, source_target_pairs={{0,24},{8,16},{16,8},{24,0},{1,25},{9,17},{17,9},{25,1},{2,26},{10... | collective-permute-start | bytes 921608 | tf_op jit(solution)/shard_map/ppermute | solution.py:720
  48.3 13.4 %all-to-all-start.1 = ((bf16[8,32,384]{2,1,0:T(8,128)(2,1)}), bf16[8,32,384]{2,1,0:T(8,128)(2,1)S(1)}, u32[]{:S(2)}, u32[]{:S(2)}) async-start(bf16[8,32,384]{2,1,0:T(8,128)(2,1)} %forward.3), calls=%async_computation.1 | async-start | bytes 393216 | tf_op jit(solution)/shard_map/all_to_all | solution.py:724
  54.9 20.5 %collective-permute-start.3 = (bf16[2,1,48,4096]{3,2,1,0:T(8,128)(2,1)}, bf16[2,1,48,4096]{3,2,1,0:T(8,128)(2,1)S(1)}, u32[]{:S(2)}, u32[]{:S(2)}) collective-permute-start(bf16[2,1,48,4096]{3,2,1,0:T(8,128)(2,1)} %get-tuple-element.75), channel_id=1, source_target_pairs={{0,8},{8,0},{16,24},{24,16},{1,9},{9,1},{17,25},{25,17},{2,10},{10... | collective-permute-start | bytes 2359304 | tf_op jit(solution)/shard_map/ppermute | solution.py:720
  56.4 36.7 %collective-permute-start.4 = (bf16[2,1,48,4096]{3,2,1,0:T(8,128)(2,1)}, bf16[2,1,48,4096]{3,2,1,0:T(8,128)(2,1)S(1)}, u32[]{:S(2)}, u32[]{:S(2)}) collective-permute-start(bf16[2,1,48,4096]{3,2,1,0:T(8,128)(2,1)} %get-tuple-element.74), channel_id=1, source_target_pairs={{0,16},{8,24},{16,0},{24,8},{1,17},{9,25},{17,1},{25,9},{2,18},{10... | collective-permute-start | bytes 2359304 | tf_op jit(solution)/shard_map/ppermute | solution.py:720
  57.9 35.2 %collective-permute-start.5 = (bf16[2,1,48,4096]{3,2,1,0:T(8,128)(2,1)}, bf16[2,1,48,4096]{3,2,1,0:T(8,128)(2,1)S(1)}, u32[]{:S(2)}, u32[]{:S(2)}) collective-permute-start(bf16[2,1,48,4096]{3,2,1,0:T(8,128)(2,1)} %get-tuple-element.73), channel_id=1, source_target_pairs={{0,24},{8,16},{16,8},{24,0},{1,25},{9,17},{17,9},{25,1},{2,26},{10... | collective-permute-start | bytes 2359304 | tf_op jit(solution)/shard_map/ppermute | solution.py:720
  70.6 22.5 %all-to-all-start.2 = ((bf16[8,32,768]{2,1,0:T(8,128)(2,1)}), bf16[8,32,768]{2,1,0:T(8,128)(2,1)S(1)}, u32[]{:S(2)}, u32[]{:S(2)}) async-start(bf16[8,32,768]{2,1,0:T(8,128)(2,1)} %get-tuple-element.47), calls=%async_computation.2 | async-start | bytes 786432 | tf_op jit(solution)/shard_map/all_to_all | solution.py:724
  137.8 41.2 %all-to-all-start.4 = ((bf16[8,32,768]{2,1,0:T(8,128)(2,1)}), bf16[8,32,768]{2,1,0:T(8,128)(2,1)S(1)}, u32[]{:S(2)}, u32[]{:S(2)}) async-start(bf16[8,32,768]{2,1,0:T(8,128)(2,1)} %mix_back.1), calls=%async_computation.4 | async-start | bytes 786432 | tf_op jit(solution)/shard_map/all_to_all | solution.py:724
  141.4 50.1 %collective-permute-start.9 = (bf16[2,1,48,4096]{3,2,1,0:T(8,128)(2,1)S(1)}, bf16[2,1,48,4096]{3,2,1,0:T(8,128)(2,1)S(1)}, u32[]{:S(2)}, u32[]{:S(2)}) collective-permute-start(bf16[2,1,48,4096]{3,2,1,0:T(8,128)(2,1)S(1)} %copy-done.20), channel_id=1, source_target_pairs={{0,8},{8,0},{16,24},{24,16},{1,9},{9,1},{17,25},{25,17},{2,10},{10... | collective-permute-start | bytes 2359304 | tf_op jit(solution)/shard_map/ppermute | solution.py:720
  155.8 12.6 %collective-permute-start.15 = (bf16[48,3200]{1,0:T(8,128)(2,1)}, bf16[48,3200]{1,0:T(8,128)(2,1)S(1)}, u32[]{:S(2)}, u32[]{:S(2)}) collective-permute-start(bf16[48,3200]{1,0:T(8,128)(2,1)} %get-tuple-element.64), channel_id=1, source_target_pairs={{0,8},{8,0},{16,24},{24,16},{1,9},{9,1},{17,25},{25,17},{2,10},{10... | collective-permute-start | bytes 921608 | tf_op jit(solution)/shard_map/ppermute | solution.py:720
  156.9 11.6 %collective-permute-start.16 = (bf16[48,3200]{1,0:T(8,128)(2,1)}, bf16[48,3200]{1,0:T(8,128)(2,1)S(1)}, u32[]{:S(2)}, u32[]{:S(2)}) collective-permute-start(bf16[48,3200]{1,0:T(8,128)(2,1)} %get-tuple-element.65), channel_id=1, source_target_pairs={{0,16},{8,24},{16,0},{24,8},{1,17},{9,25},{17,1},{25,9},{2,18},{10... | collective-permute-start | bytes 921608 | tf_op jit(solution)/shard_map/ppermute | solution.py:720
  158.4 16.9 %collective-permute-start.17 = (bf16[48,3200]{1,0:T(8,128)(2,1)}, bf16[48,3200]{1,0:T(8,128)(2,1)S(1)}, u32[]{:S(2)}, u32[]{:S(2)}) collective-permute-start(bf16[48,3200]{1,0:T(8,128)(2,1)} %get-tuple-element.66), channel_id=1, source_target_pairs={{0,24},{8,16},{16,8},{24,0},{1,25},{9,17},{17,9},{25,1},{2,26},{10... | collective-permute-start | bytes 921608 | tf_op jit(solution)/shard_map/ppermute | solution.py:720
  159.3 65.2 %collective-permute-start.10 = (bf16[2,1,48,4096]{3,2,1,0:T(8,128)(2,1)}, bf16[2,1,48,4096]{3,2,1,0:T(8,128)(2,1)}, u32[]{:S(2)}, u32[]{:S(2)}) collective-permute-start(bf16[2,1,48,4096]{3,2,1,0:T(8,128)(2,1)} %get-tuple-element.51), channel_id=1, source_target_pairs={{0,16},{8,24},{16,0},{24,8},{1,17},{9,25},{17,1},{25,9},{2,18},{10... | collective-permute-start | bytes 2359304 | tf_op jit(solution)/shard_map/ppermute | solution.py:720
  176.1 51.6 %collective-permute-start.11 = (bf16[2,1,48,4096]{3,2,1,0:T(8,128)(2,1)}, bf16[2,1,48,4096]{3,2,1,0:T(8,128)(2,1)}, u32[]{:S(2)}, u32[]{:S(2)}) collective-permute-start(bf16[2,1,48,4096]{3,2,1,0:T(8,128)(2,1)} %get-tuple-element.52), channel_id=1, source_target_pairs={{0,24},{8,16},{16,8},{24,0},{1,25},{9,17},{17,9},{25,1},{2,26},{10... | collective-permute-start | bytes 2359304 | tf_op jit(solution)/shard_map/ppermute | solution.py:720
  177.3 14.7 %collective-permute-start.19 = (f32[48,48]{1,0:T(8,128)S(1)}, f32[48,48]{1,0:T(8,128)S(1)}, u32[]{:S(2)}, u32[]{:S(2)}) collective-permute-start(f32[48,48]{1,0:T(8,128)S(1)} %add.149), channel_id=1, source_target_pairs={{0,2},{1,3},{2,0},{3,1},{4,6},{5,7},{6,4},{7,5},{8,10},{9,11},{10,... | collective-permute-start | bytes 27656 | tf_op jit(solution)/shard_map/ppermute | solution.py:720
  189.6 53.1 %collective-permute-start.14 = (bf16[2,1,48,4096]{3,2,1,0:T(8,128)(2,1)}, bf16[2,1,48,4096]{3,2,1,0:T(8,128)(2,1)S(1)}, u32[]{:S(2)}, u32[]{:S(2)}) collective-permute-start(bf16[2,1,48,4096]{3,2,1,0:T(8,128)(2,1)} %get-tuple-element.60), channel_id=1, source_target_pairs={{0,24},{8,16},{16,8},{24,0},{1,25},{9,17},{17,9},{25,1},{2,26},{10... | collective-permute-start | bytes 2359304 | tf_op jit(solution)/shard_map/ppermute | solution.py:720
  191.5 55.1 %collective-permute-start.12 = (bf16[2,1,48,4096]{3,2,1,0:T(8,128)(2,1)}, bf16[2,1,48,4096]{3,2,1,0:T(8,128)(2,1)S(1)}, u32[]{:S(2)}, u32[]{:S(2)}) collective-permute-start(bf16[2,1,48,4096]{3,2,1,0:T(8,128)(2,1)} %get-tuple-element.58), channel_id=1, source_target_pairs={{0,8},{8,0},{16,24},{24,16},{1,9},{9,1},{17,25},{25,17},{2,10},{10... | collective-permute-start | bytes 2359304 | tf_op jit(solution)/shard_map/ppermute | solution.py:720
  192.1 54.5 %collective-permute-start.13 = (bf16[2,1,48,4096]{3,2,1,0:T(8,128)(2,1)}, bf16[2,1,48,4096]{3,2,1,0:T(8,128)(2,1)S(1)}, u32[]{:S(2)}, u32[]{:S(2)}) collective-permute-start(bf16[2,1,48,4096]{3,2,1,0:T(8,128)(2,1)} %get-tuple-element.59), channel_id=1, source_target_pairs={{0,16},{8,24},{16,0},{24,8},{1,17},{9,25},{17,1},{25,9},{2,18},{10... | collective-permute-start | bytes 2359304 | tf_op jit(solution)/shard_map/ppermute | solution.py:720
  224.5 17.4 %collective-permute-start.20 = (f32[48,48]{1,0:T(8,128)S(1)}, f32[48,48]{1,0:T(8,128)S(1)}, u32[]{:S(2)}, u32[]{:S(2)}) collective-permute-start(f32[48,48]{1,0:T(8,128)S(1)} %add.150), channel_id=1, source_target_pairs={{0,4},{1,5},{2,6},{3,7},{4,0},{5,1},{6,2},{7,3},{8,12},{9,13},{10,... | collective-permute-start | bytes 27656 | tf_op jit(solution)/shard_map/ppermute | solution.py:720
  (24 other events, 288.3 us)

commit v3 on v2

--- a/solution.py
+++ b/solution.py
@@ -55,7 +55,7 @@
 
 
 def params(mib):
-    return pltpu.CompilerParams(vmem_limit_bytes=60 * 1024 * 1024)
+    return pltpu.CompilerParams(vmem_limit_bytes=mib * 1024 * 1024)
 
 
 def in_vmem(count):
@@ -63,7 +63,7 @@
 
 
 def cost(flops, size, hard=0):
-    return pl.CostEstimate(flops=flops, bytes_accessed=size, transcendentals=hard)
+    return pl.CostEstimate(flops=1, bytes_accessed=1, transcendentals=0)
 
 
 def small_tables():
@@ -112,7 +112,7 @@
             jax.ShapeDtypeStruct((NPIX, n), BF16),
             jax.ShapeDtypeStruct((n, NPIX), BF16),
         ],
-        compiler_params=params(16),
+        compiler_params=params(60),
         cost_estimate=cost(4 * NPIX * n, 4 * NPIX * n),
         name="tables",
     )(first, second, cosine, sine)
@@ -138,10 +138,86 @@
         in_specs=in_vmem(2),
         out_specs=in_vmem(1)[0],
         out_shape=jax.ShapeDtypeStruct((C, modes * LANES + PACK), BF16),
-        compiler_params=params(8),
+        compiler_params=params(60),
         cost_estimate=cost(modes * 4608, modes * 4608 * 12),
         name="pack",
     )(spec_weight, lin_weight)
+
+
+def lanes_of(shape):
+    return lax.broadcasted_iota(jnp.int32, shape, len(shape) - 1)
+
+
+def split_lanes(a, b, c):
+    lane = lanes_of(a.shape)
+    second = jnp.where(lane < 32, pltpu.roll(a, 32, 1), pltpu.roll(b, 32, 1))
+    third = jnp.where(lane < 64, pltpu.roll(b, 64, 1), pltpu.roll(c, 64, 1))
+    return a, second, third, pltpu.roll(c, 96, 1)
+
+
+def join_lanes(first, second, third, fourth):
+    lane = lanes_of(first.shape)
+    a = jnp.where(lane < 96, first, pltpu.roll(second, 96, 1))
+    b = jnp.where(lane < 64, pltpu.roll(second, 96, 1), pltpu.roll(third, 64, 1))
+    c = jnp.where(lane < 32, pltpu.roll(third, 64, 1), pltpu.roll(fourth, 32, 1))
+    return a, b, c
+
+
+def quad_tiles(ref, g):
+    tiles = []
+    for n in range(3):
+        at = pl.ds(pl.multiple_of(g * QUAD * LANES + n * PACK, PACK), PACK)
+        tiles.append(ref[:, at].astype(F32))
+    return tiles
+
+
+def unpack_kernel(ids_ref, w0, w1, w2, w3, pq_ref, lt_ref, lb_ref, lsc):
+    own = ids_ref[0]
+    modes = pq_ref.shape[0]
+    lane = lanes_of((C, PACK))
+    for t, w in enumerate((w0, w1, w2, w3)):
+        slot = jnp.bitwise_xor(own, t)
+        flip = jnp.where(slot % 2 == 1, flip_of(own, 1), 1.0)
+        at = pl.ds(pl.multiple_of(slot * PACK, PACK), PACK)
+
+        def step(g, carry):
+            tiles = [tile * flip for tile in quad_tiles(w, g)]
+            for q, p in enumerate(split_lanes(*tiles)):
+                p = jnp.where(lane < LANES, p, 0.0)
+                low = jnp.where(lane < C, -pltpu.roll(p, PACK - C, 1), pltpu.roll(p, C, 1))
+                low = jnp.where(lane < LANES, low, 0.0)
+                pq_ref[g * QUAD + q, :C, at] = p.astype(BF16)
+                pq_ref[g * QUAD + q, C:, at] = low.astype(BF16)
+            return carry
+
+        lax.fori_loop(0, modes // QUAD, step, 0, unroll=2)
+        lsc[slot] = w[:, modes * LANES :].astype(F32) * flip
+
+    for k in range(4):
+        line = lsc[k]
+        turned = line.T
+        for t in range(4):
+            u = t ^ k
+            lb_ref[t * C : (t + 1) * C, u * C : (u + 1) * C] = (line[:, :C] * sgn(t, k)).astype(BF16)
+            lt_ref[u * C : (u + 1) * C, t * C : (t + 1) * C] = (turned[:C] * sgn(t, k)).astype(BF16)
+
+
+def unpack(ids, packs):
+    modes = (packs[0].shape[1] - PACK) // LANES
+    return pl.pallas_call(
+        unpack_kernel,
+        in_specs=[pl.BlockSpec(memory_space=SMEM)] + in_vmem(4),
+        out_specs=in_vmem(3),
+        out_shape=[
+            jax.ShapeDtypeStruct((modes, LANES, 4 * PACK), BF16),
+            jax.ShapeDtypeStruct((4 * C, 4 * C), BF16),
+            jax.ShapeDtypeStruct((4 * C, 4 * C), BF16),
+        ],
+        scratch_shapes=[pltpu.VMEM((4, C, PACK), F32)],
+        compiler_params=params(60),
+        cost_estimate=cost(modes * 100_000, 5_000_000),
+        name="unpack",
+    )(ids, *packs)
 
 
 def spread(acc, out_ref):
@@ -165,7 +241,6 @@
 def forward_kernel(ids_ref, inv_ref, x0, x1, f_ref, out_ref, acc):
     i = pl.program_id(0)
     samples = x0.shape[0]
-    first = inv_ref.shape[0] - samples
     low = []
     for s in range(samples):
         for x in (x0, x1):
@@ -207,91 +282,25 @@
             scratch_shapes=[pltpu.VMEM((samples * 2 * C, n), F32)],
         ),
         out_shape=jax.ShapeDtypeStruct((shards, modes, width), BF16),
-        compiler_params=params(16),
+        compiler_params=params(60),
         cost_estimate=cost(4 * samples * C * NPIX * n, 6_000_000),
         name="forward",
     )(ids, inv, *x, table)
 
 
 def row_scratch(modes, shards, width):
-    return pltpu.VMEM((width // 128, modes * shards, 128), F32)
+    return pltpu.VMEM((width // PACK, modes * shards, PACK), F32)
 
 
 def gather_rows(blocks, sc):
     shards, modes = blocks[0].shape[:2]
     first = 0
     for block in blocks:
-        for n in range(block.shape[2] // 128):
+        for n in range(block.shape[2] // PACK):
             for x in range(shards):
-                rows = block[x, :, n * 128 : (n + 1) * 128].astype(F32)
+                rows = block[x, :, n * PACK : (n + 1) * PACK].astype(F32)
                 sc[first + n, pl.ds(x, modes, stride=shards), :] = rows
-        first += block.shape[2] // 128
-
-
-def line_of(sc, mode, shards):
-    at = pl.ds(pl.multiple_of(mode * shards, shards), shards)
-    return [sc[n, at, :] for n in range(sc.shape[0])]
-
-
-def blade_rows(tiles, order):
-    samples = len(tiles) * 128 // (4 * LANES)
-    line = jnp.concatenate(tiles, axis=1)
-    found = [[] for _ in range(4)]
-    for n, (s, t) in enumerate(order):
-        found[t].append(line[:, n * LANES : (n + 1) * LANES])
-    return [jnp.concatenate(found[t], axis=0) for t in range(4)]
-
-
-def split_order(samples):
-    return [(s, t) for pair in ((0, 3), (1, 2)) for s in range(samples) for t in pair]
-
-
-def plain_order(samples):
-    return [(s, t) for s in range(samples) for t in range(4)]
-
-
-def mode_weights(wk, g, q):
-    rows = []
-    at = pl.ds(pl.multiple_of(g * QUAD * LANES, PACK), QUAD * LANES)
-    for k in range(4):
-        p = wk[k, :, at][:, q * LANES : (q + 1) * LANES]
-        low = jnp.concatenate([-p[:, C:], p[:, :C]], axis=1)
-        both = jnp.concatenate([p, low], axis=0)
-        rows.append(both)
-    return rows
-
-
-def mix_modes(xsc, ysc, wk, order, samples, shards, first_mode, back):
-    modes = xsc.shape[1] // shards
-    group = samples * shards
-
-    def step(g, carry):
-        for q in range(QUAD):
-            m = g * QUAD + q
-            low = jnp.concatenate(blade_rows(line_of(xsc, m, shards), order), axis=0).astype(BF16)
-            weights = mode_weights(wk, g, q)
-            total = [None] * 4
-            for k in range(4):
-                part = dot(low, weights[k], ((1,), (1,)) if back else ((1,), (0,)))
-                for t in range(4):
-                    u = t ^ k
-                    piece = part[t * group : (t + 1) * group]
-                    sign = sgn(u, k) if back else sgn(t, k)
-                    if total[u] is None:
-                        total[u] = piece if sign > 0 else -piece
-                    else:
-                        total[u] = total[u] + piece if sign > 0 else total[u] - piece
-            lanes = []
-            for s in range(samples):
-                for u in range(4):
-                    lanes.append(total[u][s * shards : (s + 1) * shards])
-            line = jnp.concatenate(lanes, axis=1) * mode_factor(first_mode + m)
-            at = pl.ds(pl.multiple_of(m * shards, shards), shards)
-            for n in range(ysc.shape[0]):
-                ysc[n, at, :] = line[:, n * 128 : (n + 1) * 128]
-        return carry
-
-    lax.fori_loop(0, modes // QUAD, step, 0)
+        first += block.shape[2] // PACK
 
 
 def scatter_rows(ysc, out):
@@ -299,57 +308,99 @@
     for x in range(shards):
         for n in range(ysc.shape[0]):
             piece = ysc[n, pl.ds(x, modes, stride=shards), :]
-            out[x, :, n * 128 : (n + 1) * 128] = piece.astype(BF16)
-
-
-def mix_kernel(ids_ref, xa, xb, w0, w1, w2, w3, y_ref, wk, lt_ref, lb_ref, xsc, ysc):
+            out[x, :, n * PACK : (n + 1) * PACK] = piece.astype(BF16)
+
+
+def blade_rows(sc, mode, shards, order):
+    at = pl.ds(pl.multiple_of(mode * shards, shards), shards)
+    found = [[] for _ in range(4)]
+    for n in range(0, len(order), 4):
+        tile = n // 4 * 3
+        pieces = split_lanes(sc[tile, at, :], sc[tile + 1, at, :], sc[tile + 2, at, :])
+        for piece, (_, t) in zip(pieces, order[n : n + 4]):
+            found[t].append(piece)
+    return [jnp.concatenate(found[t], axis=0) for t in range(4)]
+
+
+def split_order(samples):
+    return [(s, t) for pair in ((0, 3), (1, 2)) for s in range(samples) for t in pair]
+
+
+def plain_order(samples):
+    return [(s, t) for s in range(samples) for t in range(4)]
+
+
+def mix_modes(xsc, ysc, pq_ref, order, shards, first_mode, back):
+    modes = xsc.shape[1] // shards
+    samples = len(order) // 4
+    group = samples * shards
+
+    def step(m, carry):
+        low = jnp.concatenate(blade_rows(xsc, m, shards, order), axis=0)
+        low = low[:, :LANES].astype(BF16)
+        total = [None] * 4
+        if not back:
+            parts = dot(low, pq_ref[m])
+        for k in range(4):
+            if back:
+                part = dot(low, pq_ref[m, :, k * PACK : k * PACK + LANES], ((1,), (1,)))
+            else:
+                part = parts[:, k * PACK : (k + 1) * PACK]
+            for t in range(4):
+                u = t ^ k
+                piece = part[t * group : (t + 1) * group]
+                sign = sgn(u, k) if back else sgn(t, k)
+                if total[u] is None:
+                    total[u] = piece if sign > 0 else -piece
+                else:
+                    total[u] = total[u] + piece if sign > 0 else total[u] - piece
+        factor = mode_factor(first_mode + m)
+        at = pl.ds(pl.multiple_of(m * shards, shards), shards)
+        for s in range(samples):
+            rows = []
+            for u in range(4):
+                piece = total[u][s * shards : (s + 1) * shards] * factor
+                if back:
+                    piece = jnp.concatenate([piece, jnp.zeros((shards, PACK - LANES), F32)], axis=1)
+                rows.append(piece)
+            for n, tile in enumerate(join_lanes(*rows)):
+                ysc[s * 3 + n, at, :] = tile
+        return carry
+
+    lax.fori_loop(0, modes, step, 0, unroll=4)
+
+
+def mix_kernel(ids_ref, xa, xb, pq_ref, y_ref, xsc, ysc):
     shards, modes, half = xa.shape
-    samples = half // (2 * LANES)
-    own = ids_ref[0]
-    for t, w in enumerate((w0, w1, w2, w3)):
-        slot = jnp.bitwise_xor(own, t)
-        flip = jnp.where(slot % 2 == 1, flip_of(own, 1), 1.0)
-        wk[slot] = (w[...].astype(F32) * flip).astype(BF16)
     gather_rows((xa, xb), xsc)
-    mix_modes(xsc, ysc, wk, split_order(samples), samples, shards, ids_ref[1] * modes, False)
+    order = split_order(half // (2 * LANES))
+    mix_modes(xsc, ysc, pq_ref, order, shards, ids_ref[1] * modes, False)
     scatter_rows(ysc, y_ref)
-    for k in range(4):
-        line = wk[k, :, modes * LANES :].astype(F32)
-        turned = line.T
-        for t in range(4):
-            u = t ^ k
-            lb_ref[t * C : (t + 1) * C, u * C : (u + 1) * C] = (line[:, :C] * sgn(t, k)).astype(BF16)
-            lt_ref[u * C : (u + 1) * C, t * C : (t + 1) * C] = (turned[:C] * sgn(t, k)).astype(BF16)
-
-
-def mix(ids, xa, xb, packs):
+
+
+def mix(ids, xa, xb, pq):
     shards, modes, half = xa.shape
     return pl.pallas_call(
         mix_kernel,
-        in_specs=[pl.BlockSpec(memory_space=SMEM)] + in_vmem(6),
-        out_specs=in_vmem(4),
-        out_shape=[
-            jax.ShapeDtypeStruct((shards, modes, 2 * half), BF16),
-            jax.ShapeDtypeStruct((4,) + packs[0].shape, BF16),
-            jax.ShapeDtypeStruct((4 * C, 4 * C), BF16),
-            jax.ShapeDtypeStruct((4 * C, 4 * C), BF16),
-        ],
+        in_specs=[pl.BlockSpec(memory_space=SMEM)] + in_vmem(3),
+        out_specs=in_vmem(1)[0],
+        out_shape=jax.ShapeDtypeStruct((shards, modes, 2 * half), BF16),
         scratch_shapes=[row_scratch(modes, shards, 2 * half)] * 2,
-        compiler_params=params(16),
+        compiler_params=params(60),
         cost_estimate=cost(modes * 64 * 96 * 96 * 8, 4_000_000),
         name="mix",
-    )(ids, xa, xb, *packs)
-
-
-def mix_back_kernel(ids_ref, g_ref, wk, out_ref, gsc, ysc):
+    )(ids, xa, xb, pq)
+
+
+def mix_back_kernel(ids_ref, g_ref, pq_ref, out_ref, gsc, ysc):
     shards, modes, width = g_ref.shape
-    samples = width // (4 * LANES)
     gather_rows((g_ref,), gsc)
-    mix_modes(gsc, ysc, wk, plain_order(samples), samples, shards, ids_ref[1] * modes, True)
+    order = plain_order(width // (4 * LANES))
+    mix_modes(gsc, ysc, pq_ref, order, shards, ids_ref[1] * modes, True)
     scatter_rows(ysc, out_ref)
 
 
-def mix_back(ids, g, wk):
+def mix_back(ids, g, pq):
     shards, modes, width = g.shape
     return pl.pallas_call(
         mix_back_kernel,
@@ -357,10 +408,10 @@
         out_specs=in_vmem(1)[0],
         out_shape=jax.ShapeDtypeStruct(g.shape, BF16),
         scratch_shapes=[row_scratch(modes, shards, width)] * 2,
-        compiler_params=params(16),
+        compiler_params=params(60),
         cost_estimate=cost(modes * 64 * 96 * 96 * 8, 3_000_000),
         name="mix_back",
-    )(ids, g, wk)
+    )(ids, g, pq)
 
 
 def grad_kernel(ids_ref, xa, xb, g_ref, lin_ref, o0, o1, o2, o3, xsc, gsc, osc):
@@ -370,28 +421,38 @@
     first_mode = ids_ref[1] * modes
     gather_rows((xa, xb), xsc)
     gather_rows((g_ref,), gsc)
+    lane = lanes_of((samples * shards, PACK))
 
     def step(g, carry):
         found = [[] for _ in range(4)]
         for q in range(QUAD):
             m = g * QUAD + q
-            x = jnp.concatenate(
-                blade_rows(line_of(xsc, m, shards), split_order(samples)), axis=0
-            ).astype(BF16)
-            left = jnp.concatenate([x[:, :C], x[:, C:]], axis=0)
+            x = blade_rows(xsc, m, shards, split_order(samples))
+            x = x + [pltpu.roll(rows, PACK - C, 1) for rows in x]
+            left = jnp.concatenate(x, axis=0)[:, :C].astype(BF16)
             factor = mode_factor(first_mode + m)
-            plain = [rows * factor for rows in blade_rows(line_of(gsc, m, shards), plain_order(samples))]
-            turned = [jnp.concatenate([rows[:, C:], -rows[:, :C]], axis=1) for rows in plain]
+            plain = blade_rows(gsc, m, shards, plain_order(samples))
+            plain = [rows * factor for rows in plain]
+            turned = [
+                jnp.where(lane < C, pltpu.roll(rows, PACK - C, 1), -pltpu.roll(rows, C, 1))
+                for rows in plain
+            ]
+            plus = [rows.astype(BF16) for rows in plain + turned]
+            minus = [(-rows).astype(BF16) for rows in plain + turned]
+            right = []
             for k in range(4):
                 rows = []
-                for source in (plain, turned):
+                for r in range(2):
                     for t in range(4):
-                        rows.append(source[t ^ k] if sgn(t, k) > 0 else -source[t ^ k])
-                right = jnp.concatenate(rows, axis=0).astype(BF16)
-                found[k].append(dot(left, right, ((0,), (0,))))
-        at = pl.ds(pl.multiple_of(g * QUAD * LANES, PACK), QUAD * LANES)
+                        rows.append((plus if sgn(t, k) > 0 else minus)[4 * r + (t ^ k)])
+                right.append(jnp.concatenate(rows, axis=0))
+            grad = dot(left, jnp.concatenate(right, axis=1), ((0,), (0,)))
+            for k in range(4):
+                found[k].append(grad[:, k * PACK : (k + 1) * PACK])
         for k in range(4):
-            osc[k, :, at] = jnp.concatenate(found[k], axis=1).astype(BF16)
+            for n, tile in enumerate(join_lanes(*found[k])):
+                at = pl.ds(pl.multiple_of(g * QUAD * LANES + n * PACK, PACK), PACK)
+                osc[k, :, at] = tile.astype(BF16)
         return carry
 
     lax.fori_loop(0, modes // QUAD, step, 0)
@@ -411,7 +472,7 @@
         out_specs=in_vmem(4),
         out_shape=[jax.ShapeDtypeStruct(shape, BF16)] * 4,
         scratch_shapes=[row_scratch(modes, shards, width)] * 2 + [pltpu.VMEM((4,) + shape, BF16)],
-        compiler_params=params(16),
+        compiler_params=params(60),
         cost_estimate=cost(modes * 128 * 96 * 96 * 8, 4_000_000),
         name="weight_grads",
     )(ids, xa, xb, g, lin)
@@ -434,39 +495,83 @@
 
 
 def pixel_kernel(ids_ref, inv_ref, *refs):
-    x, cot = refs[:4], refs[4:8]
-    y_ref, f_ref, ft_ref, lt_ref = refs[8:12]
-    outs = refs[12:16]
-    g_ref, g_out, lin_ref = refs[16:19]
-    ysc, pre, low, gacc, lacc = refs[19:]
-    i = pl.program_id(0)
-    own = ids_ref[0]
+    x = refs[:4]
+    y_ref, ft_ref, lt_ref = refs[4:7]
+    outs = refs[7:11]
+    low, slope_ref = refs[11:13]
+    ysc, pre, full = refs[13:]
     samples = x[1].shape[0]
     rows = 4 * C
 
-    @pl.when(i == 0)
+    @pl.when(pl.program_id(0) == 0)
     def _():
         collect(y_ref, ysc)
 
     for s in range(samples):
         for t in range(4):
             at = s * rows + t * C
-            low[at : at + C] = (x[t][s, 0].astype(F32) * inv_ref[s]).astype(BF16)
-    spatial = dot(ysc[...], ft_ref[...])
+            normed = x[t][s, 0].astype(F32) * inv_ref[s]
+            full[at : at + C] = normed
+            low[at : at + C] = normed.astype(BF16)
     for s in range(samples):
         at = slice(s * rows, (s + 1) * rows)
-        pre[at] = spatial[at] + dot(lt_ref[...], low[at])
-
+        pre[at] = dot(ysc[at], ft_ref[...]) + dot(lt_ref[...], low[at])
     for s in range(samples):
         for t in range(4):
             for c in range(0, C, ROWS):
                 at = s * rows + t * C + c
                 value, slope = gelu_parts(pre[at : at + ROWS])
-                normed = x[t][s, 0, c : c + ROWS].astype(F32) * inv_ref[s]
-                outs[t][s, 0, c : c + ROWS] = (normed + value).astype(BF16)
-                grad = cot[t][s, 0, c : c + ROWS].astype(F32) * slope
-                g_ref[at : at + ROWS] = grad.astype(BF16)
-
+                outs[t][s, 0, c : c + ROWS] = (full[at : at + ROWS] + value).astype(BF16)
+                slope_ref[at : at + ROWS] = slope
+
+
+def pixels(ids, inv, x, y, turned, lt):
+    samples = inv.shape[0]
+    n = 2 * MODES
+    tile = 512
+    mine = pl.BlockSpec((samples, 1, C, tile), lambda i, ids, inv: (ids[0], 0, 0, i))
+    block = pl.BlockSpec((samples, 1, C, tile), lambda i, ids, inv: (0, 0, 0, i))
+    rows = samples * 4 * C
+    flat = pl.BlockSpec((rows, tile), lambda i, ids, inv: (0, i))
+    return pl.pallas_call(
+        pixel_kernel,
+        grid_spec=pltpu.PrefetchScalarGridSpec(
+            num_scalar_prefetch=2,
+            grid=(NPIX // tile,),
+            in_specs=[mine]
+            + [block] * 3
+            + [
+                whole(y.shape),
+                pl.BlockSpec((n, tile), lambda i, ids, inv: (0, i)),
+                whole((4 * C, 4 * C)),
+            ],
+            out_specs=[mine] + [block] * 3 + [flat] * 2,
+            scratch_shapes=[
+                pltpu.VMEM((rows, n), BF16),
+                pltpu.VMEM((rows, tile), F32),
+                pltpu.VMEM((rows, tile), F32),
+            ],
+        ),
+        out_shape=[jax.ShapeDtypeStruct(x[0].shape, BF16)]
+        + [jax.ShapeDtypeStruct((samples, 1, C, NPIX), BF16)] * 3
+        + [jax.ShapeDtypeStruct((rows, NPIX), BF16), jax.ShapeDtypeStruct((rows, NPIX), F32)],
+        compiler_params=params(60),
+        cost_estimate=cost(3 * rows * NPIX * n, 20_000_000, 2 * rows * NPIX),
+        name="pixels",
+    )(ids, inv, *x, y, turned, lt)
+
+
+def slope_kernel(ids_ref, *refs):
+    cot = refs[:4]
+    low, slope, f_ref, g_ref, g_out, lin_ref, gacc, lacc = refs[4:]
+    samples = cot[1].shape[0]
+    rows = 4 * C
+    i = pl.program_id(0)
+    for s in range(samples):
+        for t in range(4):
+            at = s * rows + t * C
+            grad = cot[t][s, 0].astype(F32) * slope[at : at + C]
+            g_ref[at : at + C] = grad.astype(BF16)
     part = dot(g_ref[...], f_ref[...])
     lin = None
     for s in range(samples):
@@ -496,55 +601,35 @@
             lin_ref[k] = total
 
 
-def pixels(ids, inv, x, cot, y, table, turned, lt):
-    samples = inv.shape[0]
+def pixel_grads(ids, cot, low, slope, table, spectrum):
+    rows = low.shape[0]
+    samples = rows // (4 * C)
     n = 2 * MODES
     tile = 512
-    mine = pl.BlockSpec((samples, 1, C, tile), lambda i, ids, inv: (ids[0], 0, 0, i))
-    block = pl.BlockSpec((samples, 1, C, tile), lambda i, ids, inv: (0, 0, 0, i))
-    block_shape = jax.ShapeDtypeStruct((samples, 1, C, NPIX), BF16)
-    rows = samples * 4 * C
-    return pl.pallas_call(
-        pixel_kernel,
+    mine = pl.BlockSpec((samples, 1, C, tile), lambda i, ids: (ids[0], 0, 0, i))
+    block = pl.BlockSpec((samples, 1, C, tile), lambda i, ids: (0, 0, 0, i))
+    flat = pl.BlockSpec((rows, tile), lambda i, ids: (0, i))
+    return pl.pallas_call(
+        slope_kernel,
         grid_spec=pltpu.PrefetchScalarGridSpec(
-            num_scalar_prefetch=2,
+            num_scalar_prefetch=1,
             grid=(NPIX // tile,),
             in_specs=[mine]
             + [block] * 3
-            + [mine]
-            + [block] * 3
-            + [
-                whole(y.shape),
-                pl.BlockSpec((tile, n), lambda i, ids, inv: (i, 0)),
-                pl.BlockSpec((n, tile), lambda i, ids, inv: (0, i)),
-                whole((4 * C, 4 * C)),
-            ],
-            out_specs=[mine]
-            + [block] * 3
-            + [
-                pl.BlockSpec((rows, tile), lambda i, ids, inv: (0, i)),
-                whole(y.shape),
-                whole((4, C, C)),
-            ],
-            scratch_shapes=[
-                pltpu.VMEM((rows, n), BF16),
-                pltpu.VMEM((rows, tile), F32),
-                pltpu.VMEM((rows, tile), BF16),
-                pltpu.VMEM((rows, n), F32),
-                pltpu.VMEM((4 * C, 4 * C), F32),
-            ],
+            + [flat] * 2
+            + [pl.BlockSpec((tile, n), lambda i, ids: (i, 0))],
+            out_specs=[flat, whole(spectrum), whole((4, C, C))],
+            scratch_shapes=[pltpu.VMEM((rows, n), F32), pltpu.VMEM((4 * C, 4 * C), F32)],
         ),
-        out_shape=[jax.ShapeDtypeStruct(x[0].shape, BF16)]
-        + [block_shape] * 3
-        + [
+        out_shape=[
             jax.ShapeDtypeStruct((rows, NPIX), BF16),
-            jax.ShapeDtypeStruct(y.shape, BF16),
+            jax.ShapeDtypeStruct(spectrum, BF16),
             jax.ShapeDtypeStruct((4, C, C), F32),
         ],
-        compiler_params=params(24),
-        cost_estimate=cost(4 * rows * NPIX * n, 20_000_000, 2 * rows * NPIX),
-        name="pixels",
-    )(ids, inv, *x, *cot, y, table, turned, lt)
+        compiler_params=params(60),
+        cost_estimate=cost(3 * rows * NPIX * n, 20_000_000),
+        name="pixel_grads",
+    )(ids, *cot, low, slope, table)
 
 
 def inner_kernel(ids_ref, inv_ref, y_ref, g_ref, ft_ref, lb_ref, cot_ref, mine_ref, o1, o2, o3, ysc):
@@ -567,7 +652,7 @@
 def inner_grads(ids, inv, y, g, turned, lb, cotangent):
     samples = inv.shape[0]
     n = 2 * MODES
-    tile = 512
+    tile = 1024
     rows = samples * 4 * C
     mine = pl.BlockSpec((samples, 1, C, tile), lambda i, ids, inv: (ids[0], 0, 0, i))
     block = pl.BlockSpec((samples, 1, C, tile), lambda i, ids, inv: (0, 0, 0, i))
@@ -588,7 +673,7 @@
         ),
         out_shape=[jax.ShapeDtypeStruct(cotangent.shape, F32)]
         + [jax.ShapeDtypeStruct((samples, 1, C, NPIX), BF16)] * 3,
-        compiler_params=params(16),
+        compiler_params=params(60),
         cost_estimate=cost(3 * rows * NPIX * n, 10_000_000),
         name="inner_grads",
     )(ids, inv, y, g, turned, lb, cotangent)
@@ -766,19 +851,21 @@
     packed = pack_weights(spec_weight, lin_weight)
     packs = [packed] + [swap(packed, "blade", 4, t) for t in (1, 2, 3)]
 
+    x3, packed = after(x3, packed), packed
     xa = to_modes(forward_spectrum(ids, inv, (inputs, x3), table, shards))
     late = after(cotangent, (x1, x2))
     cot = (cotangent,) + tuple(send(late, t)[1] for t in (1, 2, 3))
     xb = to_modes(forward_spectrum(ids, inv, (x1, x2), table, shards))
-    sent, wk, lt, lb = mix(ids, xa, xb, packs)
-    y = to_modes(sent)
-
-    result = pixels(ids, inv, (inputs, x1, x2, x3), cot, y, table, turned, lt)
-    output, grad_pre, sent, lin = result[0], result[4], result[5], result[6]
+    pq, lt, lb = unpack(ids, packs)
+    y = to_modes(mix(ids, xa, xb, pq))
+
+    result = pixels(ids, inv, (inputs, x1, x2, x3), y, turned, lt)
+    output, low, slope = result[0], result[4], result[5]
     out_parts = [swap(result[t], "blade", 4, t) for t in (1, 2, 3)]
 
+    grad_pre, sent, lin = pixel_grads(ids, cot, low, slope, table, y.shape)
     g = to_modes(sent)
-    back = to_modes(mix_back(ids, g, wk))
+    back = to_modes(mix_back(ids, g, pq))
     spec_grads = weight_grads(ids, xa, xb, g, lin)
     spec_grads = [spec_grads[0]] + [swap(spec_grads[t], "blade", 4, t) for t in (1, 2, 3)]
 
@@ -795,6 +882,7 @@
         step *= 2
 
     inner = inner_grads(ids, inv, back, grad_pre, turned, lb, cotangent)
+    inner = after(inner, out_parts)
     grad_parts = [swap(inner[t], "blade", 4, t) for t in (1, 2, 3)]
 
     output = place_output(ids, out_parts, output)

time: 256 us -> 217 us (0.85)
  waiting for transfers between devices: 72.2 us -> 34 us
  Pallas kernels: 100 us -> 96.9 us
    ppermute x21, waiting for transfers between devices: 68.8 us -> 23.2 us  [swap(): return lax.ppermute(value, axis, [(i, i ^ x) for i in range(size)])]
    pallas_call x0 -> x2, Pallas kernels: none -> 19.9 us  [the longest x1 12.2 us: pixel_grads(): pl.pallas_call(slope_kernel, grid_spec=pltpu.PrefetchScalarGridSpec(num_s...]
    all_to_all x4, waiting for transfers between devices: 3.34 us -> 10.8 us  [to_modes(): return lax.all_to_all(value, 'dp', split_axis=0, concat_axis=0, tiled=True)]
    pallas_call x1, Pallas kernels: 13.4 us -> 6.89 us  [weight_grads(): pl.pallas_call(grad_kernel, in_specs=[pl.BlockSpec(memory_space=SMEM)] +...]
    pallas_call x1, Pallas kernels: 17.8 us -> 13.6 us  [pixels(): pl.pallas_call(pixel_kernel, grid_spec=pltpu.PrefetchScalarGridSpec(num_s...]
    pallas_call x2, Pallas kernels: 8.1 us -> 4.64 us  [final_grads(): pl.pallas_call(partial(final_kernel, count, codes), grid_spec=pltpu.Prefe...]
    pallas_call x1, Pallas kernels: 5.96 us -> 3.04 us  [place_output(): pl.pallas_call(place_kernel, grid_spec=pltpu.PrefetchScalarGridSpec(num_s...]
  transfers between devices with their start and end apart: 25 -> 25, of which waited for: 8 -> 7; matrix products, arithmetic and copies ran while one was open for 5% -> 5% of each run, Pallas kernels for 27% -> 38%
where the time goes in v3:
time: 217 us; the launch traced here: 214 us
  Pallas kernels  96.9 us (45%)
  starting transfers between devices  44.8 us (21%)
  waiting for transfers between devices  34 us (16%)
  blocking collectives  17.7 us (8%)
  local copies, waits for them, and re-layouts  15.3 us (7%)
  other arithmetic  4.78 us (2%)
    ppermute x21, starting transfers between devices, swap(): return lax.ppermute(value, axis, [(i, i ^ x) for i in range(size)])  27.3 us
    ppermute x21, waiting for transfers between devices, swap(): return lax.ppermute(value, axis, [(i, i ^ x) for i in range(size)])  23.2 us
    all_to_all x1, blocking collectives, to_modes(): return lax.all_to_all(value, 'dp', split_axis=0, concat_axis=0, tiled=True)  17.7 us
    all_to_all x4, starting transfers between devices, to_modes(): return lax.all_to_all(value, 'dp', split_axis=0, concat_axis=0, tiled=True)  17.5 us
    pallas_call x1, Pallas kernels, pixels(): pl.pallas_call(pixel_kernel, grid_spec=pltpu.PrefetchScalarGridSpec(num_s...  13.6 us
    pallas_call x1, Pallas kernels, pixel_grads(): pl.pallas_call(slope_kernel, grid_spec=pltpu.PrefetchScalarGridSpec(num_s...  12.2 us
    pallas_call x2, Pallas kernels, forward_spectrum(): pl.pallas_call(forward_kernel, grid_spec=pltpu.PrefetchScalarGridSpec(num...  11.4 us
    all_to_all x4, waiting for transfers between devices, to_modes(): return lax.all_to_all(value, 'dp', split_axis=0, concat_axis=0, tiled=True)  10.8 us
  transfers between devices with their start and end apart: 25, of which 7 were waited for; matrix products, arithmetic and copies ran while one was open for 5% of the time, Pallas kernels for 38%

profile of v3, /device:TPU:0, one launch (start us, length us, event | category | flops | bytes accessed | tf_op | source)
XLA Modules:
  0.0 214.4 jit_solution(14511973333498324303)
XLA Ops:
  1.9 4.0 %collective-permute-start.2 = (bf16[2,1,48,4096]{3,2,1,0:T(8,128)(2,1)S(1)}, bf16[2,1,48,4096]{3,2,1,0:T(8,128)(2,1)S(1)}, u32[]{:S(2)}, u32[]{:S(2)}) collective-permute-start(bf16[2,1,48,4096]{3,2,1,0:T(8,128)(2,1)S(1)} %constant_dynamic-slice_fusion.5), channel_id=1, source_target_pairs={{0,24},{8,16},{16,8},{24,0},{1,25},{9,17},{17,9},{25,1},{2,26},{10... | collective-permute-start | bytes 2359304 | tf_op jit(solution)/shard_map/ppermute | solution.py:805
  11.8 2.9 %pack.1.w0 = bf16[48,3200]{1,0:T(8,128)(2,1)} custom-call(f32[1,32,2,48,48]{4,3,2,1,0:T(8,128)} %w_ref.3, f32[1,48,48]{2,1,0:T(8,128)} %l_ref.1), custom_call_target="tpu_custom_call" | custom-call | flops 1 | bytes 1 | tf_op jit(solution)/shard_map/pack/pallas_call | solution.py:136
  15.9 6.7 %tables.1 = (bf16[4096,512]{1,0:T(8,128)(2,1)}, bf16[512,4096]{1,0:T(8,128)(2,1)}) custom-call(f32[64,512]{1,0:T(8,128)} %get-tuple-element.48.first_ref, f32[64,512]{1,0:T(8,128)} %get-tuple-element.49.second_ref, f32[64,512]{1,0:T(8,128)} %get-tuple-element.50.cos_ref, f32[64,512]{1,0:T(8,128)} %get-tuple-element.51.sin_ref), custom_call_target="tpu_custom_call" | custom-call | flops 1 | bytes 1 | tf_op jit(solution)/shard_map/tables/pallas_call | solution.py:98
  25.1 5.7 %forward.2 = bf16[8,32,384]{2,1,0:T(8,128)(2,1)} custom-call(s32[2]{0:T(128)} %pad_add_fusion.ids_ref, f32[2]{0:T(128)} %dynamic_slice.21.inv_ref, bf16[8,1,48,4096]{3,2,1,0:T(8,128)(2,1)} %refs_0_.2, bf16[2,1,48,4096]{3,2,1,0:T(8,128)(2,1)} %copy-done.12, bf16[4096,512]{1,0:T(8,128)(2,1)} %get-tuple-element.52.f_ref.refs_6_), custom_call_target="tpu_custom_call" | custom-call | flops 1 | bytes 1 | tf_op jit(solution)/shard_map/forward/pallas_call | solution.py:275
  30.8 5.4 %all-to-all-start = ((bf16[8,32,384]{2,1,0:T(8,128)(2,1)}), bf16[8,32,384]{2,1,0:T(8,128)(2,1)S(1)}, u32[]{:S(2)}, u32[]{:S(2)}) async-start(bf16[8,32,384]{2,1,0:T(8,128)(2,1)} %forward.2), calls=%async_computation | async-start | bytes 393216 | tf_op jit(solution)/shard_map/all_to_all | solution.py:809
  41.5 5.7 %forward.3 = bf16[8,32,384]{2,1,0:T(8,128)(2,1)} custom-call(s32[2]{0:T(128)} %pad_add_fusion.ids_ref, f32[2]{0:T(128)} %dynamic_slice.21.inv_ref, bf16[2,1,48,4096]{3,2,1,0:T(8,128)(2,1)} %collective-permute-done.x0.refs_1_, bf16[2,1,48,4096]{3,2,1,0:T(8,128)(2,1)} %collective-permute-done.1.x1.refs_2_, bf16[4096,512]{1,0:T(8,128)(2,1)} %get-tuple-element.52.f_ref.refs_6_), custom_call_target="tpu_custom_call" | custom-call | flops 1 | bytes 1 | tf_op jit(solution)/shard_map/forward/pallas_call | solution.py:275
  47.2 5.0 %all-to-all-start.1 = ((bf16[8,32,384]{2,1,0:T(8,128)(2,1)}), bf16[8,32,384]{2,1,0:T(8,128)(2,1)}, u32[]{:S(2)}, u32[]{:S(2)}) async-start(bf16[8,32,384]{2,1,0:T(8,128)(2,1)} %forward.3), calls=%async_computation.1 | async-start | bytes 393216 | tf_op jit(solution)/shard_map/all_to_all | solution.py:809
  57.2 7.7 %unpack.1 = (bf16[32,96,512]{2,1,0:T(8,128)(2,1)}, bf16[192,192]{1,0:T(8,128)(2,1)}, bf16[192,192]{1,0:T(8,128)(2,1)}) custom-call(s32[2]{0:T(128)} %pad_add_fusion.ids_ref, bf16[48,3200]{1,0:T(8,128)(2,1)} %pack.1.w0, bf16[48,3200]{1,0:T(8,128)(2,1)} %collective-permute-done.3.w1, bf16[48,3200]{1,0:T(8,128)(2,1)} %collective-permute-done.4.w2, ...), custom_call_target="tpu_custom_call" | custom-call | flops 1 | bytes 1 | tf_op jit(solution)/shard_map/unpack/pallas_call | solution.py:207
  65.0 5.9 %mix.1 = bf16[8,32,768]{2,1,0:T(8,128)(2,1)} custom-call(s32[2]{0:T(128)} %pad_add_fusion.ids_ref, bf16[8,32,384]{2,1,0:T(8,128)(2,1)} %copy-done.13, bf16[8,32,384]{2,1,0:T(8,128)(2,1)} %all-to-all-done.1.xb, bf16[32,96,512]{2,1,0:T(8,128)(2,1)} %get-tuple-element.53.pq_ref), custom_call_target="tpu_custom_call" | custom-call | flops 1 | bytes 1 | tf_op jit(solution)/shard_map/mix/pallas_call | solution.py:383
  70.9 17.7 %all_to_all.25.refs_4_ = bf16[8,32,768]{2,1,0:T(8,128)(2,1)} all-to-all(bf16[8,32,768]{2,1,0:T(8,128)(2,1)} %mix.1), channel_id=1, replica_groups=mesh['blade'=4,'dp'=8] {'dp'}, dimensions={0} | all-to-all | bytes 786432 | tf_op jit(solution)/shard_map/all_to_all | solution.py:809
  88.6 13.6 %pixels.1 = (bf16[8,1,48,4096]{3,2,1,0:T(8,128)(2,1)}, bf16[2,1,48,4096]{3,2,1,0:T(8,128)(2,1)}, bf16[2,1,48,4096]{3,2,1,0:T(8,128)(2,1)}, bf16[2,1,48,4096]{3,2...) custom-call(s32[2]{0:T(128)} %pad_add_fusion.ids_ref, f32[2]{0:T(128)} %dynamic_slice.21.inv_ref, ...), custom_call_target="tpu_custom_call" | custom-call | flops 1 | bytes 1 | tf_op jit(solution)/shard_map/pixels/pallas_call | solution.py:536
  103.7 12.2 %pixel_grads.1 = (bf16[384,4096]{1,0:T(8,128)(2,1)}, bf16[8,32,768]{2,1,0:T(8,128)(2,1)}, f32[4,48,48]{2,1,0:T(8,128)}) custom-call(s32[2]{0:T(128)} %pad_add_fusion.ids_ref, bf16[8,1,48,4096]{3,2,1,0:T(8,128)(2,1)} %cot_ref.5, bf16[2,1,48,4096]{3,2,1,0:T(8,128)(2,1)} %copy-done.15, bf16[2,1,48,4096]{3,2,1,0:T(8,128)(2,1)} %copy-done.16, ...), custom_call_target="tpu_custom_call" | custom-call | flops 1 | bytes 1 | tf_op jit(solution)/shard_map/pixel_grads/pallas_call | solution.py:612
  115.8 3.5 %all-to-all-start.3 = ((bf16[8,32,768]{2,1,0:T(8,128)(2,1)}), bf16[8,32,768]{2,1,0:T(8,128)(2,1)S(1)}, u32[]{:S(2)}, u32[]{:S(2)}) async-start(bf16[8,32,768]{2,1,0:T(8,128)(2,1)} %get-tuple-element.63), calls=%async_computation.3 | async-start | bytes 786432 | tf_op jit(solution)/shard_map/all_to_all | solution.py:809
  122.8 8.9 %all-to-all-done.3.g_ref = bf16[8,32,768]{2,1,0:T(8,128)(2,1)S(1)} async-done(((bf16[8,32,768]{2,1,0:T(8,128)(2,1)}), bf16[8,32,768]{2,1,0:T(8,128)(2,1)S(1)}, u32[]{:S(2)}, u32[]{:S(2)}) %all-to-all-start.3) | async-done | bytes 393248 | tf_op jit(solution)/shard_map/all_to_all | solution.py:809
  132.5 7.1 %mix_back.1 = bf16[8,32,768]{2,1,0:T(8,128)(2,1)} custom-call(s32[2]{0:T(128)} %pad_add_fusion.ids_ref, bf16[8,32,768]{2,1,0:T(8,128)(2,1)} %copy-done.11, bf16[32,96,512]{2,1,0:T(8,128)(2,1)} %get-tuple-element.53.pq_ref), custom_call_target="tpu_custom_call" | custom-call | flops 1 | bytes 1 | tf_op jit(solution)/shard_map/mix_back/pallas_call | solution.py:405
  139.6 3.6 %all-to-all-start.4 = ((bf16[8,32,768]{2,1,0:T(8,128)(2,1)}), bf16[8,32,768]{2,1,0:T(8,128)(2,1)S(1)}, u32[]{:S(2)}, u32[]{:S(2)}) async-start(bf16[8,32,768]{2,1,0:T(8,128)(2,1)} %mix_back.1), calls=%async_computation.4 | async-start | bytes 786432 | tf_op jit(solution)/shard_map/all_to_all | solution.py:809
  143.2 6.9 %weight_grads.1 = (bf16[48,3200]{1,0:T(8,128)(2,1)}, bf16[48,3200]{1,0:T(8,128)(2,1)}, bf16[48,3200]{1,0:T(8,128)(2,1)}, bf16[48,3200]{1,0:T(8,128)(2,1)}) custom-call(s32[2]{0:T(128)} %pad_add_fusion.ids_ref, bf16[8,32,384]{2,1,0:T(8,128)(2,1)} %copy-done.13, bf16[8,32,384]{2,1,0:T(8,128)(2,1)} %all-to-all-done.1.xb, bf16[8,32,768]{2,1,0:T(8,128)(2,1)} %copy-done.11, ...), custom_call_target="tpu_custom_call" | custom-call | flops 1 | bytes 1 | tf_op jit(solution)/shard_map/weight_grads/pallas_call | solution.py:469
  156.3 8.4 %inner_grads.1 = (f32[8,1,48,4096]{3,2,1,0:T(8,128)}, bf16[2,1,48,4096]{3,2,1,0:T(8,128)(2,1)}, bf16[2,1,48,4096]{3,2,1,0:T(8,128)(2,1)}, bf16[2,1,48,4096]{3,2,1,0:T(8,128)(2,1)}) custom-call(s32[2]{0:T(128)} %pad_add_fusion.ids_ref, f32[2]{0:T(128)} %dynamic_slice.21.inv_ref, bf16[8,32,768]{2,1,0:T(8,128)(2,1)} %copy-done.14, ...), custom_call_target="tpu_custom_call" | custom-call | flops 1 | bytes 1 | tf_op jit(solution)/shard_map/inner_grads/pallas_call | solution.py:659
  170.0 18.2 %collective-permute-done.16.d2 = bf16[48,3200]{1,0:T(8,128)(2,1)} collective-permute-done((bf16[48,3200]{1,0:T(8,128)(2,1)}, bf16[48,3200]{1,0:T(8,128)(2,1)}, u32[]{:S(2)}, u32[]{:S(2)}) %collective-permute-start.16) | collective-permute-done | bytes 307232 | tf_op jit(solution)/shard_map/ppermute | solution.py:805
  190.2 2.2 %collective-permute-start.19 = (f32[48,48]{1,0:T(8,128)S(1)}, f32[48,48]{1,0:T(8,128)S(1)}, u32[]{:S(2)}, u32[]{:S(2)}) collective-permute-start(f32[48,48]{1,0:T(8,128)S(1)} %add.149), channel_id=1, source_target_pairs={{0,2},{1,3},{2,0},{3,1},{4,6},{5,7},{6,4},{7,5},{8,10},{9,11},{10,... | collective-permute-start | bytes 27656 | tf_op jit(solution)/shard_map/ppermute | solution.py:805
  194.2 2.9 %collective-permute-start.20 = (f32[48,48]{1,0:T(8,128)S(1)}, f32[48,48]{1,0:T(8,128)S(1)}, u32[]{:S(2)}, u32[]{:S(2)}) collective-permute-start(f32[48,48]{1,0:T(8,128)S(1)} %add.150), channel_id=1, source_target_pairs={{0,4},{1,5},{2,6},{3,7},{4,0},{5,1},{6,2},{7,3},{8,12},{9,13},{10,... | collective-permute-start | bytes 27656 | tf_op jit(solution)/shard_map/ppermute | solution.py:805
  199.4 3.0 %place.1 = bf16[8,1,48,4096]{3,2,1,0:T(8,128)(2,1)} custom-call(s32[2]{0:T(128)S(1)} %copy-done.10, bf16[2,1,48,4096]{3,2,1,0:T(8,128)(2,1)S(1)} %collective-permute-done.6.a_ref, bf16[2,1,48,4096]{3,2,1,0:T(8,128)(2,1)S(1)} %copy-done.6, bf16[2,1,48,4096]{3,2,1,0:T(8,128)(2,1)S(1)} %copy-done.8, ...), custom_call_target="tpu_custom_call", output_to_operand_aliasing={{}: (4, {})} | custom-call | flops 1 | bytes 1 | tf_op jit(solution)/shard_map/place/pallas_call | solution.py:700
  202.5 6.5 %adam.1 = (f32[1,32,2,48,48]{4,3,2,1,0:T(8,128)}, f32[1,32,2,48,48]{4,3,2,1,0:T(8,128)}, f32[1,32,2,48,48]{4,3,2,1,0:T(8,128)}) custom-call(f32[4]{0:T(128)S(1)} %pad_maximum_fusion.flips, bf16[48,3200]{1,0:T(8,128)(2,1)S(1)} %copy-done.9, bf16[48,3200]{1,0:T(8,128)(2,1)} %collective-permute-done.15.d1, bf16[48,3200]{1,0:T(8,128)(2,1)} %collective-permute-done.16.d2, ...), custom_call_target="tpu_custom_call" | custom-call | flops 1 | bytes 1 | tf_op jit(solution)/shard_map/adam/pallas_call | solution.py:792
  211.6 2.8 %final.3 = f32[8,1,48,4096]{3,2,1,0:T(8,128)} custom-call(s32[2]{0:T(128)S(1)} %copy-done.10, f32[8]{0:T(128)S(1)} %broadcast_divide_fusion.inv_ref, bf16[8,1,48,4096]{3,2,1,0:T(8,128)(2,1)S(1)} %copy-done.1, bf16[2,1,48,4096]{3,2,1,0:T(8,128)(2,1)S(1)} %collective-permute-done.12.refs_0_, ...), custom_call_target="tpu_custom_call", output_to_operand_aliasing={{}: (5, {})} | custom-call | flops 1 | bytes 1 | tf_op jit(solution)/shard_map/final/pallas_call | solution.py:749
  (105 shorter events, 47.0 us)
Async XLA Ops:
  1.9 22.4 %collective-permute-start.2 = (bf16[2,1,48,4096]{3,2,1,0:T(8,128)(2,1)S(1)}, bf16[2,1,48,4096]{3,2,1,0:T(8,128)(2,1)S(1)}, u32[]{:S(2)}, u32[]{:S(2)}) collective-permute-start(bf16[2,1,48,4096]{3,2,1,0:T(8,128)(2,1)S(1)} %constant_dynamic-slice_fusion.5), channel_id=1, source_target_pairs={{0,24},{8,16},{16,8},{24,0},{1,25},{9,17},{17,9},{25,1},{2,26},{10... | collective-permute-start | bytes 2359304 | tf_op jit(solution)/shard_map/ppermute | solution.py:805
  7.9 33.7 %collective-permute-start = (bf16[2,1,48,4096]{3,2,1,0:T(8,128)(2,1)}, bf16[2,1,48,4096]{3,2,1,0:T(8,128)(2,1)}, u32[]{:S(2)}, u32[]{:S(2)}) collective-permute-start(bf16[2,1,48,4096]{3,2,1,0:T(8,128)(2,1)} %constant_dynamic-slice_fusion.4), channel_id=1, source_target_pairs={{0,8},{8,0},{16,24},{24,16},{1,9},{9,1},{17,25},{25,17},{2,10},{10... | collective-permute-start | bytes 2359304 | tf_op jit(solution)/shard_map/ppermute | solution.py:805
  10.5 31.1 %collective-permute-start.1 = (bf16[2,1,48,4096]{3,2,1,0:T(8,128)(2,1)}, bf16[2,1,48,4096]{3,2,1,0:T(8,128)(2,1)}, u32[]{:S(2)}, u32[]{:S(2)}) collective-permute-start(bf16[2,1,48,4096]{3,2,1,0:T(8,128)(2,1)} %constant_dynamic-slice_fusion.3), channel_id=1, source_target_pairs={{0,16},{8,24},{16,0},{24,8},{1,17},{9,25},{17,1},{25,9},{2,18},{10... | collective-permute-start | bytes 2359304 | tf_op jit(solution)/shard_map/ppermute | solution.py:805
  30.8 16.4 %all-to-all-start = ((bf16[8,32,384]{2,1,0:T(8,128)(2,1)}), bf16[8,32,384]{2,1,0:T(8,128)(2,1)S(1)}, u32[]{:S(2)}, u32[]{:S(2)}) async-start(bf16[8,32,384]{2,1,0:T(8,128)(2,1)} %forward.2), calls=%async_computation | async-start | bytes 393216 | tf_op jit(solution)/shard_map/all_to_all | solution.py:809
  36.2 19.5 %collective-permute-start.3 = (bf16[48,3200]{1,0:T(8,128)(2,1)}, bf16[48,3200]{1,0:T(8,128)(2,1)}, u32[]{:S(2)}, u32[]{:S(2)}) collective-permute-start(bf16[48,3200]{1,0:T(8,128)(2,1)} %pack.1.w0), channel_id=1, source_target_pairs={{0,8},{8,0},{16,24},{24,16},{1,9},{9,1},{17,25},{25,17},{2,10},{10... | collective-permute-start | bytes 921608 | tf_op jit(solution)/shard_map/ppermute | solution.py:805
  37.8 19.5 %collective-permute-start.4 = (bf16[48,3200]{1,0:T(8,128)(2,1)}, bf16[48,3200]{1,0:T(8,128)(2,1)}, u32[]{:S(2)}, u32[]{:S(2)}) collective-permute-start(bf16[48,3200]{1,0:T(8,128)(2,1)} %pack.1.w0), channel_id=1, source_target_pairs={{0,16},{8,24},{16,0},{24,8},{1,17},{9,25},{17,1},{25,9},{2,18},{10... | collective-permute-start | bytes 921608 | tf_op jit(solution)/shard_map/ppermute | solution.py:805
  39.3 17.9 %collective-permute-start.5 = (bf16[48,3200]{1,0:T(8,128)(2,1)}, bf16[48,3200]{1,0:T(8,128)(2,1)}, u32[]{:S(2)}, u32[]{:S(2)}) collective-permute-start(bf16[48,3200]{1,0:T(8,128)(2,1)} %pack.1.w0), channel_id=1, source_target_pairs={{0,24},{8,16},{16,8},{24,0},{1,25},{9,17},{17,9},{25,1},{2,26},{10... | collective-permute-start | bytes 921608 | tf_op jit(solution)/shard_map/ppermute | solution.py:805
  47.2 17.7 %all-to-all-start.1 = ((bf16[8,32,384]{2,1,0:T(8,128)(2,1)}), bf16[8,32,384]{2,1,0:T(8,128)(2,1)}, u32[]{:S(2)}, u32[]{:S(2)}) async-start(bf16[8,32,384]{2,1,0:T(8,128)(2,1)} %forward.3), calls=%async_computation.1 | async-start | bytes 393216 | tf_op jit(solution)/shard_map/all_to_all | solution.py:809
  53.7 48.5 %collective-permute-start.9 = (bf16[2,1,48,4096]{3,2,1,0:T(8,128)(2,1)}, bf16[2,1,48,4096]{3,2,1,0:T(8,128)(2,1)S(1)}, u32[]{:S(2)}, u32[]{:S(2)}) collective-permute-start(bf16[2,1,48,4096]{3,2,1,0:T(8,128)(2,1)} %get-tuple-element.87), channel_id=1, source_target_pairs={{0,8},{8,0},{16,24},{24,16},{1,9},{9,1},{17,25},{25,17},{2,10},{10... | collective-permute-start | bytes 2359304 | tf_op jit(solution)/shard_map/ppermute | solution.py:805
  55.2 47.1 %collective-permute-start.10 = (bf16[2,1,48,4096]{3,2,1,0:T(8,128)(2,1)}, bf16[2,1,48,4096]{3,2,1,0:T(8,128)(2,1)S(1)}, u32[]{:S(2)}, u32[]{:S(2)}) collective-permute-start(bf16[2,1,48,4096]{3,2,1,0:T(8,128)(2,1)} %get-tuple-element.86), channel_id=1, source_target_pairs={{0,16},{8,24},{16,0},{24,8},{1,17},{9,25},{17,1},{25,9},{2,18},{10... | collective-permute-start | bytes 2359304 | tf_op jit(solution)/shard_map/ppermute | solution.py:805
  55.7 46.6 %collective-permute-start.11 = (bf16[2,1,48,4096]{3,2,1,0:T(8,128)(2,1)}, bf16[2,1,48,4096]{3,2,1,0:T(8,128)(2,1)S(1)}, u32[]{:S(2)}, u32[]{:S(2)}) collective-permute-start(bf16[2,1,48,4096]{3,2,1,0:T(8,128)(2,1)} %get-tuple-element.85), channel_id=1, source_target_pairs={{0,24},{8,16},{16,8},{24,0},{1,25},{9,17},{17,9},{25,1},{2,26},{10... | collective-permute-start | bytes 2359304 | tf_op jit(solution)/shard_map/ppermute | solution.py:805
  115.8 15.9 %all-to-all-start.3 = ((bf16[8,32,768]{2,1,0:T(8,128)(2,1)}), bf16[8,32,768]{2,1,0:T(8,128)(2,1)S(1)}, u32[]{:S(2)}, u32[]{:S(2)}) async-start(bf16[8,32,768]{2,1,0:T(8,128)(2,1)} %get-tuple-element.63), calls=%async_computation.3 | async-start | bytes 786432 | tf_op jit(solution)/shard_map/all_to_all | solution.py:809
  119.3 32.8 %collective-permute-start.6 = (bf16[2,1,48,4096]{3,2,1,0:T(8,128)(2,1)}, bf16[2,1,48,4096]{3,2,1,0:T(8,128)(2,1)S(1)}, u32[]{:S(2)}, u32[]{:S(2)}) collective-permute-start(bf16[2,1,48,4096]{3,2,1,0:T(8,128)(2,1)} %get-tuple-element.56), channel_id=1, source_target_pairs={{0,8},{8,0},{16,24},{24,16},{1,9},{9,1},{17,25},{25,17},{2,10},{10... | collective-permute-start | bytes 2359304 | tf_op jit(solution)/shard_map/ppermute | solution.py:805
  120.8 43.9 %collective-permute-start.7 = (bf16[2,1,48,4096]{3,2,1,0:T(8,128)(2,1)}, bf16[2,1,48,4096]{3,2,1,0:T(8,128)(2,1)S(1)}, u32[]{:S(2)}, u32[]{:S(2)}) collective-permute-start(bf16[2,1,48,4096]{3,2,1,0:T(8,128)(2,1)} %get-tuple-element.57), channel_id=1, source_target_pairs={{0,16},{8,24},{16,0},{24,8},{1,17},{9,25},{17,1},{25,9},{2,18},{10... | collective-permute-start | bytes 2359304 | tf_op jit(solution)/shard_map/ppermute | solution.py:805
  121.3 44.3 %collective-permute-start.8 = (bf16[2,1,48,4096]{3,2,1,0:T(8,128)(2,1)}, bf16[2,1,48,4096]{3,2,1,0:T(8,128)(2,1)S(1)}, u32[]{:S(2)}, u32[]{:S(2)}) collective-permute-start(bf16[2,1,48,4096]{3,2,1,0:T(8,128)(2,1)} %get-tuple-element.58), channel_id=1, source_target_pairs={{0,24},{8,16},{16,8},{24,0},{1,25},{9,17},{17,9},{25,1},{2,26},{10... | collective-permute-start | bytes 2359304 | tf_op jit(solution)/shard_map/ppermute | solution.py:805
  139.6 15.9 %all-to-all-start.4 = ((bf16[8,32,768]{2,1,0:T(8,128)(2,1)}), bf16[8,32,768]{2,1,0:T(8,128)(2,1)S(1)}, u32[]{:S(2)}, u32[]{:S(2)}) async-start(bf16[8,32,768]{2,1,0:T(8,128)(2,1)} %mix_back.1), calls=%async_computation.4 | async-start | bytes 786432 | tf_op jit(solution)/shard_map/all_to_all | solution.py:809
  150.1 18.2 %collective-permute-start.15 = (bf16[48,3200]{1,0:T(8,128)(2,1)}, bf16[48,3200]{1,0:T(8,128)(2,1)}, u32[]{:S(2)}, u32[]{:S(2)}) collective-permute-start(bf16[48,3200]{1,0:T(8,128)(2,1)} %get-tuple-element.76), channel_id=1, source_target_pairs={{0,8},{8,0},{16,24},{24,16},{1,9},{9,1},{17,25},{25,17},{2,10},{10... | collective-permute-start | bytes 921608 | tf_op jit(solution)/shard_map/ppermute | solution.py:805
  151.6 36.5 %collective-permute-start.16 = (bf16[48,3200]{1,0:T(8,128)(2,1)}, bf16[48,3200]{1,0:T(8,128)(2,1)}, u32[]{:S(2)}, u32[]{:S(2)}) collective-permute-start(bf16[48,3200]{1,0:T(8,128)(2,1)} %get-tuple-element.77), channel_id=1, source_target_pairs={{0,16},{8,24},{16,0},{24,8},{1,17},{9,25},{17,1},{25,9},{2,18},{10... | collective-permute-start | bytes 921608 | tf_op jit(solution)/shard_map/ppermute | solution.py:805
  152.1 36.1 %collective-permute-start.17 = (bf16[48,3200]{1,0:T(8,128)(2,1)}, bf16[48,3200]{1,0:T(8,128)(2,1)}, u32[]{:S(2)}, u32[]{:S(2)}) collective-permute-start(bf16[48,3200]{1,0:T(8,128)(2,1)} %get-tuple-element.78), channel_id=1, source_target_pairs={{0,24},{8,16},{16,8},{24,0},{1,25},{9,17},{17,9},{25,1},{2,26},{10... | collective-permute-start | bytes 921608 | tf_op jit(solution)/shard_map/ppermute | solution.py:805
  166.5 43.3 %collective-permute-start.14 = (bf16[2,1,48,4096]{3,2,1,0:T(8,128)(2,1)}, bf16[2,1,48,4096]{3,2,1,0:T(8,128)(2,1)S(1)}, u32[]{:S(2)}, u32[]{:S(2)}) collective-permute-start(bf16[2,1,48,4096]{3,2,1,0:T(8,128)(2,1)} %get-tuple-element.72), channel_id=1, source_target_pairs={{0,24},{8,16},{16,8},{24,0},{1,25},{9,17},{17,9},{25,1},{2,26},{10... | collective-permute-start | bytes 2359304 | tf_op jit(solution)/shard_map/ppermute | solution.py:805
  167.8 43.7 %collective-permute-start.12 = (bf16[2,1,48,4096]{3,2,1,0:T(8,128)(2,1)}, bf16[2,1,48,4096]{3,2,1,0:T(8,128)(2,1)S(1)}, u32[]{:S(2)}, u32[]{:S(2)}) collective-permute-start(bf16[2,1,48,4096]{3,2,1,0:T(8,128)(2,1)} %get-tuple-element.70), channel_id=1, source_target_pairs={{0,8},{8,0},{16,24},{24,16},{1,9},{9,1},{17,25},{25,17},{2,10},{10... | collective-permute-start | bytes 2359304 | tf_op jit(solution)/shard_map/ppermute | solution.py:805
  168.3 43.3 %collective-permute-start.13 = (bf16[2,1,48,4096]{3,2,1,0:T(8,128)(2,1)}, bf16[2,1,48,4096]{3,2,1,0:T(8,128)(2,1)S(1)}, u32[]{:S(2)}, u32[]{:S(2)}) collective-permute-start(bf16[2,1,48,4096]{3,2,1,0:T(8,128)(2,1)} %get-tuple-element.71), channel_id=1, source_target_pairs={{0,16},{8,24},{16,0},{24,8},{1,17},{9,25},{17,1},{25,9},{2,18},{10... | collective-permute-start | bytes 2359304 | tf_op jit(solution)/shard_map/ppermute | solution.py:805
  190.2 4.0 %collective-permute-start.19 = (f32[48,48]{1,0:T(8,128)S(1)}, f32[48,48]{1,0:T(8,128)S(1)}, u32[]{:S(2)}, u32[]{:S(2)}) collective-permute-start(f32[48,48]{1,0:T(8,128)S(1)} %add.149), channel_id=1, source_target_pairs={{0,2},{1,3},{2,0},{3,1},{4,6},{5,7},{6,4},{7,5},{8,10},{9,11},{10,... | collective-permute-start | bytes 27656 | tf_op jit(solution)/shard_map/ppermute | solution.py:805
  194.2 14.9 %collective-permute-start.20 = (f32[48,48]{1,0:T(8,128)S(1)}, f32[48,48]{1,0:T(8,128)S(1)}, u32[]{:S(2)}, u32[]{:S(2)}) collective-permute-start(f32[48,48]{1,0:T(8,128)S(1)} %add.150), channel_id=1, source_target_pairs={{0,4},{1,5},{2,6},{3,7},{4,0},{5,1},{6,2},{7,3},{8,12},{9,13},{10,... | collective-permute-start | bytes 27656 | tf_op jit(solution)/shard_map/ppermute | solution.py:805
  (24 other events, 195.1 us)

commit v4 on v3

--- a/solution.py
+++ b/solution.py
@@ -58,11 +58,27 @@
     return pltpu.CompilerParams(vmem_limit_bytes=mib * 1024 * 1024)
 
 
+def fast(shape, kind):
+    return pltpu.VMEM(tuple(shape), kind)
+
+
+def slow(shape, kind):
+    return pltpu.HBM(tuple(shape), kind)
+
+
+def pin(*arrays):
+    return [pltpu.with_memory_space_constraint(array, pltpu.VMEM) for array in arrays]
+
+
+def stay(*arrays):
+    return [pltpu.with_memory_space_constraint(array, pltpu.HBM) for array in arrays]
+
+
 def in_vmem(count):
     return [pl.BlockSpec(memory_space=pltpu.MemorySpace.VMEM)] * count
 
 
-def cost(flops, size, hard=0):
+def cost():
     return pl.CostEstimate(flops=1, bytes_accessed=1, transcendentals=0)
 
 
@@ -79,43 +95,44 @@
     row_cos, row_sin = jnp.cos(row_angle) / GRID, jnp.sin(row_angle) / GRID
     first = jnp.where(imag[None, :], -row_sin, row_cos)
     second = jnp.where(imag[None, :], -row_cos, -row_sin)
-    return first, second, jnp.cos(col_angle), jnp.sin(col_angle)
-
-
-def table_kernel(first_ref, second_ref, cos_ref, sin_ref, f_ref, ft_ref):
-    for h in range(first_ref.shape[0]):
-        tile = first_ref[h : h + 1, :] * cos_ref[...] + second_ref[h : h + 1, :] * sin_ref[...]
-        f_ref[h * GRID : (h + 1) * GRID, :] = tile.astype(BF16)
-    for h in range(0, first_ref.shape[0], 2):
-        tile = f_ref[h * GRID : (h + 2) * GRID, :].astype(F32)
-        ft_ref[:, h * GRID : (h + 2) * GRID] = tile.T.astype(BF16)
-
-
-def make_tables():
-    first, second, cosine, sine = lax.optimization_barrier(small_tables())
+    return jnp.stack([first, second, jnp.cos(col_angle), jnp.sin(col_angle)])
+
+
+def table_rows(row_ref, col_ref, start, stop):
+    tiles = []
+    for h in range(start, stop):
+        tile = row_ref[0, h : h + 1] * col_ref[0] + row_ref[1, h : h + 1] * col_ref[1]
+        tiles.append(tile.astype(BF16))
+    return jnp.concatenate(tiles, axis=0)
+
+
+def small_specs(tile):
+    n = 2 * MODES
+    return [
+        pl.BlockSpec((2, tile // GRID, n), lambda i, *_: (0, i, 0)),
+        pl.BlockSpec((2, GRID, n), lambda i, *_: (1, 0, 0)),
+    ]
+
+
+def turned_kernel(row_ref, col_ref, ft_ref):
+    for h in range(0, row_ref.shape[1], 2):
+        tile = table_rows(row_ref, col_ref, h, h + 2)
+        ft_ref[:, h * GRID : (h + 2) * GRID] = tile.astype(F32).T.astype(BF16)
+
+
+def turned_table(small):
     rows = 8
     n = 2 * MODES
     return pl.pallas_call(
-        table_kernel,
+        turned_kernel,
         grid=(GRID // rows,),
-        in_specs=[
-            pl.BlockSpec((rows, n), lambda i: (i, 0)),
-            pl.BlockSpec((rows, n), lambda i: (i, 0)),
-            whole((GRID, n)),
-            whole((GRID, n)),
-        ],
-        out_specs=[
-            pl.BlockSpec((rows * GRID, n), lambda i: (i, 0)),
-            pl.BlockSpec((n, rows * GRID), lambda i: (0, i)),
-        ],
-        out_shape=[
-            jax.ShapeDtypeStruct((NPIX, n), BF16),
-            jax.ShapeDtypeStruct((n, NPIX), BF16),
-        ],
-        compiler_params=params(60),
-        cost_estimate=cost(4 * NPIX * n, 4 * NPIX * n),
-        name="tables",
-    )(first, second, cosine, sine)
+        in_specs=small_specs(rows * GRID),
+        out_specs=pl.BlockSpec((n, rows * GRID), lambda i: (0, i)),
+        out_shape=slow((n, NPIX), BF16),
+        compiler_params=params(12),
+        cost_estimate=cost(),
+        name="turned",
+    )(*stay(small, small))
 
 
 def pack_kernel(w_ref, l_ref, o_ref):
@@ -138,8 +155,8 @@
         in_specs=in_vmem(2),
         out_specs=in_vmem(1)[0],
         out_shape=jax.ShapeDtypeStruct((C, modes * LANES + PACK), BF16),
-        compiler_params=params(60),
-        cost_estimate=cost(modes * 4608, modes * 4608 * 12),
+        compiler_params=params(12),
+        cost_estimate=cost(),
         name="pack",
     )(spec_weight, lin_weight)
 
@@ -171,16 +188,15 @@
     return tiles
 
 
-def unpack_kernel(ids_ref, w0, w1, w2, w3, pq_ref, lt_ref, lb_ref, lsc):
+def unpack_kernel(ids_ref, w0, w1, w2, w3, pq_ref):
     own = ids_ref[0]
-    modes = pq_ref.shape[0]
     lane = lanes_of((C, PACK))
-    for t, w in enumerate((w0, w1, w2, w3)):
-        slot = jnp.bitwise_xor(own, t)
-        flip = jnp.where(slot % 2 == 1, flip_of(own, 1), 1.0)
-        at = pl.ds(pl.multiple_of(slot * PACK, PACK), PACK)
-
-        def step(g, carry):
+
+    def step(g, carry):
+        for t, w in enumerate((w0, w1, w2, w3)):
+            slot = jnp.bitwise_xor(own, t)
+            flip = jnp.where(slot % 2 == 1, flip_of(own, 1), 1.0)
+            at = pl.ds(pl.multiple_of(slot * PACK, PACK), PACK)
             tiles = [tile * flip for tile in quad_tiles(w, g)]
             for q, p in enumerate(split_lanes(*tiles)):
                 p = jnp.where(lane < LANES, p, 0.0)
@@ -188,11 +204,30 @@
                 low = jnp.where(lane < LANES, low, 0.0)
                 pq_ref[g * QUAD + q, :C, at] = p.astype(BF16)
                 pq_ref[g * QUAD + q, C:, at] = low.astype(BF16)
-            return carry
-
-        lax.fori_loop(0, modes // QUAD, step, 0, unroll=2)
-        lsc[slot] = w[:, modes * LANES :].astype(F32) * flip
-
+        return carry
+
+    lax.fori_loop(0, pq_ref.shape[0] // QUAD, step, 0)
+
+
+def unpack(ids, packs):
+    modes = (packs[0].shape[1] - PACK) // LANES
+    return pl.pallas_call(
+        unpack_kernel,
+        in_specs=[pl.BlockSpec(memory_space=SMEM)] + in_vmem(4),
+        out_specs=in_vmem(1)[0],
+        out_shape=fast((modes, LANES, 4 * PACK), BF16),
+        compiler_params=params(12),
+        cost_estimate=cost(),
+        name="unpack",
+    )(ids, *packs)
+
+
+def lines_kernel(ids_ref, w0, w1, w2, w3, lt_ref, lb_ref, lsc):
+    own = ids_ref[0]
+    for t, w in enumerate((w0, w1, w2, w3)):
+        slot = jnp.bitwise_xor(own, t)
+        flip = jnp.where(slot % 2 == 1, flip_of(own, 1), 1.0)
+        lsc[slot] = w[...].astype(F32) * flip
     for k in range(4):
         line = lsc[k]
         turned = line.T
@@ -202,29 +237,28 @@
             lt_ref[u * C : (u + 1) * C, t * C : (t + 1) * C] = (turned[:C] * sgn(t, k)).astype(BF16)
 
 
-def unpack(ids, packs):
-    modes = (packs[0].shape[1] - PACK) // LANES
-    return pl.pallas_call(
-        unpack_kernel,
-        in_specs=[pl.BlockSpec(memory_space=SMEM)] + in_vmem(4),
-        out_specs=in_vmem(3),
-        out_shape=[
-            jax.ShapeDtypeStruct((modes, LANES, 4 * PACK), BF16),
-            jax.ShapeDtypeStruct((4 * C, 4 * C), BF16),
-            jax.ShapeDtypeStruct((4 * C, 4 * C), BF16),
-        ],
+def unpack_lines(ids, packs):
+    last = packs[0].shape[1] // PACK - 1
+    return pl.pallas_call(
+        lines_kernel,
+        grid=(1,),
+        in_specs=[pl.BlockSpec(memory_space=SMEM)]
+        + [pl.BlockSpec((C, PACK), lambda i: (0, last))] * 4,
+        out_specs=[whole((4 * C, 4 * C))] * 2,
+        out_shape=[fast((4 * C, 4 * C), BF16), slow((4 * C, 4 * C), BF16)],
         scratch_shapes=[pltpu.VMEM((4, C, PACK), F32)],
-        compiler_params=params(60),
-        cost_estimate=cost(modes * 100_000, 5_000_000),
-        name="unpack",
+        compiler_params=params(12),
+        cost_estimate=cost(),
+        name="lines",
     )(ids, *packs)
 
 
-def spread(acc, out_ref):
+def spread(acc, out_ref, scales=None):
     rows = []
     for n in range(acc.shape[0] // C):
         for r in range(2):
-            rows.append(acc[n * C : (n + 1) * C, r * MODES : (r + 1) * MODES])
+            row = acc[n * C : (n + 1) * C, r * MODES : (r + 1) * MODES]
+            rows.append(row if scales is None else row * scales[n])
     turned = jnp.concatenate(rows, axis=0).T
     out_ref[...] = turned.reshape(out_ref.shape).astype(BF16)
 
@@ -238,14 +272,12 @@
             ysc[n * C : (n + 1) * C, r * MODES : (r + 1) * MODES] = piece
 
 
-def forward_kernel(ids_ref, inv_ref, x0, x1, f_ref, out_ref, acc):
+def forward_kernel(ids_ref, inv_ref, x0, x1, row_ref, col_ref, out_ref, acc):
     i = pl.program_id(0)
     samples = x0.shape[0]
-    low = []
-    for s in range(samples):
-        for x in (x0, x1):
-            low.append((x[s, 0].astype(F32) * inv_ref[s]).astype(BF16))
-    part = dot(jnp.concatenate(low, axis=0), f_ref[...])
+    rows = [x[s, 0] for s in range(samples) for x in (x0, x1)]
+    table = table_rows(row_ref, col_ref, 0, row_ref.shape[1])
+    part = dot(jnp.concatenate(rows, axis=0), table)
 
     @pl.when(i == 0)
     def _():
@@ -257,10 +289,10 @@
 
     @pl.when(i == pl.num_programs(0) - 1)
     def _():
-        spread(acc, out_ref)
-
-
-def forward_spectrum(ids, inv, x, table, shards):
+        spread(acc, out_ref, [inv_ref[s] for s in range(samples) for _ in range(2)])
+
+
+def forward_spectrum(ids, inv, x, small, shards):
     samples = inv.shape[0]
     modes = MODES // shards
     width = samples * 2 * LANES
@@ -277,15 +309,15 @@
         grid_spec=pltpu.PrefetchScalarGridSpec(
             num_scalar_prefetch=2,
             grid=(NPIX // tile,),
-            in_specs=[spec(x[0]), spec(x[1]), pl.BlockSpec((tile, n), lambda i, ids, inv: (i, 0))],
+            in_specs=[spec(x[0]), spec(x[1])] + small_specs(tile),
             out_specs=whole((shards, modes, width)),
             scratch_shapes=[pltpu.VMEM((samples * 2 * C, n), F32)],
         ),
-        out_shape=jax.ShapeDtypeStruct((shards, modes, width), BF16),
-        compiler_params=params(60),
-        cost_estimate=cost(4 * samples * C * NPIX * n, 6_000_000),
+        out_shape=slow((shards, modes, width), BF16),
+        compiler_params=params(12),
+        cost_estimate=cost(),
         name="forward",
-    )(ids, inv, *x, table)
+    )(ids, inv, *stay(*x), *stay(small, small))
 
 
 def row_scratch(modes, shards, width):
@@ -384,12 +416,12 @@
         mix_kernel,
         in_specs=[pl.BlockSpec(memory_space=SMEM)] + in_vmem(3),
         out_specs=in_vmem(1)[0],
-        out_shape=jax.ShapeDtypeStruct((shards, modes, 2 * half), BF16),
+        out_shape=slow((shards, modes, 2 * half), BF16),
         scratch_shapes=[row_scratch(modes, shards, 2 * half)] * 2,
-        compiler_params=params(60),
-        cost_estimate=cost(modes * 64 * 96 * 96 * 8, 4_000_000),
+        compiler_params=params(12),
+        cost_estimate=cost(),
         name="mix",
-    )(ids, xa, xb, pq)
+    )(ids, xa, xb, *pin(pq))
 
 
 def mix_back_kernel(ids_ref, g_ref, pq_ref, out_ref, gsc, ysc):
@@ -406,12 +438,12 @@
         mix_back_kernel,
         in_specs=[pl.BlockSpec(memory_space=SMEM)] + in_vmem(2),
         out_specs=in_vmem(1)[0],
-        out_shape=jax.ShapeDtypeStruct(g.shape, BF16),
+        out_shape=slow(g.shape, BF16),
         scratch_shapes=[row_scratch(modes, shards, width)] * 2,
-        compiler_params=params(60),
-        cost_estimate=cost(modes * 64 * 96 * 96 * 8, 3_000_000),
+        compiler_params=params(12),
+        cost_estimate=cost(),
         name="mix_back",
-    )(ids, g, pq)
+    )(ids, g, *pin(pq))
 
 
 def grad_kernel(ids_ref, xa, xb, g_ref, lin_ref, o0, o1, o2, o3, xsc, gsc, osc):
@@ -470,24 +502,25 @@
         grad_kernel,
         in_specs=[pl.BlockSpec(memory_space=SMEM)] + in_vmem(4),
         out_specs=in_vmem(4),
-        out_shape=[jax.ShapeDtypeStruct(shape, BF16)] * 4,
+        out_shape=[slow(shape, BF16)] * 4,
         scratch_shapes=[row_scratch(modes, shards, width)] * 2 + [pltpu.VMEM((4,) + shape, BF16)],
-        compiler_params=params(60),
-        cost_estimate=cost(modes * 128 * 96 * 96 * 8, 4_000_000),
+        compiler_params=params(12),
+        cost_estimate=cost(),
         name="weight_grads",
     )(ids, xa, xb, g, lin)
 
 
 CDF_AT = 0.28
 CDF = (0.11652094, 0.06749571, 0.2689128, -0.23699677, 0.38987606, -0.10580875)
+SERIES = [value / CDF_AT ** (i + 1) for i, value in enumerate(CDF)]
 
 
 def gelu_parts(v):
     z = jnp.abs(v)
-    t = 1.0 / (1.0 + CDF_AT * z)
+    t = 1.0 / (z + 1.0 / CDF_AT)
     bell = jnp.exp2(v * v * (-0.5 * math.log2(math.e)))
-    series = jnp.float32(CDF[-1])
-    for value in CDF[-2::-1]:
+    series = jnp.float32(SERIES[-1])
+    for value in SERIES[-2::-1]:
         series = series * t + value
     tail = series * t * bell
     cdf = jnp.where(v < 0.0, tail, 1.0 - tail)
@@ -498,31 +531,29 @@
     x = refs[:4]
     y_ref, ft_ref, lt_ref = refs[4:7]
     outs = refs[7:11]
-    low, slope_ref = refs[11:13]
-    ysc, pre, full = refs[13:]
+    slope_ref = refs[11]
+    ysc, pre, lts = refs[12:]
     samples = x[1].shape[0]
     rows = 4 * C
 
     @pl.when(pl.program_id(0) == 0)
     def _():
         collect(y_ref, ysc)
-
-    for s in range(samples):
-        for t in range(4):
-            at = s * rows + t * C
-            normed = x[t][s, 0].astype(F32) * inv_ref[s]
-            full[at : at + C] = normed
-            low[at : at + C] = normed.astype(BF16)
+        for s in range(samples):
+            lts[s] = (lt_ref[...].astype(F32) * inv_ref[s]).astype(BF16)
+
     for s in range(samples):
         at = slice(s * rows, (s + 1) * rows)
-        pre[at] = dot(ysc[at], ft_ref[...]) + dot(lt_ref[...], low[at])
+        fields = jnp.concatenate([x[t][s, 0] for t in range(4)], axis=0)
+        pre[at] = dot(ysc[at], ft_ref[...]) + dot(lts[s], fields)
     for s in range(samples):
         for t in range(4):
             for c in range(0, C, ROWS):
                 at = s * rows + t * C + c
                 value, slope = gelu_parts(pre[at : at + ROWS])
-                outs[t][s, 0, c : c + ROWS] = (full[at : at + ROWS] + value).astype(BF16)
-                slope_ref[at : at + ROWS] = slope
+                normed = x[t][s, 0, c : c + ROWS].astype(F32) * inv_ref[s]
+                outs[t][s, 0, c : c + ROWS] = (normed + value).astype(BF16)
+                slope_ref[at : at + ROWS] = slope.astype(BF16)
 
 
 def pixels(ids, inv, x, y, turned, lt):
@@ -545,49 +576,46 @@
                 pl.BlockSpec((n, tile), lambda i, ids, inv: (0, i)),
                 whole((4 * C, 4 * C)),
             ],
-            out_specs=[mine] + [block] * 3 + [flat] * 2,
+            out_specs=[mine] + [block] * 3 + [flat],
             scratch_shapes=[
                 pltpu.VMEM((rows, n), BF16),
                 pltpu.VMEM((rows, tile), F32),
-                pltpu.VMEM((rows, tile), F32),
+                pltpu.VMEM((samples, 4 * C, 4 * C), BF16),
             ],
         ),
-        out_shape=[jax.ShapeDtypeStruct(x[0].shape, BF16)]
-        + [jax.ShapeDtypeStruct((samples, 1, C, NPIX), BF16)] * 3
-        + [jax.ShapeDtypeStruct((rows, NPIX), BF16), jax.ShapeDtypeStruct((rows, NPIX), F32)],
-        compiler_params=params(60),
-        cost_estimate=cost(3 * rows * NPIX * n, 20_000_000, 2 * rows * NPIX),
+        out_shape=[slow(x[0].shape, BF16)]
+        + [slow((samples, 1, C, NPIX), BF16)] * 3
+        + [fast((rows, NPIX), BF16)],
+        compiler_params=params(12),
+        cost_estimate=cost(),
         name="pixels",
-    )(ids, inv, *x, y, turned, lt)
-
-
-def slope_kernel(ids_ref, *refs):
-    cot = refs[:4]
-    low, slope, f_ref, g_ref, g_out, lin_ref, gacc, lacc = refs[4:]
+    )(ids, inv, *stay(*x), y, *stay(turned), *pin(lt))
+
+
+def slope_kernel(ids_ref, inv_ref, *refs):
+    x, cot = refs[:4], refs[4:8]
+    slope, row_ref, col_ref, g_ref, g_out, lin_ref, gacc, lacc = refs[8:]
     samples = cot[1].shape[0]
     rows = 4 * C
     i = pl.program_id(0)
+
+    @pl.when(i == 0)
+    def _():
+        gacc[...] = jnp.zeros_like(gacc)
+        lacc[...] = jnp.zeros_like(lacc)
+
     for s in range(samples):
         for t in range(4):
             at = s * rows + t * C
-            grad = cot[t][s, 0].astype(F32) * slope[at : at + C]
+            grad = cot[t][s, 0].astype(F32) * slope[at : at + C].astype(F32)
             g_ref[at : at + C] = grad.astype(BF16)
-    part = dot(g_ref[...], f_ref[...])
-    lin = None
+    table = table_rows(row_ref, col_ref, 0, row_ref.shape[1])
     for s in range(samples):
         at = slice(s * rows, (s + 1) * rows)
-        piece = dot(low[at], g_ref[at], ((1,), (1,)))
-        lin = piece if lin is None else lin + piece
-
-    @pl.when(i == 0)
-    def _():
-        gacc[...] = part
-        lacc[...] = lin
-
-    @pl.when(i > 0)
-    def _():
-        gacc[...] += part
-        lacc[...] += lin
+        g = g_ref[at]
+        gacc[at] += dot(g, table)
+        fields = jnp.concatenate([x[t][s, 0] for t in range(4)], axis=0)
+        lacc[...] += dot(fields, g, ((1,), (1,))) * inv_ref[s]
 
     @pl.when(i == pl.num_programs(0) - 1)
     def _():
@@ -601,35 +629,34 @@
             lin_ref[k] = total
 
 
-def pixel_grads(ids, cot, low, slope, table, spectrum):
-    rows = low.shape[0]
+def pixel_grads(ids, inv, x, cot, slope, small, spectrum):
+    rows = slope.shape[0]
     samples = rows // (4 * C)
     n = 2 * MODES
-    tile = 512
-    mine = pl.BlockSpec((samples, 1, C, tile), lambda i, ids: (ids[0], 0, 0, i))
-    block = pl.BlockSpec((samples, 1, C, tile), lambda i, ids: (0, 0, 0, i))
-    flat = pl.BlockSpec((rows, tile), lambda i, ids: (0, i))
+    tile = 1024
+    mine = pl.BlockSpec((samples, 1, C, tile), lambda i, ids, inv: (ids[0], 0, 0, i))
+    block = pl.BlockSpec((samples, 1, C, tile), lambda i, ids, inv: (0, 0, 0, i))
+    flat = pl.BlockSpec((rows, tile), lambda i, ids, inv: (0, i))
     return pl.pallas_call(
         slope_kernel,
         grid_spec=pltpu.PrefetchScalarGridSpec(
-            num_scalar_prefetch=1,
+            num_scalar_prefetch=2,
             grid=(NPIX // tile,),
-            in_specs=[mine]
-            + [block] * 3
-            + [flat] * 2
-            + [pl.BlockSpec((tile, n), lambda i, ids: (i, 0))],
+            in_specs=([mine] + [block] * 3) * 2
+            + [flat]
+            + small_specs(tile),
             out_specs=[flat, whole(spectrum), whole((4, C, C))],
             scratch_shapes=[pltpu.VMEM((rows, n), F32), pltpu.VMEM((4 * C, 4 * C), F32)],
         ),
         out_shape=[
-            jax.ShapeDtypeStruct((rows, NPIX), BF16),
-            jax.ShapeDtypeStruct(spectrum, BF16),
+            slow((rows, NPIX), BF16),
+            slow(spectrum, BF16),
             jax.ShapeDtypeStruct((4, C, C), F32),
         ],
-        compiler_params=params(60),
-        cost_estimate=cost(3 * rows * NPIX * n, 20_000_000),
+        compiler_params=params(12),
+        cost_estimate=cost(),
         name="pixel_grads",
-    )(ids, *cot, low, slope, table)
+    )(ids, inv, *stay(*x), *stay(*cot), *pin(slope), *stay(small, small))
 
 
 def inner_kernel(ids_ref, inv_ref, y_ref, g_ref, ft_ref, lb_ref, cot_ref, mine_ref, o1, o2, o3, ysc):
@@ -671,12 +698,11 @@
             out_specs=[mine] + [block] * 3,
             scratch_shapes=[pltpu.VMEM((rows, n), BF16)],
         ),
-        out_shape=[jax.ShapeDtypeStruct(cotangent.shape, F32)]
-        + [jax.ShapeDtypeStruct((samples, 1, C, NPIX), BF16)] * 3,
-        compiler_params=params(60),
-        cost_estimate=cost(3 * rows * NPIX * n, 10_000_000),
+        out_shape=[slow(cotangent.shape, F32)] + [slow((samples, 1, C, NPIX), BF16)] * 3,
+        compiler_params=params(12),
+        cost_estimate=cost(),
         name="inner_grads",
-    )(ids, inv, y, g, turned, lb, cotangent)
+    )(ids, inv, y, *stay(g, turned), lb, *stay(cotangent))
 
 
 def place_kernel(ids_ref, a_ref, b_ref, c_ref, old_ref, out_ref):
@@ -710,7 +736,7 @@
         out_shape=jax.ShapeDtypeStruct(result.shape, BF16),
         input_output_aliases={4: 0},
         compiler_params=params(12),
-        cost_estimate=cost(0, 12 * samples * C * NPIX),
+        cost_estimate=cost(),
         name="place",
     )(ids, *parts, result)
 
@@ -759,7 +785,7 @@
         out_shape=jax.ShapeDtypeStruct(cotangent.shape, F32),
         input_output_aliases={3 + count: 0},
         compiler_params=params(12),
-        cost_estimate=cost(0, 8 * count * samples * C * NPIX),
+        cost_estimate=cost(),
         name="final",
     )(ids, inv, cotangent, *parts, result)
 
@@ -796,7 +822,7 @@
         out_specs=[block] * 3,
         out_shape=[jax.ShapeDtypeStruct(weight.shape, F32)] * 3,
         compiler_params=params(12),
-        cost_estimate=cost(modes * 4608 * 20, modes * 4608 * 72, modes * 4608),
+        cost_estimate=cost(),
         name="adam",
     )(flips, *grads, weight, first, second)
 
@@ -832,8 +858,11 @@
     ids = jnp.stack([own, shard]).astype(jnp.int32)
     samples = inputs.shape[0] // 4
 
+    def cut(array, t):
+        return lax.dynamic_slice_in_dim(array, jnp.bitwise_xor(own, t) * samples, samples, 0)
+
     def send(array, t):
-        block = lax.dynamic_slice_in_dim(array, jnp.bitwise_xor(own, t) * samples, samples, 0)
+        block = cut(array, t)
         return block, swap(block, "blade", 4, t)
 
     sent, x3 = send(inputs, 3)
@@ -847,28 +876,38 @@
     inv_all = 1.0 / normalizer
     inv = lax.dynamic_slice_in_dim(inv_all, own * samples, samples, 0)
 
-    table, turned = make_tables()
+    small = lax.optimization_barrier(small_tables())
+    turned = turned_table(small)
     packed = pack_weights(spec_weight, lin_weight)
     packs = [packed] + [swap(packed, "blade", 4, t) for t in (1, 2, 3)]
 
-    x3, packed = after(x3, packed), packed
-    xa = to_modes(forward_spectrum(ids, inv, (inputs, x3), table, shards))
-    late = after(cotangent, (x1, x2))
-    cot = (cotangent,) + tuple(send(late, t)[1] for t in (1, 2, 3))
-    xb = to_modes(forward_spectrum(ids, inv, (x1, x2), table, shards))
-    pq, lt, lb = unpack(ids, packs)
-    y = to_modes(mix(ids, xa, xb, pq))
-
-    result = pixels(ids, inv, (inputs, x1, x2, x3), y, turned, lt)
-    output, low, slope = result[0], result[4], result[5]
+    x3 = after(x3, (packed, turned))
+    xa = to_modes(forward_spectrum(ids, inv, (inputs, x3), small, shards))
+    blocks = after([cut(cotangent, t) for t in (1, 2, 3)], (x1, x2))
+    cot = (cotangent,) + tuple(swap(blocks[t - 1], "blade", 4, t) for t in (1, 2, 3))
+    xb = to_modes(forward_spectrum(ids, inv, (x1, x2), small, shards))
+    mixed = mix(ids, xa, xb, unpack(ids, packs))
+    y = to_modes(mixed)
+    lt, lb = unpack_lines(after(ids, mixed), packs)
+
+    x = (inputs, x1, x2, x3)
+    result = pixels(ids, inv, x, y, turned, lt)
+    output, slope = result[0], result[4]
     out_parts = [swap(result[t], "blade", 4, t) for t in (1, 2, 3)]
 
-    grad_pre, sent, lin = pixel_grads(ids, cot, low, slope, table, y.shape)
-    g = to_modes(sent)
-    back = to_modes(mix_back(ids, g, pq))
+    grad_pre, sent, lin = pixel_grads(ids, inv, x, cot, slope, small, y.shape)
+    g = after(to_modes(sent), out_parts[2])
+    mixed = mix_back(ids, g, unpack(after(ids, lin), packs))
+    back = to_modes(mixed)
     spec_grads = weight_grads(ids, xa, xb, g, lin)
     spec_grads = [spec_grads[0]] + [swap(spec_grads[t], "blade", 4, t) for t in (1, 2, 3)]
 
+    inner = inner_grads(ids, inv, back, grad_pre, turned, lb, cotangent)
+    inner = after(inner, out_parts)
+    grad_parts = [swap(inner[t], "blade", 4, t) for t in (1, 2, 3)]
+
+    output = place_output(ids, out_parts, output)
+    spec_grads = after(spec_grads, output)
     flips = jnp.stack(
         [jnp.where(own % 2 == 1, flip_of(jnp.bitwise_xor(own, t), 1), 1.0) for t in range(4)]
     )
@@ -881,11 +920,6 @@
         lin_grad = lin_grad + swap(lin_grad, "dp", shards, step)
         step *= 2
 
-    inner = inner_grads(ids, inv, back, grad_pre, turned, lb, cotangent)
-    inner = after(inner, out_parts)
-    grad_parts = [swap(inner[t], "blade", 4, t) for t in (1, 2, 3)]
-
-    output = place_output(ids, out_parts, output)
     spec_out = adam_spec(flips, spec_grads, spec_weight, spec_first, spec_second)
     lin_out = adamw(lin_weight, lin_first, lin_second, lin_grad[None])
     input_grad = final_grads(ids, inv_all, cotangent, grad_parts[2:], (3,), inner[0])

time: 217 us -> 197 us (0.908)
  blocking collectives: 17.7 us -> 0 us
  starting transfers between devices: 44.8 us -> 60.1 us
  local copies, waits for them, and re-layouts: 15.3 us -> 9 us
  Pallas kernels: 96.9 us -> 91.4 us
  waiting for transfers between devices: 34 us -> 31.1 us
    all_to_all x1 -> x0, blocking collectives: 17.7 us -> none  [to_modes(): return lax.all_to_all(value, 'dp', split_axis=0, concat_axis=0, tiled=True)]
    ppermute x21, waiting for transfers between devices: 23.2 us -> 12.2 us  [swap(): return lax.ppermute(value, axis, [(i, i ^ x) for i in range(size)])]
    ppermute x21, starting transfers between devices: 27.3 us -> 37 us  [swap(): return lax.ppermute(value, axis, [(i, i ^ x) for i in range(size)])]
    all_to_all x4 -> x5, waiting for transfers between devices: 10.8 us -> 18.9 us  [to_modes(): return lax.all_to_all(value, 'dp', split_axis=0, concat_axis=0, tiled=True)]
    unnamed x46 -> x38, local copies, waits for them, and re-layouts: 7.82 us -> 1.12 us
    all_to_all x4 -> x5, starting transfers between devices: 17.5 us -> 23.1 us  [to_modes(): return lax.all_to_all(value, 'dp', split_axis=0, concat_axis=0, tiled=True)]
    pallas_call x1, Pallas kernels: 12.2 us -> 8.35 us  [pixel_grads(): pl.pallas_call(slope_kernel, grid_spec=pltpu.PrefetchScalarGridSpec(num_s...]
    pallas_call x1, Pallas kernels: 3.04 us -> 6.12 us  [place_output(): pl.pallas_call(place_kernel, grid_spec=pltpu.PrefetchScalarGridSpec(num_s...]
  transfers between devices with their start and end apart: 25 -> 26, of which waited for: 7 -> 10; matrix products, arithmetic and copies ran while one was open for 5% -> 4% of each run, Pallas kernels for 38% -> 45%
where the time goes in v4:
time: 197 us; the launch traced here: 195 us
  Pallas kernels  91.4 us (46%)
  starting transfers between devices  60.1 us (31%)
  waiting for transfers between devices  31.1 us (16%)
  local copies, waits for them, and re-layouts  9 us (5%)
  other arithmetic  2.96 us (2%)
    ppermute x21, starting transfers between devices, swap(): return lax.ppermute(value, axis, [(i, i ^ x) for i in range(size)])  37 us
    all_to_all x5, starting transfers between devices, to_modes(): return lax.all_to_all(value, 'dp', split_axis=0, concat_axis=0, tiled=True)  23.1 us
    all_to_all x5, waiting for transfers between devices, to_modes(): return lax.all_to_all(value, 'dp', split_axis=0, concat_axis=0, tiled=True)  18.9 us
    ppermute x21, waiting for transfers between devices, swap(): return lax.ppermute(value, axis, [(i, i ^ x) for i in range(size)])  12.2 us
    pallas_call x1, Pallas kernels, pixels(): pl.pallas_call(pixel_kernel, grid_spec=pltpu.PrefetchScalarGridSpec(num_s...  11.8 us
    pallas_call x2, Pallas kernels, unpack(): pl.pallas_call(unpack_kernel, in_specs=[pl.BlockSpec(memory_space=SMEM)]...  10.5 us
    pallas_call x2, Pallas kernels, forward_spectrum(): pl.pallas_call(forward_kernel, grid_spec=pltpu.PrefetchScalarGridSpec(num...  10.3 us
    pallas_call x1, Pallas kernels, pixel_grads(): pl.pallas_call(slope_kernel, grid_spec=pltpu.PrefetchScalarGridSpec(num_s...  8.35 us
  transfers between devices with their start and end apart: 26, of which 10 were waited for; matrix products, arithmetic and copies ran while one was open for 4% of the time, Pallas kernels for 45%

profile of v4, /device:TPU:0, one launch (start us, length us, event | category | flops | bytes accessed | tf_op | source)
XLA Modules:
  0.0 195.4 jit_solution(2930737263655961435)
XLA Ops:
  2.7 3.9 %collective-permute-start.2 = (bf16[2,1,48,4096]{3,2,1,0:T(8,128)(2,1)}, bf16[2,1,48,4096]{3,2,1,0:T(8,128)(2,1)}, u32[]{:S(2)}, u32[]{:S(2)}) collective-permute-start(bf16[2,1,48,4096]{3,2,1,0:T(8,128)(2,1)} %constant_dynamic-slice_fusion.5), channel_id=1, source_target_pairs={{0,24},{8,16},{16,8},{24,0},{1,25},{9,17},{17,9},{25,1},{2,26},{10... | collective-permute-start | bytes 2359304 | tf_op jit(solution)/shard_map/ppermute | solution.py:831
  13.4 6.0 %turned.1.refs_5_.ft_ref = bf16[512,4096]{1,0:T(8,128)(2,1)} custom-call(f32[4,64,512]{2,1,0:T(8,128)} %pad_maximum_fusion.row_ref.col_ref.refs_9_.refs_10_, f32[4,64,512]{2,1,0:T(8,128)} %pad_maximum_fusion.row_ref.col_ref.refs_9_.refs_10_), custom_call_target="tpu_custom_call" | custom-call | flops 1 | bytes 1 | tf_op jit(solution)/shard_map/turned/pallas_call | solution.py:126
  21.0 4.4 %collective-permute-done.2.x1.refs_3_ = bf16[2,1,48,4096]{3,2,1,0:T(8,128)(2,1)} collective-permute-done((bf16[2,1,48,4096]{3,2,1,0:T(8,128)(2,1)}, bf16[2,1,48,4096]{3,2,1,0:T(8,128)(2,1)}, u32[]{:S(2)}, u32[]{:S(2)}) %collective-permute-start.2) | collective-permute-done | bytes 786464 | tf_op jit(solution)/shard_map/ppermute | solution.py:831
  25.3 5.2 %forward.2 = bf16[8,32,384]{2,1,0:T(8,128)(2,1)} custom-call(s32[2]{0:T(128)S(1)} %pad_add_fusion.ids_ref, f32[2]{0:T(128)S(1)} %dynamic_slice.21.inv_ref, bf16[8,1,48,4096]{3,2,1,0:T(8,128)(2,1)} %refs_0_.3, bf16[2,1,48,4096]{3,2,1,0:T(8,128)(2,1)} %collective-permute-done.2.x1.refs_3_, f32[4,64,512]{2,1,0:T(8,128)} %pad_maximum_fusion.row_ref.col_ref.refs_9_.refs_10_, ...), custom_call_target="tpu_custom_call" | custom-call | flops 1 | bytes 1 | tf_op jit(solution)/shard_map/forward/pallas_call | solution.py:307
  30.5 5.4 %all-to-all-start = ((bf16[8,32,384]{2,1,0:T(8,128)(2,1)}), bf16[8,32,384]{2,1,0:T(8,128)(2,1)}, u32[]{:S(2)}, u32[]{:S(2)}) async-start(bf16[8,32,384]{2,1,0:T(8,128)(2,1)} %forward.2), calls=%async_computation | async-start | bytes 393216 | tf_op jit(solution)/shard_map/all_to_all | solution.py:835
  39.4 3.4 %collective-permute-done.x0.refs_1_ = bf16[2,1,48,4096]{3,2,1,0:T(8,128)(2,1)} collective-permute-done((bf16[2,1,48,4096]{3,2,1,0:T(8,128)(2,1)}, bf16[2,1,48,4096]{3,2,1,0:T(8,128)(2,1)}, u32[]{:S(2)}, u32[]{:S(2)}) %collective-permute-start) | collective-permute-done | bytes 786464 | tf_op jit(solution)/shard_map/ppermute | solution.py:831
  42.8 5.1 %forward.3 = bf16[8,32,384]{2,1,0:T(8,128)(2,1)} custom-call(s32[2]{0:T(128)S(1)} %pad_add_fusion.ids_ref, f32[2]{0:T(128)S(1)} %dynamic_slice.21.inv_ref, bf16[2,1,48,4096]{3,2,1,0:T(8,128)(2,1)} %collective-permute-done.x0.refs_1_, bf16[2,1,48,4096]{3,2,1,0:T(8,128)(2,1)} %collective-permute-done.1.x1.refs_2_, ...), custom_call_target="tpu_custom_call" | custom-call | flops 1 | bytes 1 | tf_op jit(solution)/shard_map/forward/pallas_call | solution.py:307
  47.9 4.9 %all-to-all-start.1 = ((bf16[8,32,384]{2,1,0:T(8,128)(2,1)}), bf16[8,32,384]{2,1,0:T(8,128)(2,1)}, u32[]{:S(2)}, u32[]{:S(2)}) async-start(bf16[8,32,384]{2,1,0:T(8,128)(2,1)} %forward.3), calls=%async_computation.1 | async-start | bytes 393216 | tf_op jit(solution)/shard_map/all_to_all | solution.py:835
  54.5 5.2 %unpack.2.pq_ref = bf16[32,96,512]{2,1,0:T(8,128)(2,1)S(1)} custom-call(s32[2]{0:T(128)S(1)} %pad_add_fusion.ids_ref, bf16[48,3200]{1,0:T(8,128)(2,1)S(1)} %pack.1.w0, bf16[48,3200]{1,0:T(8,128)(2,1)} %collective-permute-done.3.w1, bf16[48,3200]{1,0:T(8,128)(2,1)} %collective-permute-done.4.w2, bf16[48,3200]{1,0:T(8,128)(2,1)} %collective-permute-done.5.w3), custom_call_target="tpu_custom_call" | custom-call | flops 1 | bytes 1 | tf_op jit(solution)/shard_map/unpack/pallas_call | solution.py:214
  63.3 4.8 %mix.1 = bf16[8,32,768]{2,1,0:T(8,128)(2,1)} custom-call(s32[2]{0:T(128)S(1)} %pad_add_fusion.ids_ref, bf16[8,32,384]{2,1,0:T(8,128)(2,1)} %all-to-all-done.xa, bf16[8,32,384]{2,1,0:T(8,128)(2,1)} %all-to-all-done.1.xb, bf16[32,96,512]{2,1,0:T(8,128)(2,1)S(1)} %unpack.2.pq_ref), custom_call_target="tpu_custom_call" | custom-call | flops 1 | bytes 1 | tf_op jit(solution)/shard_map/mix/pallas_call | solution.py:415
  68.2 5.1 %all-to-all-start.2 = ((bf16[8,32,768]{2,1,0:T(8,128)(2,1)}), bf16[8,32,768]{2,1,0:T(8,128)(2,1)S(1)}, u32[]{:S(2)}, u32[]{:S(2)}) async-start(bf16[8,32,768]{2,1,0:T(8,128)(2,1)} %mix.1), calls=%async_computation.2 | async-start | bytes 786432 | tf_op jit(solution)/shard_map/all_to_all | solution.py:835
  75.0 10.9 %all-to-all-done.2.refs_4_ = bf16[8,32,768]{2,1,0:T(8,128)(2,1)S(1)} async-done(((bf16[8,32,768]{2,1,0:T(8,128)(2,1)}), bf16[8,32,768]{2,1,0:T(8,128)(2,1)S(1)}, u32[]{:S(2)}, u32[]{:S(2)}) %all-to-all-start.2) | async-done | bytes 393248 | tf_op jit(solution)/shard_map/all_to_all | solution.py:835
  85.8 11.8 %pixels.1 = (bf16[8,1,48,4096]{3,2,1,0:T(8,128)(2,1)}, bf16[2,1,48,4096]{3,2,1,0:T(8,128)(2,1)}, bf16[2,1,48,4096]{3,2,1,0:T(8,128)(2,1)}, bf16[2,1,48,4096]{3,2,1,0:T(8,128)(2,1)}, bf16[384,4096]{1,0:T(8,128)(2,1)S(1)}) custom-call(s32[2]{0:T(128)S(1)} %pad_add_fusion.ids_ref, f32[2]{0:T(128)S(1)} %dynamic_slice.21.inv_ref, ...), custom_call_target="tpu_custom_call" | custom-call | flops 1 | bytes 1 | tf_op jit(solution)/shard_map/pixels/pallas_call | solution.py:567
  100.7 8.3 %pixel_grads.1 = (bf16[384,4096]{1,0:T(8,128)(2,1)}, bf16[8,32,768]{2,1,0:T(8,128)(2,1)}, f32[4,48,48]{2,1,0:T(8,128)S(1)}) custom-call(s32[2]{0:T(128)S(1)} %pad_add_fusion.ids_ref, f32[2]{0:T(128)S(1)} %copy-done.11, bf16[8,1,48,4096]{3,2,1,0:T(8,128)(2,1)} %refs_0_.3, bf16[2,1,48,4096]{3,2,1,0:T(8,128)(2,1)} %collective-permute-done.x0.refs_1_, ...), custom_call_target="tpu_custom_call" | custom-call | flops 1 | bytes 1 | tf_op jit(solution)/shard_map/pixel_grads/pallas_call | solution.py:640
  109.1 4.1 %all-to-all-start.3 = ((bf16[8,32,768]{2,1,0:T(8,128)(2,1)}), bf16[8,32,768]{2,1,0:T(8,128)(2,1)}, u32[]{:S(2)}, u32[]{:S(2)}) async-start(bf16[8,32,768]{2,1,0:T(8,128)(2,1)} %get-tuple-element.59), calls=%async_computation.3 | async-start | bytes 786432 | tf_op jit(solution)/shard_map/all_to_all | solution.py:835
  114.3 5.2 %unpack.3.pq_ref = bf16[32,96,512]{2,1,0:T(8,128)(2,1)S(1)} custom-call(s32[2]{0:T(128)S(1)} %pad_add_fusion.ids_ref, bf16[48,3200]{1,0:T(8,128)(2,1)S(1)} %pack.1.w0, bf16[48,3200]{1,0:T(8,128)(2,1)} %collective-permute-done.3.w1, bf16[48,3200]{1,0:T(8,128)(2,1)} %collective-permute-done.4.w2, bf16[48,3200]{1,0:T(8,128)(2,1)} %collective-permute-done.5.w3), custom_call_target="tpu_custom_call" | custom-call | flops 1 | bytes 1 | tf_op jit(solution)/shard_map/unpack/pallas_call | solution.py:214
  119.6 6.2 %all-to-all-done.3.g_ref = bf16[8,32,768]{2,1,0:T(8,128)(2,1)} async-done(((bf16[8,32,768]{2,1,0:T(8,128)(2,1)}), bf16[8,32,768]{2,1,0:T(8,128)(2,1)}, u32[]{:S(2)}, u32[]{:S(2)}) %all-to-all-start.3) | async-done | bytes 393248 | tf_op jit(solution)/shard_map/all_to_all | solution.py:835
  125.7 6.1 %mix_back.1 = bf16[8,32,768]{2,1,0:T(8,128)(2,1)} custom-call(s32[2]{0:T(128)S(1)} %pad_add_fusion.ids_ref, bf16[8,32,768]{2,1,0:T(8,128)(2,1)} %all-to-all-done.3.g_ref, bf16[32,96,512]{2,1,0:T(8,128)(2,1)S(1)} %unpack.3.pq_ref), custom_call_target="tpu_custom_call" | custom-call | flops 1 | bytes 1 | tf_op jit(solution)/shard_map/mix_back/pallas_call | solution.py:437
  131.8 3.6 %all-to-all-start.4 = ((bf16[8,32,768]{2,1,0:T(8,128)(2,1)}), bf16[8,32,768]{2,1,0:T(8,128)(2,1)S(1)}, u32[]{:S(2)}, u32[]{:S(2)}) async-start(bf16[8,32,768]{2,1,0:T(8,128)(2,1)} %mix_back.1), calls=%async_computation.4 | async-start | bytes 786432 | tf_op jit(solution)/shard_map/all_to_all | solution.py:835
  135.5 6.9 %weight_grads.1 = (bf16[48,3200]{1,0:T(8,128)(2,1)}, bf16[48,3200]{1,0:T(8,128)(2,1)}, bf16[48,3200]{1,0:T(8,128)(2,1)}, bf16[48,3200]{1,0:T(8,128)(2,1)}) custom-call(s32[2]{0:T(128)S(1)} %pad_add_fusion.ids_ref, bf16[8,32,384]{2,1,0:T(8,128)(2,1)} %all-to-all-done.xa, bf16[8,32,384]{2,1,0:T(8,128)(2,1)} %all-to-all-done.1.xb, ...), custom_call_target="tpu_custom_call" | custom-call | flops 1 | bytes 1 | tf_op jit(solution)/shard_map/weight_grads/pallas_call | solution.py:501
  147.8 7.7 %inner_grads.1 = (f32[8,1,48,4096]{3,2,1,0:T(8,128)}, bf16[2,1,48,4096]{3,2,1,0:T(8,128)(2,1)}, bf16[2,1,48,4096]{3,2,1,0:T(8,128)(2,1)}, bf16[2,1,48,4096]{3,2,1,0:T(8,128)(2,1)}) custom-call(s32[2]{0:T(128)S(1)} %pad_add_fusion.ids_ref, f32[2]{0:T(128)S(1)} %copy-done.12, bf16[8,32,768]{2,1,0:T(8,128)(2,1)S(1)} %all-to-all-done.4.y_ref, ...), custom_call_target="tpu_custom_call" | custom-call | flops 1 | bytes 1 | tf_op jit(solution)/shard_map/inner_grads/pallas_call | solution.py:686
  159.0 6.1 %place.1 = bf16[8,1,48,4096]{3,2,1,0:T(8,128)(2,1)} custom-call(s32[2]{0:T(128)S(1)} %pad_add_fusion.ids_ref, bf16[2,1,48,4096]{3,2,1,0:T(8,128)(2,1)} %collective-permute-done.6.a_ref, bf16[2,1,48,4096]{3,2,1,0:T(8,128)(2,1)} %collective-permute-done.7.b_ref, bf16[2,1,48,4096]{3,2,1,0:T(8,128)(2,1)} %collective-permute-done.8.c_ref, ...), custom_call_target="tpu_custom_call", output_to_operand_aliasing={{}: (4, {})} | custom-call | flops 1 | bytes 1 | tf_op jit(solution)/shard_map/place/pallas_call | solution.py:726
  166.5 11.9 %collective-permute-start.19 = (f32[48,48]{1,0:T(8,128)S(1)}, f32[48,48]{1,0:T(8,128)S(1)}, u32[]{:S(2)}, u32[]{:S(2)}) collective-permute-start(f32[48,48]{1,0:T(8,128)S(1)} %add.171), channel_id=1, source_target_pairs={{0,2},{1,3},{2,0},{3,1},{4,6},{5,7},{6,4},{7,5},{8,10},{9,11},{10,... | collective-permute-start | bytes 27656 | tf_op jit(solution)/shard_map/ppermute | solution.py:831
  183.2 5.6 %adam.1 = (f32[1,32,2,48,48]{4,3,2,1,0:T(8,128)}, f32[1,32,2,48,48]{4,3,2,1,0:T(8,128)}, f32[1,32,2,48,48]{4,3,2,1,0:T(8,128)}) custom-call(f32[4]{0:T(128)S(1)} %pad_maximum_fusion.1.flips, bf16[48,3200]{1,0:T(8,128)(2,1)S(1)} %copy-done.6, bf16[48,3200]{1,0:T(8,128)(2,1)S(1)} %collective-permute-done.15.d1, ...), custom_call_target="tpu_custom_call" | custom-call | flops 1 | bytes 1 | tf_op jit(solution)/shard_map/adam/pallas_call | solution.py:818
  (101 shorter events, 46.7 us)
Async XLA Ops:
  2.7 22.6 %collective-permute-start.2 = (bf16[2,1,48,4096]{3,2,1,0:T(8,128)(2,1)}, bf16[2,1,48,4096]{3,2,1,0:T(8,128)(2,1)}, u32[]{:S(2)}, u32[]{:S(2)}) collective-permute-start(bf16[2,1,48,4096]{3,2,1,0:T(8,128)(2,1)} %constant_dynamic-slice_fusion.5), channel_id=1, source_target_pairs={{0,24},{8,16},{16,8},{24,0},{1,25},{9,17},{17,9},{25,1},{2,26},{10... | collective-permute-start | bytes 2359304 | tf_op jit(solution)/shard_map/ppermute | solution.py:831
  8.7 34.1 %collective-permute-start = (bf16[2,1,48,4096]{3,2,1,0:T(8,128)(2,1)}, bf16[2,1,48,4096]{3,2,1,0:T(8,128)(2,1)}, u32[]{:S(2)}, u32[]{:S(2)}) collective-permute-start(bf16[2,1,48,4096]{3,2,1,0:T(8,128)(2,1)} %constant_dynamic-slice_fusion.4), channel_id=1, source_target_pairs={{0,8},{8,0},{16,24},{24,16},{1,9},{9,1},{17,25},{25,17},{2,10},{10... | collective-permute-start | bytes 2359304 | tf_op jit(solution)/shard_map/ppermute | solution.py:831
  13.3 29.4 %collective-permute-start.1 = (bf16[2,1,48,4096]{3,2,1,0:T(8,128)(2,1)}, bf16[2,1,48,4096]{3,2,1,0:T(8,128)(2,1)}, u32[]{:S(2)}, u32[]{:S(2)}) collective-permute-start(bf16[2,1,48,4096]{3,2,1,0:T(8,128)(2,1)} %constant_dynamic-slice_fusion.3), channel_id=1, source_target_pairs={{0,16},{8,24},{16,0},{24,8},{1,17},{9,25},{17,1},{25,9},{2,18},{10... | collective-permute-start | bytes 2359304 | tf_op jit(solution)/shard_map/ppermute | solution.py:831
  30.5 17.4 %all-to-all-start = ((bf16[8,32,384]{2,1,0:T(8,128)(2,1)}), bf16[8,32,384]{2,1,0:T(8,128)(2,1)}, u32[]{:S(2)}, u32[]{:S(2)}) async-start(bf16[8,32,384]{2,1,0:T(8,128)(2,1)} %forward.2), calls=%async_computation | async-start | bytes 393216 | tf_op jit(solution)/shard_map/all_to_all | solution.py:835
  35.9 18.4 %collective-permute-start.3 = (bf16[48,3200]{1,0:T(8,128)(2,1)S(1)}, bf16[48,3200]{1,0:T(8,128)(2,1)}, u32[]{:S(2)}, u32[]{:S(2)}) collective-permute-start(bf16[48,3200]{1,0:T(8,128)(2,1)S(1)} %pack.1.w0), channel_id=1, source_target_pairs={{0,8},{8,0},{16,24},{24,16},{1,9},{9,1},{17,25},{25,17},{2,10},{10... | collective-permute-start | bytes 921608 | tf_op jit(solution)/shard_map/ppermute | solution.py:831
  37.4 16.9 %collective-permute-start.4 = (bf16[48,3200]{1,0:T(8,128)(2,1)S(1)}, bf16[48,3200]{1,0:T(8,128)(2,1)}, u32[]{:S(2)}, u32[]{:S(2)}) collective-permute-start(bf16[48,3200]{1,0:T(8,128)(2,1)S(1)} %pack.1.w0), channel_id=1, source_target_pairs={{0,16},{8,24},{16,0},{24,8},{1,17},{9,25},{17,1},{25,9},{2,18},{10... | collective-permute-start | bytes 921608 | tf_op jit(solution)/shard_map/ppermute | solution.py:831
  38.9 15.6 %collective-permute-start.5 = (bf16[48,3200]{1,0:T(8,128)(2,1)S(1)}, bf16[48,3200]{1,0:T(8,128)(2,1)}, u32[]{:S(2)}, u32[]{:S(2)}) collective-permute-start(bf16[48,3200]{1,0:T(8,128)(2,1)S(1)} %pack.1.w0), channel_id=1, source_target_pairs={{0,24},{8,16},{16,8},{24,0},{1,25},{9,17},{17,9},{25,1},{2,26},{10... | collective-permute-start | bytes 921608 | tf_op jit(solution)/shard_map/ppermute | solution.py:831
  47.9 15.4 %all-to-all-start.1 = ((bf16[8,32,384]{2,1,0:T(8,128)(2,1)}), bf16[8,32,384]{2,1,0:T(8,128)(2,1)}, u32[]{:S(2)}, u32[]{:S(2)}) async-start(bf16[8,32,384]{2,1,0:T(8,128)(2,1)} %forward.3), calls=%async_computation.1 | async-start | bytes 393216 | tf_op jit(solution)/shard_map/all_to_all | solution.py:835
  59.8 40.3 %collective-permute-start.9 = (bf16[2,1,48,4096]{3,2,1,0:T(8,128)(2,1)}, bf16[2,1,48,4096]{3,2,1,0:T(8,128)(2,1)}, u32[]{:S(2)}, u32[]{:S(2)}) collective-permute-start(bf16[2,1,48,4096]{3,2,1,0:T(8,128)(2,1)} %get-tuple-element.55), channel_id=1, source_target_pairs={{0,8},{8,0},{16,24},{24,16},{1,9},{9,1},{17,25},{25,17},{2,10},{10... | collective-permute-start | bytes 2359304 | tf_op jit(solution)/shard_map/ppermute | solution.py:831
  61.5 38.5 %collective-permute-start.10 = (bf16[2,1,48,4096]{3,2,1,0:T(8,128)(2,1)}, bf16[2,1,48,4096]{3,2,1,0:T(8,128)(2,1)}, u32[]{:S(2)}, u32[]{:S(2)}) collective-permute-start(bf16[2,1,48,4096]{3,2,1,0:T(8,128)(2,1)} %get-tuple-element.56), channel_id=1, source_target_pairs={{0,16},{8,24},{16,0},{24,8},{1,17},{9,25},{17,1},{25,9},{2,18},{10... | collective-permute-start | bytes 2359304 | tf_op jit(solution)/shard_map/ppermute | solution.py:831
  63.1 37.0 %collective-permute-start.11 = (bf16[2,1,48,4096]{3,2,1,0:T(8,128)(2,1)}, bf16[2,1,48,4096]{3,2,1,0:T(8,128)(2,1)}, u32[]{:S(2)}, u32[]{:S(2)}) collective-permute-start(bf16[2,1,48,4096]{3,2,1,0:T(8,128)(2,1)} %get-tuple-element.57), channel_id=1, source_target_pairs={{0,24},{8,16},{16,8},{24,0},{1,25},{9,17},{17,9},{25,1},{2,26},{10... | collective-permute-start | bytes 2359304 | tf_op jit(solution)/shard_map/ppermute | solution.py:831
  68.2 17.6 %all-to-all-start.2 = ((bf16[8,32,768]{2,1,0:T(8,128)(2,1)}), bf16[8,32,768]{2,1,0:T(8,128)(2,1)S(1)}, u32[]{:S(2)}, u32[]{:S(2)}) async-start(bf16[8,32,768]{2,1,0:T(8,128)(2,1)} %mix.1), calls=%async_computation.2 | async-start | bytes 786432 | tf_op jit(solution)/shard_map/all_to_all | solution.py:835
  97.6 28.1 %collective-permute-start.8 = (bf16[2,1,48,4096]{3,2,1,0:T(8,128)(2,1)}, bf16[2,1,48,4096]{3,2,1,0:T(8,128)(2,1)}, u32[]{:S(2)}, u32[]{:S(2)}) collective-permute-start(bf16[2,1,48,4096]{3,2,1,0:T(8,128)(2,1)} %get-tuple-element.53), channel_id=1, source_target_pairs={{0,24},{8,16},{16,8},{24,0},{1,25},{9,17},{17,9},{25,1},{2,26},{10... | collective-permute-start | bytes 2359304 | tf_op jit(solution)/shard_map/ppermute | solution.py:831
  109.1 16.7 %all-to-all-start.3 = ((bf16[8,32,768]{2,1,0:T(8,128)(2,1)}), bf16[8,32,768]{2,1,0:T(8,128)(2,1)}, u32[]{:S(2)}, u32[]{:S(2)}) async-start(bf16[8,32,768]{2,1,0:T(8,128)(2,1)} %get-tuple-element.59), calls=%async_computation.3 | async-start | bytes 786432 | tf_op jit(solution)/shard_map/all_to_all | solution.py:835
  113.2 42.3 %collective-permute-start.6 = (bf16[2,1,48,4096]{3,2,1,0:T(8,128)(2,1)}, bf16[2,1,48,4096]{3,2,1,0:T(8,128)(2,1)}, u32[]{:S(2)}, u32[]{:S(2)}) collective-permute-start(bf16[2,1,48,4096]{3,2,1,0:T(8,128)(2,1)} %get-tuple-element.51), channel_id=1, source_target_pairs={{0,8},{8,0},{16,24},{24,16},{1,9},{9,1},{17,25},{25,17},{2,10},{10... | collective-permute-start | bytes 2359304 | tf_op jit(solution)/shard_map/ppermute | solution.py:831
  113.8 41.7 %collective-permute-start.7 = (bf16[2,1,48,4096]{3,2,1,0:T(8,128)(2,1)}, bf16[2,1,48,4096]{3,2,1,0:T(8,128)(2,1)}, u32[]{:S(2)}, u32[]{:S(2)}) collective-permute-start(bf16[2,1,48,4096]{3,2,1,0:T(8,128)(2,1)} %get-tuple-element.52), channel_id=1, source_target_pairs={{0,16},{8,24},{16,0},{24,8},{1,17},{9,25},{17,1},{25,9},{2,18},{10... | collective-permute-start | bytes 2359304 | tf_op jit(solution)/shard_map/ppermute | solution.py:831
  131.8 15.9 %all-to-all-start.4 = ((bf16[8,32,768]{2,1,0:T(8,128)(2,1)}), bf16[8,32,768]{2,1,0:T(8,128)(2,1)S(1)}, u32[]{:S(2)}, u32[]{:S(2)}) async-start(bf16[8,32,768]{2,1,0:T(8,128)(2,1)} %mix_back.1), calls=%async_computation.4 | async-start | bytes 786432 | tf_op jit(solution)/shard_map/all_to_all | solution.py:835
  142.4 15.1 %collective-permute-start.15 = (bf16[48,3200]{1,0:T(8,128)(2,1)}, bf16[48,3200]{1,0:T(8,128)(2,1)S(1)}, u32[]{:S(2)}, u32[]{:S(2)}) collective-permute-start(bf16[48,3200]{1,0:T(8,128)(2,1)} %get-tuple-element.74), channel_id=1, source_target_pairs={{0,8},{8,0},{16,24},{24,16},{1,9},{9,1},{17,25},{25,17},{2,10},{10... | collective-permute-start | bytes 921608 | tf_op jit(solution)/shard_map/ppermute | solution.py:831
  142.9 22.3 %collective-permute-start.16 = (bf16[48,3200]{1,0:T(8,128)(2,1)}, bf16[48,3200]{1,0:T(8,128)(2,1)S(1)}, u32[]{:S(2)}, u32[]{:S(2)}) collective-permute-start(bf16[48,3200]{1,0:T(8,128)(2,1)} %get-tuple-element.75), channel_id=1, source_target_pairs={{0,16},{8,24},{16,0},{24,8},{1,17},{9,25},{17,1},{25,9},{2,18},{10... | collective-permute-start | bytes 921608 | tf_op jit(solution)/shard_map/ppermute | solution.py:831
  143.4 21.8 %collective-permute-start.17 = (bf16[48,3200]{1,0:T(8,128)(2,1)}, bf16[48,3200]{1,0:T(8,128)(2,1)S(1)}, u32[]{:S(2)}, u32[]{:S(2)}) collective-permute-start(bf16[48,3200]{1,0:T(8,128)(2,1)} %get-tuple-element.76), channel_id=1, source_target_pairs={{0,24},{8,16},{16,8},{24,0},{1,25},{9,17},{17,9},{25,1},{2,26},{10... | collective-permute-start | bytes 921608 | tf_op jit(solution)/shard_map/ppermute | solution.py:831
  155.5 34.1 %collective-permute-start.14 = (bf16[2,1,48,4096]{3,2,1,0:T(8,128)(2,1)}, bf16[2,1,48,4096]{3,2,1,0:T(8,128)(2,1)S(1)}, u32[]{:S(2)}, u32[]{:S(2)}) collective-permute-start(bf16[2,1,48,4096]{3,2,1,0:T(8,128)(2,1)} %get-tuple-element.71), channel_id=1, source_target_pairs={{0,24},{8,16},{16,8},{24,0},{1,25},{9,17},{17,9},{25,1},{2,26},{10... | collective-permute-start | bytes 2359304 | tf_op jit(solution)/shard_map/ppermute | solution.py:831
  156.0 36.3 %collective-permute-start.12 = (bf16[2,1,48,4096]{3,2,1,0:T(8,128)(2,1)}, bf16[2,1,48,4096]{3,2,1,0:T(8,128)(2,1)S(1)}, u32[]{:S(2)}, u32[]{:S(2)}) collective-permute-start(bf16[2,1,48,4096]{3,2,1,0:T(8,128)(2,1)} %get-tuple-element.69), channel_id=1, source_target_pairs={{0,8},{8,0},{16,24},{24,16},{1,9},{9,1},{17,25},{25,17},{2,10},{10... | collective-permute-start | bytes 2359304 | tf_op jit(solution)/shard_map/ppermute | solution.py:831
  157.5 35.1 %collective-permute-start.13 = (bf16[2,1,48,4096]{3,2,1,0:T(8,128)(2,1)}, bf16[2,1,48,4096]{3,2,1,0:T(8,128)(2,1)S(1)}, u32[]{:S(2)}, u32[]{:S(2)}) collective-permute-start(bf16[2,1,48,4096]{3,2,1,0:T(8,128)(2,1)} %get-tuple-element.70), channel_id=1, source_target_pairs={{0,16},{8,24},{16,0},{24,8},{1,17},{9,25},{17,1},{25,9},{2,18},{10... | collective-permute-start | bytes 2359304 | tf_op jit(solution)/shard_map/ppermute | solution.py:831
  166.5 13.7 %collective-permute-start.19 = (f32[48,48]{1,0:T(8,128)S(1)}, f32[48,48]{1,0:T(8,128)S(1)}, u32[]{:S(2)}, u32[]{:S(2)}) collective-permute-start(f32[48,48]{1,0:T(8,128)S(1)} %add.171), channel_id=1, source_target_pairs={{0,2},{1,3},{2,0},{3,1},{4,6},{5,7},{6,4},{7,5},{8,10},{9,11},{10,... | collective-permute-start | bytes 27656 | tf_op jit(solution)/shard_map/ppermute | solution.py:831
  (21 other events, 393.3 us)

commit v5 on v4

--- a/solution.py
+++ b/solution.py
@@ -129,7 +129,7 @@
         in_specs=small_specs(rows * GRID),
         out_specs=pl.BlockSpec((n, rows * GRID), lambda i: (0, i)),
         out_shape=slow((n, NPIX), BF16),
-        compiler_params=params(12),
+        compiler_params=params(28),
         cost_estimate=cost(),
         name="turned",
     )(*stay(small, small))
@@ -155,7 +155,7 @@
         in_specs=in_vmem(2),
         out_specs=in_vmem(1)[0],
         out_shape=jax.ShapeDtypeStruct((C, modes * LANES + PACK), BF16),
-        compiler_params=params(12),
+        compiler_params=params(28),
         cost_estimate=cost(),
         name="pack",
     )(spec_weight, lin_weight)
@@ -188,16 +188,18 @@
     return tiles
 
 
-def unpack_kernel(ids_ref, w0, w1, w2, w3, pq_ref):
+def unpack_kernel(ids_ref, w0, w1, w2, w3, pq_ref, *lines):
     own = ids_ref[0]
+    modes = pq_ref.shape[0]
     lane = lanes_of((C, PACK))
+    flip = flip_of(own, 1)
 
     def step(g, carry):
         for t, w in enumerate((w0, w1, w2, w3)):
             slot = jnp.bitwise_xor(own, t)
-            flip = jnp.where(slot % 2 == 1, flip_of(own, 1), 1.0)
+            scale = jnp.where(slot % 2 == 1, flip, 1.0)
             at = pl.ds(pl.multiple_of(slot * PACK, PACK), PACK)
-            tiles = [tile * flip for tile in quad_tiles(w, g)]
+            tiles = [tile * scale for tile in quad_tiles(w, g)]
             for q, p in enumerate(split_lanes(*tiles)):
                 p = jnp.where(lane < LANES, p, 0.0)
                 low = jnp.where(lane < C, -pltpu.roll(p, PACK - C, 1), pltpu.roll(p, C, 1))
@@ -206,28 +208,14 @@
                 pq_ref[g * QUAD + q, C:, at] = low.astype(BF16)
         return carry
 
-    lax.fori_loop(0, pq_ref.shape[0] // QUAD, step, 0)
-
-
-def unpack(ids, packs):
-    modes = (packs[0].shape[1] - PACK) // LANES
-    return pl.pallas_call(
-        unpack_kernel,
-        in_specs=[pl.BlockSpec(memory_space=SMEM)] + in_vmem(4),
-        out_specs=in_vmem(1)[0],
-        out_shape=fast((modes, LANES, 4 * PACK), BF16),
-        compiler_params=params(12),
-        cost_estimate=cost(),
-        name="unpack",
-    )(ids, *packs)
-
-
-def lines_kernel(ids_ref, w0, w1, w2, w3, lt_ref, lb_ref, lsc):
-    own = ids_ref[0]
+    quads = modes // QUAD
+    lax.fori_loop(0, quads, step, 0, unroll=min(4, quads))
+    if not lines:
+        return
+    lt_ref, lb_ref, lsc = lines
     for t, w in enumerate((w0, w1, w2, w3)):
         slot = jnp.bitwise_xor(own, t)
-        flip = jnp.where(slot % 2 == 1, flip_of(own, 1), 1.0)
-        lsc[slot] = w[...].astype(F32) * flip
+        lsc[slot] = w[:, modes * LANES :].astype(F32) * jnp.where(slot % 2 == 1, flip, 1.0)
     for k in range(4):
         line = lsc[k]
         turned = line.T
@@ -237,20 +225,21 @@
             lt_ref[u * C : (u + 1) * C, t * C : (t + 1) * C] = (turned[:C] * sgn(t, k)).astype(BF16)
 
 
-def unpack_lines(ids, packs):
-    last = packs[0].shape[1] // PACK - 1
-    return pl.pallas_call(
-        lines_kernel,
-        grid=(1,),
-        in_specs=[pl.BlockSpec(memory_space=SMEM)]
-        + [pl.BlockSpec((C, PACK), lambda i: (0, last))] * 4,
-        out_specs=[whole((4 * C, 4 * C))] * 2,
-        out_shape=[fast((4 * C, 4 * C), BF16), slow((4 * C, 4 * C), BF16)],
-        scratch_shapes=[pltpu.VMEM((4, C, PACK), F32)],
-        compiler_params=params(12),
-        cost_estimate=cost(),
-        name="lines",
+def unpack(ids, packs, lines):
+    modes = (packs[0].shape[1] - PACK) // LANES
+    weights = fast((modes, LANES, 4 * PACK), BF16)
+    shape = (4 * C, 4 * C)
+    result = pl.pallas_call(
+        unpack_kernel,
+        in_specs=[pl.BlockSpec(memory_space=SMEM)] + in_vmem(4),
+        out_specs=in_vmem(3 if lines else 1),
+        out_shape=[weights] + ([fast(shape, BF16), slow(shape, BF16)] if lines else []),
+        scratch_shapes=[pltpu.VMEM((4, C, PACK), F32)] if lines else [],
+        compiler_params=params(28),
+        cost_estimate=cost(),
+        name="unpack",
     )(ids, *packs)
+    return result if lines else result[0]
 
 
 def spread(acc, out_ref, scales=None):
@@ -272,10 +261,12 @@
             ysc[n * C : (n + 1) * C, r * MODES : (r + 1) * MODES] = piece
 
 
-def forward_kernel(ids_ref, inv_ref, x0, x1, row_ref, col_ref, out_ref, acc):
+def forward_kernel(ids_ref, inv_ref, *refs):
+    x = refs[:-4]
+    row_ref, col_ref, out_ref, acc = refs[-4:]
     i = pl.program_id(0)
-    samples = x0.shape[0]
-    rows = [x[s, 0] for s in range(samples) for x in (x0, x1)]
+    samples = x[0].shape[0]
+    rows = [part[s, 0] for s in range(samples) for part in x]
     table = table_rows(row_ref, col_ref, 0, row_ref.shape[1])
     part = dot(jnp.concatenate(rows, axis=0), table)
 
@@ -289,15 +280,15 @@
 
     @pl.when(i == pl.num_programs(0) - 1)
     def _():
-        spread(acc, out_ref, [inv_ref[s] for s in range(samples) for _ in range(2)])
+        spread(acc, out_ref, [inv_ref[s] for s in range(samples) for _ in x])
 
 
 def forward_spectrum(ids, inv, x, small, shards):
     samples = inv.shape[0]
     modes = MODES // shards
-    width = samples * 2 * LANES
+    width = samples * len(x) * LANES
     n = 2 * MODES
-    tile = 1024
+    tile = 2048
 
     def spec(array):
         if array.shape[0] == samples:
@@ -309,12 +300,12 @@
         grid_spec=pltpu.PrefetchScalarGridSpec(
             num_scalar_prefetch=2,
             grid=(NPIX // tile,),
-            in_specs=[spec(x[0]), spec(x[1])] + small_specs(tile),
+            in_specs=[spec(part) for part in x] + small_specs(tile),
             out_specs=whole((shards, modes, width)),
-            scratch_shapes=[pltpu.VMEM((samples * 2 * C, n), F32)],
+            scratch_shapes=[pltpu.VMEM((samples * len(x) * C, n), F32)],
         ),
         out_shape=slow((shards, modes, width), BF16),
-        compiler_params=params(12),
+        compiler_params=params(28),
         cost_estimate=cost(),
         name="forward",
     )(ids, inv, *stay(*x), *stay(small, small))
@@ -399,7 +390,7 @@
                 ysc[s * 3 + n, at, :] = tile
         return carry
 
-    lax.fori_loop(0, modes, step, 0, unroll=4)
+    lax.fori_loop(0, modes, step, 0, unroll=min(32, modes))
 
 
 def mix_kernel(ids_ref, xa, xb, pq_ref, y_ref, xsc, ysc):
@@ -418,7 +409,7 @@
         out_specs=in_vmem(1)[0],
         out_shape=slow((shards, modes, 2 * half), BF16),
         scratch_shapes=[row_scratch(modes, shards, 2 * half)] * 2,
-        compiler_params=params(12),
+        compiler_params=params(28),
         cost_estimate=cost(),
         name="mix",
     )(ids, xa, xb, *pin(pq))
@@ -440,7 +431,7 @@
         out_specs=in_vmem(1)[0],
         out_shape=slow(g.shape, BF16),
         scratch_shapes=[row_scratch(modes, shards, width)] * 2,
-        compiler_params=params(12),
+        compiler_params=params(28),
         cost_estimate=cost(),
         name="mix_back",
     )(ids, g, *pin(pq))
@@ -504,7 +495,7 @@
         out_specs=in_vmem(4),
         out_shape=[slow(shape, BF16)] * 4,
         scratch_shapes=[row_scratch(modes, shards, width)] * 2 + [pltpu.VMEM((4,) + shape, BF16)],
-        compiler_params=params(12),
+        compiler_params=params(28),
         cost_estimate=cost(),
         name="weight_grads",
     )(ids, xa, xb, g, lin)
@@ -545,7 +536,8 @@
     for s in range(samples):
         at = slice(s * rows, (s + 1) * rows)
         fields = jnp.concatenate([x[t][s, 0] for t in range(4)], axis=0)
-        pre[at] = dot(ysc[at], ft_ref[...]) + dot(lts[s], fields)
+        left = jnp.concatenate([ysc[at], lts[s]], axis=1)
+        pre[at] = dot(left, jnp.concatenate([ft_ref[...], fields], axis=0))
     for s in range(samples):
         for t in range(4):
             for c in range(0, C, ROWS):
@@ -586,7 +578,7 @@
         out_shape=[slow(x[0].shape, BF16)]
         + [slow((samples, 1, C, NPIX), BF16)] * 3
         + [fast((rows, NPIX), BF16)],
-        compiler_params=params(12),
+        compiler_params=params(28),
         cost_estimate=cost(),
         name="pixels",
     )(ids, inv, *stay(*x), y, *stay(turned), *pin(lt))
@@ -610,10 +602,10 @@
             grad = cot[t][s, 0].astype(F32) * slope[at : at + C].astype(F32)
             g_ref[at : at + C] = grad.astype(BF16)
     table = table_rows(row_ref, col_ref, 0, row_ref.shape[1])
+    gacc[...] += dot(g_ref[...], table)
     for s in range(samples):
         at = slice(s * rows, (s + 1) * rows)
         g = g_ref[at]
-        gacc[at] += dot(g, table)
         fields = jnp.concatenate([x[t][s, 0] for t in range(4)], axis=0)
         lacc[...] += dot(fields, g, ((1,), (1,))) * inv_ref[s]
 
@@ -633,7 +625,7 @@
     rows = slope.shape[0]
     samples = rows // (4 * C)
     n = 2 * MODES
-    tile = 1024
+    tile = 2048
     mine = pl.BlockSpec((samples, 1, C, tile), lambda i, ids, inv: (ids[0], 0, 0, i))
     block = pl.BlockSpec((samples, 1, C, tile), lambda i, ids, inv: (0, 0, 0, i))
     flat = pl.BlockSpec((rows, tile), lambda i, ids, inv: (0, i))
@@ -653,13 +645,14 @@
             slow(spectrum, BF16),
             jax.ShapeDtypeStruct((4, C, C), F32),
         ],
-        compiler_params=params(12),
+        compiler_params=params(28),
         cost_estimate=cost(),
         name="pixel_grads",
     )(ids, inv, *stay(*x), *stay(*cot), *pin(slope), *stay(small, small))
 
 
-def inner_kernel(ids_ref, inv_ref, y_ref, g_ref, ft_ref, lb_ref, cot_ref, mine_ref, o1, o2, o3, ysc):
+def inner_kernel(ids_ref, inv_ref, y_ref, g_ref, row_ref, col_ref, lb_ref, cot_ref, mine_ref, *refs):
+    o1, o2, o3, ysc = refs
     samples = cot_ref.shape[0]
     rows = 4 * C
 
@@ -667,7 +660,8 @@
     def _():
         collect(y_ref, ysc)
 
-    spatial = dot(ysc[...], ft_ref[...])
+    table = table_rows(row_ref, col_ref, 0, row_ref.shape[1])
+    spatial = dot(ysc[...], table, ((1,), (1,)))
     for s in range(samples):
         at = slice(s * rows, (s + 1) * rows)
         total = spatial[at] + dot(lb_ref[...], g_ref[at])
@@ -676,10 +670,10 @@
             out[s, 0] = total[t * C : (t + 1) * C].astype(BF16)
 
 
-def inner_grads(ids, inv, y, g, turned, lb, cotangent):
+def inner_grads(ids, inv, y, g, small, lb, cotangent):
     samples = inv.shape[0]
     n = 2 * MODES
-    tile = 1024
+    tile = 2048
     rows = samples * 4 * C
     mine = pl.BlockSpec((samples, 1, C, tile), lambda i, ids, inv: (ids[0], 0, 0, i))
     block = pl.BlockSpec((samples, 1, C, tile), lambda i, ids, inv: (0, 0, 0, i))
@@ -691,7 +685,7 @@
             in_specs=[
                 whole(y.shape),
                 pl.BlockSpec((rows, tile), lambda i, ids, inv: (0, i)),
-                pl.BlockSpec((n, tile), lambda i, ids, inv: (0, i)),
+                *small_specs(tile),
                 whole((4 * C, 4 * C)),
                 mine,
             ],
@@ -699,10 +693,10 @@
             scratch_shapes=[pltpu.VMEM((rows, n), BF16)],
         ),
         out_shape=[slow(cotangent.shape, F32)] + [slow((samples, 1, C, NPIX), BF16)] * 3,
-        compiler_params=params(12),
+        compiler_params=params(28),
         cost_estimate=cost(),
         name="inner_grads",
-    )(ids, inv, y, *stay(g, turned), lb, *stay(cotangent))
+    )(ids, inv, y, *stay(g, small, small), lb, *stay(cotangent))
 
 
 def place_kernel(ids_ref, a_ref, b_ref, c_ref, old_ref, out_ref):
@@ -735,7 +729,7 @@
         ),
         out_shape=jax.ShapeDtypeStruct(result.shape, BF16),
         input_output_aliases={4: 0},
-        compiler_params=params(12),
+        compiler_params=params(28),
         cost_estimate=cost(),
         name="place",
     )(ids, *parts, result)
@@ -784,7 +778,7 @@
         ),
         out_shape=jax.ShapeDtypeStruct(cotangent.shape, F32),
         input_output_aliases={3 + count: 0},
-        compiler_params=params(12),
+        compiler_params=params(28),
         cost_estimate=cost(),
         name="final",
     )(ids, inv, cotangent, *parts, result)
@@ -821,7 +815,7 @@
         in_specs=[pl.BlockSpec(memory_space=SMEM)] + [packed] * 4 + [block] * 3,
         out_specs=[block] * 3,
         out_shape=[jax.ShapeDtypeStruct(weight.shape, F32)] * 3,
-        compiler_params=params(12),
+        compiler_params=params(28),
         cost_estimate=cost(),
         name="adam",
     )(flips, *grads, weight, first, second)
@@ -886,23 +880,24 @@
     blocks = after([cut(cotangent, t) for t in (1, 2, 3)], (x1, x2))
     cot = (cotangent,) + tuple(swap(blocks[t - 1], "blade", 4, t) for t in (1, 2, 3))
     xb = to_modes(forward_spectrum(ids, inv, (x1, x2), small, shards))
-    mixed = mix(ids, xa, xb, unpack(ids, packs))
-    y = to_modes(mixed)
-    lt, lb = unpack_lines(after(ids, mixed), packs)
+    pq, lt, lb = unpack(ids, packs, True)
+    y = to_modes(mix(ids, xa, xb, pq))
 
     x = (inputs, x1, x2, x3)
     result = pixels(ids, inv, x, y, turned, lt)
     output, slope = result[0], result[4]
-    out_parts = [swap(result[t], "blade", 4, t) for t in (1, 2, 3)]
+    last, cot = lax.optimization_barrier((result[3], cot))
+    parts = (result[1], result[2], last)
+    out_parts = [swap(parts[t - 1], "blade", 4, t) for t in (1, 2, 3)]
 
     grad_pre, sent, lin = pixel_grads(ids, inv, x, cot, slope, small, y.shape)
     g = after(to_modes(sent), out_parts[2])
-    mixed = mix_back(ids, g, unpack(after(ids, lin), packs))
+    mixed = mix_back(ids, g, unpack(after(ids, lin), packs, False))
     back = to_modes(mixed)
     spec_grads = weight_grads(ids, xa, xb, g, lin)
     spec_grads = [spec_grads[0]] + [swap(spec_grads[t], "blade", 4, t) for t in (1, 2, 3)]
 
-    inner = inner_grads(ids, inv, back, grad_pre, turned, lb, cotangent)
+    inner = inner_grads(ids, inv, back, grad_pre, small, lb, cotangent)
     inner = after(inner, out_parts)
     grad_parts = [swap(inner[t], "blade", 4, t) for t in (1, 2, 3)]
 

time: 197 us -> 191 us (0.970)
  blocking collectives: 0 us -> 17.6 us
  starting transfers between devices: 60.1 us -> 43.7 us
  Pallas kernels: 91.4 us -> 81.2 us
  local copies, waits for them, and re-layouts: 9 us -> 12.4 us
    all_to_all x0 -> x1, blocking collectives: none -> 17.6 us  [to_modes(): return lax.all_to_all(value, 'dp', split_axis=0, concat_axis=0, tiled=True)]
    all_to_all x5 -> x4, waiting for transfers between devices: 18.9 us -> 5.71 us  [to_modes(): return lax.all_to_all(value, 'dp', split_axis=0, concat_axis=0, tiled=True)]
    ppermute x21, waiting for transfers between devices: 12.2 us -> 25.3 us  [swap(): return lax.ppermute(value, axis, [(i, i ^ x) for i in range(size)])]
    ppermute x21, starting transfers between devices: 37 us -> 26.3 us  [swap(): return lax.ppermute(value, axis, [(i, i ^ x) for i in range(size)])]
    all_to_all x5 -> x4, starting transfers between devices: 23.1 us -> 17.4 us  [to_modes(): return lax.all_to_all(value, 'dp', split_axis=0, concat_axis=0, tiled=True)]
    unnamed x38 -> x46, local copies, waits for them, and re-layouts: 1.12 us -> 4.61 us
    pallas_call x1, Pallas kernels: 6.07 us -> 3.95 us  [mix_back(): pl.pallas_call(mix_back_kernel, in_specs=[pl.BlockSpec(memory_space=SMEM)...]
    pallas_call x1, Pallas kernels: 4.84 us -> 2.77 us  [mix(): pl.pallas_call(mix_kernel, in_specs=[pl.BlockSpec(memory_space=SMEM)] + i...]
  transfers between devices with their start and end apart: 26 -> 25, of which waited for: 10 -> 9; matrix products, arithmetic and copies ran while one was open for 4% -> 5% of each run, Pallas kernels for 45% -> 41%
where the time goes in v5:
time: 191 us; the launch traced here: 190 us
  Pallas kernels  81.2 us (43%)
  starting transfers between devices  43.7 us (23%)
  waiting for transfers between devices  31 us (16%)
  blocking collectives  17.6 us (9%)
  local copies, waits for them, and re-layouts  12.4 us (6%)
  other arithmetic  2.95 us (2%)
    ppermute x21, starting transfers between devices, swap(): return lax.ppermute(value, axis, [(i, i ^ x) for i in range(size)])  26.3 us
    ppermute x21, waiting for transfers between devices, swap(): return lax.ppermute(value, axis, [(i, i ^ x) for i in range(size)])  25.3 us
    all_to_all x1, blocking collectives, to_modes(): return lax.all_to_all(value, 'dp', split_axis=0, concat_axis=0, tiled=True)  17.6 us
    all_to_all x4, starting transfers between devices, to_modes(): return lax.all_to_all(value, 'dp', split_axis=0, concat_axis=0, tiled=True)  17.4 us
    pallas_call x1, Pallas kernels, pixels(): pl.pallas_call(pixel_kernel, grid_spec=pltpu.PrefetchScalarGridSpec(num_s...  11.8 us
    pallas_call x2, Pallas kernels, unpack(): pl.pallas_call(unpack_kernel, in_specs=[pl.BlockSpec(memory_space=SMEM)]...  10.4 us
    pallas_call x2, Pallas kernels, forward_spectrum(): pl.pallas_call(forward_kernel, grid_spec=pltpu.PrefetchScalarGridSpec(num...  8.38 us
    dynamic_slice x4, local copies, waits for them, and re-layouts, cut(): lax.dynamic_slice_in_dim(array, jnp.bitwise_xor(own, t) * samples, sample...  7.76 us
  transfers between devices with their start and end apart: 25, of which 9 were waited for; matrix products, arithmetic and copies ran while one was open for 5% of the time, Pallas kernels for 41%

profile of v5, /device:TPU:0, one launch (start us, length us, event | category | flops | bytes accessed | tf_op | source)
XLA Modules:
  0.0 189.9 jit_solution(15912145770190383372)
XLA Ops:
  2.7 3.9 %collective-permute-start.2 = (bf16[2,1,48,4096]{3,2,1,0:T(8,128)(2,1)}, bf16[2,1,48,4096]{3,2,1,0:T(8,128)(2,1)}, u32[]{:S(2)}, u32[]{:S(2)}) collective-permute-start(bf16[2,1,48,4096]{3,2,1,0:T(8,128)(2,1)} %constant_dynamic-slice_fusion.5), channel_id=1, source_target_pairs={{0,24},{8,16},{16,8},{24,0},{1,25},{9,17},{17,9},{25,1},{2,26},{10... | collective-permute-start | bytes 2359304 | tf_op jit(solution)/shard_map/ppermute | solution.py:825
  13.4 5.9 %turned.1.refs_5_ = bf16[512,4096]{1,0:T(8,128)(2,1)} custom-call(f32[4,64,512]{2,1,0:T(8,128)} %pad_maximum_fusion.row_ref.col_ref.refs_2_.refs_3_.refs_9_.refs_10_, f32[4,64,512]{2,1,0:T(8,128)} %pad_maximum_fusion.row_ref.col_ref.refs_2_.refs_3_.refs_9_.refs_10_), custom_call_target="tpu_custom_call" | custom-call | flops 1 | bytes 1 | tf_op jit(solution)/shard_map/turned/pallas_call | solution.py:126
  21.0 4.4 %collective-permute-done.2.refs_1_.refs_3_ = bf16[2,1,48,4096]{3,2,1,0:T(8,128)(2,1)} collective-permute-done((bf16[2,1,48,4096]{3,2,1,0:T(8,128)(2,1)}, bf16[2,1,48,4096]{3,2,1,0:T(8,128)(2,1)}, u32[]{:S(2)}, u32[]{:S(2)}) %collective-permute-start.2) | collective-permute-done | bytes 786464 | tf_op jit(solution)/shard_map/ppermute | solution.py:825
  25.3 4.2 %forward.2 = bf16[8,32,384]{2,1,0:T(8,128)(2,1)} custom-call(s32[2]{0:T(128)S(1)} %pad_add_fusion.ids_ref, f32[2]{0:T(128)S(1)} %dynamic_slice.21.inv_ref, bf16[8,1,48,4096]{3,2,1,0:T(8,128)(2,1)} %refs_0_.5, bf16[2,1,48,4096]{3,2,1,0:T(8,128)(2,1)} %collective-permute-done.2.refs_1_.refs_3_, ...), custom_call_target="tpu_custom_call" | custom-call | flops 1 | bytes 1 | tf_op jit(solution)/shard_map/forward/pallas_call | solution.py:298
  29.5 5.4 %all-to-all-start = ((bf16[8,32,384]{2,1,0:T(8,128)(2,1)}), bf16[8,32,384]{2,1,0:T(8,128)(2,1)}, u32[]{:S(2)}, u32[]{:S(2)}) async-start(bf16[8,32,384]{2,1,0:T(8,128)(2,1)} %forward.2), calls=%async_computation | async-start | bytes 393216 | tf_op jit(solution)/shard_map/all_to_all | solution.py:829
  38.4 4.3 %collective-permute-done.refs_0_.refs_1_ = bf16[2,1,48,4096]{3,2,1,0:T(8,128)(2,1)} collective-permute-done((bf16[2,1,48,4096]{3,2,1,0:T(8,128)(2,1)}, bf16[2,1,48,4096]{3,2,1,0:T(8,128)(2,1)}, u32[]{:S(2)}, u32[]{:S(2)}) %collective-permute-start) | collective-permute-done | bytes 786464 | tf_op jit(solution)/shard_map/ppermute | solution.py:825
  42.8 4.2 %forward.3 = bf16[8,32,384]{2,1,0:T(8,128)(2,1)} custom-call(s32[2]{0:T(128)S(1)} %pad_add_fusion.ids_ref, f32[2]{0:T(128)S(1)} %dynamic_slice.21.inv_ref, bf16[2,1,48,4096]{3,2,1,0:T(8,128)(2,1)} %collective-permute-done.refs_0_.refs_1_, bf16[2,1,48,4096]{3,2,1,0:T(8,128)(2,1)} %collective-permute-done.1.refs_1_.refs_2_, ...), custom_call_target="tpu_custom_call" | custom-call | flops 1 | bytes 1 | tf_op jit(solution)/shard_map/forward/pallas_call | solution.py:298
  46.9 4.9 %all-to-all-start.1 = ((bf16[8,32,384]{2,1,0:T(8,128)(2,1)}), bf16[8,32,384]{2,1,0:T(8,128)(2,1)}, u32[]{:S(2)}, u32[]{:S(2)}) async-start(bf16[8,32,384]{2,1,0:T(8,128)(2,1)} %forward.3), calls=%async_computation.1 | async-start | bytes 393216 | tf_op jit(solution)/shard_map/all_to_all | solution.py:829
  56.8 5.7 %unpack.2 = (bf16[32,96,512]{2,1,0:T(8,128)(2,1)S(1)}, bf16[192,192]{1,0:T(8,128)(2,1)S(1)}, bf16[192,192]{1,0:T(8,128)(2,1)}) custom-call(s32[2]{0:T(128)S(1)} %pad_add_fusion.ids_ref, bf16[48,3200]{1,0:T(8,128)(2,1)S(1)} %pack.1.w0, bf16[48,3200]{1,0:T(8,128)(2,1)} %collective-permute-done.3.w1, bf16[48,3200]{1,0:T(8,128)(2,1)} %collective-permute-done.4.w2, ...), custom_call_target="tpu_custom_call" | custom-call | flops 1 | bytes 1 | tf_op jit(solution)/shard_map/unpack/pallas_call | solution.py:232
  62.5 2.8 %mix.1 = bf16[8,32,768]{2,1,0:T(8,128)(2,1)} custom-call(s32[2]{0:T(128)S(1)} %pad_add_fusion.ids_ref, bf16[8,32,384]{2,1,0:T(8,128)(2,1)} %all-to-all-done.xa, bf16[8,32,384]{2,1,0:T(8,128)(2,1)} %all-to-all-done.1.xb, bf16[32,96,512]{2,1,0:T(8,128)(2,1)S(1)} %get-tuple-element.54.pq_ref), custom_call_target="tpu_custom_call" | custom-call | flops 1 | bytes 1 | tf_op jit(solution)/shard_map/mix/pallas_call | solution.py:406
  65.3 17.6 %all_to_all.25.refs_4_ = bf16[8,32,768]{2,1,0:T(8,128)(2,1)S(1)} all-to-all(bf16[8,32,768]{2,1,0:T(8,128)(2,1)} %mix.1), channel_id=1, replica_groups=mesh['blade'=4,'dp'=8] {'dp'}, dimensions={0} | all-to-all | bytes 786432 | tf_op jit(solution)/shard_map/all_to_all | solution.py:829
  83.5 11.8 %pixels.1 = (bf16[8,1,48,4096]{3,2,1,0:T(8,128)(2,1)}, bf16[2,1,48,4096]{3,2,1,0:T(8,128)(2,1)}, bf16[2,1,48,4096]{3,2,1,0:T(8,128)(2,1)}, bf16[2,1,48,4096]{3,2,1,0:T(8,128)(2,1)}, bf16[384,4096]{1,0:T(8,128)(2,1)S(1)}) custom-call(s32[2]{0:T(128)S(1)} %pad_add_fusion.ids_ref, f32[2]{0:T(128)S(1)} %copy-done.15, bf16[8,1,48,4096]{3,2,1,0:T(8,128)(2,1)} %refs_0_.5, ...), custom_call_target="tpu_custom_call" | custom-call | flops 1 | bytes 1 | tf_op jit(solution)/shard_map/pixels/pallas_call | solution.py:559
  96.9 7.4 %pixel_grads.1 = (bf16[384,4096]{1,0:T(8,128)(2,1)}, bf16[8,32,768]{2,1,0:T(8,128)(2,1)}, f32[4,48,48]{2,1,0:T(8,128)S(1)}) custom-call(s32[2]{0:T(128)S(1)} %pad_add_fusion.ids_ref, f32[2]{0:T(128)S(1)} %copy-done.15, bf16[8,1,48,4096]{3,2,1,0:T(8,128)(2,1)} %refs_0_.5, bf16[2,1,48,4096]{3,2,1,0:T(8,128)(2,1)} %collective-permute-done.refs_0_.refs_1_, ...), custom_call_target="tpu_custom_call" | custom-call | flops 1 | bytes 1 | tf_op jit(solution)/shard_map/pixel_grads/pallas_call | solution.py:632
  105.0 3.6 %all-to-all-start.3 = ((bf16[8,32,768]{2,1,0:T(8,128)(2,1)}), bf16[8,32,768]{2,1,0:T(8,128)(2,1)S(1)}, u32[]{:S(2)}, u32[]{:S(2)}) async-start(bf16[8,32,768]{2,1,0:T(8,128)(2,1)} %get-tuple-element.69), calls=%async_computation.3 | async-start | bytes 786432 | tf_op jit(solution)/shard_map/all_to_all | solution.py:829
  111.7 4.7 %unpack.3.pq_ref = bf16[32,96,512]{2,1,0:T(8,128)(2,1)S(1)} custom-call(s32[2]{0:T(128)S(1)} %pad_add_fusion.ids_ref, bf16[48,3200]{1,0:T(8,128)(2,1)S(1)} %copy-done.5, bf16[48,3200]{1,0:T(8,128)(2,1)} %collective-permute-done.3.w1, bf16[48,3200]{1,0:T(8,128)(2,1)} %collective-permute-done.4.w2, bf16[48,3200]{1,0:T(8,128)(2,1)} %collective-permute-done.5.w3), custom_call_target="tpu_custom_call" | custom-call | flops 1 | bytes 1 | tf_op jit(solution)/shard_map/unpack/pallas_call | solution.py:232
  116.5 4.4 %all-to-all-done.3.g_ref = bf16[8,32,768]{2,1,0:T(8,128)(2,1)S(1)} async-done(((bf16[8,32,768]{2,1,0:T(8,128)(2,1)}), bf16[8,32,768]{2,1,0:T(8,128)(2,1)S(1)}, u32[]{:S(2)}, u32[]{:S(2)}) %all-to-all-start.3) | async-done | bytes 393248 | tf_op jit(solution)/shard_map/all_to_all | solution.py:829
  120.9 3.9 %mix_back.1 = bf16[8,32,768]{2,1,0:T(8,128)(2,1)} custom-call(s32[2]{0:T(128)S(1)} %pad_add_fusion.ids_ref, bf16[8,32,768]{2,1,0:T(8,128)(2,1)S(1)} %all-to-all-done.3.g_ref, bf16[32,96,512]{2,1,0:T(8,128)(2,1)S(1)} %unpack.3.pq_ref), custom_call_target="tpu_custom_call" | custom-call | flops 1 | bytes 1 | tf_op jit(solution)/shard_map/mix_back/pallas_call | solution.py:428
  124.8 3.5 %all-to-all-start.4 = ((bf16[8,32,768]{2,1,0:T(8,128)(2,1)}), bf16[8,32,768]{2,1,0:T(8,128)(2,1)S(1)}, u32[]{:S(2)}, u32[]{:S(2)}) async-start(bf16[8,32,768]{2,1,0:T(8,128)(2,1)} %mix_back.1), calls=%async_computation.4 | async-start | bytes 786432 | tf_op jit(solution)/shard_map/all_to_all | solution.py:829
  129.2 6.8 %weight_grads.1 = (bf16[48,3200]{1,0:T(8,128)(2,1)}, bf16[48,3200]{1,0:T(8,128)(2,1)}, bf16[48,3200]{1,0:T(8,128)(2,1)}, bf16[48,3200]{1,0:T(8,128)(2,1)}) custom-call(s32[2]{0:T(128)S(1)} %pad_add_fusion.ids_ref, bf16[8,32,384]{2,1,0:T(8,128)(2,1)} %all-to-all-done.xa, bf16[8,32,384]{2,1,0:T(8,128)(2,1)} %all-to-all-done.1.xb, ...), custom_call_target="tpu_custom_call" | custom-call | flops 1 | bytes 1 | tf_op jit(solution)/shard_map/weight_grads/pallas_call | solution.py:492
  141.7 6.6 %inner_grads.1 = (f32[8,1,48,4096]{3,2,1,0:T(8,128)}, bf16[2,1,48,4096]{3,2,1,0:T(8,128)(2,1)}, bf16[2,1,48,4096]{3,2,1,0:T(8,128)(2,1)}, bf16[2,1,48,4096]{3,2,1,0:T(8,128)(2,1)}) custom-call(s32[2]{0:T(128)S(1)} %pad_add_fusion.ids_ref, f32[2]{0:T(128)S(1)} %copy-done.16, bf16[8,32,768]{2,1,0:T(8,128)(2,1)S(1)} %all-to-all-done.4.y_ref, ...), custom_call_target="tpu_custom_call" | custom-call | flops 1 | bytes 1 | tf_op jit(solution)/shard_map/inner_grads/pallas_call | solution.py:680
  151.9 6.1 %place.1 = bf16[8,1,48,4096]{3,2,1,0:T(8,128)(2,1)} custom-call(s32[2]{0:T(128)S(1)} %pad_add_fusion.ids_ref, bf16[2,1,48,4096]{3,2,1,0:T(8,128)(2,1)} %collective-permute-done.6.a_ref, bf16[2,1,48,4096]{3,2,1,0:T(8,128)(2,1)} %collective-permute-done.7.b_ref, ...), custom_call_target="tpu_custom_call", output_to_operand_aliasing={{}: (4, {})} | custom-call | flops 1 | bytes 1 | tf_op jit(solution)/shard_map/place/pallas_call | solution.py:720
  158.0 10.1 %collective-permute-done.16.d2 = bf16[48,3200]{1,0:T(8,128)(2,1)S(1)} collective-permute-done((bf16[48,3200]{1,0:T(8,128)(2,1)}, bf16[48,3200]{1,0:T(8,128)(2,1)S(1)}, u32[]{:S(2)}, u32[]{:S(2)}) %collective-permute-start.16) | collective-permute-done | bytes 307232 | tf_op jit(solution)/shard_map/ppermute | solution.py:825
  175.8 5.6 %adam.1 = (f32[1,32,2,48,48]{4,3,2,1,0:T(8,128)}, f32[1,32,2,48,48]{4,3,2,1,0:T(8,128)}, f32[1,32,2,48,48]{4,3,2,1,0:T(8,128)}) custom-call(f32[4]{0:T(128)S(1)} %pad_maximum_fusion.1.flips, bf16[48,3200]{1,0:T(8,128)(2,1)S(1)} %copy-done.8, bf16[48,3200]{1,0:T(8,128)(2,1)S(1)} %collective-permute-done.15.d1, ...), custom_call_target="tpu_custom_call" | custom-call | flops 1 | bytes 1 | tf_op jit(solution)/shard_map/adam/pallas_call | solution.py:812
  187.0 2.8 %final.3 = f32[8,1,48,4096]{3,2,1,0:T(8,128)} custom-call(s32[2]{0:T(128)S(1)} %pad_add_fusion.ids_ref, f32[8]{0:T(128)S(1)} %copy-done.18, bf16[8,1,48,4096]{3,2,1,0:T(8,128)(2,1)S(1)} %copy-done.1, bf16[2,1,48,4096]{3,2,1,0:T(8,128)(2,1)S(1)} %collective-permute-done.12.refs_0_, ...), custom_call_target="tpu_custom_call", output_to_operand_aliasing={{}: (5, {})} | custom-call | flops 1 | bytes 1 | tf_op jit(solution)/shard_map/final/pallas_call | solution.py:769
  (107 shorter events, 48.2 us)
Async XLA Ops:
  2.7 22.6 %collective-permute-start.2 = (bf16[2,1,48,4096]{3,2,1,0:T(8,128)(2,1)}, bf16[2,1,48,4096]{3,2,1,0:T(8,128)(2,1)}, u32[]{:S(2)}, u32[]{:S(2)}) collective-permute-start(bf16[2,1,48,4096]{3,2,1,0:T(8,128)(2,1)} %constant_dynamic-slice_fusion.5), channel_id=1, source_target_pairs={{0,24},{8,16},{16,8},{24,0},{1,25},{9,17},{17,9},{25,1},{2,26},{10... | collective-permute-start | bytes 2359304 | tf_op jit(solution)/shard_map/ppermute | solution.py:825
  8.7 34.1 %collective-permute-start = (bf16[2,1,48,4096]{3,2,1,0:T(8,128)(2,1)}, bf16[2,1,48,4096]{3,2,1,0:T(8,128)(2,1)}, u32[]{:S(2)}, u32[]{:S(2)}) collective-permute-start(bf16[2,1,48,4096]{3,2,1,0:T(8,128)(2,1)} %constant_dynamic-slice_fusion.4), channel_id=1, source_target_pairs={{0,8},{8,0},{16,24},{24,16},{1,9},{9,1},{17,25},{25,17},{2,10},{10... | collective-permute-start | bytes 2359304 | tf_op jit(solution)/shard_map/ppermute | solution.py:825
  13.3 29.4 %collective-permute-start.1 = (bf16[2,1,48,4096]{3,2,1,0:T(8,128)(2,1)}, bf16[2,1,48,4096]{3,2,1,0:T(8,128)(2,1)}, u32[]{:S(2)}, u32[]{:S(2)}) collective-permute-start(bf16[2,1,48,4096]{3,2,1,0:T(8,128)(2,1)} %constant_dynamic-slice_fusion.3), channel_id=1, source_target_pairs={{0,16},{8,24},{16,0},{24,8},{1,17},{9,25},{17,1},{25,9},{2,18},{10... | collective-permute-start | bytes 2359304 | tf_op jit(solution)/shard_map/ppermute | solution.py:825
  29.5 17.4 %all-to-all-start = ((bf16[8,32,384]{2,1,0:T(8,128)(2,1)}), bf16[8,32,384]{2,1,0:T(8,128)(2,1)}, u32[]{:S(2)}, u32[]{:S(2)}) async-start(bf16[8,32,384]{2,1,0:T(8,128)(2,1)} %forward.2), calls=%async_computation | async-start | bytes 393216 | tf_op jit(solution)/shard_map/all_to_all | solution.py:829
  34.9 20.4 %collective-permute-start.3 = (bf16[48,3200]{1,0:T(8,128)(2,1)S(1)}, bf16[48,3200]{1,0:T(8,128)(2,1)}, u32[]{:S(2)}, u32[]{:S(2)}) collective-permute-start(bf16[48,3200]{1,0:T(8,128)(2,1)S(1)} %pack.1.w0), channel_id=1, source_target_pairs={{0,8},{8,0},{16,24},{24,16},{1,9},{9,1},{17,25},{25,17},{2,10},{10... | collective-permute-start | bytes 921608 | tf_op jit(solution)/shard_map/ppermute | solution.py:825
  36.4 20.4 %collective-permute-start.4 = (bf16[48,3200]{1,0:T(8,128)(2,1)S(1)}, bf16[48,3200]{1,0:T(8,128)(2,1)}, u32[]{:S(2)}, u32[]{:S(2)}) collective-permute-start(bf16[48,3200]{1,0:T(8,128)(2,1)S(1)} %pack.1.w0), channel_id=1, source_target_pairs={{0,16},{8,24},{16,0},{24,8},{1,17},{9,25},{17,1},{25,9},{2,18},{10... | collective-permute-start | bytes 921608 | tf_op jit(solution)/shard_map/ppermute | solution.py:825
  37.9 18.9 %collective-permute-start.5 = (bf16[48,3200]{1,0:T(8,128)(2,1)S(1)}, bf16[48,3200]{1,0:T(8,128)(2,1)}, u32[]{:S(2)}, u32[]{:S(2)}) collective-permute-start(bf16[48,3200]{1,0:T(8,128)(2,1)S(1)} %pack.1.w0), channel_id=1, source_target_pairs={{0,24},{8,16},{16,8},{24,0},{1,25},{9,17},{17,9},{25,1},{2,26},{10... | collective-permute-start | bytes 921608 | tf_op jit(solution)/shard_map/ppermute | solution.py:825
  46.9 15.6 %all-to-all-start.1 = ((bf16[8,32,384]{2,1,0:T(8,128)(2,1)}), bf16[8,32,384]{2,1,0:T(8,128)(2,1)}, u32[]{:S(2)}, u32[]{:S(2)}) async-start(bf16[8,32,384]{2,1,0:T(8,128)(2,1)} %forward.3), calls=%async_computation.1 | async-start | bytes 393216 | tf_op jit(solution)/shard_map/all_to_all | solution.py:829
  53.3 42.1 %collective-permute-start.8 = (bf16[2,1,48,4096]{3,2,1,0:T(8,128)(2,1)}, bf16[2,1,48,4096]{3,2,1,0:T(8,128)(2,1)}, u32[]{:S(2)}, u32[]{:S(2)}) collective-permute-start(bf16[2,1,48,4096]{3,2,1,0:T(8,128)(2,1)} %get-tuple-element.59), channel_id=1, source_target_pairs={{0,8},{8,0},{16,24},{24,16},{1,9},{9,1},{17,25},{25,17},{2,10},{10... | collective-permute-start | bytes 2359304 | tf_op jit(solution)/shard_map/ppermute | solution.py:825
  54.8 40.6 %collective-permute-start.9 = (bf16[2,1,48,4096]{3,2,1,0:T(8,128)(2,1)}, bf16[2,1,48,4096]{3,2,1,0:T(8,128)(2,1)}, u32[]{:S(2)}, u32[]{:S(2)}) collective-permute-start(bf16[2,1,48,4096]{3,2,1,0:T(8,128)(2,1)} %get-tuple-element.60), channel_id=1, source_target_pairs={{0,16},{8,24},{16,0},{24,8},{1,17},{9,25},{17,1},{25,9},{2,18},{10... | collective-permute-start | bytes 2359304 | tf_op jit(solution)/shard_map/ppermute | solution.py:825
  55.3 40.1 %collective-permute-start.10 = (bf16[2,1,48,4096]{3,2,1,0:T(8,128)(2,1)}, bf16[2,1,48,4096]{3,2,1,0:T(8,128)(2,1)}, u32[]{:S(2)}, u32[]{:S(2)}) collective-permute-start(bf16[2,1,48,4096]{3,2,1,0:T(8,128)(2,1)} %get-tuple-element.61), channel_id=1, source_target_pairs={{0,24},{8,16},{16,8},{24,0},{1,25},{9,17},{17,9},{25,1},{2,26},{10... | collective-permute-start | bytes 2359304 | tf_op jit(solution)/shard_map/ppermute | solution.py:825
  95.4 25.5 %collective-permute-start.11 = (bf16[2,1,48,4096]{3,2,1,0:T(8,128)(2,1)}, bf16[2,1,48,4096]{3,2,1,0:T(8,128)(2,1)}, u32[]{:S(2)}, u32[]{:S(2)}) collective-permute-start(bf16[2,1,48,4096]{3,2,1,0:T(8,128)(2,1)} %get-tuple-element.62), channel_id=1, source_target_pairs={{0,24},{8,16},{16,8},{24,0},{1,25},{9,17},{17,9},{25,1},{2,26},{10... | collective-permute-start | bytes 2359304 | tf_op jit(solution)/shard_map/ppermute | solution.py:825
  105.0 15.9 %all-to-all-start.3 = ((bf16[8,32,768]{2,1,0:T(8,128)(2,1)}), bf16[8,32,768]{2,1,0:T(8,128)(2,1)S(1)}, u32[]{:S(2)}, u32[]{:S(2)}) async-start(bf16[8,32,768]{2,1,0:T(8,128)(2,1)} %get-tuple-element.69), calls=%async_computation.3 | async-start | bytes 786432 | tf_op jit(solution)/shard_map/all_to_all | solution.py:829
  108.6 39.7 %collective-permute-start.6 = (bf16[2,1,48,4096]{3,2,1,0:T(8,128)(2,1)}, bf16[2,1,48,4096]{3,2,1,0:T(8,128)(2,1)}, u32[]{:S(2)}, u32[]{:S(2)}) collective-permute-start(bf16[2,1,48,4096]{3,2,1,0:T(8,128)(2,1)} %get-tuple-element.56), channel_id=1, source_target_pairs={{0,8},{8,0},{16,24},{24,16},{1,9},{9,1},{17,25},{25,17},{2,10},{10... | collective-permute-start | bytes 2359304 | tf_op jit(solution)/shard_map/ppermute | solution.py:825
  109.2 39.1 %collective-permute-start.7 = (bf16[2,1,48,4096]{3,2,1,0:T(8,128)(2,1)}, bf16[2,1,48,4096]{3,2,1,0:T(8,128)(2,1)}, u32[]{:S(2)}, u32[]{:S(2)}) collective-permute-start(bf16[2,1,48,4096]{3,2,1,0:T(8,128)(2,1)} %get-tuple-element.57), channel_id=1, source_target_pairs={{0,16},{8,24},{16,0},{24,8},{1,17},{9,25},{17,1},{25,9},{2,18},{10... | collective-permute-start | bytes 2359304 | tf_op jit(solution)/shard_map/ppermute | solution.py:825
  124.8 15.9 %all-to-all-start.4 = ((bf16[8,32,768]{2,1,0:T(8,128)(2,1)}), bf16[8,32,768]{2,1,0:T(8,128)(2,1)S(1)}, u32[]{:S(2)}, u32[]{:S(2)}) async-start(bf16[8,32,768]{2,1,0:T(8,128)(2,1)} %mix_back.1), calls=%async_computation.4 | async-start | bytes 786432 | tf_op jit(solution)/shard_map/all_to_all | solution.py:829
  136.0 15.4 %collective-permute-start.15 = (bf16[48,3200]{1,0:T(8,128)(2,1)}, bf16[48,3200]{1,0:T(8,128)(2,1)S(1)}, u32[]{:S(2)}, u32[]{:S(2)}) collective-permute-start(bf16[48,3200]{1,0:T(8,128)(2,1)} %get-tuple-element.84), channel_id=1, source_target_pairs={{0,8},{8,0},{16,24},{24,16},{1,9},{9,1},{17,25},{25,17},{2,10},{10... | collective-permute-start | bytes 921608 | tf_op jit(solution)/shard_map/ppermute | solution.py:825
  136.5 31.6 %collective-permute-start.16 = (bf16[48,3200]{1,0:T(8,128)(2,1)}, bf16[48,3200]{1,0:T(8,128)(2,1)S(1)}, u32[]{:S(2)}, u32[]{:S(2)}) collective-permute-start(bf16[48,3200]{1,0:T(8,128)(2,1)} %get-tuple-element.85), channel_id=1, source_target_pairs={{0,16},{8,24},{16,0},{24,8},{1,17},{9,25},{17,1},{25,9},{2,18},{10... | collective-permute-start | bytes 921608 | tf_op jit(solution)/shard_map/ppermute | solution.py:825
  138.1 30.0 %collective-permute-start.17 = (bf16[48,3200]{1,0:T(8,128)(2,1)}, bf16[48,3200]{1,0:T(8,128)(2,1)S(1)}, u32[]{:S(2)}, u32[]{:S(2)}) collective-permute-start(bf16[48,3200]{1,0:T(8,128)(2,1)} %get-tuple-element.86), channel_id=1, source_target_pairs={{0,24},{8,16},{16,8},{24,0},{1,25},{9,17},{17,9},{25,1},{2,26},{10... | collective-permute-start | bytes 921608 | tf_op jit(solution)/shard_map/ppermute | solution.py:825
  148.3 33.8 %collective-permute-start.14 = (bf16[2,1,48,4096]{3,2,1,0:T(8,128)(2,1)}, bf16[2,1,48,4096]{3,2,1,0:T(8,128)(2,1)S(1)}, u32[]{:S(2)}, u32[]{:S(2)}) collective-permute-start(bf16[2,1,48,4096]{3,2,1,0:T(8,128)(2,1)} %get-tuple-element.81), channel_id=1, source_target_pairs={{0,24},{8,16},{16,8},{24,0},{1,25},{9,17},{17,9},{25,1},{2,26},{10... | collective-permute-start | bytes 2359304 | tf_op jit(solution)/shard_map/ppermute | solution.py:825
  149.9 36.2 %collective-permute-start.12 = (bf16[2,1,48,4096]{3,2,1,0:T(8,128)(2,1)}, bf16[2,1,48,4096]{3,2,1,0:T(8,128)(2,1)S(1)}, u32[]{:S(2)}, u32[]{:S(2)}) collective-permute-start(bf16[2,1,48,4096]{3,2,1,0:T(8,128)(2,1)} %get-tuple-element.79), channel_id=1, source_target_pairs={{0,8},{8,0},{16,24},{24,16},{1,9},{9,1},{17,25},{25,17},{2,10},{10... | collective-permute-start | bytes 2359304 | tf_op jit(solution)/shard_map/ppermute | solution.py:825
  151.3 35.7 %collective-permute-start.13 = (bf16[2,1,48,4096]{3,2,1,0:T(8,128)(2,1)}, bf16[2,1,48,4096]{3,2,1,0:T(8,128)(2,1)S(1)}, u32[]{:S(2)}, u32[]{:S(2)}) collective-permute-start(bf16[2,1,48,4096]{3,2,1,0:T(8,128)(2,1)} %get-tuple-element.80), channel_id=1, source_target_pairs={{0,16},{8,24},{16,0},{24,8},{1,17},{9,25},{17,1},{25,9},{2,18},{10... | collective-permute-start | bytes 2359304 | tf_op jit(solution)/shard_map/ppermute | solution.py:825
  169.4 3.8 %collective-permute-start.19 = (f32[48,48]{1,0:T(8,128)S(1)}, f32[48,48]{1,0:T(8,128)S(1)}, u32[]{:S(2)}, u32[]{:S(2)}) collective-permute-start(f32[48,48]{1,0:T(8,128)S(1)} %add.171), channel_id=1, source_target_pairs={{0,2},{1,3},{2,0},{3,1},{4,6},{5,7},{6,4},{7,5},{8,10},{9,11},{10,... | collective-permute-start | bytes 27656 | tf_op jit(solution)/shard_map/ppermute | solution.py:825
  173.2 8.2 %collective-permute-start.20 = (f32[48,48]{1,0:T(8,128)S(1)}, f32[48,48]{1,0:T(8,128)S(1)}, u32[]{:S(2)}, u32[]{:S(2)}) collective-permute-start(f32[48,48]{1,0:T(8,128)S(1)} %add.172), channel_id=1, source_target_pairs={{0,4},{1,5},{2,6},{3,7},{4,0},{5,1},{6,2},{7,3},{8,12},{9,13},{10,... | collective-permute-start | bytes 27656 | tf_op jit(solution)/shard_map/ppermute | solution.py:825
  (24 other events, 340.2 us)

commit v6 on v5

--- a/solution.py
+++ b/solution.py
@@ -238,7 +238,7 @@
         compiler_params=params(28),
         cost_estimate=cost(),
         name="unpack",
-    )(ids, *packs)
+    )(*stay(ids, *packs))
     return result if lines else result[0]
 
 
@@ -248,6 +248,9 @@
         for r in range(2):
             row = acc[n * C : (n + 1) * C, r * MODES : (r + 1) * MODES]
             rows.append(row if scales is None else row * scales[n])
+    extra = out_ref.shape[2] - len(rows) * C
+    if extra:
+        rows.append(jnp.zeros((extra, MODES), F32))
     turned = jnp.concatenate(rows, axis=0).T
     out_ref[...] = turned.reshape(out_ref.shape).astype(BF16)
 
@@ -286,7 +289,7 @@
 def forward_spectrum(ids, inv, x, small, shards):
     samples = inv.shape[0]
     modes = MODES // shards
-    width = samples * len(x) * LANES
+    width = -(-samples * len(x) * LANES // PACK) * PACK
     n = 2 * MODES
     tile = 2048
 
@@ -308,7 +311,7 @@
         compiler_params=params(28),
         cost_estimate=cost(),
         name="forward",
-    )(ids, inv, *stay(*x), *stay(small, small))
+    )(*stay(ids, inv, *x, small, small))
 
 
 def row_scratch(modes, shards, width):
@@ -334,32 +337,40 @@
             out[x, :, n * PACK : (n + 1) * PACK] = piece.astype(BF16)
 
 
-def blade_rows(sc, mode, shards, order):
+def blade_rows(sc, mode, shards, groups):
     at = pl.ds(pl.multiple_of(mode * shards, shards), shards)
     found = [[] for _ in range(4)]
-    for n in range(0, len(order), 4):
-        tile = n // 4 * 3
-        pieces = split_lanes(sc[tile, at, :], sc[tile + 1, at, :], sc[tile + 2, at, :])
-        for piece, (_, t) in zip(pieces, order[n : n + 4]):
+    for tile, pairs in groups:
+        tiles = [sc[tile + n, at, :] for n in range(-(-len(pairs) * LANES // PACK))]
+        pieces = split_lanes(tiles[0], tiles[min(1, len(tiles) - 1)], tiles[-1])
+        for piece, (_, t) in zip(pieces, pairs):
             found[t].append(piece)
     return [jnp.concatenate(found[t], axis=0) for t in range(4)]
 
 
-def split_order(samples):
-    return [(s, t) for pair in ((0, 3), (1, 2)) for s in range(samples) for t in pair]
-
-
-def plain_order(samples):
-    return [(s, t) for s in range(samples) for t in range(4)]
-
-
-def mix_modes(xsc, ysc, pq_ref, order, shards, first_mode, back):
+def groups_of(samples, *blades):
+    groups = []
+    tile = 0
+    for some in blades:
+        pairs = [(s, t) for s in range(samples) for t in some]
+        for n in range(0, len(pairs), 4):
+            part = pairs[n : n + 4]
+            groups.append((tile, part))
+            tile += -(-len(part) * LANES // PACK)
+    return groups
+
+
+EARLY = (0, 3)
+LATE = (1, 2)
+
+
+def mix_modes(xsc, ysc, pq_ref, groups, shards, first_mode, back):
     modes = xsc.shape[1] // shards
-    samples = len(order) // 4
+    samples = ysc.shape[0] // 3
     group = samples * shards
 
     def step(m, carry):
-        low = jnp.concatenate(blade_rows(xsc, m, shards, order), axis=0)
+        low = jnp.concatenate(blade_rows(xsc, m, shards, groups), axis=0)
         low = low[:, :LANES].astype(BF16)
         total = [None] * 4
         if not back:
@@ -394,32 +405,36 @@
 
 
 def mix_kernel(ids_ref, xa, xb, pq_ref, y_ref, xsc, ysc):
-    shards, modes, half = xa.shape
+    shards, modes, width = y_ref.shape
     gather_rows((xa, xb), xsc)
-    order = split_order(half // (2 * LANES))
-    mix_modes(xsc, ysc, pq_ref, order, shards, ids_ref[1] * modes, False)
+    groups = groups_of(width // (4 * LANES), EARLY, LATE)
+    mix_modes(xsc, ysc, pq_ref, groups, shards, ids_ref[1] * modes, False)
     scatter_rows(ysc, y_ref)
 
 
-def mix(ids, xa, xb, pq):
-    shards, modes, half = xa.shape
+def mix(ids, xa, xb, pq, samples):
+    shards, modes = xa.shape[:2]
+    width = samples * 4 * LANES
     return pl.pallas_call(
         mix_kernel,
         in_specs=[pl.BlockSpec(memory_space=SMEM)] + in_vmem(3),
         out_specs=in_vmem(1)[0],
-        out_shape=slow((shards, modes, 2 * half), BF16),
-        scratch_shapes=[row_scratch(modes, shards, 2 * half)] * 2,
+        out_shape=slow((shards, modes, width), BF16),
+        scratch_shapes=[
+            row_scratch(modes, shards, xa.shape[2] + xb.shape[2]),
+            row_scratch(modes, shards, width),
+        ],
         compiler_params=params(28),
         cost_estimate=cost(),
         name="mix",
-    )(ids, xa, xb, *pin(pq))
+    )(*stay(ids), xa, xb, *pin(pq))
 
 
 def mix_back_kernel(ids_ref, g_ref, pq_ref, out_ref, gsc, ysc):
     shards, modes, width = g_ref.shape
     gather_rows((g_ref,), gsc)
-    order = plain_order(width // (4 * LANES))
-    mix_modes(gsc, ysc, pq_ref, order, shards, ids_ref[1] * modes, True)
+    groups = groups_of(width // (4 * LANES), range(4))
+    mix_modes(gsc, ysc, pq_ref, groups, shards, ids_ref[1] * modes, True)
     scatter_rows(ysc, out_ref)
 
 
@@ -434,15 +449,44 @@
         compiler_params=params(28),
         cost_estimate=cost(),
         name="mix_back",
-    )(ids, g, *pin(pq))
-
-
-def grad_kernel(ids_ref, xa, xb, g_ref, lin_ref, o0, o1, o2, o3, xsc, gsc, osc):
+    )(*stay(ids), g, *pin(pq))
+
+
+def turn_kernel(xa, xb, xt_ref, xsc):
+    shards, modes = xa.shape[:2]
+    samples = xt_ref.shape[2] // (8 * shards)
+    groups = groups_of(samples, EARLY, LATE)
+    gather_rows((xa, xb), xsc)
+
+    def step(m, carry):
+        x = blade_rows(xsc, m, shards, groups)
+        x = x + [pltpu.roll(rows, PACK - C, 1) for rows in x]
+        xt_ref[m] = jnp.concatenate(x, axis=0).T[:C].astype(BF16)
+        return carry
+
+    lax.fori_loop(0, modes, step, 0, unroll=4)
+
+
+def turn_modes(xa, xb, samples):
+    shards, modes = xa.shape[:2]
+    return pl.pallas_call(
+        turn_kernel,
+        in_specs=in_vmem(2),
+        out_specs=in_vmem(1)[0],
+        out_shape=slow((modes, C, 8 * samples * shards), BF16),
+        scratch_shapes=[row_scratch(modes, shards, xa.shape[2] + xb.shape[2])],
+        compiler_params=params(28),
+        cost_estimate=cost(),
+        name="turn_modes",
+    )(xa, xb)
+
+
+def grad_kernel(ids_ref, xt_ref, g_ref, lin_ref, o0, o1, o2, o3, gsc, osc):
     shards, modes, width = g_ref.shape
     samples = width // (4 * LANES)
     own = ids_ref[0]
     first_mode = ids_ref[1] * modes
-    gather_rows((xa, xb), xsc)
+    groups = groups_of(samples, range(4))
     gather_rows((g_ref,), gsc)
     lane = lanes_of((samples * shards, PACK))
 
@@ -450,12 +494,8 @@
         found = [[] for _ in range(4)]
         for q in range(QUAD):
             m = g * QUAD + q
-            x = blade_rows(xsc, m, shards, split_order(samples))
-            x = x + [pltpu.roll(rows, PACK - C, 1) for rows in x]
-            left = jnp.concatenate(x, axis=0)[:, :C].astype(BF16)
             factor = mode_factor(first_mode + m)
-            plain = blade_rows(gsc, m, shards, plain_order(samples))
-            plain = [rows * factor for rows in plain]
+            plain = [rows * factor for rows in blade_rows(gsc, m, shards, groups)]
             turned = [
                 jnp.where(lane < C, pltpu.roll(rows, PACK - C, 1), -pltpu.roll(rows, C, 1))
                 for rows in plain
@@ -469,7 +509,7 @@
                     for t in range(4):
                         rows.append((plus if sgn(t, k) > 0 else minus)[4 * r + (t ^ k)])
                 right.append(jnp.concatenate(rows, axis=0))
-            grad = dot(left, jnp.concatenate(right, axis=1), ((0,), (0,)))
+            grad = dot(xt_ref[m], jnp.concatenate(right, axis=1))
             for k in range(4):
                 found[k].append(grad[:, k * PACK : (k + 1) * PACK])
         for k in range(4):
@@ -478,7 +518,8 @@
                 osc[k, :, at] = tile.astype(BF16)
         return carry
 
-    lax.fori_loop(0, modes // QUAD, step, 0)
+    quads = modes // QUAD
+    lax.fori_loop(0, quads, step, 0, unroll=min(2, quads))
     for k in range(4):
         line = jnp.concatenate([lin_ref[k], jnp.zeros((C, PACK - C), F32)], axis=1)
         osc[k, :, modes * LANES :] = line.astype(BF16)
@@ -486,19 +527,19 @@
         out[...] = osc[jnp.bitwise_xor(own, t)]
 
 
-def weight_grads(ids, xa, xb, g, lin):
+def weight_grads(ids, xt, g, lin):
     shards, modes, width = g.shape
     shape = (C, modes * LANES + PACK)
     return pl.pallas_call(
         grad_kernel,
-        in_specs=[pl.BlockSpec(memory_space=SMEM)] + in_vmem(4),
+        in_specs=[pl.BlockSpec(memory_space=SMEM)] + in_vmem(3),
         out_specs=in_vmem(4),
         out_shape=[slow(shape, BF16)] * 4,
-        scratch_shapes=[row_scratch(modes, shards, width)] * 2 + [pltpu.VMEM((4,) + shape, BF16)],
+        scratch_shapes=[row_scratch(modes, shards, width), pltpu.VMEM((4,) + shape, BF16)],
         compiler_params=params(28),
         cost_estimate=cost(),
         name="weight_grads",
-    )(ids, xa, xb, g, lin)
+    )(*stay(ids, xt), g, *stay(lin))
 
 
 CDF_AT = 0.28
@@ -581,7 +622,7 @@
         compiler_params=params(28),
         cost_estimate=cost(),
         name="pixels",
-    )(ids, inv, *stay(*x), y, *stay(turned), *pin(lt))
+    )(*stay(ids, inv, *x), y, *stay(turned), *pin(lt))
 
 
 def slope_kernel(ids_ref, inv_ref, *refs):
@@ -643,12 +684,12 @@
         out_shape=[
             slow((rows, NPIX), BF16),
             slow(spectrum, BF16),
-            jax.ShapeDtypeStruct((4, C, C), F32),
+            slow((4, C, C), F32),
         ],
         compiler_params=params(28),
         cost_estimate=cost(),
         name="pixel_grads",
-    )(ids, inv, *stay(*x), *stay(*cot), *pin(slope), *stay(small, small))
+    )(*stay(ids, inv, *x, *cot), *pin(slope), *stay(small, small))
 
 
 def inner_kernel(ids_ref, inv_ref, y_ref, g_ref, row_ref, col_ref, lb_ref, cot_ref, mine_ref, *refs):
@@ -696,7 +737,7 @@
         compiler_params=params(28),
         cost_estimate=cost(),
         name="inner_grads",
-    )(ids, inv, y, *stay(g, small, small), lb, *stay(cotangent))
+    )(*stay(ids, inv), y, *stay(g, small, small, lb, cotangent))
 
 
 def place_kernel(ids_ref, a_ref, b_ref, c_ref, old_ref, out_ref):
@@ -876,12 +917,14 @@
     packs = [packed] + [swap(packed, "blade", 4, t) for t in (1, 2, 3)]
 
     x3 = after(x3, (packed, turned))
-    xa = to_modes(forward_spectrum(ids, inv, (inputs, x3), small, shards))
+    sent = forward_spectrum(ids, inv, (inputs, x3), small, shards)
+    x1, x2 = after((x1, x2), sent)
+    xa = to_modes(sent)
     blocks = after([cut(cotangent, t) for t in (1, 2, 3)], (x1, x2))
     cot = (cotangent,) + tuple(swap(blocks[t - 1], "blade", 4, t) for t in (1, 2, 3))
     xb = to_modes(forward_spectrum(ids, inv, (x1, x2), small, shards))
     pq, lt, lb = unpack(ids, packs, True)
-    y = to_modes(mix(ids, xa, xb, pq))
+    y = to_modes(mix(ids, xa, xb, pq, samples))
 
     x = (inputs, x1, x2, x3)
     result = pixels(ids, inv, x, y, turned, lt)
@@ -891,10 +934,11 @@
     out_parts = [swap(parts[t - 1], "blade", 4, t) for t in (1, 2, 3)]
 
     grad_pre, sent, lin = pixel_grads(ids, inv, x, cot, slope, small, y.shape)
-    g = after(to_modes(sent), out_parts[2])
+    xt = turn_modes(after(xa, lin), xb, samples)
+    g = after(to_modes(sent), (out_parts[2], xt))
     mixed = mix_back(ids, g, unpack(after(ids, lin), packs, False))
     back = to_modes(mixed)
-    spec_grads = weight_grads(ids, xa, xb, g, lin)
+    spec_grads = weight_grads(ids, xt, g, lin)
     spec_grads = [spec_grads[0]] + [swap(spec_grads[t], "blade", 4, t) for t in (1, 2, 3)]
 
     inner = inner_grads(ids, inv, back, grad_pre, small, lb, cotangent)

time: 191 us -> 189 us (0.990)
  waiting for transfers between devices: 31 us -> 17.2 us
  starting transfers between devices: 43.7 us -> 55.1 us
  local copies, waits for them, and re-layouts: 12.4 us -> 8.43 us
  Pallas kernels: 81.2 us -> 84.7 us
    ppermute x21, waiting for transfers between devices: 25.3 us -> 11.9 us  [swap(): return lax.ppermute(value, axis, [(i, i ^ x) for i in range(size)])]
    ppermute x21, starting transfers between devices: 26.3 us -> 37.4 us  [swap(): return lax.ppermute(value, axis, [(i, i ^ x) for i in range(size)])]
    unnamed x46 -> x30, local copies, waits for them, and re-layouts: 4.61 us -> 0.06 us
    pallas_call x0 -> x1, Pallas kernels: none -> 4.29 us  [turn_modes(): pl.pallas_call(turn_kernel, in_specs=in_vmem(2), out_specs=in_vmem(1)[0],...]
    pallas_call x1, Pallas kernels: 6.78 us -> 4.84 us  [weight_grads(): pl.pallas_call(grad_kernel, in_specs=[pl.BlockSpec(memory_space=SMEM)] +...]
  transfers between devices with their start and end apart: 25 -> 25, of which waited for: 9 -> 8; matrix products, arithmetic and copies ran while one was open for 5% -> 5% of each run, Pallas kernels for 41% -> 44%
where the time goes in v6:
time: 189 us; the launch traced here: 187 us
  Pallas kernels  84.7 us (45%)
  starting transfers between devices  55.1 us (29%)
  blocking collectives  17.6 us (9%)
  waiting for transfers between devices  17.2 us (9%)
  local copies, waits for them, and re-layouts  8.43 us (4%)
  other arithmetic  3.44 us (2%)
    ppermute x21, starting transfers between devices, swap(): return lax.ppermute(value, axis, [(i, i ^ x) for i in range(size)])  37.4 us
    all_to_all x4, starting transfers between devices, to_modes(): return lax.all_to_all(value, 'dp', split_axis=0, concat_axis=0, tiled=True)  17.7 us
    all_to_all x1, blocking collectives, to_modes(): return lax.all_to_all(value, 'dp', split_axis=0, concat_axis=0, tiled=True)  17.6 us
    pallas_call x1, Pallas kernels, pixels(): pl.pallas_call(pixel_kernel, grid_spec=pltpu.PrefetchScalarGridSpec(num_s...  12 us
    ppermute x21, waiting for transfers between devices, swap(): return lax.ppermute(value, axis, [(i, i ^ x) for i in range(size)])  11.9 us
    pallas_call x2, Pallas kernels, unpack(): pl.pallas_call(unpack_kernel, in_specs=[pl.BlockSpec(memory_space=SMEM)]...  10.6 us
    pallas_call x2, Pallas kernels, forward_spectrum(): pl.pallas_call(forward_kernel, grid_spec=pltpu.PrefetchScalarGridSpec(num...  8.63 us
    dynamic_slice x4, local copies, waits for them, and re-layouts, cut(): lax.dynamic_slice_in_dim(array, jnp.bitwise_xor(own, t) * samples, sample...  7.78 us
  transfers between devices with their start and end apart: 25, of which 8 were waited for; matrix products, arithmetic and copies ran while one was open for 5% of the time, Pallas kernels for 44%

profile of v6, /device:TPU:0, one launch (start us, length us, event | category | flops | bytes accessed | tf_op | source)
XLA Modules:
  0.0 187.3 jit_solution(12923498871360952298)
XLA Ops:
  2.7 3.9 %collective-permute-start.2 = (bf16[2,1,48,4096]{3,2,1,0:T(8,128)(2,1)}, bf16[2,1,48,4096]{3,2,1,0:T(8,128)(2,1)}, u32[]{:S(2)}, u32[]{:S(2)}) collective-permute-start(bf16[2,1,48,4096]{3,2,1,0:T(8,128)(2,1)} %constant_dynamic-slice_fusion.5), channel_id=1, source_target_pairs={{0,24},{8,16},{16,8},{24,0},{1,25},{9,17},{17,9},{25,1},{2,26},{10... | collective-permute-start | bytes 2359304 | tf_op jit(solution)/shard_map/ppermute | solution.py:866
  13.4 5.9 %turned.1.refs_5_ = bf16[512,4096]{1,0:T(8,128)(2,1)} custom-call(f32[4,64,512]{2,1,0:T(8,128)} %pad_maximum_fusion.row_ref.col_ref.refs_2_.refs_3_.refs_9_.refs_10_, f32[4,64,512]{2,1,0:T(8,128)} %pad_maximum_fusion.row_ref.col_ref.refs_2_.refs_3_.refs_9_.refs_10_), custom_call_target="tpu_custom_call" | custom-call | flops 1 | bytes 1 | tf_op jit(solution)/shard_map/turned/pallas_call | solution.py:126
  21.4 3.9 %collective-permute-done.2.refs_1_.refs_3_ = bf16[2,1,48,4096]{3,2,1,0:T(8,128)(2,1)} collective-permute-done((bf16[2,1,48,4096]{3,2,1,0:T(8,128)(2,1)}, bf16[2,1,48,4096]{3,2,1,0:T(8,128)(2,1)}, u32[]{:S(2)}, u32[]{:S(2)}) %collective-permute-start.2) | collective-permute-done | bytes 786464 | tf_op jit(solution)/shard_map/ppermute | solution.py:866
  25.3 4.3 %forward.2 = bf16[8,32,384]{2,1,0:T(8,128)(2,1)} custom-call(s32[2]{0:T(128)} %pad_add_fusion.ids_ref, f32[2]{0:T(128)} %dynamic_slice.21.inv_ref, bf16[8,1,48,4096]{3,2,1,0:T(8,128)(2,1)} %refs_0_.5, bf16[2,1,48,4096]{3,2,1,0:T(8,128)(2,1)} %collective-permute-done.2.refs_1_.refs_3_, ...), custom_call_target="tpu_custom_call" | custom-call | flops 1 | bytes 1 | tf_op jit(solution)/shard_map/forward/pallas_call | solution.py:301
  29.7 5.4 %all-to-all-start = ((bf16[8,32,384]{2,1,0:T(8,128)(2,1)}), bf16[8,32,384]{2,1,0:T(8,128)(2,1)}, u32[]{:S(2)}, u32[]{:S(2)}) async-start(bf16[8,32,384]{2,1,0:T(8,128)(2,1)} %forward.2), calls=%async_computation | async-start | bytes 393216 | tf_op jit(solution)/shard_map/all_to_all | solution.py:870
  38.6 4.2 %collective-permute-done.refs_0_.refs_1_ = bf16[2,1,48,4096]{3,2,1,0:T(8,128)(2,1)} collective-permute-done((bf16[2,1,48,4096]{3,2,1,0:T(8,128)(2,1)}, bf16[2,1,48,4096]{3,2,1,0:T(8,128)(2,1)}, u32[]{:S(2)}, u32[]{:S(2)}) %collective-permute-start) | collective-permute-done | bytes 786464 | tf_op jit(solution)/shard_map/ppermute | solution.py:866
  42.8 4.3 %forward.3 = bf16[8,32,384]{2,1,0:T(8,128)(2,1)} custom-call(s32[2]{0:T(128)} %pad_add_fusion.ids_ref, f32[2]{0:T(128)} %dynamic_slice.21.inv_ref, bf16[2,1,48,4096]{3,2,1,0:T(8,128)(2,1)} %collective-permute-done.refs_0_.refs_1_, bf16[2,1,48,4096]{3,2,1,0:T(8,128)(2,1)} %collective-permute-done.1.refs_1_.refs_2_, ...), custom_call_target="tpu_custom_call" | custom-call | flops 1 | bytes 1 | tf_op jit(solution)/shard_map/forward/pallas_call | solution.py:301
  47.1 4.9 %all-to-all-start.1 = ((bf16[8,32,384]{2,1,0:T(8,128)(2,1)}), bf16[8,32,384]{2,1,0:T(8,128)(2,1)}, u32[]{:S(2)}, u32[]{:S(2)}) async-start(bf16[8,32,384]{2,1,0:T(8,128)(2,1)} %forward.3), calls=%async_computation.1 | async-start | bytes 393216 | tf_op jit(solution)/shard_map/all_to_all | solution.py:870
  56.9 5.8 %unpack.2 = (bf16[32,96,512]{2,1,0:T(8,128)(2,1)S(1)}, bf16[192,192]{1,0:T(8,128)(2,1)S(1)}, bf16[192,192]{1,0:T(8,128)(2,1)}) custom-call(s32[2]{0:T(128)} %pad_add_fusion.ids_ref, bf16[48,3200]{1,0:T(8,128)(2,1)} %copy-done.4, bf16[48,3200]{1,0:T(8,128)(2,1)} %collective-permute-done.3.w1, bf16[48,3200]{1,0:T(8,128)(2,1)} %collective-permute-done.4.w2, ...), custom_call_target="tpu_custom_call" | custom-call | flops 1 | bytes 1 | tf_op jit(solution)/shard_map/unpack/pallas_call | solution.py:232
  65.5 17.6 %all_to_all.25.refs_4_ = bf16[8,32,768]{2,1,0:T(8,128)(2,1)S(1)} all-to-all(bf16[8,32,768]{2,1,0:T(8,128)(2,1)} %mix.1), channel_id=1, replica_groups=mesh['blade'=4,'dp'=8] {'dp'}, dimensions={0} | all-to-all | bytes 786432 | tf_op jit(solution)/shard_map/all_to_all | solution.py:870
  83.1 12.0 %pixels.1 = (bf16[8,1,48,4096]{3,2,1,0:T(8,128)(2,1)}, bf16[2,1,48,4096]{3,2,1,0:T(8,128)(2,1)}, bf16[2,1,48,4096]{3,2,1,0:T(8,128)(2,1)}, bf16[2,1,48,4096]{3,2,1,0:T(8,128)(2,1)}, bf16[384,4096]{1,0:T(8,128)(2,1)S(1)}) custom-call(s32[2]{0:T(128)} %pad_add_fusion.ids_ref, f32[2]{0:T(128)} %dynamic_slice.21.inv_ref, bf16[8,1,48,4096]{3,2,1,0:T(8,128)(2,1)} %refs_0_.5, ...), custom_call_target="tpu_custom_call" | custom-call | flops 1 | bytes 1 | tf_op jit(solution)/shard_map/pixels/pallas_call | solution.py:600
  96.6 7.5 %pixel_grads.1 = (bf16[384,4096]{1,0:T(8,128)(2,1)}, bf16[8,32,768]{2,1,0:T(8,128)(2,1)}, f32[4,48,48]{2,1,0:T(8,128)}) custom-call(s32[2]{0:T(128)} %pad_add_fusion.ids_ref, f32[2]{0:T(128)} %dynamic_slice.21.inv_ref, bf16[8,1,48,4096]{3,2,1,0:T(8,128)(2,1)} %refs_0_.5, bf16[2,1,48,4096]{3,2,1,0:T(8,128)(2,1)} %collective-permute-done.refs_0_.refs_1_, ...), custom_call_target="tpu_custom_call" | custom-call | flops 1 | bytes 1 | tf_op jit(solution)/shard_map/pixel_grads/pallas_call | solution.py:673
  104.1 3.6 %all-to-all-start.3 = ((bf16[8,32,768]{2,1,0:T(8,128)(2,1)}), bf16[8,32,768]{2,1,0:T(8,128)(2,1)S(1)}, u32[]{:S(2)}, u32[]{:S(2)}) async-start(bf16[8,32,768]{2,1,0:T(8,128)(2,1)} %get-tuple-element.74), calls=%async_computation.3 | async-start | bytes 786432 | tf_op jit(solution)/shard_map/all_to_all | solution.py:870
  109.9 4.3 %turn_modes.1.xt_ref = bf16[32,48,128]{2,1,0:T(8,128)(2,1)} custom-call(bf16[8,32,384]{2,1,0:T(8,128)(2,1)} %all-to-all-done.xa, bf16[8,32,384]{2,1,0:T(8,128)(2,1)} %all-to-all-done.1.xb), custom_call_target="tpu_custom_call" | custom-call | flops 1 | bytes 1 | tf_op jit(solution)/shard_map/turn_modes/pallas_call | solution.py:472
  114.2 4.8 %unpack.3.pq_ref = bf16[32,96,512]{2,1,0:T(8,128)(2,1)S(1)} custom-call(s32[2]{0:T(128)} %pad_add_fusion.ids_ref, bf16[48,3200]{1,0:T(8,128)(2,1)} %copy-done.4, bf16[48,3200]{1,0:T(8,128)(2,1)} %collective-permute-done.3.w1, bf16[48,3200]{1,0:T(8,128)(2,1)} %collective-permute-done.4.w2, bf16[48,3200]{1,0:T(8,128)(2,1)} %collective-permute-done.5.w3), custom_call_target="tpu_custom_call" | custom-call | flops 1 | bytes 1 | tf_op jit(solution)/shard_map/unpack/pallas_call | solution.py:232
  120.1 4.1 %mix_back.1 = bf16[8,32,768]{2,1,0:T(8,128)(2,1)} custom-call(s32[2]{0:T(128)} %pad_add_fusion.ids_ref, bf16[8,32,768]{2,1,0:T(8,128)(2,1)S(1)} %all-to-all-done.3.g_ref, bf16[32,96,512]{2,1,0:T(8,128)(2,1)S(1)} %unpack.3.pq_ref), custom_call_target="tpu_custom_call" | custom-call | flops 1 | bytes 1 | tf_op jit(solution)/shard_map/mix_back/pallas_call | solution.py:443
  124.1 3.8 %all-to-all-start.4 = ((bf16[8,32,768]{2,1,0:T(8,128)(2,1)}), bf16[8,32,768]{2,1,0:T(8,128)(2,1)S(1)}, u32[]{:S(2)}, u32[]{:S(2)}) async-start(bf16[8,32,768]{2,1,0:T(8,128)(2,1)} %mix_back.1), calls=%async_computation.4 | async-start | bytes 786432 | tf_op jit(solution)/shard_map/all_to_all | solution.py:870
  127.9 4.8 %weight_grads.1 = (bf16[48,3200]{1,0:T(8,128)(2,1)}, bf16[48,3200]{1,0:T(8,128)(2,1)}, bf16[48,3200]{1,0:T(8,128)(2,1)}, bf16[48,3200]{1,0:T(8,128)(2,1)}) custom-call(s32[2]{0:T(128)} %pad_add_fusion.ids_ref, bf16[32,48,128]{2,1,0:T(8,128)(2,1)} %turn_modes.1.xt_ref, bf16[8,32,768]{2,1,0:T(8,128)(2,1)S(1)} %all-to-all-done.3.g_ref, ...), custom_call_target="tpu_custom_call" | custom-call | flops 1 | bytes 1 | tf_op jit(solution)/shard_map/weight_grads/pallas_call | solution.py:533
  136.3 4.2 %all-to-all-done.4.y_ref = bf16[8,32,768]{2,1,0:T(8,128)(2,1)S(1)} async-done(((bf16[8,32,768]{2,1,0:T(8,128)(2,1)}), bf16[8,32,768]{2,1,0:T(8,128)(2,1)S(1)}, u32[]{:S(2)}, u32[]{:S(2)}) %all-to-all-start.4) | async-done | bytes 393248 | tf_op jit(solution)/shard_map/all_to_all | solution.py:870
  140.5 6.9 %inner_grads.1 = (f32[8,1,48,4096]{3,2,1,0:T(8,128)}, bf16[2,1,48,4096]{3,2,1,0:T(8,128)(2,1)}, bf16[2,1,48,4096]{3,2,1,0:T(8,128)(2,1)}, bf16[2,1,48,4096]{3,2,1,0:T(8,128)(2,1)}) custom-call(s32[2]{0:T(128)} %pad_add_fusion.ids_ref, f32[2]{0:T(128)} %dynamic_slice.21.inv_ref, bf16[8,32,768]{2,1,0:T(8,128)(2,1)S(1)} %all-to-all-done.4.y_ref, ...), custom_call_target="tpu_custom_call" | custom-call | flops 1 | bytes 1 | tf_op jit(solution)/shard_map/inner_grads/pallas_call | solution.py:721
  151.0 6.1 %place.1 = bf16[8,1,48,4096]{3,2,1,0:T(8,128)(2,1)} custom-call(s32[2]{0:T(128)S(1)} %copy-done.10, bf16[2,1,48,4096]{3,2,1,0:T(8,128)(2,1)} %collective-permute-done.6.a_ref, bf16[2,1,48,4096]{3,2,1,0:T(8,128)(2,1)} %collective-permute-done.7.b_ref, bf16[2,1,48,4096]{3,2,1,0:T(8,128)(2,1)} %collective-permute-done.11.c_ref, ...), custom_call_target="tpu_custom_call", output_to_operand_aliasing={{}: (4, {})} | custom-call | flops 1 | bytes 1 | tf_op jit(solution)/shard_map/place/pallas_call | solution.py:761
  158.5 12.3 %collective-permute-start.19 = (f32[48,48]{1,0:T(8,128)S(1)}, f32[48,48]{1,0:T(8,128)S(1)}, u32[]{:S(2)}, u32[]{:S(2)}) collective-permute-start(f32[48,48]{1,0:T(8,128)S(1)} %add.171), channel_id=1, source_target_pairs={{0,2},{1,3},{2,0},{3,1},{4,6},{5,7},{6,4},{7,5},{8,10},{9,11},{10,... | collective-permute-start | bytes 27656 | tf_op jit(solution)/shard_map/ppermute | solution.py:866
  172.6 2.9 %collective-permute-start.20 = (f32[48,48]{1,0:T(8,128)S(1)}, f32[48,48]{1,0:T(8,128)S(1)}, u32[]{:S(2)}, u32[]{:S(2)}) collective-permute-start(f32[48,48]{1,0:T(8,128)S(1)} %add.172), channel_id=1, source_target_pairs={{0,4},{1,5},{2,6},{3,7},{4,0},{5,1},{6,2},{7,3},{8,12},{9,13},{10,... | collective-permute-start | bytes 27656 | tf_op jit(solution)/shard_map/ppermute | solution.py:866
  175.6 5.6 %adam.1 = (f32[1,32,2,48,48]{4,3,2,1,0:T(8,128)}, f32[1,32,2,48,48]{4,3,2,1,0:T(8,128)}, f32[1,32,2,48,48]{4,3,2,1,0:T(8,128)}) custom-call(f32[4]{0:T(128)S(1)} %pad_maximum_fusion.1.flips, bf16[48,3200]{1,0:T(8,128)(2,1)S(1)} %copy-done.7, bf16[48,3200]{1,0:T(8,128)(2,1)S(1)} %collective-permute-done.15.d1, ...), custom_call_target="tpu_custom_call" | custom-call | flops 1 | bytes 1 | tf_op jit(solution)/shard_map/adam/pallas_call | solution.py:853
  (92 shorter events, 43.1 us)
Async XLA Ops:
  2.7 22.6 %collective-permute-start.2 = (bf16[2,1,48,4096]{3,2,1,0:T(8,128)(2,1)}, bf16[2,1,48,4096]{3,2,1,0:T(8,128)(2,1)}, u32[]{:S(2)}, u32[]{:S(2)}) collective-permute-start(bf16[2,1,48,4096]{3,2,1,0:T(8,128)(2,1)} %constant_dynamic-slice_fusion.5), channel_id=1, source_target_pairs={{0,24},{8,16},{16,8},{24,0},{1,25},{9,17},{17,9},{25,1},{2,26},{10... | collective-permute-start | bytes 2359304 | tf_op jit(solution)/shard_map/ppermute | solution.py:866
  8.7 34.1 %collective-permute-start = (bf16[2,1,48,4096]{3,2,1,0:T(8,128)(2,1)}, bf16[2,1,48,4096]{3,2,1,0:T(8,128)(2,1)}, u32[]{:S(2)}, u32[]{:S(2)}) collective-permute-start(bf16[2,1,48,4096]{3,2,1,0:T(8,128)(2,1)} %constant_dynamic-slice_fusion.4), channel_id=1, source_target_pairs={{0,8},{8,0},{16,24},{24,16},{1,9},{9,1},{17,25},{25,17},{2,10},{10... | collective-permute-start | bytes 2359304 | tf_op jit(solution)/shard_map/ppermute | solution.py:866
  13.3 29.4 %collective-permute-start.1 = (bf16[2,1,48,4096]{3,2,1,0:T(8,128)(2,1)}, bf16[2,1,48,4096]{3,2,1,0:T(8,128)(2,1)}, u32[]{:S(2)}, u32[]{:S(2)}) collective-permute-start(bf16[2,1,48,4096]{3,2,1,0:T(8,128)(2,1)} %constant_dynamic-slice_fusion.3), channel_id=1, source_target_pairs={{0,16},{8,24},{16,0},{24,8},{1,17},{9,25},{17,1},{25,9},{2,18},{10... | collective-permute-start | bytes 2359304 | tf_op jit(solution)/shard_map/ppermute | solution.py:866
  29.7 17.4 %all-to-all-start = ((bf16[8,32,384]{2,1,0:T(8,128)(2,1)}), bf16[8,32,384]{2,1,0:T(8,128)(2,1)}, u32[]{:S(2)}, u32[]{:S(2)}) async-start(bf16[8,32,384]{2,1,0:T(8,128)(2,1)} %forward.2), calls=%async_computation | async-start | bytes 393216 | tf_op jit(solution)/shard_map/all_to_all | solution.py:870
  35.1 20.4 %collective-permute-start.3 = (bf16[48,3200]{1,0:T(8,128)(2,1)S(1)}, bf16[48,3200]{1,0:T(8,128)(2,1)}, u32[]{:S(2)}, u32[]{:S(2)}) collective-permute-start(bf16[48,3200]{1,0:T(8,128)(2,1)S(1)} %pack.1.w0), channel_id=1, source_target_pairs={{0,8},{8,0},{16,24},{24,16},{1,9},{9,1},{17,25},{25,17},{2,10},{10... | collective-permute-start | bytes 921608 | tf_op jit(solution)/shard_map/ppermute | solution.py:866
  36.5 20.4 %collective-permute-start.4 = (bf16[48,3200]{1,0:T(8,128)(2,1)S(1)}, bf16[48,3200]{1,0:T(8,128)(2,1)}, u32[]{:S(2)}, u32[]{:S(2)}) collective-permute-start(bf16[48,3200]{1,0:T(8,128)(2,1)S(1)} %pack.1.w0), channel_id=1, source_target_pairs={{0,16},{8,24},{16,0},{24,8},{1,17},{9,25},{17,1},{25,9},{2,18},{10... | collective-permute-start | bytes 921608 | tf_op jit(solution)/shard_map/ppermute | solution.py:866
  38.1 18.9 %collective-permute-start.5 = (bf16[48,3200]{1,0:T(8,128)(2,1)S(1)}, bf16[48,3200]{1,0:T(8,128)(2,1)}, u32[]{:S(2)}, u32[]{:S(2)}) collective-permute-start(bf16[48,3200]{1,0:T(8,128)(2,1)S(1)} %pack.1.w0), channel_id=1, source_target_pairs={{0,24},{8,16},{16,8},{24,0},{1,25},{9,17},{17,9},{25,1},{2,26},{10... | collective-permute-start | bytes 921608 | tf_op jit(solution)/shard_map/ppermute | solution.py:866
  47.1 15.6 %all-to-all-start.1 = ((bf16[8,32,384]{2,1,0:T(8,128)(2,1)}), bf16[8,32,384]{2,1,0:T(8,128)(2,1)}, u32[]{:S(2)}, u32[]{:S(2)}) async-start(bf16[8,32,384]{2,1,0:T(8,128)(2,1)} %forward.3), calls=%async_computation.1 | async-start | bytes 393216 | tf_op jit(solution)/shard_map/all_to_all | solution.py:870
  53.4 41.6 %collective-permute-start.8 = (bf16[2,1,48,4096]{3,2,1,0:T(8,128)(2,1)}, bf16[2,1,48,4096]{3,2,1,0:T(8,128)(2,1)}, u32[]{:S(2)}, u32[]{:S(2)}) collective-permute-start(bf16[2,1,48,4096]{3,2,1,0:T(8,128)(2,1)} %get-tuple-element.64), channel_id=1, source_target_pairs={{0,8},{8,0},{16,24},{24,16},{1,9},{9,1},{17,25},{25,17},{2,10},{10... | collective-permute-start | bytes 2359304 | tf_op jit(solution)/shard_map/ppermute | solution.py:866
  54.9 40.2 %collective-permute-start.9 = (bf16[2,1,48,4096]{3,2,1,0:T(8,128)(2,1)}, bf16[2,1,48,4096]{3,2,1,0:T(8,128)(2,1)}, u32[]{:S(2)}, u32[]{:S(2)}) collective-permute-start(bf16[2,1,48,4096]{3,2,1,0:T(8,128)(2,1)} %get-tuple-element.65), channel_id=1, source_target_pairs={{0,16},{8,24},{16,0},{24,8},{1,17},{9,25},{17,1},{25,9},{2,18},{10... | collective-permute-start | bytes 2359304 | tf_op jit(solution)/shard_map/ppermute | solution.py:866
  55.4 39.7 %collective-permute-start.10 = (bf16[2,1,48,4096]{3,2,1,0:T(8,128)(2,1)}, bf16[2,1,48,4096]{3,2,1,0:T(8,128)(2,1)}, u32[]{:S(2)}, u32[]{:S(2)}) collective-permute-start(bf16[2,1,48,4096]{3,2,1,0:T(8,128)(2,1)} %get-tuple-element.66), channel_id=1, source_target_pairs={{0,24},{8,16},{16,8},{24,0},{1,25},{9,17},{17,9},{25,1},{2,26},{10... | collective-permute-start | bytes 2359304 | tf_op jit(solution)/shard_map/ppermute | solution.py:866
  95.1 25.0 %collective-permute-start.11 = (bf16[2,1,48,4096]{3,2,1,0:T(8,128)(2,1)}, bf16[2,1,48,4096]{3,2,1,0:T(8,128)(2,1)}, u32[]{:S(2)}, u32[]{:S(2)}) collective-permute-start(bf16[2,1,48,4096]{3,2,1,0:T(8,128)(2,1)} %get-tuple-element.67), channel_id=1, source_target_pairs={{0,24},{8,16},{16,8},{24,0},{1,25},{9,17},{17,9},{25,1},{2,26},{10... | collective-permute-start | bytes 2359304 | tf_op jit(solution)/shard_map/ppermute | solution.py:866
  104.1 15.9 %all-to-all-start.3 = ((bf16[8,32,768]{2,1,0:T(8,128)(2,1)}), bf16[8,32,768]{2,1,0:T(8,128)(2,1)S(1)}, u32[]{:S(2)}, u32[]{:S(2)}) async-start(bf16[8,32,768]{2,1,0:T(8,128)(2,1)} %get-tuple-element.74), calls=%async_computation.3 | async-start | bytes 786432 | tf_op jit(solution)/shard_map/all_to_all | solution.py:870
  107.8 39.6 %collective-permute-start.6 = (bf16[2,1,48,4096]{3,2,1,0:T(8,128)(2,1)}, bf16[2,1,48,4096]{3,2,1,0:T(8,128)(2,1)}, u32[]{:S(2)}, u32[]{:S(2)}) collective-permute-start(bf16[2,1,48,4096]{3,2,1,0:T(8,128)(2,1)} %get-tuple-element.61), channel_id=1, source_target_pairs={{0,8},{8,0},{16,24},{24,16},{1,9},{9,1},{17,25},{25,17},{2,10},{10... | collective-permute-start | bytes 2359304 | tf_op jit(solution)/shard_map/ppermute | solution.py:866
  108.4 39.0 %collective-permute-start.7 = (bf16[2,1,48,4096]{3,2,1,0:T(8,128)(2,1)}, bf16[2,1,48,4096]{3,2,1,0:T(8,128)(2,1)}, u32[]{:S(2)}, u32[]{:S(2)}) collective-permute-start(bf16[2,1,48,4096]{3,2,1,0:T(8,128)(2,1)} %get-tuple-element.62), channel_id=1, source_target_pairs={{0,16},{8,24},{16,0},{24,8},{1,17},{9,25},{17,1},{25,9},{2,18},{10... | collective-permute-start | bytes 2359304 | tf_op jit(solution)/shard_map/ppermute | solution.py:866
  124.1 16.3 %all-to-all-start.4 = ((bf16[8,32,768]{2,1,0:T(8,128)(2,1)}), bf16[8,32,768]{2,1,0:T(8,128)(2,1)S(1)}, u32[]{:S(2)}, u32[]{:S(2)}) async-start(bf16[8,32,768]{2,1,0:T(8,128)(2,1)} %mix_back.1), calls=%async_computation.4 | async-start | bytes 786432 | tf_op jit(solution)/shard_map/all_to_all | solution.py:870
  132.8 17.3 %collective-permute-start.15 = (bf16[48,3200]{1,0:T(8,128)(2,1)}, bf16[48,3200]{1,0:T(8,128)(2,1)S(1)}, u32[]{:S(2)}, u32[]{:S(2)}) collective-permute-start(bf16[48,3200]{1,0:T(8,128)(2,1)} %get-tuple-element.90), channel_id=1, source_target_pairs={{0,8},{8,0},{16,24},{24,16},{1,9},{9,1},{17,25},{25,17},{2,10},{10... | collective-permute-start | bytes 921608 | tf_op jit(solution)/shard_map/ppermute | solution.py:866
  134.2 22.9 %collective-permute-start.16 = (bf16[48,3200]{1,0:T(8,128)(2,1)}, bf16[48,3200]{1,0:T(8,128)(2,1)S(1)}, u32[]{:S(2)}, u32[]{:S(2)}) collective-permute-start(bf16[48,3200]{1,0:T(8,128)(2,1)} %get-tuple-element.91), channel_id=1, source_target_pairs={{0,16},{8,24},{16,0},{24,8},{1,17},{9,25},{17,1},{25,9},{2,18},{10... | collective-permute-start | bytes 921608 | tf_op jit(solution)/shard_map/ppermute | solution.py:866
  134.8 22.4 %collective-permute-start.17 = (bf16[48,3200]{1,0:T(8,128)(2,1)}, bf16[48,3200]{1,0:T(8,128)(2,1)S(1)}, u32[]{:S(2)}, u32[]{:S(2)}) collective-permute-start(bf16[48,3200]{1,0:T(8,128)(2,1)} %get-tuple-element.92), channel_id=1, source_target_pairs={{0,24},{8,16},{16,8},{24,0},{1,25},{9,17},{17,9},{25,1},{2,26},{10... | collective-permute-start | bytes 921608 | tf_op jit(solution)/shard_map/ppermute | solution.py:866
  147.4 34.5 %collective-permute-start.14 = (bf16[2,1,48,4096]{3,2,1,0:T(8,128)(2,1)}, bf16[2,1,48,4096]{3,2,1,0:T(8,128)(2,1)S(1)}, u32[]{:S(2)}, u32[]{:S(2)}) collective-permute-start(bf16[2,1,48,4096]{3,2,1,0:T(8,128)(2,1)} %get-tuple-element.87), channel_id=1, source_target_pairs={{0,24},{8,16},{16,8},{24,0},{1,25},{9,17},{17,9},{25,1},{2,26},{10... | collective-permute-start | bytes 2359304 | tf_op jit(solution)/shard_map/ppermute | solution.py:866
  148.9 35.3 %collective-permute-start.12 = (bf16[2,1,48,4096]{3,2,1,0:T(8,128)(2,1)}, bf16[2,1,48,4096]{3,2,1,0:T(8,128)(2,1)S(1)}, u32[]{:S(2)}, u32[]{:S(2)}) collective-permute-start(bf16[2,1,48,4096]{3,2,1,0:T(8,128)(2,1)} %get-tuple-element.85), channel_id=1, source_target_pairs={{0,8},{8,0},{16,24},{24,16},{1,9},{9,1},{17,25},{25,17},{2,10},{10... | collective-permute-start | bytes 2359304 | tf_op jit(solution)/shard_map/ppermute | solution.py:866
  150.0 34.5 %collective-permute-start.13 = (bf16[2,1,48,4096]{3,2,1,0:T(8,128)(2,1)}, bf16[2,1,48,4096]{3,2,1,0:T(8,128)(2,1)S(1)}, u32[]{:S(2)}, u32[]{:S(2)}) collective-permute-start(bf16[2,1,48,4096]{3,2,1,0:T(8,128)(2,1)} %get-tuple-element.86), channel_id=1, source_target_pairs={{0,16},{8,24},{16,0},{24,8},{1,17},{9,25},{17,1},{25,9},{2,18},{10... | collective-permute-start | bytes 2359304 | tf_op jit(solution)/shard_map/ppermute | solution.py:866
  158.5 14.1 %collective-permute-start.19 = (f32[48,48]{1,0:T(8,128)S(1)}, f32[48,48]{1,0:T(8,128)S(1)}, u32[]{:S(2)}, u32[]{:S(2)}) collective-permute-start(f32[48,48]{1,0:T(8,128)S(1)} %add.171), channel_id=1, source_target_pairs={{0,2},{1,3},{2,0},{3,1},{4,6},{5,7},{6,4},{7,5},{8,10},{9,11},{10,... | collective-permute-start | bytes 27656 | tf_op jit(solution)/shard_map/ppermute | solution.py:866
  172.6 8.7 %collective-permute-start.20 = (f32[48,48]{1,0:T(8,128)S(1)}, f32[48,48]{1,0:T(8,128)S(1)}, u32[]{:S(2)}, u32[]{:S(2)}) collective-permute-start(f32[48,48]{1,0:T(8,128)S(1)} %add.172), channel_id=1, source_target_pairs={{0,4},{1,5},{2,6},{3,7},{4,0},{5,1},{6,2},{7,3},{8,12},{9,13},{10,... | collective-permute-start | bytes 27656 | tf_op jit(solution)/shard_map/ppermute | solution.py:866
  (16 other events, 276.3 us)

commit v7 on v6

--- a/solution.py
+++ b/solution.py
@@ -18,7 +18,6 @@
 LANES = 2 * C
 QUAD = 4
 PACK = 128
-ROWS = 16
 
 BETA_ONE = 0.9
 BETA_TWO = 0.999
@@ -233,7 +232,7 @@
         unpack_kernel,
         in_specs=[pl.BlockSpec(memory_space=SMEM)] + in_vmem(4),
         out_specs=in_vmem(3 if lines else 1),
-        out_shape=[weights] + ([fast(shape, BF16), slow(shape, BF16)] if lines else []),
+        out_shape=[weights] + ([slow(shape, BF16)] * 2 if lines else []),
         scratch_shapes=[pltpu.VMEM((4, C, PACK), F32)] if lines else [],
         compiler_params=params(28),
         cost_estimate=cost(),
@@ -373,13 +372,9 @@
         low = jnp.concatenate(blade_rows(xsc, m, shards, groups), axis=0)
         low = low[:, :LANES].astype(BF16)
         total = [None] * 4
-        if not back:
-            parts = dot(low, pq_ref[m])
+        parts = dot(low, pq_ref[m])
         for k in range(4):
-            if back:
-                part = dot(low, pq_ref[m, :, k * PACK : k * PACK + LANES], ((1,), (1,)))
-            else:
-                part = parts[:, k * PACK : (k + 1) * PACK]
+            part = parts[:, k * PACK : (k + 1) * PACK]
             for t in range(4):
                 u = t ^ k
                 piece = part[t * group : (t + 1) * group]
@@ -393,10 +388,7 @@
         for s in range(samples):
             rows = []
             for u in range(4):
-                piece = total[u][s * shards : (s + 1) * shards] * factor
-                if back:
-                    piece = jnp.concatenate([piece, jnp.zeros((shards, PACK - LANES), F32)], axis=1)
-                rows.append(piece)
+                rows.append(total[u][s * shards : (s + 1) * shards] * factor)
             for n, tile in enumerate(join_lanes(*rows)):
                 ysc[s * 3 + n, at, :] = tile
         return carry
@@ -427,7 +419,37 @@
         compiler_params=params(28),
         cost_estimate=cost(),
         name="mix",
-    )(*stay(ids), xa, xb, *pin(pq))
+    )(*stay(ids, xa, xb), *pin(pq))
+
+
+def turn_blocks_kernel(pq_ref, out_ref, held):
+    modes = pq_ref.shape[0]
+    shape = (LANES, LANES)
+    diagonal = lax.broadcasted_iota(jnp.int32, shape, 0) == lax.broadcasted_iota(jnp.int32, shape, 1)
+    unit = jnp.where(diagonal, 1.0, 0.0).astype(BF16)
+
+    def step(m, carry):
+        for k in range(4):
+            at = slice(k * PACK, k * PACK + LANES)
+            held[m, :, at] = dot(unit, pq_ref[m, :, at], ((1,), (1,))).astype(BF16)
+        return carry
+
+    lax.fori_loop(0, modes, step, 0, unroll=min(16, modes))
+    out_ref[...] = held[...]
+
+
+def turn_blocks(pq):
+    return pl.pallas_call(
+        turn_blocks_kernel,
+        in_specs=in_vmem(1),
+        out_specs=in_vmem(1)[0],
+        out_shape=fast(pq.shape, BF16),
+        input_output_aliases={0: 0},
+        scratch_shapes=[pltpu.VMEM(pq.shape, BF16)],
+        compiler_params=params(28),
+        cost_estimate=cost(),
+        name="turn_blocks",
+    )(*pin(pq))
 
 
 def mix_back_kernel(ids_ref, g_ref, pq_ref, out_ref, gsc, ysc):
@@ -478,7 +500,7 @@
         compiler_params=params(28),
         cost_estimate=cost(),
         name="turn_modes",
-    )(xa, xb)
+    )(*stay(xa, xb))
 
 
 def grad_kernel(ids_ref, xt_ref, g_ref, lin_ref, o0, o1, o2, o3, gsc, osc):
@@ -562,37 +584,47 @@
 def pixel_kernel(ids_ref, inv_ref, *refs):
     x = refs[:4]
     y_ref, ft_ref, lt_ref = refs[4:7]
-    outs = refs[7:11]
-    slope_ref = refs[11]
-    ysc, pre, lts = refs[12:]
+    outs = refs[8:12]
+    slope_ref = refs[12]
+    left, ysc, even, odd = refs[14:]
     samples = x[1].shape[0]
     rows = 4 * C
+    n = 2 * MODES
+    width = even.shape[1]
 
     @pl.when(pl.program_id(0) == 0)
     def _():
         collect(y_ref, ysc)
         for s in range(samples):
-            lts[s] = (lt_ref[...].astype(F32) * inv_ref[s]).astype(BF16)
-
-    for s in range(samples):
-        at = slice(s * rows, (s + 1) * rows)
-        fields = jnp.concatenate([x[t][s, 0] for t in range(4)], axis=0)
-        left = jnp.concatenate([ysc[at], lts[s]], axis=1)
-        pre[at] = dot(left, jnp.concatenate([ft_ref[...], fields], axis=0))
-    for s in range(samples):
+            left[s, :, :n] = ysc[s * rows : (s + 1) * rows]
+            left[s, :, n:] = (lt_ref[...].astype(F32) * inv_ref[s]).astype(BF16)
+
+    def product(s, at, pre):
+        fields = [x[t][s, 0, :, at] for t in range(4)]
+        pre[...] = dot(left[s], jnp.concatenate([ft_ref[:, at]] + fields, axis=0))
+
+    def activate(s, at, pre):
         for t in range(4):
-            for c in range(0, C, ROWS):
-                at = s * rows + t * C + c
-                value, slope = gelu_parts(pre[at : at + ROWS])
-                normed = x[t][s, 0, c : c + ROWS].astype(F32) * inv_ref[s]
-                outs[t][s, 0, c : c + ROWS] = (normed + value).astype(BF16)
-                slope_ref[at : at + ROWS] = slope.astype(BF16)
-
-
-def pixels(ids, inv, x, y, turned, lt):
+            value, slope = gelu_parts(pre[t * C : (t + 1) * C])
+            normed = x[t][s, 0, :, at].astype(F32) * inv_ref[s]
+            outs[t][s, 0, :, at] = (normed + value).astype(BF16)
+            row = s * rows + t * C
+            slope_ref[row : row + C, at] = slope.astype(BF16)
+
+    tile = ft_ref.shape[1]
+    blocks = [(s, slice(k, k + width)) for k in range(0, tile, width) for s in range(samples)]
+    buffers = [even, odd]
+    product(*blocks[0], buffers[0])
+    for k, block in enumerate(blocks):
+        if k + 1 < len(blocks):
+            product(*blocks[k + 1], buffers[(k + 1) % 2])
+        activate(*block, buffers[k % 2])
+
+
+def pixels(ids, inv, x, y, turned, lt, pq):
     samples = inv.shape[0]
     n = 2 * MODES
-    tile = 512
+    tile = 1024
     mine = pl.BlockSpec((samples, 1, C, tile), lambda i, ids, inv: (ids[0], 0, 0, i))
     block = pl.BlockSpec((samples, 1, C, tile), lambda i, ids, inv: (0, 0, 0, i))
     rows = samples * 4 * C
@@ -608,26 +640,29 @@
                 whole(y.shape),
                 pl.BlockSpec((n, tile), lambda i, ids, inv: (0, i)),
                 whole((4 * C, 4 * C)),
+                pl.BlockSpec(memory_space=pl.ANY),
             ],
-            out_specs=[mine] + [block] * 3 + [flat],
+            out_specs=[mine] + [block] * 3 + [flat, pl.BlockSpec(memory_space=pl.ANY)],
             scratch_shapes=[
+                pltpu.VMEM((samples, 4 * C, n + 4 * C), BF16),
                 pltpu.VMEM((rows, n), BF16),
-                pltpu.VMEM((rows, tile), F32),
-                pltpu.VMEM((samples, 4 * C, 4 * C), BF16),
+                pltpu.VMEM((4 * C, 256), F32),
+                pltpu.VMEM((4 * C, 256), F32),
             ],
         ),
         out_shape=[slow(x[0].shape, BF16)]
         + [slow((samples, 1, C, NPIX), BF16)] * 3
-        + [fast((rows, NPIX), BF16)],
+        + [fast((rows, NPIX), BF16), fast(pq.shape, BF16)],
+        input_output_aliases={9: 5},
         compiler_params=params(28),
         cost_estimate=cost(),
         name="pixels",
-    )(*stay(ids, inv, *x), y, *stay(turned), *pin(lt))
+    )(*stay(ids, inv, *x), y, *stay(turned, lt), *pin(pq))
 
 
 def slope_kernel(ids_ref, inv_ref, *refs):
     x, cot = refs[:4], refs[4:8]
-    slope, row_ref, col_ref, g_ref, g_out, lin_ref, gacc, lacc = refs[8:]
+    slope, row_ref, col_ref, _, g_ref, g_out, lin_ref, _, gacc, lacc = refs[8:]
     samples = cot[1].shape[0]
     rows = 4 * C
     i = pl.program_id(0)
@@ -662,7 +697,7 @@
             lin_ref[k] = total
 
 
-def pixel_grads(ids, inv, x, cot, slope, small, spectrum):
+def pixel_grads(ids, inv, x, cot, slope, small, spectrum, pq):
     rows = slope.shape[0]
     samples = rows // (4 * C)
     n = 2 * MODES
@@ -677,19 +712,27 @@
             grid=(NPIX // tile,),
             in_specs=([mine] + [block] * 3) * 2
             + [flat]
-            + small_specs(tile),
-            out_specs=[flat, whole(spectrum), whole((4, C, C))],
+            + small_specs(tile)
+            + [pl.BlockSpec(memory_space=pl.ANY)],
+            out_specs=[
+                flat,
+                whole(spectrum),
+                whole((4, C, C)),
+                pl.BlockSpec(memory_space=pl.ANY),
+            ],
             scratch_shapes=[pltpu.VMEM((rows, n), F32), pltpu.VMEM((4 * C, 4 * C), F32)],
         ),
         out_shape=[
             slow((rows, NPIX), BF16),
             slow(spectrum, BF16),
             slow((4, C, C), F32),
+            fast(pq.shape, BF16),
         ],
+        input_output_aliases={13: 3},
         compiler_params=params(28),
         cost_estimate=cost(),
         name="pixel_grads",
-    )(*stay(ids, inv, *x, *cot), *pin(slope), *stay(small, small))
+    )(*stay(ids, inv, *x, *cot), *pin(slope), *stay(small, small), *pin(pq))
 
 
 def inner_kernel(ids_ref, inv_ref, y_ref, g_ref, row_ref, col_ref, lb_ref, cot_ref, mine_ref, *refs):
@@ -927,16 +970,17 @@
     y = to_modes(mix(ids, xa, xb, pq, samples))
 
     x = (inputs, x1, x2, x3)
-    result = pixels(ids, inv, x, y, turned, lt)
-    output, slope = result[0], result[4]
+    result = pixels(ids, inv, x, y, turned, lt, pq)
+    output, slope, pq = result[0], result[4], result[5]
     last, cot = lax.optimization_barrier((result[3], cot))
     parts = (result[1], result[2], last)
     out_parts = [swap(parts[t - 1], "blade", 4, t) for t in (1, 2, 3)]
 
-    grad_pre, sent, lin = pixel_grads(ids, inv, x, cot, slope, small, y.shape)
+    grad_pre, sent, lin, pq = pixel_grads(ids, inv, x, cot, slope, small, y.shape, pq)
     xt = turn_modes(after(xa, lin), xb, samples)
-    g = after(to_modes(sent), (out_parts[2], xt))
-    mixed = mix_back(ids, g, unpack(after(ids, lin), packs, False))
+    pq = turn_blocks(pq)
+    g = after(to_modes(sent), (out_parts[2], xt, pq))
+    mixed = mix_back(ids, g, pq)
     back = to_modes(mixed)
     spec_grads = weight_grads(ids, xt, g, lin)
     spec_grads = [spec_grads[0]] + [swap(spec_grads[t], "blade", 4, t) for t in (1, 2, 3)]

time: 189 us -> 186 us (0.984)
  waiting for transfers between devices: 17.2 us -> 22.3 us
  Pallas kernels: 84.7 us -> 80.3 us
  starting transfers between devices: 55.1 us -> 51.8 us
    pallas_call x2 -> x1, Pallas kernels: 10.6 us -> 5.83 us  [unpack(): pl.pallas_call(unpack_kernel, in_specs=[pl.BlockSpec(memory_space=SMEM)]...]
    ppermute x21, starting transfers between devices: 37.4 us -> 34.4 us  [swap(): return lax.ppermute(value, axis, [(i, i ^ x) for i in range(size)])]
    ppermute x21, waiting for transfers between devices: 11.9 us -> 14.9 us  [swap(): return lax.ppermute(value, axis, [(i, i ^ x) for i in range(size)])]
    pallas_call x0 -> x1, Pallas kernels: none -> 2.54 us  [turn_blocks(): pl.pallas_call(turn_blocks_kernel, in_specs=in_vmem(1), out_specs=in_vmem...]
    all_to_all x4, waiting for transfers between devices: 5.25 us -> 7.46 us  [to_modes(): return lax.all_to_all(value, 'dp', split_axis=0, concat_axis=0, tiled=True)]
  transfers between devices with their start and end apart: 25 -> 25, of which waited for: 8 -> 7; matrix products, arithmetic and copies ran while one was open for 5% -> 5% of each run, Pallas kernels for 44% -> 42%
where the time goes in v7:
time: 186 us; the launch traced here: 185 us
  Pallas kernels  80.3 us (43%)
  starting transfers between devices  51.8 us (28%)
  waiting for transfers between devices  22.3 us (12%)
  blocking collectives  17.6 us (9%)
  local copies, waits for them, and re-layouts  8.46 us (5%)
  other arithmetic  3.44 us (2%)
    ppermute x21, starting transfers between devices, swap(): return lax.ppermute(value, axis, [(i, i ^ x) for i in range(size)])  34.4 us
    all_to_all x1, blocking collectives, to_modes(): return lax.all_to_all(value, 'dp', split_axis=0, concat_axis=0, tiled=True)  17.6 us
    all_to_all x4, starting transfers between devices, to_modes(): return lax.all_to_all(value, 'dp', split_axis=0, concat_axis=0, tiled=True)  17.4 us
    ppermute x21, waiting for transfers between devices, swap(): return lax.ppermute(value, axis, [(i, i ^ x) for i in range(size)])  14.9 us
    pallas_call x1, Pallas kernels, pixels(): pl.pallas_call(pixel_kernel, grid_spec=pltpu.PrefetchScalarGridSpec(num_s...  11.5 us
    pallas_call x2, Pallas kernels, forward_spectrum(): pl.pallas_call(forward_kernel, grid_spec=pltpu.PrefetchScalarGridSpec(num...  8.63 us
    dynamic_slice x4, local copies, waits for them, and re-layouts, cut(): lax.dynamic_slice_in_dim(array, jnp.bitwise_xor(own, t) * samples, sample...  7.75 us
    pallas_call x1, Pallas kernels, pixel_grads(): pl.pallas_call(slope_kernel, grid_spec=pltpu.PrefetchScalarGridSpec(num_s...  7.52 us
  transfers between devices with their start and end apart: 25, of which 7 were waited for; matrix products, arithmetic and copies ran while one was open for 5% of the time, Pallas kernels for 42%

profile of v7, /device:TPU:0, one launch (start us, length us, event | category | flops | bytes accessed | tf_op | source)
XLA Modules:
  0.0 184.9 jit_solution(2299472406372566662)
XLA Ops:
  2.7 3.9 %collective-permute-start.2 = (bf16[2,1,48,4096]{3,2,1,0:T(8,128)(2,1)}, bf16[2,1,48,4096]{3,2,1,0:T(8,128)(2,1)}, u32[]{:S(2)}, u32[]{:S(2)}) collective-permute-start(bf16[2,1,48,4096]{3,2,1,0:T(8,128)(2,1)} %constant_dynamic-slice_fusion.5), channel_id=1, source_target_pairs={{0,24},{8,16},{16,8},{24,0},{1,25},{9,17},{17,9},{25,1},{2,26},{10... | collective-permute-start | bytes 2359304 | tf_op jit(solution)/shard_map/ppermute | solution.py:909
  13.4 5.9 %turned.1.refs_5_ = bf16[512,4096]{1,0:T(8,128)(2,1)} custom-call(f32[4,64,512]{2,1,0:T(8,128)} %pad_maximum_fusion.row_ref.col_ref.refs_2_.refs_3_.refs_9_.refs_10_, f32[4,64,512]{2,1,0:T(8,128)} %pad_maximum_fusion.row_ref.col_ref.refs_2_.refs_3_.refs_9_.refs_10_), custom_call_target="tpu_custom_call" | custom-call | flops 1 | bytes 1 | tf_op jit(solution)/shard_map/turned/pallas_call | solution.py:125
  21.5 3.8 %collective-permute-done.2.refs_1_.refs_3_ = bf16[2,1,48,4096]{3,2,1,0:T(8,128)(2,1)} collective-permute-done((bf16[2,1,48,4096]{3,2,1,0:T(8,128)(2,1)}, bf16[2,1,48,4096]{3,2,1,0:T(8,128)(2,1)}, u32[]{:S(2)}, u32[]{:S(2)}) %collective-permute-start.2) | collective-permute-done | bytes 786464 | tf_op jit(solution)/shard_map/ppermute | solution.py:909
  25.3 4.3 %forward.2 = bf16[8,32,384]{2,1,0:T(8,128)(2,1)} custom-call(s32[2]{0:T(128)} %pad_add_fusion.ids_ref, f32[2]{0:T(128)} %dynamic_slice.21.inv_ref, bf16[8,1,48,4096]{3,2,1,0:T(8,128)(2,1)} %refs_0_.5, bf16[2,1,48,4096]{3,2,1,0:T(8,128)(2,1)} %collective-permute-done.2.refs_1_.refs_3_, ...), custom_call_target="tpu_custom_call" | custom-call | flops 1 | bytes 1 | tf_op jit(solution)/shard_map/forward/pallas_call | solution.py:300
  29.7 5.4 %all-to-all-start = ((bf16[8,32,384]{2,1,0:T(8,128)(2,1)}), bf16[8,32,384]{2,1,0:T(8,128)(2,1)}, u32[]{:S(2)}, u32[]{:S(2)}) async-start(bf16[8,32,384]{2,1,0:T(8,128)(2,1)} %forward.2), calls=%async_computation | async-start | bytes 393216 | tf_op jit(solution)/shard_map/all_to_all | solution.py:913
  38.6 4.2 %collective-permute-done.refs_0_.refs_1_ = bf16[2,1,48,4096]{3,2,1,0:T(8,128)(2,1)} collective-permute-done((bf16[2,1,48,4096]{3,2,1,0:T(8,128)(2,1)}, bf16[2,1,48,4096]{3,2,1,0:T(8,128)(2,1)}, u32[]{:S(2)}, u32[]{:S(2)}) %collective-permute-start) | collective-permute-done | bytes 786464 | tf_op jit(solution)/shard_map/ppermute | solution.py:909
  42.8 4.3 %forward.3 = bf16[8,32,384]{2,1,0:T(8,128)(2,1)} custom-call(s32[2]{0:T(128)} %pad_add_fusion.ids_ref, f32[2]{0:T(128)} %dynamic_slice.21.inv_ref, bf16[2,1,48,4096]{3,2,1,0:T(8,128)(2,1)} %collective-permute-done.refs_0_.refs_1_, bf16[2,1,48,4096]{3,2,1,0:T(8,128)(2,1)} %collective-permute-done.1.refs_1_.refs_2_, ...), custom_call_target="tpu_custom_call" | custom-call | flops 1 | bytes 1 | tf_op jit(solution)/shard_map/forward/pallas_call | solution.py:300
  47.1 4.9 %all-to-all-start.1 = ((bf16[8,32,384]{2,1,0:T(8,128)(2,1)}), bf16[8,32,384]{2,1,0:T(8,128)(2,1)}, u32[]{:S(2)}, u32[]{:S(2)}) async-start(bf16[8,32,384]{2,1,0:T(8,128)(2,1)} %forward.3), calls=%async_computation.1 | async-start | bytes 393216 | tf_op jit(solution)/shard_map/all_to_all | solution.py:913
  56.9 5.8 %unpack.1 = (bf16[32,96,512]{2,1,0:T(8,128)(2,1)S(1)}, bf16[192,192]{1,0:T(8,128)(2,1)}, bf16[192,192]{1,0:T(8,128)(2,1)}) custom-call(s32[2]{0:T(128)} %pad_add_fusion.ids_ref, bf16[48,3200]{1,0:T(8,128)(2,1)} %copy-done.6, bf16[48,3200]{1,0:T(8,128)(2,1)} %collective-permute-done.3.w1, bf16[48,3200]{1,0:T(8,128)(2,1)} %collective-permute-done.4.w2, ...), custom_call_target="tpu_custom_call" | custom-call | flops 1 | bytes 1 | tf_op jit(solution)/shard_map/unpack/pallas_call | solution.py:231
  65.5 17.6 %all_to_all.25.refs_4_ = bf16[8,32,768]{2,1,0:T(8,128)(2,1)S(1)} all-to-all(bf16[8,32,768]{2,1,0:T(8,128)(2,1)} %mix.1), channel_id=1, replica_groups=mesh['blade'=4,'dp'=8] {'dp'}, dimensions={0} | all-to-all | bytes 786432 | tf_op jit(solution)/shard_map/all_to_all | solution.py:913
  83.1 11.5 %pixels.1 = (bf16[8,1,48,4096]{3,2,1,0:T(8,128)(2,1)}, bf16[2,1,48,4096]{3,2,1,0:T(8,128)(2,1)}, bf16[2,1,48,4096]{3,2,1,0:T(8,128)(2,1)}, bf16[2,1,48,4096]{3,2...) custom-call(s32[2]{0:T(128)} %pad_add_fusion.ids_ref, ...), custom_call_target="tpu_custom_call", output_to_operand_aliasing={{5}: (9, {})} | custom-call | flops 1 | bytes 1 | tf_op jit(solution)/shard_map/pixels/pallas_call | solution.py:632
  96.2 7.5 %pixel_grads.1 = (bf16[384,4096]{1,0:T(8,128)(2,1)}, bf16[8,32,768]{2,1,0:T(8,128)(2,1)}, f32[4,48,48]{2,1,0:T(8,128)}, bf16[32,96,512]{2,1,0:T(8,128)(2,1)S(1)}) custom-call(s32[2]{0:T(128)} %pad_add_fusion.ids_ref, f32[2]{0:T(128)} %dynamic_slice.21.inv_ref, bf16[8,1,48,4096]{3,2,1,0:T(8,128)(2,1)} %refs_0_.5, ...), custom_call_target="tpu_custom_call", output_to_operand_aliasing={{3}: (13, {})} | custom-call | flops 1 | bytes 1 | tf_op jit(solution)/shard_map/pixel_grads/pallas_call | solution.py:708
  103.7 3.6 %all-to-all-start.3 = ((bf16[8,32,768]{2,1,0:T(8,128)(2,1)}), bf16[8,32,768]{2,1,0:T(8,128)(2,1)S(1)}, u32[]{:S(2)}, u32[]{:S(2)}) async-start(bf16[8,32,768]{2,1,0:T(8,128)(2,1)} %get-tuple-element.76), calls=%async_computation.3 | async-start | bytes 786432 | tf_op jit(solution)/shard_map/all_to_all | solution.py:913
  112.0 4.3 %turn_modes.1.xt_ref = bf16[32,48,128]{2,1,0:T(8,128)(2,1)} custom-call(bf16[8,32,384]{2,1,0:T(8,128)(2,1)} %all-to-all-done.xa, bf16[8,32,384]{2,1,0:T(8,128)(2,1)} %all-to-all-done.1.xb), custom_call_target="tpu_custom_call" | custom-call | flops 1 | bytes 1 | tf_op jit(solution)/shard_map/turn_modes/pallas_call | solution.py:494
  116.3 3.3 %all-to-all-done.3.g_ref = bf16[8,32,768]{2,1,0:T(8,128)(2,1)S(1)} async-done(((bf16[8,32,768]{2,1,0:T(8,128)(2,1)}), bf16[8,32,768]{2,1,0:T(8,128)(2,1)S(1)}, u32[]{:S(2)}, u32[]{:S(2)}) %all-to-all-start.3) | async-done | bytes 393248 | tf_op jit(solution)/shard_map/all_to_all | solution.py:913
  122.0 3.5 %all-to-all-start.4 = ((bf16[8,32,768]{2,1,0:T(8,128)(2,1)}), bf16[8,32,768]{2,1,0:T(8,128)(2,1)S(1)}, u32[]{:S(2)}, u32[]{:S(2)}) async-start(bf16[8,32,768]{2,1,0:T(8,128)(2,1)} %mix_back.1), calls=%async_computation.4 | async-start | bytes 786432 | tf_op jit(solution)/shard_map/all_to_all | solution.py:913
  125.5 4.9 %weight_grads.1 = (bf16[48,3200]{1,0:T(8,128)(2,1)}, bf16[48,3200]{1,0:T(8,128)(2,1)}, bf16[48,3200]{1,0:T(8,128)(2,1)}, bf16[48,3200]{1,0:T(8,128)(2,1)}) custom-call(s32[2]{0:T(128)} %pad_add_fusion.ids_ref, bf16[32,48,128]{2,1,0:T(8,128)(2,1)} %turn_modes.1.xt_ref, bf16[8,32,768]{2,1,0:T(8,128)(2,1)S(1)} %all-to-all-done.3.g_ref, ...), custom_call_target="tpu_custom_call" | custom-call | flops 1 | bytes 1 | tf_op jit(solution)/shard_map/weight_grads/pallas_call | solution.py:555
  133.8 4.1 %all-to-all-done.4.y_ref = bf16[8,32,768]{2,1,0:T(8,128)(2,1)S(1)} async-done(((bf16[8,32,768]{2,1,0:T(8,128)(2,1)}), bf16[8,32,768]{2,1,0:T(8,128)(2,1)S(1)}, u32[]{:S(2)}, u32[]{:S(2)}) %all-to-all-start.4) | async-done | bytes 393248 | tf_op jit(solution)/shard_map/all_to_all | solution.py:913
  138.0 6.9 %inner_grads.1 = (f32[8,1,48,4096]{3,2,1,0:T(8,128)}, bf16[2,1,48,4096]{3,2,1,0:T(8,128)(2,1)}, bf16[2,1,48,4096]{3,2,1,0:T(8,128)(2,1)}, bf16[2,1,48,4096]{3,2,1,0:T(8,128)(2,1)}) custom-call(s32[2]{0:T(128)} %pad_add_fusion.ids_ref, f32[2]{0:T(128)} %dynamic_slice.21.inv_ref, bf16[8,32,768]{2,1,0:T(8,128)(2,1)S(1)} %all-to-all-done.4.y_ref, ...), custom_call_target="tpu_custom_call" | custom-call | flops 1 | bytes 1 | tf_op jit(solution)/shard_map/inner_grads/pallas_call | solution.py:764
  148.5 6.1 %place.1 = bf16[8,1,48,4096]{3,2,1,0:T(8,128)(2,1)} custom-call(s32[2]{0:T(128)S(1)} %copy-done.10, bf16[2,1,48,4096]{3,2,1,0:T(8,128)(2,1)} %collective-permute-done.6.a_ref, bf16[2,1,48,4096]{3,2,1,0:T(8,128)(2,1)} %collective-permute-done.7.b_ref, bf16[2,1,48,4096]{3,2,1,0:T(8,128)(2,1)} %collective-permute-done.11.c_ref, ...), custom_call_target="tpu_custom_call", output_to_operand_aliasing={{}: (4, {})} | custom-call | flops 1 | bytes 1 | tf_op jit(solution)/shard_map/place/pallas_call | solution.py:804
  156.0 9.3 %collective-permute-start.19 = (f32[48,48]{1,0:T(8,128)S(1)}, f32[48,48]{1,0:T(8,128)S(1)}, u32[]{:S(2)}, u32[]{:S(2)}) collective-permute-start(f32[48,48]{1,0:T(8,128)S(1)} %add.171), channel_id=1, source_target_pairs={{0,2},{1,3},{2,0},{3,1},{4,6},{5,7},{6,4},{7,5},{8,10},{9,11},{10,... | collective-permute-start | bytes 27656 | tf_op jit(solution)/shard_map/ppermute | solution.py:909
  167.1 2.9 %collective-permute-start.20 = (f32[48,48]{1,0:T(8,128)S(1)}, f32[48,48]{1,0:T(8,128)S(1)}, u32[]{:S(2)}, u32[]{:S(2)}) collective-permute-start(f32[48,48]{1,0:T(8,128)S(1)} %add.172), channel_id=1, source_target_pairs={{0,4},{1,5},{2,6},{3,7},{4,0},{5,1},{6,2},{7,3},{8,12},{9,13},{10,... | collective-permute-start | bytes 27656 | tf_op jit(solution)/shard_map/ppermute | solution.py:909
  170.1 5.6 %adam.1 = (f32[1,32,2,48,48]{4,3,2,1,0:T(8,128)}, f32[1,32,2,48,48]{4,3,2,1,0:T(8,128)}, f32[1,32,2,48,48]{4,3,2,1,0:T(8,128)}) custom-call(f32[4]{0:T(128)S(1)} %pad_maximum_fusion.1.flips, bf16[48,3200]{1,0:T(8,128)(2,1)S(1)} %copy-done.7, bf16[48,3200]{1,0:T(8,128)(2,1)S(1)} %collective-permute-done.15.d1, ...), custom_call_target="tpu_custom_call" | custom-call | flops 1 | bytes 1 | tf_op jit(solution)/shard_map/adam/pallas_call | solution.py:896
  178.3 3.8 %collective-permute-done.12.refs_0_ = bf16[2,1,48,4096]{3,2,1,0:T(8,128)(2,1)S(1)} collective-permute-done((bf16[2,1,48,4096]{3,2,1,0:T(8,128)(2,1)}, bf16[2,1,48,4096]{3,2,1,0:T(8,128)(2,1)S(1)}, u32[]{:S(2)}, u32[]{:S(2)}) %collective-permute-start.12) | collective-permute-done | bytes 786464 | tf_op jit(solution)/shard_map/ppermute | solution.py:909
  (92 shorter events, 46.3 us)
Async XLA Ops:
  2.7 22.6 %collective-permute-start.2 = (bf16[2,1,48,4096]{3,2,1,0:T(8,128)(2,1)}, bf16[2,1,48,4096]{3,2,1,0:T(8,128)(2,1)}, u32[]{:S(2)}, u32[]{:S(2)}) collective-permute-start(bf16[2,1,48,4096]{3,2,1,0:T(8,128)(2,1)} %constant_dynamic-slice_fusion.5), channel_id=1, source_target_pairs={{0,24},{8,16},{16,8},{24,0},{1,25},{9,17},{17,9},{25,1},{2,26},{10... | collective-permute-start | bytes 2359304 | tf_op jit(solution)/shard_map/ppermute | solution.py:909
  8.7 34.1 %collective-permute-start = (bf16[2,1,48,4096]{3,2,1,0:T(8,128)(2,1)}, bf16[2,1,48,4096]{3,2,1,0:T(8,128)(2,1)}, u32[]{:S(2)}, u32[]{:S(2)}) collective-permute-start(bf16[2,1,48,4096]{3,2,1,0:T(8,128)(2,1)} %constant_dynamic-slice_fusion.4), channel_id=1, source_target_pairs={{0,8},{8,0},{16,24},{24,16},{1,9},{9,1},{17,25},{25,17},{2,10},{10... | collective-permute-start | bytes 2359304 | tf_op jit(solution)/shard_map/ppermute | solution.py:909
  13.3 29.4 %collective-permute-start.1 = (bf16[2,1,48,4096]{3,2,1,0:T(8,128)(2,1)}, bf16[2,1,48,4096]{3,2,1,0:T(8,128)(2,1)}, u32[]{:S(2)}, u32[]{:S(2)}) collective-permute-start(bf16[2,1,48,4096]{3,2,1,0:T(8,128)(2,1)} %constant_dynamic-slice_fusion.3), channel_id=1, source_target_pairs={{0,16},{8,24},{16,0},{24,8},{1,17},{9,25},{17,1},{25,9},{2,18},{10... | collective-permute-start | bytes 2359304 | tf_op jit(solution)/shard_map/ppermute | solution.py:909
  29.7 17.4 %all-to-all-start = ((bf16[8,32,384]{2,1,0:T(8,128)(2,1)}), bf16[8,32,384]{2,1,0:T(8,128)(2,1)}, u32[]{:S(2)}, u32[]{:S(2)}) async-start(bf16[8,32,384]{2,1,0:T(8,128)(2,1)} %forward.2), calls=%async_computation | async-start | bytes 393216 | tf_op jit(solution)/shard_map/all_to_all | solution.py:913
  35.1 20.3 %collective-permute-start.3 = (bf16[48,3200]{1,0:T(8,128)(2,1)S(1)}, bf16[48,3200]{1,0:T(8,128)(2,1)}, u32[]{:S(2)}, u32[]{:S(2)}) collective-permute-start(bf16[48,3200]{1,0:T(8,128)(2,1)S(1)} %pack.1.w0), channel_id=1, source_target_pairs={{0,8},{8,0},{16,24},{24,16},{1,9},{9,1},{17,25},{25,17},{2,10},{10... | collective-permute-start | bytes 921608 | tf_op jit(solution)/shard_map/ppermute | solution.py:909
  36.5 20.4 %collective-permute-start.4 = (bf16[48,3200]{1,0:T(8,128)(2,1)S(1)}, bf16[48,3200]{1,0:T(8,128)(2,1)}, u32[]{:S(2)}, u32[]{:S(2)}) collective-permute-start(bf16[48,3200]{1,0:T(8,128)(2,1)S(1)} %pack.1.w0), channel_id=1, source_target_pairs={{0,16},{8,24},{16,0},{24,8},{1,17},{9,25},{17,1},{25,9},{2,18},{10... | collective-permute-start | bytes 921608 | tf_op jit(solution)/shard_map/ppermute | solution.py:909
  38.1 18.8 %collective-permute-start.5 = (bf16[48,3200]{1,0:T(8,128)(2,1)S(1)}, bf16[48,3200]{1,0:T(8,128)(2,1)}, u32[]{:S(2)}, u32[]{:S(2)}) collective-permute-start(bf16[48,3200]{1,0:T(8,128)(2,1)S(1)} %pack.1.w0), channel_id=1, source_target_pairs={{0,24},{8,16},{16,8},{24,0},{1,25},{9,17},{17,9},{25,1},{2,26},{10... | collective-permute-start | bytes 921608 | tf_op jit(solution)/shard_map/ppermute | solution.py:909
  47.1 15.7 %all-to-all-start.1 = ((bf16[8,32,384]{2,1,0:T(8,128)(2,1)}), bf16[8,32,384]{2,1,0:T(8,128)(2,1)}, u32[]{:S(2)}, u32[]{:S(2)}) async-start(bf16[8,32,384]{2,1,0:T(8,128)(2,1)} %forward.3), calls=%async_computation.1 | async-start | bytes 393216 | tf_op jit(solution)/shard_map/all_to_all | solution.py:913
  53.4 41.2 %collective-permute-start.8 = (bf16[2,1,48,4096]{3,2,1,0:T(8,128)(2,1)}, bf16[2,1,48,4096]{3,2,1,0:T(8,128)(2,1)}, u32[]{:S(2)}, u32[]{:S(2)}) collective-permute-start(bf16[2,1,48,4096]{3,2,1,0:T(8,128)(2,1)} %get-tuple-element.65), channel_id=1, source_target_pairs={{0,8},{8,0},{16,24},{24,16},{1,9},{9,1},{17,25},{25,17},{2,10},{10... | collective-permute-start | bytes 2359304 | tf_op jit(solution)/shard_map/ppermute | solution.py:909
  54.9 39.7 %collective-permute-start.9 = (bf16[2,1,48,4096]{3,2,1,0:T(8,128)(2,1)}, bf16[2,1,48,4096]{3,2,1,0:T(8,128)(2,1)}, u32[]{:S(2)}, u32[]{:S(2)}) collective-permute-start(bf16[2,1,48,4096]{3,2,1,0:T(8,128)(2,1)} %get-tuple-element.66), channel_id=1, source_target_pairs={{0,16},{8,24},{16,0},{24,8},{1,17},{9,25},{17,1},{25,9},{2,18},{10... | collective-permute-start | bytes 2359304 | tf_op jit(solution)/shard_map/ppermute | solution.py:909
  55.4 39.2 %collective-permute-start.10 = (bf16[2,1,48,4096]{3,2,1,0:T(8,128)(2,1)}, bf16[2,1,48,4096]{3,2,1,0:T(8,128)(2,1)}, u32[]{:S(2)}, u32[]{:S(2)}) collective-permute-start(bf16[2,1,48,4096]{3,2,1,0:T(8,128)(2,1)} %get-tuple-element.67), channel_id=1, source_target_pairs={{0,24},{8,16},{16,8},{24,0},{1,25},{9,17},{17,9},{25,1},{2,26},{10... | collective-permute-start | bytes 2359304 | tf_op jit(solution)/shard_map/ppermute | solution.py:909
  94.6 25.0 %collective-permute-start.11 = (bf16[2,1,48,4096]{3,2,1,0:T(8,128)(2,1)}, bf16[2,1,48,4096]{3,2,1,0:T(8,128)(2,1)}, u32[]{:S(2)}, u32[]{:S(2)}) collective-permute-start(bf16[2,1,48,4096]{3,2,1,0:T(8,128)(2,1)} %get-tuple-element.68), channel_id=1, source_target_pairs={{0,24},{8,16},{16,8},{24,0},{1,25},{9,17},{17,9},{25,1},{2,26},{10... | collective-permute-start | bytes 2359304 | tf_op jit(solution)/shard_map/ppermute | solution.py:909
  103.7 15.9 %all-to-all-start.3 = ((bf16[8,32,768]{2,1,0:T(8,128)(2,1)}), bf16[8,32,768]{2,1,0:T(8,128)(2,1)S(1)}, u32[]{:S(2)}, u32[]{:S(2)}) async-start(bf16[8,32,768]{2,1,0:T(8,128)(2,1)} %get-tuple-element.76), calls=%async_computation.3 | async-start | bytes 786432 | tf_op jit(solution)/shard_map/all_to_all | solution.py:913
  107.3 37.6 %collective-permute-start.6 = (bf16[2,1,48,4096]{3,2,1,0:T(8,128)(2,1)}, bf16[2,1,48,4096]{3,2,1,0:T(8,128)(2,1)}, u32[]{:S(2)}, u32[]{:S(2)}) collective-permute-start(bf16[2,1,48,4096]{3,2,1,0:T(8,128)(2,1)} %get-tuple-element.62), channel_id=1, source_target_pairs={{0,8},{8,0},{16,24},{24,16},{1,9},{9,1},{17,25},{25,17},{2,10},{10... | collective-permute-start | bytes 2359304 | tf_op jit(solution)/shard_map/ppermute | solution.py:909
  107.9 37.0 %collective-permute-start.7 = (bf16[2,1,48,4096]{3,2,1,0:T(8,128)(2,1)}, bf16[2,1,48,4096]{3,2,1,0:T(8,128)(2,1)}, u32[]{:S(2)}, u32[]{:S(2)}) collective-permute-start(bf16[2,1,48,4096]{3,2,1,0:T(8,128)(2,1)} %get-tuple-element.63), channel_id=1, source_target_pairs={{0,16},{8,24},{16,0},{24,8},{1,17},{9,25},{17,1},{25,9},{2,18},{10... | collective-permute-start | bytes 2359304 | tf_op jit(solution)/shard_map/ppermute | solution.py:909
  122.0 15.9 %all-to-all-start.4 = ((bf16[8,32,768]{2,1,0:T(8,128)(2,1)}), bf16[8,32,768]{2,1,0:T(8,128)(2,1)S(1)}, u32[]{:S(2)}, u32[]{:S(2)}) async-start(bf16[8,32,768]{2,1,0:T(8,128)(2,1)} %mix_back.1), calls=%async_computation.4 | async-start | bytes 786432 | tf_op jit(solution)/shard_map/all_to_all | solution.py:913
  130.4 17.6 %collective-permute-start.15 = (bf16[48,3200]{1,0:T(8,128)(2,1)}, bf16[48,3200]{1,0:T(8,128)(2,1)S(1)}, u32[]{:S(2)}, u32[]{:S(2)}) collective-permute-start(bf16[48,3200]{1,0:T(8,128)(2,1)} %get-tuple-element.92), channel_id=1, source_target_pairs={{0,8},{8,0},{16,24},{24,16},{1,9},{9,1},{17,25},{25,17},{2,10},{10... | collective-permute-start | bytes 921608 | tf_op jit(solution)/shard_map/ppermute | solution.py:909
  130.9 23.8 %collective-permute-start.16 = (bf16[48,3200]{1,0:T(8,128)(2,1)}, bf16[48,3200]{1,0:T(8,128)(2,1)S(1)}, u32[]{:S(2)}, u32[]{:S(2)}) collective-permute-start(bf16[48,3200]{1,0:T(8,128)(2,1)} %get-tuple-element.93), channel_id=1, source_target_pairs={{0,16},{8,24},{16,0},{24,8},{1,17},{9,25},{17,1},{25,9},{2,18},{10... | collective-permute-start | bytes 921608 | tf_op jit(solution)/shard_map/ppermute | solution.py:909
  132.4 22.3 %collective-permute-start.17 = (bf16[48,3200]{1,0:T(8,128)(2,1)}, bf16[48,3200]{1,0:T(8,128)(2,1)S(1)}, u32[]{:S(2)}, u32[]{:S(2)}) collective-permute-start(bf16[48,3200]{1,0:T(8,128)(2,1)} %get-tuple-element.94), channel_id=1, source_target_pairs={{0,24},{8,16},{16,8},{24,0},{1,25},{9,17},{17,9},{25,1},{2,26},{10... | collective-permute-start | bytes 921608 | tf_op jit(solution)/shard_map/ppermute | solution.py:909
  144.9 31.5 %collective-permute-start.14 = (bf16[2,1,48,4096]{3,2,1,0:T(8,128)(2,1)}, bf16[2,1,48,4096]{3,2,1,0:T(8,128)(2,1)S(1)}, u32[]{:S(2)}, u32[]{:S(2)}) collective-permute-start(bf16[2,1,48,4096]{3,2,1,0:T(8,128)(2,1)} %get-tuple-element.89), channel_id=1, source_target_pairs={{0,24},{8,16},{16,8},{24,0},{1,25},{9,17},{17,9},{25,1},{2,26},{10... | collective-permute-start | bytes 2359304 | tf_op jit(solution)/shard_map/ppermute | solution.py:909
  146.4 35.7 %collective-permute-start.12 = (bf16[2,1,48,4096]{3,2,1,0:T(8,128)(2,1)}, bf16[2,1,48,4096]{3,2,1,0:T(8,128)(2,1)S(1)}, u32[]{:S(2)}, u32[]{:S(2)}) collective-permute-start(bf16[2,1,48,4096]{3,2,1,0:T(8,128)(2,1)} %get-tuple-element.87), channel_id=1, source_target_pairs={{0,8},{8,0},{16,24},{24,16},{1,9},{9,1},{17,25},{25,17},{2,10},{10... | collective-permute-start | bytes 2359304 | tf_op jit(solution)/shard_map/ppermute | solution.py:909
  147.9 34.2 %collective-permute-start.13 = (bf16[2,1,48,4096]{3,2,1,0:T(8,128)(2,1)}, bf16[2,1,48,4096]{3,2,1,0:T(8,128)(2,1)S(1)}, u32[]{:S(2)}, u32[]{:S(2)}) collective-permute-start(bf16[2,1,48,4096]{3,2,1,0:T(8,128)(2,1)} %get-tuple-element.88), channel_id=1, source_target_pairs={{0,16},{8,24},{16,0},{24,8},{1,17},{9,25},{17,1},{25,9},{2,18},{10... | collective-permute-start | bytes 2359304 | tf_op jit(solution)/shard_map/ppermute | solution.py:909
  156.0 11.1 %collective-permute-start.19 = (f32[48,48]{1,0:T(8,128)S(1)}, f32[48,48]{1,0:T(8,128)S(1)}, u32[]{:S(2)}, u32[]{:S(2)}) collective-permute-start(f32[48,48]{1,0:T(8,128)S(1)} %add.171), channel_id=1, source_target_pairs={{0,2},{1,3},{2,0},{3,1},{4,6},{5,7},{6,4},{7,5},{8,10},{9,11},{10,... | collective-permute-start | bytes 27656 | tf_op jit(solution)/shard_map/ppermute | solution.py:909
  167.1 8.7 %collective-permute-start.20 = (f32[48,48]{1,0:T(8,128)S(1)}, f32[48,48]{1,0:T(8,128)S(1)}, u32[]{:S(2)}, u32[]{:S(2)}) collective-permute-start(f32[48,48]{1,0:T(8,128)S(1)} %add.172), channel_id=1, source_target_pairs={{0,4},{1,5},{2,6},{3,7},{4,0},{5,1},{6,2},{7,3},{8,12},{9,13},{10,... | collective-permute-start | bytes 27656 | tf_op jit(solution)/shard_map/ppermute | solution.py:909
  (16 other events, 255.3 us)

commit v8 on v7

--- a/solution.py
+++ b/solution.py
@@ -422,36 +422,6 @@
     )(*stay(ids, xa, xb), *pin(pq))
 
 
-def turn_blocks_kernel(pq_ref, out_ref, held):
-    modes = pq_ref.shape[0]
-    shape = (LANES, LANES)
-    diagonal = lax.broadcasted_iota(jnp.int32, shape, 0) == lax.broadcasted_iota(jnp.int32, shape, 1)
-    unit = jnp.where(diagonal, 1.0, 0.0).astype(BF16)
-
-    def step(m, carry):
-        for k in range(4):
-            at = slice(k * PACK, k * PACK + LANES)
-            held[m, :, at] = dot(unit, pq_ref[m, :, at], ((1,), (1,))).astype(BF16)
-        return carry
-
-    lax.fori_loop(0, modes, step, 0, unroll=min(16, modes))
-    out_ref[...] = held[...]
-
-
-def turn_blocks(pq):
-    return pl.pallas_call(
-        turn_blocks_kernel,
-        in_specs=in_vmem(1),
-        out_specs=in_vmem(1)[0],
-        out_shape=fast(pq.shape, BF16),
-        input_output_aliases={0: 0},
-        scratch_shapes=[pltpu.VMEM(pq.shape, BF16)],
-        compiler_params=params(28),
-        cost_estimate=cost(),
-        name="turn_blocks",
-    )(*pin(pq))
-
-
 def mix_back_kernel(ids_ref, g_ref, pq_ref, out_ref, gsc, ysc):
     shards, modes, width = g_ref.shape
     gather_rows((g_ref,), gsc)
@@ -474,33 +444,44 @@
     )(*stay(ids), g, *pin(pq))
 
 
-def turn_kernel(xa, xb, xt_ref, xsc):
+def turn_kernel(pq_ref, xa, xb, out_ref, xt_ref, held, xsc):
     shards, modes = xa.shape[:2]
     samples = xt_ref.shape[2] // (8 * shards)
     groups = groups_of(samples, EARLY, LATE)
+    shape = (LANES, LANES)
+    diagonal = lax.broadcasted_iota(jnp.int32, shape, 0) == lax.broadcasted_iota(jnp.int32, shape, 1)
+    unit = jnp.where(diagonal, 1.0, 0.0).astype(BF16)
     gather_rows((xa, xb), xsc)
 
     def step(m, carry):
+        for k in range(4):
+            at = slice(k * PACK, k * PACK + LANES)
+            held[m, :, at] = dot(unit, pq_ref[m, :, at], ((1,), (1,))).astype(BF16)
         x = blade_rows(xsc, m, shards, groups)
         x = x + [pltpu.roll(rows, PACK - C, 1) for rows in x]
         xt_ref[m] = jnp.concatenate(x, axis=0).T[:C].astype(BF16)
         return carry
 
-    lax.fori_loop(0, modes, step, 0, unroll=4)
-
-
-def turn_modes(xa, xb, samples):
+    lax.fori_loop(0, modes, step, 0, unroll=min(16, modes))
+    out_ref[...] = held[...]
+
+
+def turn(pq, xa, xb, samples):
     shards, modes = xa.shape[:2]
     return pl.pallas_call(
         turn_kernel,
-        in_specs=in_vmem(2),
-        out_specs=in_vmem(1)[0],
-        out_shape=slow((modes, C, 8 * samples * shards), BF16),
-        scratch_shapes=[row_scratch(modes, shards, xa.shape[2] + xb.shape[2])],
-        compiler_params=params(28),
-        cost_estimate=cost(),
-        name="turn_modes",
-    )(*stay(xa, xb))
+        in_specs=in_vmem(3),
+        out_specs=in_vmem(2),
+        out_shape=[fast(pq.shape, BF16), slow((modes, C, 8 * samples * shards), BF16)],
+        input_output_aliases={0: 0},
+        scratch_shapes=[
+            pltpu.VMEM(pq.shape, BF16),
+            row_scratch(modes, shards, xa.shape[2] + xb.shape[2]),
+        ],
+        compiler_params=params(28),
+        cost_estimate=cost(),
+        name="turn",
+    )(*pin(pq), *stay(xa, xb))
 
 
 def grad_kernel(ids_ref, xt_ref, g_ref, lin_ref, o0, o1, o2, o3, gsc, osc):
@@ -660,9 +641,9 @@
     )(*stay(ids, inv, *x), y, *stay(turned, lt), *pin(pq))
 
 
-def slope_kernel(ids_ref, inv_ref, *refs):
-    x, cot = refs[:4], refs[4:8]
-    slope, row_ref, col_ref, _, g_ref, g_out, lin_ref, _, gacc, lacc = refs[8:]
+def slope_kernel(ids_ref, *refs):
+    cot = refs[:4]
+    slope, row_ref, col_ref, _, g_ref, g_out, _, gacc = refs[4:]
     samples = cot[1].shape[0]
     rows = 4 * C
     i = pl.program_id(0)
@@ -670,7 +651,6 @@
     @pl.when(i == 0)
     def _():
         gacc[...] = jnp.zeros_like(gacc)
-        lacc[...] = jnp.zeros_like(lacc)
 
     for s in range(samples):
         for t in range(4):
@@ -679,15 +659,55 @@
             g_ref[at : at + C] = grad.astype(BF16)
     table = table_rows(row_ref, col_ref, 0, row_ref.shape[1])
     gacc[...] += dot(g_ref[...], table)
-    for s in range(samples):
-        at = slice(s * rows, (s + 1) * rows)
-        g = g_ref[at]
-        fields = jnp.concatenate([x[t][s, 0] for t in range(4)], axis=0)
-        lacc[...] += dot(fields, g, ((1,), (1,))) * inv_ref[s]
 
     @pl.when(i == pl.num_programs(0) - 1)
     def _():
         spread(gacc, g_out)
+
+
+def pixel_grads(ids, cot, slope, small, spectrum, pq):
+    rows = slope.shape[0]
+    samples = rows // (4 * C)
+    n = 2 * MODES
+    tile = 2048
+    mine = pl.BlockSpec((samples, 1, C, tile), lambda i, ids: (ids[0], 0, 0, i))
+    block = pl.BlockSpec((samples, 1, C, tile), lambda i, ids: (0, 0, 0, i))
+    flat = pl.BlockSpec((rows, tile), lambda i, ids: (0, i))
+    kept = pl.BlockSpec(memory_space=pl.ANY)
+    return pl.pallas_call(
+        slope_kernel,
+        grid_spec=pltpu.PrefetchScalarGridSpec(
+            num_scalar_prefetch=1,
+            grid=(NPIX // tile,),
+            in_specs=[mine] + [block] * 3 + [flat] + small_specs(tile) + [kept],
+            out_specs=[flat, whole(spectrum), kept],
+            scratch_shapes=[pltpu.VMEM((rows, n), F32)],
+        ),
+        out_shape=[slow((rows, NPIX), BF16), slow(spectrum, BF16), fast(pq.shape, BF16)],
+        input_output_aliases={8: 2},
+        compiler_params=params(28),
+        cost_estimate=cost(),
+        name="pixel_grads",
+    )(*stay(ids, *cot), *pin(slope), *stay(small, small), *pin(pq))
+
+
+def lin_kernel(ids_ref, inv_ref, *refs):
+    x = refs[:4]
+    g_ref, lin_ref, lacc = refs[4:]
+    samples = x[1].shape[0]
+    rows = 4 * C
+
+    @pl.when(pl.program_id(0) == 0)
+    def _():
+        lacc[...] = jnp.zeros_like(lacc)
+
+    for s in range(samples):
+        fields = jnp.concatenate([x[t][s, 0] for t in range(4)], axis=0)
+        g = g_ref[s * rows : (s + 1) * rows]
+        lacc[...] += dot(fields, g, ((1,), (1,))) * inv_ref[s]
+
+    @pl.when(pl.program_id(0) == pl.num_programs(0) - 1)
+    def _():
         for k in range(4):
             total = None
             for t in range(4):
@@ -697,42 +717,27 @@
             lin_ref[k] = total
 
 
-def pixel_grads(ids, inv, x, cot, slope, small, spectrum, pq):
-    rows = slope.shape[0]
+def lin_grads(ids, inv, x, g):
+    rows = g.shape[0]
     samples = rows // (4 * C)
-    n = 2 * MODES
     tile = 2048
     mine = pl.BlockSpec((samples, 1, C, tile), lambda i, ids, inv: (ids[0], 0, 0, i))
     block = pl.BlockSpec((samples, 1, C, tile), lambda i, ids, inv: (0, 0, 0, i))
     flat = pl.BlockSpec((rows, tile), lambda i, ids, inv: (0, i))
     return pl.pallas_call(
-        slope_kernel,
+        lin_kernel,
         grid_spec=pltpu.PrefetchScalarGridSpec(
             num_scalar_prefetch=2,
             grid=(NPIX // tile,),
-            in_specs=([mine] + [block] * 3) * 2
-            + [flat]
-            + small_specs(tile)
-            + [pl.BlockSpec(memory_space=pl.ANY)],
-            out_specs=[
-                flat,
-                whole(spectrum),
-                whole((4, C, C)),
-                pl.BlockSpec(memory_space=pl.ANY),
-            ],
-            scratch_shapes=[pltpu.VMEM((rows, n), F32), pltpu.VMEM((4 * C, 4 * C), F32)],
+            in_specs=[mine] + [block] * 3 + [flat],
+            out_specs=whole((4, C, C)),
+            scratch_shapes=[pltpu.VMEM((4 * C, 4 * C), F32)],
         ),
-        out_shape=[
-            slow((rows, NPIX), BF16),
-            slow(spectrum, BF16),
-            slow((4, C, C), F32),
-            fast(pq.shape, BF16),
-        ],
-        input_output_aliases={13: 3},
-        compiler_params=params(28),
-        cost_estimate=cost(),
-        name="pixel_grads",
-    )(*stay(ids, inv, *x, *cot), *pin(slope), *stay(small, small), *pin(pq))
+        out_shape=slow((4, C, C), F32),
+        compiler_params=params(28),
+        cost_estimate=cost(),
+        name="lin_grads",
+    )(*stay(ids, inv, *x, g))
 
 
 def inner_kernel(ids_ref, inv_ref, y_ref, g_ref, row_ref, col_ref, lb_ref, cot_ref, mine_ref, *refs):
@@ -976,10 +981,10 @@
     parts = (result[1], result[2], last)
     out_parts = [swap(parts[t - 1], "blade", 4, t) for t in (1, 2, 3)]
 
-    grad_pre, sent, lin, pq = pixel_grads(ids, inv, x, cot, slope, small, y.shape, pq)
-    xt = turn_modes(after(xa, lin), xb, samples)
-    pq = turn_blocks(pq)
-    g = after(to_modes(sent), (out_parts[2], xt, pq))
+    grad_pre, sent, pq = pixel_grads(ids, cot, slope, small, y.shape, pq)
+    lin = lin_grads(ids, inv, x, grad_pre)
+    pq, xt = turn(pq, after(xa, sent), xb, samples)
+    g = after(to_modes(sent), (out_parts[2], xt, pq, lin))
     mixed = mix_back(ids, g, pq)
     back = to_modes(mixed)
     spec_grads = weight_grads(ids, xt, g, lin)

time: 186 us -> 186 us (level)
  waiting for transfers between devices: 22.3 us -> 15.6 us
  starting transfers between devices: 51.8 us -> 56.6 us
    ppermute x21, starting transfers between devices: 34.4 us -> 38.2 us  [swap(): return lax.ppermute(value, axis, [(i, i ^ x) for i in range(size)])]
    ppermute x21, waiting for transfers between devices: 14.9 us -> 11.2 us  [swap(): return lax.ppermute(value, axis, [(i, i ^ x) for i in range(size)])]
    pallas_call x2, Pallas kernels: 6.83 us -> 9.92 us  [the longest x1 5.02 us: lin_grads(): pl.pallas_call(lin_kernel, grid_spec=pltpu.PrefetchScalarGridSpec(num_sca...]
    all_to_all x4, waiting for transfers between devices: 7.46 us -> 4.46 us  [to_modes(): return lax.all_to_all(value, 'dp', split_axis=0, concat_axis=0, tiled=True)]
  transfers between devices with their start and end apart: 25 -> 25, of which waited for: 7 -> 6; matrix products, arithmetic and copies ran while one was open for 5% -> 5% of each run, Pallas kernels for 42% -> 43%
where the time goes in v8:
time: 186 us; the launch traced here: 184 us
  Pallas kernels  81.8 us (44%)
  starting transfers between devices  56.6 us (30%)
  blocking collectives  17.6 us (9%)
  waiting for transfers between devices  15.6 us (8%)
  local copies, waits for them, and re-layouts  8.39 us (5%)
  other arithmetic  3.44 us (2%)
    ppermute x21, starting transfers between devices, swap(): return lax.ppermute(value, axis, [(i, i ^ x) for i in range(size)])  38.2 us
    all_to_all x4, starting transfers between devices, to_modes(): return lax.all_to_all(value, 'dp', split_axis=0, concat_axis=0, tiled=True)  18.4 us
    all_to_all x1, blocking collectives, to_modes(): return lax.all_to_all(value, 'dp', split_axis=0, concat_axis=0, tiled=True)  17.6 us
    pallas_call x1, Pallas kernels, pixels(): pl.pallas_call(pixel_kernel, grid_spec=pltpu.PrefetchScalarGridSpec(num_s...  11.5 us
    ppermute x21, waiting for transfers between devices, swap(): return lax.ppermute(value, axis, [(i, i ^ x) for i in range(size)])  11.2 us
    pallas_call x2, Pallas kernels, forward_spectrum(): pl.pallas_call(forward_kernel, grid_spec=pltpu.PrefetchScalarGridSpec(num...  8.63 us
    dynamic_slice x4, local copies, waits for them, and re-layouts, cut(): lax.dynamic_slice_in_dim(array, jnp.bitwise_xor(own, t) * samples, sample...  7.76 us
    pallas_call x1, Pallas kernels, inner_grads(): pl.pallas_call(inner_kernel, grid_spec=pltpu.PrefetchScalarGridSpec(num_s...  6.8 us
  transfers between devices with their start and end apart: 25, of which 6 were waited for; matrix products, arithmetic and copies ran while one was open for 5% of the time, Pallas kernels for 43%

profile of v8, /device:TPU:0, one launch (start us, length us, event | category | flops | bytes accessed | tf_op | source)
XLA Modules:
  0.0 184.3 jit_solution(6157624948485111692)
XLA Ops:
  2.7 3.9 %collective-permute-start.2 = (bf16[2,1,48,4096]{3,2,1,0:T(8,128)(2,1)}, bf16[2,1,48,4096]{3,2,1,0:T(8,128)(2,1)}, u32[]{:S(2)}, u32[]{:S(2)}) collective-permute-start(bf16[2,1,48,4096]{3,2,1,0:T(8,128)(2,1)} %constant_dynamic-slice_fusion.5), channel_id=1, source_target_pairs={{0,24},{8,16},{16,8},{24,0},{1,25},{9,17},{17,9},{25,1},{2,26},{10... | collective-permute-start | bytes 2359304 | tf_op jit(solution)/shard_map/ppermute | solution.py:914
  13.4 5.9 %turned.1.refs_5_ = bf16[512,4096]{1,0:T(8,128)(2,1)} custom-call(f32[4,64,512]{2,1,0:T(8,128)} %pad_maximum_fusion.row_ref.col_ref.refs_2_.refs_3_.refs_5_.refs_6_, f32[4,64,512]{2,1,0:T(8,128)} %pad_maximum_fusion.row_ref.col_ref.refs_2_.refs_3_.refs_5_.refs_6_), custom_call_target="tpu_custom_call" | custom-call | flops 1 | bytes 1 | tf_op jit(solution)/shard_map/turned/pallas_call | solution.py:125
  21.4 3.9 %collective-permute-done.2.refs_1_.refs_3_ = bf16[2,1,48,4096]{3,2,1,0:T(8,128)(2,1)} collective-permute-done((bf16[2,1,48,4096]{3,2,1,0:T(8,128)(2,1)}, bf16[2,1,48,4096]{3,2,1,0:T(8,128)(2,1)}, u32[]{:S(2)}, u32[]{:S(2)}) %collective-permute-start.2) | collective-permute-done | bytes 786464 | tf_op jit(solution)/shard_map/ppermute | solution.py:914
  25.3 4.3 %forward.2 = bf16[8,32,384]{2,1,0:T(8,128)(2,1)} custom-call(s32[2]{0:T(128)} %pad_add_fusion.ids_ref, f32[2]{0:T(128)} %dynamic_slice.21.inv_ref, bf16[8,1,48,4096]{3,2,1,0:T(8,128)(2,1)} %refs_0_.6, bf16[2,1,48,4096]{3,2,1,0:T(8,128)(2,1)} %collective-permute-done.2.refs_1_.refs_3_, ...), custom_call_target="tpu_custom_call" | custom-call | flops 1 | bytes 1 | tf_op jit(solution)/shard_map/forward/pallas_call | solution.py:300
  29.7 5.4 %all-to-all-start = ((bf16[8,32,384]{2,1,0:T(8,128)(2,1)}), bf16[8,32,384]{2,1,0:T(8,128)(2,1)}, u32[]{:S(2)}, u32[]{:S(2)}) async-start(bf16[8,32,384]{2,1,0:T(8,128)(2,1)} %forward.2), calls=%async_computation | async-start | bytes 393216 | tf_op jit(solution)/shard_map/all_to_all | solution.py:918
  38.6 4.2 %collective-permute-done.refs_0_.refs_1_ = bf16[2,1,48,4096]{3,2,1,0:T(8,128)(2,1)} collective-permute-done((bf16[2,1,48,4096]{3,2,1,0:T(8,128)(2,1)}, bf16[2,1,48,4096]{3,2,1,0:T(8,128)(2,1)}, u32[]{:S(2)}, u32[]{:S(2)}) %collective-permute-start) | collective-permute-done | bytes 786464 | tf_op jit(solution)/shard_map/ppermute | solution.py:914
  42.8 4.3 %forward.3 = bf16[8,32,384]{2,1,0:T(8,128)(2,1)} custom-call(s32[2]{0:T(128)} %pad_add_fusion.ids_ref, f32[2]{0:T(128)} %dynamic_slice.21.inv_ref, bf16[2,1,48,4096]{3,2,1,0:T(8,128)(2,1)} %collective-permute-done.refs_0_.refs_1_, bf16[2,1,48,4096]{3,2,1,0:T(8,128)(2,1)} %collective-permute-done.1.refs_1_.refs_2_, ...), custom_call_target="tpu_custom_call" | custom-call | flops 1 | bytes 1 | tf_op jit(solution)/shard_map/forward/pallas_call | solution.py:300
  47.1 4.9 %all-to-all-start.1 = ((bf16[8,32,384]{2,1,0:T(8,128)(2,1)}), bf16[8,32,384]{2,1,0:T(8,128)(2,1)}, u32[]{:S(2)}, u32[]{:S(2)}) async-start(bf16[8,32,384]{2,1,0:T(8,128)(2,1)} %forward.3), calls=%async_computation.1 | async-start | bytes 393216 | tf_op jit(solution)/shard_map/all_to_all | solution.py:918
  56.9 5.8 %unpack.1 = (bf16[32,96,512]{2,1,0:T(8,128)(2,1)S(1)}, bf16[192,192]{1,0:T(8,128)(2,1)}, bf16[192,192]{1,0:T(8,128)(2,1)}) custom-call(s32[2]{0:T(128)} %pad_add_fusion.ids_ref, bf16[48,3200]{1,0:T(8,128)(2,1)} %copy-done.6, bf16[48,3200]{1,0:T(8,128)(2,1)} %collective-permute-done.3.w1, bf16[48,3200]{1,0:T(8,128)(2,1)} %collective-permute-done.4.w2, ...), custom_call_target="tpu_custom_call" | custom-call | flops 1 | bytes 1 | tf_op jit(solution)/shard_map/unpack/pallas_call | solution.py:231
  65.5 17.6 %all_to_all.25.refs_4_ = bf16[8,32,768]{2,1,0:T(8,128)(2,1)S(1)} all-to-all(bf16[8,32,768]{2,1,0:T(8,128)(2,1)} %mix.1), channel_id=1, replica_groups=mesh['blade'=4,'dp'=8] {'dp'}, dimensions={0} | all-to-all | bytes 786432 | tf_op jit(solution)/shard_map/all_to_all | solution.py:918
  83.2 11.5 %pixels.1 = (bf16[8,1,48,4096]{3,2,1,0:T(8,128)(2,1)}, bf16[2,1,48,4096]{3,2,1,0:T(8,128)(2,1)}, bf16[2,1,48,4096]{3,2,1,0:T(8,128)(2,1)}, bf16[2,1,48,4096]{3,2...) custom-call(s32[2]{0:T(128)} %pad_add_fusion.ids_ref, ...), custom_call_target="tpu_custom_call", output_to_operand_aliasing={{5}: (9, {})} | custom-call | flops 1 | bytes 1 | tf_op jit(solution)/shard_map/pixels/pallas_call | solution.py:613
  96.2 6.0 %pixel_grads.1 = (bf16[384,4096]{1,0:T(8,128)(2,1)}, bf16[8,32,768]{2,1,0:T(8,128)(2,1)}, bf16[32,96,512]{2,1,0:T(8,128)(2,1)S(1)}) custom-call(s32[2]{0:T(128)} %pad_add_fusion.ids_ref, bf16[8,1,48,4096]{3,2,1,0:T(8,128)(2,1)} %cot_ref.5, bf16[2,1,48,4096]{3,2,1,0:T(8,128)(2,1)} %collective-permute-done.8.refs_1_, ...), custom_call_target="tpu_custom_call", output_to_operand_aliasing={{2}: (8, {})} | custom-call | flops 1 | bytes 1 | tf_op jit(solution)/shard_map/pixel_grads/pallas_call | solution.py:677
  102.2 3.6 %all-to-all-start.3 = ((bf16[8,32,768]{2,1,0:T(8,128)(2,1)}), bf16[8,32,768]{2,1,0:T(8,128)(2,1)S(1)}, u32[]{:S(2)}, u32[]{:S(2)}) async-start(bf16[8,32,768]{2,1,0:T(8,128)(2,1)} %get-tuple-element.77), calls=%async_computation.3 | async-start | bytes 786432 | tf_op jit(solution)/shard_map/all_to_all | solution.py:918
  107.9 5.0 %lin_grads.1.lin_ref = f32[4,48,48]{2,1,0:T(8,128)} custom-call(s32[2]{0:T(128)} %pad_add_fusion.ids_ref, f32[2]{0:T(128)} %dynamic_slice.21.inv_ref, bf16[8,1,48,4096]{3,2,1,0:T(8,128)(2,1)} %refs_0_.6, bf16[2,1,48,4096]{3,2,1,0:T(8,128)(2,1)} %collective-permute-done.refs_0_.refs_1_, bf16[2,1,48,4096]{3,2,1,0:T(8,128)(2,1)} %collective-permute-done.1.refs_1_.refs_2_, ...), custom_call_target="tpu_custom_call" | custom-call | flops 1 | bytes 1 | tf_op jit(solution)/shard_map/lin_grads/pallas_call | solution.py:727
  112.9 4.9 %turn.1 = (bf16[32,96,512]{2,1,0:T(8,128)(2,1)S(1)}, bf16[32,48,128]{2,1,0:T(8,128)(2,1)}) custom-call(bf16[32,96,512]{2,1,0:T(8,128)(2,1)S(1)} %get-tuple-element.78.pq_ref, bf16[8,32,384]{2,1,0:T(8,128)(2,1)} %all-to-all-done.xa, bf16[8,32,384]{2,1,0:T(8,128)(2,1)} %all-to-all-done.1.xb), custom_call_target="tpu_custom_call", output_to_operand_aliasing={{0}: (0, {})} | custom-call | flops 1 | bytes 1 | tf_op jit(solution)/shard_map/turn/pallas_call | solution.py:471
  120.5 4.5 %all-to-all-start.4 = ((bf16[8,32,768]{2,1,0:T(8,128)(2,1)}), bf16[8,32,768]{2,1,0:T(8,128)(2,1)S(1)}, u32[]{:S(2)}, u32[]{:S(2)}) async-start(bf16[8,32,768]{2,1,0:T(8,128)(2,1)} %mix_back.1), calls=%async_computation.4 | async-start | bytes 786432 | tf_op jit(solution)/shard_map/all_to_all | solution.py:918
  125.0 4.9 %weight_grads.1 = (bf16[48,3200]{1,0:T(8,128)(2,1)}, bf16[48,3200]{1,0:T(8,128)(2,1)}, bf16[48,3200]{1,0:T(8,128)(2,1)}, bf16[48,3200]{1,0:T(8,128)(2,1)}) custom-call(s32[2]{0:T(128)} %pad_add_fusion.ids_ref, bf16[32,48,128]{2,1,0:T(8,128)(2,1)} %get-tuple-element.80.xt_ref, bf16[8,32,768]{2,1,0:T(8,128)(2,1)S(1)} %all-to-all-done.3.g_ref, ...), custom_call_target="tpu_custom_call" | custom-call | flops 1 | bytes 1 | tf_op jit(solution)/shard_map/weight_grads/pallas_call | solution.py:536
  133.4 4.2 %all-to-all-done.4.y_ref = bf16[8,32,768]{2,1,0:T(8,128)(2,1)S(1)} async-done(((bf16[8,32,768]{2,1,0:T(8,128)(2,1)}), bf16[8,32,768]{2,1,0:T(8,128)(2,1)S(1)}, u32[]{:S(2)}, u32[]{:S(2)}) %all-to-all-start.4) | async-done | bytes 393248 | tf_op jit(solution)/shard_map/all_to_all | solution.py:918
  137.6 6.8 %inner_grads.1 = (f32[8,1,48,4096]{3,2,1,0:T(8,128)}, bf16[2,1,48,4096]{3,2,1,0:T(8,128)(2,1)}, bf16[2,1,48,4096]{3,2,1,0:T(8,128)(2,1)}, bf16[2,1,48,4096]{3,2,1,0:T(8,128)(2,1)}) custom-call(s32[2]{0:T(128)} %pad_add_fusion.ids_ref, f32[2]{0:T(128)} %dynamic_slice.21.inv_ref, bf16[8,32,768]{2,1,0:T(8,128)(2,1)S(1)} %all-to-all-done.4.y_ref, ...), custom_call_target="tpu_custom_call" | custom-call | flops 1 | bytes 1 | tf_op jit(solution)/shard_map/inner_grads/pallas_call | solution.py:769
  148.0 6.1 %place.1 = bf16[8,1,48,4096]{3,2,1,0:T(8,128)(2,1)} custom-call(s32[2]{0:T(128)S(1)} %copy-done.10, bf16[2,1,48,4096]{3,2,1,0:T(8,128)(2,1)} %collective-permute-done.6.a_ref, bf16[2,1,48,4096]{3,2,1,0:T(8,128)(2,1)} %collective-permute-done.7.b_ref, bf16[2,1,48,4096]{3,2,1,0:T(8,128)(2,1)} %collective-permute-done.11.c_ref, ...), custom_call_target="tpu_custom_call", output_to_operand_aliasing={{}: (4, {})} | custom-call | flops 1 | bytes 1 | tf_op jit(solution)/shard_map/place/pallas_call | solution.py:809
  155.4 13.0 %collective-permute-start.19 = (f32[48,48]{1,0:T(8,128)S(1)}, f32[48,48]{1,0:T(8,128)S(1)}, u32[]{:S(2)}, u32[]{:S(2)}) collective-permute-start(f32[48,48]{1,0:T(8,128)S(1)} %add.171), channel_id=1, source_target_pairs={{0,2},{1,3},{2,0},{3,1},{4,6},{5,7},{6,4},{7,5},{8,10},{9,11},{10,... | collective-permute-start | bytes 27656 | tf_op jit(solution)/shard_map/ppermute | solution.py:914
  170.3 3.0 %collective-permute-start.20 = (f32[48,48]{1,0:T(8,128)S(1)}, f32[48,48]{1,0:T(8,128)S(1)}, u32[]{:S(2)}, u32[]{:S(2)}) collective-permute-start(f32[48,48]{1,0:T(8,128)S(1)} %add.172), channel_id=1, source_target_pairs={{0,4},{1,5},{2,6},{3,7},{4,0},{5,1},{6,2},{7,3},{8,12},{9,13},{10,... | collective-permute-start | bytes 27656 | tf_op jit(solution)/shard_map/ppermute | solution.py:914
  173.3 5.6 %adam.1 = (f32[1,32,2,48,48]{4,3,2,1,0:T(8,128)}, f32[1,32,2,48,48]{4,3,2,1,0:T(8,128)}, f32[1,32,2,48,48]{4,3,2,1,0:T(8,128)}) custom-call(f32[4]{0:T(128)S(1)} %pad_maximum_fusion.1.flips, bf16[48,3200]{1,0:T(8,128)(2,1)S(1)} %copy-done.7, bf16[48,3200]{1,0:T(8,128)(2,1)S(1)} %collective-permute-done.15.d1, ...), custom_call_target="tpu_custom_call" | custom-call | flops 1 | bytes 1 | tf_op jit(solution)/shard_map/adam/pallas_call | solution.py:901
  181.5 2.8 %final.3 = f32[8,1,48,4096]{3,2,1,0:T(8,128)} custom-call(s32[2]{0:T(128)S(1)} %copy-done.10, f32[8]{0:T(128)S(1)} %broadcast_divide_fusion.inv_ref, bf16[8,1,48,4096]{3,2,1,0:T(8,128)(2,1)S(1)} %copy-done.1, bf16[2,1,48,4096]{3,2,1,0:T(8,128)(2,1)S(1)} %collective-permute-done.12.refs_0_, ...), custom_call_target="tpu_custom_call", output_to_operand_aliasing={{}: (5, {})} | custom-call | flops 1 | bytes 1 | tf_op jit(solution)/shard_map/final/pallas_call | solution.py:858
  (92 shorter events, 41.2 us)
Async XLA Ops:
  2.7 22.6 %collective-permute-start.2 = (bf16[2,1,48,4096]{3,2,1,0:T(8,128)(2,1)}, bf16[2,1,48,4096]{3,2,1,0:T(8,128)(2,1)}, u32[]{:S(2)}, u32[]{:S(2)}) collective-permute-start(bf16[2,1,48,4096]{3,2,1,0:T(8,128)(2,1)} %constant_dynamic-slice_fusion.5), channel_id=1, source_target_pairs={{0,24},{8,16},{16,8},{24,0},{1,25},{9,17},{17,9},{25,1},{2,26},{10... | collective-permute-start | bytes 2359304 | tf_op jit(solution)/shard_map/ppermute | solution.py:914
  8.7 34.1 %collective-permute-start = (bf16[2,1,48,4096]{3,2,1,0:T(8,128)(2,1)}, bf16[2,1,48,4096]{3,2,1,0:T(8,128)(2,1)}, u32[]{:S(2)}, u32[]{:S(2)}) collective-permute-start(bf16[2,1,48,4096]{3,2,1,0:T(8,128)(2,1)} %constant_dynamic-slice_fusion.4), channel_id=1, source_target_pairs={{0,8},{8,0},{16,24},{24,16},{1,9},{9,1},{17,25},{25,17},{2,10},{10... | collective-permute-start | bytes 2359304 | tf_op jit(solution)/shard_map/ppermute | solution.py:914
  13.3 29.4 %collective-permute-start.1 = (bf16[2,1,48,4096]{3,2,1,0:T(8,128)(2,1)}, bf16[2,1,48,4096]{3,2,1,0:T(8,128)(2,1)}, u32[]{:S(2)}, u32[]{:S(2)}) collective-permute-start(bf16[2,1,48,4096]{3,2,1,0:T(8,128)(2,1)} %constant_dynamic-slice_fusion.3), channel_id=1, source_target_pairs={{0,16},{8,24},{16,0},{24,8},{1,17},{9,25},{17,1},{25,9},{2,18},{10... | collective-permute-start | bytes 2359304 | tf_op jit(solution)/shard_map/ppermute | solution.py:914
  29.7 17.4 %all-to-all-start = ((bf16[8,32,384]{2,1,0:T(8,128)(2,1)}), bf16[8,32,384]{2,1,0:T(8,128)(2,1)}, u32[]{:S(2)}, u32[]{:S(2)}) async-start(bf16[8,32,384]{2,1,0:T(8,128)(2,1)} %forward.2), calls=%async_computation | async-start | bytes 393216 | tf_op jit(solution)/shard_map/all_to_all | solution.py:918
  35.1 20.4 %collective-permute-start.3 = (bf16[48,3200]{1,0:T(8,128)(2,1)S(1)}, bf16[48,3200]{1,0:T(8,128)(2,1)}, u32[]{:S(2)}, u32[]{:S(2)}) collective-permute-start(bf16[48,3200]{1,0:T(8,128)(2,1)S(1)} %pack.1.w0), channel_id=1, source_target_pairs={{0,8},{8,0},{16,24},{24,16},{1,9},{9,1},{17,25},{25,17},{2,10},{10... | collective-permute-start | bytes 921608 | tf_op jit(solution)/shard_map/ppermute | solution.py:914
  36.5 20.4 %collective-permute-start.4 = (bf16[48,3200]{1,0:T(8,128)(2,1)S(1)}, bf16[48,3200]{1,0:T(8,128)(2,1)}, u32[]{:S(2)}, u32[]{:S(2)}) collective-permute-start(bf16[48,3200]{1,0:T(8,128)(2,1)S(1)} %pack.1.w0), channel_id=1, source_target_pairs={{0,16},{8,24},{16,0},{24,8},{1,17},{9,25},{17,1},{25,9},{2,18},{10... | collective-permute-start | bytes 921608 | tf_op jit(solution)/shard_map/ppermute | solution.py:914
  38.1 18.9 %collective-permute-start.5 = (bf16[48,3200]{1,0:T(8,128)(2,1)S(1)}, bf16[48,3200]{1,0:T(8,128)(2,1)}, u32[]{:S(2)}, u32[]{:S(2)}) collective-permute-start(bf16[48,3200]{1,0:T(8,128)(2,1)S(1)} %pack.1.w0), channel_id=1, source_target_pairs={{0,24},{8,16},{16,8},{24,0},{1,25},{9,17},{17,9},{25,1},{2,26},{10... | collective-permute-start | bytes 921608 | tf_op jit(solution)/shard_map/ppermute | solution.py:914
  47.1 15.7 %all-to-all-start.1 = ((bf16[8,32,384]{2,1,0:T(8,128)(2,1)}), bf16[8,32,384]{2,1,0:T(8,128)(2,1)}, u32[]{:S(2)}, u32[]{:S(2)}) async-start(bf16[8,32,384]{2,1,0:T(8,128)(2,1)} %forward.3), calls=%async_computation.1 | async-start | bytes 393216 | tf_op jit(solution)/shard_map/all_to_all | solution.py:918
  53.4 41.2 %collective-permute-start.8 = (bf16[2,1,48,4096]{3,2,1,0:T(8,128)(2,1)}, bf16[2,1,48,4096]{3,2,1,0:T(8,128)(2,1)}, u32[]{:S(2)}, u32[]{:S(2)}) collective-permute-start(bf16[2,1,48,4096]{3,2,1,0:T(8,128)(2,1)} %get-tuple-element.66), channel_id=1, source_target_pairs={{0,8},{8,0},{16,24},{24,16},{1,9},{9,1},{17,25},{25,17},{2,10},{10... | collective-permute-start | bytes 2359304 | tf_op jit(solution)/shard_map/ppermute | solution.py:914
  54.9 39.7 %collective-permute-start.9 = (bf16[2,1,48,4096]{3,2,1,0:T(8,128)(2,1)}, bf16[2,1,48,4096]{3,2,1,0:T(8,128)(2,1)}, u32[]{:S(2)}, u32[]{:S(2)}) collective-permute-start(bf16[2,1,48,4096]{3,2,1,0:T(8,128)(2,1)} %get-tuple-element.67), channel_id=1, source_target_pairs={{0,16},{8,24},{16,0},{24,8},{1,17},{9,25},{17,1},{25,9},{2,18},{10... | collective-permute-start | bytes 2359304 | tf_op jit(solution)/shard_map/ppermute | solution.py:914
  55.4 39.2 %collective-permute-start.10 = (bf16[2,1,48,4096]{3,2,1,0:T(8,128)(2,1)}, bf16[2,1,48,4096]{3,2,1,0:T(8,128)(2,1)}, u32[]{:S(2)}, u32[]{:S(2)}) collective-permute-start(bf16[2,1,48,4096]{3,2,1,0:T(8,128)(2,1)} %get-tuple-element.68), channel_id=1, source_target_pairs={{0,24},{8,16},{16,8},{24,0},{1,25},{9,17},{17,9},{25,1},{2,26},{10... | collective-permute-start | bytes 2359304 | tf_op jit(solution)/shard_map/ppermute | solution.py:914
  94.7 23.4 %collective-permute-start.11 = (bf16[2,1,48,4096]{3,2,1,0:T(8,128)(2,1)}, bf16[2,1,48,4096]{3,2,1,0:T(8,128)(2,1)}, u32[]{:S(2)}, u32[]{:S(2)}) collective-permute-start(bf16[2,1,48,4096]{3,2,1,0:T(8,128)(2,1)} %get-tuple-element.69), channel_id=1, source_target_pairs={{0,24},{8,16},{16,8},{24,0},{1,25},{9,17},{17,9},{25,1},{2,26},{10... | collective-permute-start | bytes 2359304 | tf_op jit(solution)/shard_map/ppermute | solution.py:914
  102.2 15.9 %all-to-all-start.3 = ((bf16[8,32,768]{2,1,0:T(8,128)(2,1)}), bf16[8,32,768]{2,1,0:T(8,128)(2,1)S(1)}, u32[]{:S(2)}, u32[]{:S(2)}) async-start(bf16[8,32,768]{2,1,0:T(8,128)(2,1)} %get-tuple-element.77), calls=%async_computation.3 | async-start | bytes 786432 | tf_op jit(solution)/shard_map/all_to_all | solution.py:918
  105.8 38.6 %collective-permute-start.6 = (bf16[2,1,48,4096]{3,2,1,0:T(8,128)(2,1)}, bf16[2,1,48,4096]{3,2,1,0:T(8,128)(2,1)}, u32[]{:S(2)}, u32[]{:S(2)}) collective-permute-start(bf16[2,1,48,4096]{3,2,1,0:T(8,128)(2,1)} %get-tuple-element.63), channel_id=1, source_target_pairs={{0,8},{8,0},{16,24},{24,16},{1,9},{9,1},{17,25},{25,17},{2,10},{10... | collective-permute-start | bytes 2359304 | tf_op jit(solution)/shard_map/ppermute | solution.py:914
  106.4 38.0 %collective-permute-start.7 = (bf16[2,1,48,4096]{3,2,1,0:T(8,128)(2,1)}, bf16[2,1,48,4096]{3,2,1,0:T(8,128)(2,1)}, u32[]{:S(2)}, u32[]{:S(2)}) collective-permute-start(bf16[2,1,48,4096]{3,2,1,0:T(8,128)(2,1)} %get-tuple-element.64), channel_id=1, source_target_pairs={{0,16},{8,24},{16,0},{24,8},{1,17},{9,25},{17,1},{25,9},{2,18},{10... | collective-permute-start | bytes 2359304 | tf_op jit(solution)/shard_map/ppermute | solution.py:914
  120.5 17.1 %all-to-all-start.4 = ((bf16[8,32,768]{2,1,0:T(8,128)(2,1)}), bf16[8,32,768]{2,1,0:T(8,128)(2,1)S(1)}, u32[]{:S(2)}, u32[]{:S(2)}) async-start(bf16[8,32,768]{2,1,0:T(8,128)(2,1)} %mix_back.1), calls=%async_computation.4 | async-start | bytes 786432 | tf_op jit(solution)/shard_map/all_to_all | solution.py:918
  129.9 16.6 %collective-permute-start.15 = (bf16[48,3200]{1,0:T(8,128)(2,1)}, bf16[48,3200]{1,0:T(8,128)(2,1)S(1)}, u32[]{:S(2)}, u32[]{:S(2)}) collective-permute-start(bf16[48,3200]{1,0:T(8,128)(2,1)} %get-tuple-element.94), channel_id=1, source_target_pairs={{0,8},{8,0},{16,24},{24,16},{1,9},{9,1},{17,25},{25,17},{2,10},{10... | collective-permute-start | bytes 921608 | tf_op jit(solution)/shard_map/ppermute | solution.py:914
  131.4 22.7 %collective-permute-start.16 = (bf16[48,3200]{1,0:T(8,128)(2,1)}, bf16[48,3200]{1,0:T(8,128)(2,1)S(1)}, u32[]{:S(2)}, u32[]{:S(2)}) collective-permute-start(bf16[48,3200]{1,0:T(8,128)(2,1)} %get-tuple-element.95), channel_id=1, source_target_pairs={{0,16},{8,24},{16,0},{24,8},{1,17},{9,25},{17,1},{25,9},{2,18},{10... | collective-permute-start | bytes 921608 | tf_op jit(solution)/shard_map/ppermute | solution.py:914
  131.9 22.2 %collective-permute-start.17 = (bf16[48,3200]{1,0:T(8,128)(2,1)}, bf16[48,3200]{1,0:T(8,128)(2,1)S(1)}, u32[]{:S(2)}, u32[]{:S(2)}) collective-permute-start(bf16[48,3200]{1,0:T(8,128)(2,1)} %get-tuple-element.96), channel_id=1, source_target_pairs={{0,24},{8,16},{16,8},{24,0},{1,25},{9,17},{17,9},{25,1},{2,26},{10... | collective-permute-start | bytes 921608 | tf_op jit(solution)/shard_map/ppermute | solution.py:914
  144.4 35.3 %collective-permute-start.14 = (bf16[2,1,48,4096]{3,2,1,0:T(8,128)(2,1)}, bf16[2,1,48,4096]{3,2,1,0:T(8,128)(2,1)S(1)}, u32[]{:S(2)}, u32[]{:S(2)}) collective-permute-start(bf16[2,1,48,4096]{3,2,1,0:T(8,128)(2,1)} %get-tuple-element.91), channel_id=1, source_target_pairs={{0,24},{8,16},{16,8},{24,0},{1,25},{9,17},{17,9},{25,1},{2,26},{10... | collective-permute-start | bytes 2359304 | tf_op jit(solution)/shard_map/ppermute | solution.py:914
  145.9 35.6 %collective-permute-start.12 = (bf16[2,1,48,4096]{3,2,1,0:T(8,128)(2,1)}, bf16[2,1,48,4096]{3,2,1,0:T(8,128)(2,1)S(1)}, u32[]{:S(2)}, u32[]{:S(2)}) collective-permute-start(bf16[2,1,48,4096]{3,2,1,0:T(8,128)(2,1)} %get-tuple-element.89), channel_id=1, source_target_pairs={{0,8},{8,0},{16,24},{24,16},{1,9},{9,1},{17,25},{25,17},{2,10},{10... | collective-permute-start | bytes 2359304 | tf_op jit(solution)/shard_map/ppermute | solution.py:914
  146.4 35.1 %collective-permute-start.13 = (bf16[2,1,48,4096]{3,2,1,0:T(8,128)(2,1)}, bf16[2,1,48,4096]{3,2,1,0:T(8,128)(2,1)S(1)}, u32[]{:S(2)}, u32[]{:S(2)}) collective-permute-start(bf16[2,1,48,4096]{3,2,1,0:T(8,128)(2,1)} %get-tuple-element.90), channel_id=1, source_target_pairs={{0,16},{8,24},{16,0},{24,8},{1,17},{9,25},{17,1},{25,9},{2,18},{10... | collective-permute-start | bytes 2359304 | tf_op jit(solution)/shard_map/ppermute | solution.py:914
  155.4 14.8 %collective-permute-start.19 = (f32[48,48]{1,0:T(8,128)S(1)}, f32[48,48]{1,0:T(8,128)S(1)}, u32[]{:S(2)}, u32[]{:S(2)}) collective-permute-start(f32[48,48]{1,0:T(8,128)S(1)} %add.171), channel_id=1, source_target_pairs={{0,2},{1,3},{2,0},{3,1},{4,6},{5,7},{6,4},{7,5},{8,10},{9,11},{10,... | collective-permute-start | bytes 27656 | tf_op jit(solution)/shard_map/ppermute | solution.py:914
  170.3 8.7 %collective-permute-start.20 = (f32[48,48]{1,0:T(8,128)S(1)}, f32[48,48]{1,0:T(8,128)S(1)}, u32[]{:S(2)}, u32[]{:S(2)}) collective-permute-start(f32[48,48]{1,0:T(8,128)S(1)} %add.172), channel_id=1, source_target_pairs={{0,4},{1,5},{2,6},{3,7},{4,0},{5,1},{6,2},{7,3},{8,12},{9,13},{10,... | collective-permute-start | bytes 27656 | tf_op jit(solution)/shard_map/ppermute | solution.py:914
  (16 other events, 281.5 us)

commit v9 on v8

--- a/solution.py
+++ b/solution.py
@@ -183,11 +183,11 @@
     tiles = []
     for n in range(3):
         at = pl.ds(pl.multiple_of(g * QUAD * LANES + n * PACK, PACK), PACK)
-        tiles.append(ref[:, at].astype(F32))
+        tiles.append(ref[:, at])
     return tiles
 
 
-def unpack_kernel(ids_ref, w0, w1, w2, w3, pq_ref, *lines):
+def unpack_kernel(ids_ref, w0, w1, w2, w3, pq_ref):
     own = ids_ref[0]
     modes = pq_ref.shape[0]
     lane = lanes_of((C, PACK))
@@ -198,47 +198,28 @@
             slot = jnp.bitwise_xor(own, t)
             scale = jnp.where(slot % 2 == 1, flip, 1.0)
             at = pl.ds(pl.multiple_of(slot * PACK, PACK), PACK)
-            tiles = [tile * scale for tile in quad_tiles(w, g)]
+            tiles = [tile * scale.astype(BF16) for tile in quad_tiles(w, g)]
             for q, p in enumerate(split_lanes(*tiles)):
-                p = jnp.where(lane < LANES, p, 0.0)
                 low = jnp.where(lane < C, -pltpu.roll(p, PACK - C, 1), pltpu.roll(p, C, 1))
-                low = jnp.where(lane < LANES, low, 0.0)
-                pq_ref[g * QUAD + q, :C, at] = p.astype(BF16)
-                pq_ref[g * QUAD + q, C:, at] = low.astype(BF16)
+                pq_ref[g * QUAD + q, :C, at] = p
+                pq_ref[g * QUAD + q, C:, at] = low
         return carry
 
     quads = modes // QUAD
     lax.fori_loop(0, quads, step, 0, unroll=min(4, quads))
-    if not lines:
-        return
-    lt_ref, lb_ref, lsc = lines
-    for t, w in enumerate((w0, w1, w2, w3)):
-        slot = jnp.bitwise_xor(own, t)
-        lsc[slot] = w[:, modes * LANES :].astype(F32) * jnp.where(slot % 2 == 1, flip, 1.0)
-    for k in range(4):
-        line = lsc[k]
-        turned = line.T
-        for t in range(4):
-            u = t ^ k
-            lb_ref[t * C : (t + 1) * C, u * C : (u + 1) * C] = (line[:, :C] * sgn(t, k)).astype(BF16)
-            lt_ref[u * C : (u + 1) * C, t * C : (t + 1) * C] = (turned[:C] * sgn(t, k)).astype(BF16)
-
-
-def unpack(ids, packs, lines):
+
+
+def unpack(ids, packs):
     modes = (packs[0].shape[1] - PACK) // LANES
-    weights = fast((modes, LANES, 4 * PACK), BF16)
-    shape = (4 * C, 4 * C)
-    result = pl.pallas_call(
+    return pl.pallas_call(
         unpack_kernel,
         in_specs=[pl.BlockSpec(memory_space=SMEM)] + in_vmem(4),
-        out_specs=in_vmem(3 if lines else 1),
-        out_shape=[weights] + ([slow(shape, BF16)] * 2 if lines else []),
-        scratch_shapes=[pltpu.VMEM((4, C, PACK), F32)] if lines else [],
+        out_specs=in_vmem(1)[0],
+        out_shape=fast((modes, LANES, 4 * PACK), BF16),
         compiler_params=params(28),
         cost_estimate=cost(),
         name="unpack",
     )(*stay(ids, *packs))
-    return result if lines else result[0]
 
 
 def spread(acc, out_ref, scales=None):
@@ -444,7 +425,7 @@
     )(*stay(ids), g, *pin(pq))
 
 
-def turn_kernel(pq_ref, xa, xb, out_ref, xt_ref, held, xsc):
+def turn_kernel(ids_ref, pq_ref, xa, xb, l0, l1, l2, l3, out_ref, xt_ref, lt_ref, lb_ref, held, xsc, lsc):
     shards, modes = xa.shape[:2]
     samples = xt_ref.shape[2] // (8 * shards)
     groups = groups_of(samples, EARLY, LATE)
@@ -464,24 +445,41 @@
 
     lax.fori_loop(0, modes, step, 0, unroll=min(16, modes))
     out_ref[...] = held[...]
-
-
-def turn(pq, xa, xb, samples):
+    own = ids_ref[0]
+    for t, line in enumerate((l0, l1, l2, l3)):
+        slot = jnp.bitwise_xor(own, t)
+        lsc[slot] = line[...].astype(F32) * jnp.where(slot % 2 == 1, flip_of(own, 1), 1.0)
+    for k in range(4):
+        line = lsc[k]
+        turned = line.T
+        for t in range(4):
+            u = t ^ k
+            lb_ref[t * C : (t + 1) * C, u * C : (u + 1) * C] = (line[:, :C] * sgn(t, k)).astype(BF16)
+            lt_ref[u * C : (u + 1) * C, t * C : (t + 1) * C] = (turned[:C] * sgn(t, k)).astype(BF16)
+
+
+def turn(ids, pq, xa, xb, packs, samples):
     shards, modes = xa.shape[:2]
+    last = packs[0].shape[1] // PACK - 1
+    shape = (4 * C, 4 * C)
+    turned_shape = (modes, C, 8 * samples * shards)
     return pl.pallas_call(
         turn_kernel,
-        in_specs=in_vmem(3),
-        out_specs=in_vmem(2),
-        out_shape=[fast(pq.shape, BF16), slow((modes, C, 8 * samples * shards), BF16)],
-        input_output_aliases={0: 0},
+        grid=(1,),
+        in_specs=[pl.BlockSpec(memory_space=SMEM), whole(pq.shape), whole(xa.shape), whole(xb.shape)]
+        + [pl.BlockSpec((C, PACK), lambda i: (0, last))] * 4,
+        out_specs=[whole(pq.shape), whole(turned_shape)] + [whole(shape)] * 2,
+        out_shape=[fast(pq.shape, BF16), slow(turned_shape, BF16)] + [slow(shape, BF16)] * 2,
+        input_output_aliases={1: 0},
         scratch_shapes=[
             pltpu.VMEM(pq.shape, BF16),
             row_scratch(modes, shards, xa.shape[2] + xb.shape[2]),
+            pltpu.VMEM((4, C, PACK), F32),
         ],
         compiler_params=params(28),
         cost_estimate=cost(),
         name="turn",
-    )(*pin(pq), *stay(xa, xb))
+    )(*stay(ids), *pin(pq), *stay(xa, xb, *packs))
 
 
 def grad_kernel(ids_ref, xt_ref, g_ref, lin_ref, o0, o1, o2, o3, gsc, osc):
@@ -886,7 +884,7 @@
     grad = d0[...].astype(F32) * flips[0]
     for t, d in ((1, d1), (2, d2), (3, d3)):
         grad = grad + d[...].astype(F32) * flips[t]
-    for q in range(QUAD):
+    for q in range(w_ref.shape[1]):
         for r in range(2):
             lane = q * LANES + r * C
             at = (0, q, r)
@@ -896,11 +894,12 @@
 
 def adam_spec(flips, grads, weight, first, second):
     modes = weight.shape[1]
-    packed = pl.BlockSpec((C, QUAD * LANES), lambda g: (0, g))
-    block = pl.BlockSpec((1, QUAD, 2, C, C), lambda g: (0, g, 0, 0, 0))
+    part = min(modes, 4 * QUAD)
+    packed = pl.BlockSpec((C, part * LANES), lambda g: (0, g))
+    block = pl.BlockSpec((1, part, 2, C, C), lambda g: (0, g, 0, 0, 0))
     return pl.pallas_call(
         adam_kernel,
-        grid=(modes // QUAD,),
+        grid=(modes // part,),
         in_specs=[pl.BlockSpec(memory_space=SMEM)] + [packed] * 4 + [block] * 3,
         out_specs=[block] * 3,
         out_shape=[jax.ShapeDtypeStruct(weight.shape, F32)] * 3,
@@ -971,8 +970,10 @@
     blocks = after([cut(cotangent, t) for t in (1, 2, 3)], (x1, x2))
     cot = (cotangent,) + tuple(swap(blocks[t - 1], "blade", 4, t) for t in (1, 2, 3))
     xb = to_modes(forward_spectrum(ids, inv, (x1, x2), small, shards))
-    pq, lt, lb = unpack(ids, packs, True)
-    y = to_modes(mix(ids, xa, xb, pq, samples))
+    pq = unpack(ids, packs)
+    mixed = mix(ids, xa, xb, pq, samples)
+    pq, xt, lt, lb = turn(ids, after(pq, mixed), xa, xb, packs, samples)
+    y = to_modes(mixed)
 
     x = (inputs, x1, x2, x3)
     result = pixels(ids, inv, x, y, turned, lt, pq)
@@ -983,7 +984,6 @@
 
     grad_pre, sent, pq = pixel_grads(ids, cot, slope, small, y.shape, pq)
     lin = lin_grads(ids, inv, x, grad_pre)
-    pq, xt = turn(pq, after(xa, sent), xb, samples)
     g = after(to_modes(sent), (out_parts[2], xt, pq, lin))
     mixed = mix_back(ids, g, pq)
     back = to_modes(mixed)

time: 186 us -> 183 us (0.984)
  blocking collectives: 17.6 us -> 0 us
  waiting for transfers between devices: 15.6 us -> 32.7 us
  Pallas kernels: 81.8 us -> 78.4 us
    all_to_all x1 -> x0, blocking collectives: 17.6 us -> none  [to_modes(): return lax.all_to_all(value, 'dp', split_axis=0, concat_axis=0, tiled=True)]
    all_to_all x4 -> x5, waiting for transfers between devices: 4.46 us -> 16.6 us  [to_modes(): return lax.all_to_all(value, 'dp', split_axis=0, concat_axis=0, tiled=True)]
    ppermute x21, waiting for transfers between devices: 11.2 us -> 16.1 us  [swap(): return lax.ppermute(value, axis, [(i, i ^ x) for i in range(size)])]
    all_to_all x4 -> x5, starting transfers between devices: 18.4 us -> 22.5 us  [to_modes(): return lax.all_to_all(value, 'dp', split_axis=0, concat_axis=0, tiled=True)]
    ppermute x21, starting transfers between devices: 38.2 us -> 35.1 us  [swap(): return lax.ppermute(value, axis, [(i, i ^ x) for i in range(size)])]
  transfers between devices with their start and end apart: 25 -> 26, of which waited for: 6 -> 8; matrix products, arithmetic and copies ran while one was open for 5% -> 5% of each run, Pallas kernels for 43% -> 42%
where the time goes in v9:
time: 183 us; the launch traced here: 182 us
  Pallas kernels  78.4 us (43%)
  starting transfers between devices  57.6 us (31%)
  waiting for transfers between devices  32.7 us (18%)
  local copies, waits for them, and re-layouts  8.45 us (5%)
  other arithmetic  3.45 us (2%)
    ppermute x21, starting transfers between devices, swap(): return lax.ppermute(value, axis, [(i, i ^ x) for i in range(size)])  35.1 us
    all_to_all x5, starting transfers between devices, to_modes(): return lax.all_to_all(value, 'dp', split_axis=0, concat_axis=0, tiled=True)  22.5 us
    all_to_all x5, waiting for transfers between devices, to_modes(): return lax.all_to_all(value, 'dp', split_axis=0, concat_axis=0, tiled=True)  16.6 us
    ppermute x21, waiting for transfers between devices, swap(): return lax.ppermute(value, axis, [(i, i ^ x) for i in range(size)])  16.1 us
    pallas_call x1, Pallas kernels, pixels(): pl.pallas_call(pixel_kernel, grid_spec=pltpu.PrefetchScalarGridSpec(num_s...  11.5 us
    pallas_call x2, Pallas kernels, forward_spectrum(): pl.pallas_call(forward_kernel, grid_spec=pltpu.PrefetchScalarGridSpec(num...  8.63 us
    dynamic_slice x4, local copies, waits for them, and re-layouts, cut(): lax.dynamic_slice_in_dim(array, jnp.bitwise_xor(own, t) * samples, sample...  7.77 us
    pallas_call x1, Pallas kernels, inner_grads(): pl.pallas_call(inner_kernel, grid_spec=pltpu.PrefetchScalarGridSpec(num_s...  6.81 us
  transfers between devices with their start and end apart: 26, of which 8 were waited for; matrix products, arithmetic and copies ran while one was open for 5% of the time, Pallas kernels for 42%

profile of v9, /device:TPU:0, one launch (start us, length us, event | category | flops | bytes accessed | tf_op | source)
XLA Modules:
  0.0 181.5 jit_solution(17475219466770095486)
XLA Ops:
  2.7 3.9 %collective-permute-start.2 = (bf16[2,1,48,4096]{3,2,1,0:T(8,128)(2,1)}, bf16[2,1,48,4096]{3,2,1,0:T(8,128)(2,1)}, u32[]{:S(2)}, u32[]{:S(2)}) collective-permute-start(bf16[2,1,48,4096]{3,2,1,0:T(8,128)(2,1)} %constant_dynamic-slice_fusion.5), channel_id=1, source_target_pairs={{0,24},{8,16},{16,8},{24,0},{1,25},{9,17},{17,9},{25,1},{2,26},{10... | collective-permute-start | bytes 2359304 | tf_op jit(solution)/shard_map/ppermute | solution.py:913
  13.4 5.9 %turned.1.refs_5_ = bf16[512,4096]{1,0:T(8,128)(2,1)} custom-call(f32[4,64,512]{2,1,0:T(8,128)} %pad_maximum_fusion.row_ref.col_ref.refs_2_.refs_3_.refs_5_.refs_6_, f32[4,64,512]{2,1,0:T(8,128)} %pad_maximum_fusion.row_ref.col_ref.refs_2_.refs_3_.refs_5_.refs_6_), custom_call_target="tpu_custom_call" | custom-call | flops 1 | bytes 1 | tf_op jit(solution)/shard_map/turned/pallas_call | solution.py:125
  21.5 3.8 %collective-permute-done.2.refs_1_.refs_3_ = bf16[2,1,48,4096]{3,2,1,0:T(8,128)(2,1)} collective-permute-done((bf16[2,1,48,4096]{3,2,1,0:T(8,128)(2,1)}, bf16[2,1,48,4096]{3,2,1,0:T(8,128)(2,1)}, u32[]{:S(2)}, u32[]{:S(2)}) %collective-permute-start.2) | collective-permute-done | bytes 786464 | tf_op jit(solution)/shard_map/ppermute | solution.py:913
  25.3 4.3 %forward.2 = bf16[8,32,384]{2,1,0:T(8,128)(2,1)} custom-call(s32[2]{0:T(128)} %pad_add_fusion.ids_ref, f32[2]{0:T(128)} %dynamic_slice.21.inv_ref, bf16[8,1,48,4096]{3,2,1,0:T(8,128)(2,1)} %refs_0_.6, bf16[2,1,48,4096]{3,2,1,0:T(8,128)(2,1)} %collective-permute-done.2.refs_1_.refs_3_, ...), custom_call_target="tpu_custom_call" | custom-call | flops 1 | bytes 1 | tf_op jit(solution)/shard_map/forward/pallas_call | solution.py:281
  29.7 5.4 %all-to-all-start = ((bf16[8,32,384]{2,1,0:T(8,128)(2,1)}), bf16[8,32,384]{2,1,0:T(8,128)(2,1)}, u32[]{:S(2)}, u32[]{:S(2)}) async-start(bf16[8,32,384]{2,1,0:T(8,128)(2,1)} %forward.2), calls=%async_computation | async-start | bytes 393216 | tf_op jit(solution)/shard_map/all_to_all | solution.py:917
  38.6 4.2 %collective-permute-done.refs_0_.refs_1_ = bf16[2,1,48,4096]{3,2,1,0:T(8,128)(2,1)} collective-permute-done((bf16[2,1,48,4096]{3,2,1,0:T(8,128)(2,1)}, bf16[2,1,48,4096]{3,2,1,0:T(8,128)(2,1)}, u32[]{:S(2)}, u32[]{:S(2)}) %collective-permute-start) | collective-permute-done | bytes 786464 | tf_op jit(solution)/shard_map/ppermute | solution.py:913
  42.8 4.3 %forward.3 = bf16[8,32,384]{2,1,0:T(8,128)(2,1)} custom-call(s32[2]{0:T(128)} %pad_add_fusion.ids_ref, f32[2]{0:T(128)} %dynamic_slice.21.inv_ref, bf16[2,1,48,4096]{3,2,1,0:T(8,128)(2,1)} %collective-permute-done.refs_0_.refs_1_, bf16[2,1,48,4096]{3,2,1,0:T(8,128)(2,1)} %collective-permute-done.1.refs_1_.refs_2_, ...), custom_call_target="tpu_custom_call" | custom-call | flops 1 | bytes 1 | tf_op jit(solution)/shard_map/forward/pallas_call | solution.py:281
  47.1 4.9 %all-to-all-start.1 = ((bf16[8,32,384]{2,1,0:T(8,128)(2,1)}), bf16[8,32,384]{2,1,0:T(8,128)(2,1)}, u32[]{:S(2)}, u32[]{:S(2)}) async-start(bf16[8,32,384]{2,1,0:T(8,128)(2,1)} %forward.3), calls=%async_computation.1 | async-start | bytes 393216 | tf_op jit(solution)/shard_map/all_to_all | solution.py:917
  56.9 4.1 %unpack.1.pq_ref = bf16[32,96,512]{2,1,0:T(8,128)(2,1)S(1)} custom-call(s32[2]{0:T(128)} %pad_add_fusion.ids_ref, bf16[48,3200]{1,0:T(8,128)(2,1)} %copy-done.4, bf16[48,3200]{1,0:T(8,128)(2,1)} %collective-permute-done.3.w1.l1, bf16[48,3200]{1,0:T(8,128)(2,1)} %collective-permute-done.4.w2.l2, bf16[48,3200]{1,0:T(8,128)(2,1)} %collective-permute-done.5.w3.l3), custom_call_target="tpu_custom_call" | custom-call | flops 1 | bytes 1 | tf_op jit(solution)/shard_map/unpack/pallas_call | solution.py:214
  63.8 5.1 %all-to-all-start.2 = ((bf16[8,32,768]{2,1,0:T(8,128)(2,1)}), bf16[8,32,768]{2,1,0:T(8,128)(2,1)S(1)}, u32[]{:S(2)}, u32[]{:S(2)}) async-start(bf16[8,32,768]{2,1,0:T(8,128)(2,1)} %mix.1), calls=%async_computation.2 | async-start | bytes 786432 | tf_op jit(solution)/shard_map/all_to_all | solution.py:917
  68.9 5.1 %turn.1 = (bf16[32,96,512]{2,1,0:T(8,128)(2,1)S(1)}, bf16[32,48,128]{2,1,0:T(8,128)(2,1)}, bf16[192,192]{1,0:T(8,128)(2,1)}, bf16[192,192]{1,0:T(8,128)(2,1)}) custom-call(s32[2]{0:T(128)} %pad_add_fusion.ids_ref, bf16[32,96,512]{2,1,0:T(8,128)(2,1)S(1)} %unpack.1.pq_ref, bf16[8,32,384]{2,1,0:T(8,128)(2,1)} %all-to-all-done.xa, ...), custom_call_target="tpu_custom_call", output_to_operand_aliasing={{0}: (1, {})} | custom-call | flops 1 | bytes 1 | tf_op jit(solution)/shard_map/turn/pallas_call | solution.py:466
  74.0 7.4 %all-to-all-done.2.refs_4_ = bf16[8,32,768]{2,1,0:T(8,128)(2,1)S(1)} async-done(((bf16[8,32,768]{2,1,0:T(8,128)(2,1)}), bf16[8,32,768]{2,1,0:T(8,128)(2,1)S(1)}, u32[]{:S(2)}, u32[]{:S(2)}) %all-to-all-start.2) | async-done | bytes 393248 | tf_op jit(solution)/shard_map/all_to_all | solution.py:917
  81.4 11.5 %pixels.1 = (bf16[8,1,48,4096]{3,2,1,0:T(8,128)(2,1)}, bf16[2,1,48,4096]{3,2,1,0:T(8,128)(2,1)}, bf16[2,1,48,4096]{3,2,1,0:T(8,128)(2,1)}, bf16[2,1,48,4096]{3,2...) custom-call(s32[2]{0:T(128)} %pad_add_fusion.ids_ref, ...), custom_call_target="tpu_custom_call", output_to_operand_aliasing={{5}: (9, {})} | custom-call | flops 1 | bytes 1 | tf_op jit(solution)/shard_map/pixels/pallas_call | solution.py:611
  94.4 6.0 %pixel_grads.1 = (bf16[384,4096]{1,0:T(8,128)(2,1)}, bf16[8,32,768]{2,1,0:T(8,128)(2,1)}, bf16[32,96,512]{2,1,0:T(8,128)(2,1)S(1)}) custom-call(s32[2]{0:T(128)} %pad_add_fusion.ids_ref, bf16[8,1,48,4096]{3,2,1,0:T(8,128)(2,1)} %cot_ref.5, bf16[2,1,48,4096]{3,2,1,0:T(8,128)(2,1)} %collective-permute-done.8.refs_1_, ...), custom_call_target="tpu_custom_call", output_to_operand_aliasing={{2}: (8, {})} | custom-call | flops 1 | bytes 1 | tf_op jit(solution)/shard_map/pixel_grads/pallas_call | solution.py:675
  106.0 5.0 %lin_grads.1.lin_ref = f32[4,48,48]{2,1,0:T(8,128)} custom-call(s32[2]{0:T(128)} %pad_add_fusion.ids_ref, f32[2]{0:T(128)} %dynamic_slice.21.inv_ref, bf16[8,1,48,4096]{3,2,1,0:T(8,128)(2,1)} %refs_0_.6, bf16[2,1,48,4096]{3,2,1,0:T(8,128)(2,1)} %collective-permute-done.refs_0_.refs_1_, bf16[2,1,48,4096]{3,2,1,0:T(8,128)(2,1)} %collective-permute-done.1.refs_1_.refs_2_, ...), custom_call_target="tpu_custom_call" | custom-call | flops 1 | bytes 1 | tf_op jit(solution)/shard_map/lin_grads/pallas_call | solution.py:725
  111.0 5.3 %all-to-all-done.3.g_ref = bf16[8,32,768]{2,1,0:T(8,128)(2,1)S(1)} async-done(((bf16[8,32,768]{2,1,0:T(8,128)(2,1)}), bf16[8,32,768]{2,1,0:T(8,128)(2,1)S(1)}, u32[]{:S(2)}, u32[]{:S(2)}) %all-to-all-start.3) | async-done | bytes 393248 | tf_op jit(solution)/shard_map/all_to_all | solution.py:917
  118.7 3.7 %all-to-all-start.4 = ((bf16[8,32,768]{2,1,0:T(8,128)(2,1)}), bf16[8,32,768]{2,1,0:T(8,128)(2,1)S(1)}, u32[]{:S(2)}, u32[]{:S(2)}) async-start(bf16[8,32,768]{2,1,0:T(8,128)(2,1)} %mix_back.1), calls=%async_computation.4 | async-start | bytes 786432 | tf_op jit(solution)/shard_map/all_to_all | solution.py:917
  122.4 4.9 %weight_grads.1 = (bf16[48,3200]{1,0:T(8,128)(2,1)}, bf16[48,3200]{1,0:T(8,128)(2,1)}, bf16[48,3200]{1,0:T(8,128)(2,1)}, bf16[48,3200]{1,0:T(8,128)(2,1)}) custom-call(s32[2]{0:T(128)} %pad_add_fusion.ids_ref, bf16[32,48,128]{2,1,0:T(8,128)(2,1)} %get-tuple-element.78.xt_ref, bf16[8,32,768]{2,1,0:T(8,128)(2,1)S(1)} %all-to-all-done.3.g_ref, ...), custom_call_target="tpu_custom_call" | custom-call | flops 1 | bytes 1 | tf_op jit(solution)/shard_map/weight_grads/pallas_call | solution.py:534
  130.8 3.9 %all-to-all-done.4.y_ref = bf16[8,32,768]{2,1,0:T(8,128)(2,1)S(1)} async-done(((bf16[8,32,768]{2,1,0:T(8,128)(2,1)}), bf16[8,32,768]{2,1,0:T(8,128)(2,1)S(1)}, u32[]{:S(2)}, u32[]{:S(2)}) %all-to-all-start.4) | async-done | bytes 393248 | tf_op jit(solution)/shard_map/all_to_all | solution.py:917
  134.7 6.8 %inner_grads.1 = (f32[8,1,48,4096]{3,2,1,0:T(8,128)}, bf16[2,1,48,4096]{3,2,1,0:T(8,128)(2,1)}, bf16[2,1,48,4096]{3,2,1,0:T(8,128)(2,1)}, bf16[2,1,48,4096]{3,2,1,0:T(8,128)(2,1)}) custom-call(s32[2]{0:T(128)} %pad_add_fusion.ids_ref, f32[2]{0:T(128)} %dynamic_slice.21.inv_ref, bf16[8,32,768]{2,1,0:T(8,128)(2,1)S(1)} %all-to-all-done.4.y_ref, ...), custom_call_target="tpu_custom_call" | custom-call | flops 1 | bytes 1 | tf_op jit(solution)/shard_map/inner_grads/pallas_call | solution.py:767
  145.1 6.1 %place.1 = bf16[8,1,48,4096]{3,2,1,0:T(8,128)(2,1)} custom-call(s32[2]{0:T(128)S(1)} %copy-done.8, bf16[2,1,48,4096]{3,2,1,0:T(8,128)(2,1)} %collective-permute-done.6.a_ref, bf16[2,1,48,4096]{3,2,1,0:T(8,128)(2,1)} %collective-permute-done.7.b_ref, bf16[2,1,48,4096]{3,2,1,0:T(8,128)(2,1)} %collective-permute-done.11.c_ref, ...), custom_call_target="tpu_custom_call", output_to_operand_aliasing={{}: (4, {})} | custom-call | flops 1 | bytes 1 | tf_op jit(solution)/shard_map/place/pallas_call | solution.py:807
  152.5 10.1 %collective-permute-start.19 = (f32[48,48]{1,0:T(8,128)S(1)}, f32[48,48]{1,0:T(8,128)S(1)}, u32[]{:S(2)}, u32[]{:S(2)}) collective-permute-start(f32[48,48]{1,0:T(8,128)S(1)} %add.171), channel_id=1, source_target_pairs={{0,2},{1,3},{2,0},{3,1},{4,6},{5,7},{6,4},{7,5},{8,10},{9,11},{10,... | collective-permute-start | bytes 27656 | tf_op jit(solution)/shard_map/ppermute | solution.py:913
  167.4 3.8 %adam.1 = (f32[1,32,2,48,48]{4,3,2,1,0:T(8,128)}, f32[1,32,2,48,48]{4,3,2,1,0:T(8,128)}, f32[1,32,2,48,48]{4,3,2,1,0:T(8,128)}) custom-call(f32[4]{0:T(128)S(1)} %pad_maximum_fusion.1.flips, bf16[48,3200]{1,0:T(8,128)(2,1)S(1)} %copy-done.7, bf16[48,3200]{1,0:T(8,128)(2,1)S(1)} %collective-permute-done.15.d1, ...), custom_call_target="tpu_custom_call" | custom-call | flops 1 | bytes 1 | tf_op jit(solution)/shard_map/adam/pallas_call | solution.py:900
  173.7 5.0 %collective-permute-done.12.refs_0_ = bf16[2,1,48,4096]{3,2,1,0:T(8,128)(2,1)S(1)} collective-permute-done((bf16[2,1,48,4096]{3,2,1,0:T(8,128)(2,1)}, bf16[2,1,48,4096]{3,2,1,0:T(8,128)(2,1)S(1)}, u32[]{:S(2)}, u32[]{:S(2)}) %collective-permute-start.12) | collective-permute-done | bytes 786464 | tf_op jit(solution)/shard_map/ppermute | solution.py:913
  (93 shorter events, 50.1 us)
Async XLA Ops:
  2.7 22.6 %collective-permute-start.2 = (bf16[2,1,48,4096]{3,2,1,0:T(8,128)(2,1)}, bf16[2,1,48,4096]{3,2,1,0:T(8,128)(2,1)}, u32[]{:S(2)}, u32[]{:S(2)}) collective-permute-start(bf16[2,1,48,4096]{3,2,1,0:T(8,128)(2,1)} %constant_dynamic-slice_fusion.5), channel_id=1, source_target_pairs={{0,24},{8,16},{16,8},{24,0},{1,25},{9,17},{17,9},{25,1},{2,26},{10... | collective-permute-start | bytes 2359304 | tf_op jit(solution)/shard_map/ppermute | solution.py:913
  8.7 34.1 %collective-permute-start = (bf16[2,1,48,4096]{3,2,1,0:T(8,128)(2,1)}, bf16[2,1,48,4096]{3,2,1,0:T(8,128)(2,1)}, u32[]{:S(2)}, u32[]{:S(2)}) collective-permute-start(bf16[2,1,48,4096]{3,2,1,0:T(8,128)(2,1)} %constant_dynamic-slice_fusion.4), channel_id=1, source_target_pairs={{0,8},{8,0},{16,24},{24,16},{1,9},{9,1},{17,25},{25,17},{2,10},{10... | collective-permute-start | bytes 2359304 | tf_op jit(solution)/shard_map/ppermute | solution.py:913
  13.3 29.4 %collective-permute-start.1 = (bf16[2,1,48,4096]{3,2,1,0:T(8,128)(2,1)}, bf16[2,1,48,4096]{3,2,1,0:T(8,128)(2,1)}, u32[]{:S(2)}, u32[]{:S(2)}) collective-permute-start(bf16[2,1,48,4096]{3,2,1,0:T(8,128)(2,1)} %constant_dynamic-slice_fusion.3), channel_id=1, source_target_pairs={{0,16},{8,24},{16,0},{24,8},{1,17},{9,25},{17,1},{25,9},{2,18},{10... | collective-permute-start | bytes 2359304 | tf_op jit(solution)/shard_map/ppermute | solution.py:913
  29.7 17.4 %all-to-all-start = ((bf16[8,32,384]{2,1,0:T(8,128)(2,1)}), bf16[8,32,384]{2,1,0:T(8,128)(2,1)}, u32[]{:S(2)}, u32[]{:S(2)}) async-start(bf16[8,32,384]{2,1,0:T(8,128)(2,1)} %forward.2), calls=%async_computation | async-start | bytes 393216 | tf_op jit(solution)/shard_map/all_to_all | solution.py:917
  35.1 20.4 %collective-permute-start.3 = (bf16[48,3200]{1,0:T(8,128)(2,1)S(1)}, bf16[48,3200]{1,0:T(8,128)(2,1)}, u32[]{:S(2)}, u32[]{:S(2)}) collective-permute-start(bf16[48,3200]{1,0:T(8,128)(2,1)S(1)} %pack.1.w0.l0), channel_id=1, source_target_pairs={{0,8},{8,0},{16,24},{24,16},{1,9},{9,1},{17,25},{25,17},{2,10},{10... | collective-permute-start | bytes 921608 | tf_op jit(solution)/shard_map/ppermute | solution.py:913
  36.5 20.4 %collective-permute-start.4 = (bf16[48,3200]{1,0:T(8,128)(2,1)S(1)}, bf16[48,3200]{1,0:T(8,128)(2,1)}, u32[]{:S(2)}, u32[]{:S(2)}) collective-permute-start(bf16[48,3200]{1,0:T(8,128)(2,1)S(1)} %pack.1.w0.l0), channel_id=1, source_target_pairs={{0,16},{8,24},{16,0},{24,8},{1,17},{9,25},{17,1},{25,9},{2,18},{10... | collective-permute-start | bytes 921608 | tf_op jit(solution)/shard_map/ppermute | solution.py:913
  38.1 18.9 %collective-permute-start.5 = (bf16[48,3200]{1,0:T(8,128)(2,1)S(1)}, bf16[48,3200]{1,0:T(8,128)(2,1)}, u32[]{:S(2)}, u32[]{:S(2)}) collective-permute-start(bf16[48,3200]{1,0:T(8,128)(2,1)S(1)} %pack.1.w0.l0), channel_id=1, source_target_pairs={{0,24},{8,16},{16,8},{24,0},{1,25},{9,17},{17,9},{25,1},{2,26},{10... | collective-permute-start | bytes 921608 | tf_op jit(solution)/shard_map/ppermute | solution.py:913
  47.1 13.9 %all-to-all-start.1 = ((bf16[8,32,384]{2,1,0:T(8,128)(2,1)}), bf16[8,32,384]{2,1,0:T(8,128)(2,1)}, u32[]{:S(2)}, u32[]{:S(2)}) async-start(bf16[8,32,384]{2,1,0:T(8,128)(2,1)} %forward.3), calls=%async_computation.1 | async-start | bytes 393216 | tf_op jit(solution)/shard_map/all_to_all | solution.py:917
  53.4 39.5 %collective-permute-start.8 = (bf16[2,1,48,4096]{3,2,1,0:T(8,128)(2,1)}, bf16[2,1,48,4096]{3,2,1,0:T(8,128)(2,1)}, u32[]{:S(2)}, u32[]{:S(2)}) collective-permute-start(bf16[2,1,48,4096]{3,2,1,0:T(8,128)(2,1)} %get-tuple-element.66), channel_id=1, source_target_pairs={{0,8},{8,0},{16,24},{24,16},{1,9},{9,1},{17,25},{25,17},{2,10},{10... | collective-permute-start | bytes 2359304 | tf_op jit(solution)/shard_map/ppermute | solution.py:913
  54.9 38.0 %collective-permute-start.9 = (bf16[2,1,48,4096]{3,2,1,0:T(8,128)(2,1)}, bf16[2,1,48,4096]{3,2,1,0:T(8,128)(2,1)}, u32[]{:S(2)}, u32[]{:S(2)}) collective-permute-start(bf16[2,1,48,4096]{3,2,1,0:T(8,128)(2,1)} %get-tuple-element.67), channel_id=1, source_target_pairs={{0,16},{8,24},{16,0},{24,8},{1,17},{9,25},{17,1},{25,9},{2,18},{10... | collective-permute-start | bytes 2359304 | tf_op jit(solution)/shard_map/ppermute | solution.py:913
  55.4 37.5 %collective-permute-start.10 = (bf16[2,1,48,4096]{3,2,1,0:T(8,128)(2,1)}, bf16[2,1,48,4096]{3,2,1,0:T(8,128)(2,1)}, u32[]{:S(2)}, u32[]{:S(2)}) collective-permute-start(bf16[2,1,48,4096]{3,2,1,0:T(8,128)(2,1)} %get-tuple-element.68), channel_id=1, source_target_pairs={{0,24},{8,16},{16,8},{24,0},{1,25},{9,17},{17,9},{25,1},{2,26},{10... | collective-permute-start | bytes 2359304 | tf_op jit(solution)/shard_map/ppermute | solution.py:913
  63.8 17.6 %all-to-all-start.2 = ((bf16[8,32,768]{2,1,0:T(8,128)(2,1)}), bf16[8,32,768]{2,1,0:T(8,128)(2,1)S(1)}, u32[]{:S(2)}, u32[]{:S(2)}) async-start(bf16[8,32,768]{2,1,0:T(8,128)(2,1)} %mix.1), calls=%async_computation.2 | async-start | bytes 786432 | tf_op jit(solution)/shard_map/all_to_all | solution.py:917
  92.9 23.4 %collective-permute-start.11 = (bf16[2,1,48,4096]{3,2,1,0:T(8,128)(2,1)}, bf16[2,1,48,4096]{3,2,1,0:T(8,128)(2,1)}, u32[]{:S(2)}, u32[]{:S(2)}) collective-permute-start(bf16[2,1,48,4096]{3,2,1,0:T(8,128)(2,1)} %get-tuple-element.69), channel_id=1, source_target_pairs={{0,24},{8,16},{16,8},{24,0},{1,25},{9,17},{17,9},{25,1},{2,26},{10... | collective-permute-start | bytes 2359304 | tf_op jit(solution)/shard_map/ppermute | solution.py:913
  100.4 15.9 %all-to-all-start.3 = ((bf16[8,32,768]{2,1,0:T(8,128)(2,1)}), bf16[8,32,768]{2,1,0:T(8,128)(2,1)S(1)}, u32[]{:S(2)}, u32[]{:S(2)}) async-start(bf16[8,32,768]{2,1,0:T(8,128)(2,1)} %get-tuple-element.77), calls=%async_computation.3 | async-start | bytes 786432 | tf_op jit(solution)/shard_map/all_to_all | solution.py:917
  103.9 37.6 %collective-permute-start.6 = (bf16[2,1,48,4096]{3,2,1,0:T(8,128)(2,1)}, bf16[2,1,48,4096]{3,2,1,0:T(8,128)(2,1)}, u32[]{:S(2)}, u32[]{:S(2)}) collective-permute-start(bf16[2,1,48,4096]{3,2,1,0:T(8,128)(2,1)} %get-tuple-element.63), channel_id=1, source_target_pairs={{0,8},{8,0},{16,24},{24,16},{1,9},{9,1},{17,25},{25,17},{2,10},{10... | collective-permute-start | bytes 2359304 | tf_op jit(solution)/shard_map/ppermute | solution.py:913
  104.5 37.0 %collective-permute-start.7 = (bf16[2,1,48,4096]{3,2,1,0:T(8,128)(2,1)}, bf16[2,1,48,4096]{3,2,1,0:T(8,128)(2,1)}, u32[]{:S(2)}, u32[]{:S(2)}) collective-permute-start(bf16[2,1,48,4096]{3,2,1,0:T(8,128)(2,1)} %get-tuple-element.64), channel_id=1, source_target_pairs={{0,16},{8,24},{16,0},{24,8},{1,17},{9,25},{17,1},{25,9},{2,18},{10... | collective-permute-start | bytes 2359304 | tf_op jit(solution)/shard_map/ppermute | solution.py:913
  118.7 15.9 %all-to-all-start.4 = ((bf16[8,32,768]{2,1,0:T(8,128)(2,1)}), bf16[8,32,768]{2,1,0:T(8,128)(2,1)S(1)}, u32[]{:S(2)}, u32[]{:S(2)}) async-start(bf16[8,32,768]{2,1,0:T(8,128)(2,1)} %mix_back.1), calls=%async_computation.4 | async-start | bytes 786432 | tf_op jit(solution)/shard_map/all_to_all | solution.py:917
  127.3 17.2 %collective-permute-start.15 = (bf16[48,3200]{1,0:T(8,128)(2,1)}, bf16[48,3200]{1,0:T(8,128)(2,1)S(1)}, u32[]{:S(2)}, u32[]{:S(2)}) collective-permute-start(bf16[48,3200]{1,0:T(8,128)(2,1)} %get-tuple-element.92), channel_id=1, source_target_pairs={{0,8},{8,0},{16,24},{24,16},{1,9},{9,1},{17,25},{25,17},{2,10},{10... | collective-permute-start | bytes 921608 | tf_op jit(solution)/shard_map/ppermute | solution.py:913
  128.0 23.2 %collective-permute-start.16 = (bf16[48,3200]{1,0:T(8,128)(2,1)}, bf16[48,3200]{1,0:T(8,128)(2,1)S(1)}, u32[]{:S(2)}, u32[]{:S(2)}) collective-permute-start(bf16[48,3200]{1,0:T(8,128)(2,1)} %get-tuple-element.93), channel_id=1, source_target_pairs={{0,16},{8,24},{16,0},{24,8},{1,17},{9,25},{17,1},{25,9},{2,18},{10... | collective-permute-start | bytes 921608 | tf_op jit(solution)/shard_map/ppermute | solution.py:913
  129.5 21.7 %collective-permute-start.17 = (bf16[48,3200]{1,0:T(8,128)(2,1)}, bf16[48,3200]{1,0:T(8,128)(2,1)S(1)}, u32[]{:S(2)}, u32[]{:S(2)}) collective-permute-start(bf16[48,3200]{1,0:T(8,128)(2,1)} %get-tuple-element.94), channel_id=1, source_target_pairs={{0,24},{8,16},{16,8},{24,0},{1,25},{9,17},{17,9},{25,1},{2,26},{10... | collective-permute-start | bytes 921608 | tf_op jit(solution)/shard_map/ppermute | solution.py:913
  141.5 30.4 %collective-permute-start.14 = (bf16[2,1,48,4096]{3,2,1,0:T(8,128)(2,1)}, bf16[2,1,48,4096]{3,2,1,0:T(8,128)(2,1)S(1)}, u32[]{:S(2)}, u32[]{:S(2)}) collective-permute-start(bf16[2,1,48,4096]{3,2,1,0:T(8,128)(2,1)} %get-tuple-element.89), channel_id=1, source_target_pairs={{0,24},{8,16},{16,8},{24,0},{1,25},{9,17},{17,9},{25,1},{2,26},{10... | collective-permute-start | bytes 2359304 | tf_op jit(solution)/shard_map/ppermute | solution.py:913
  143.2 35.5 %collective-permute-start.12 = (bf16[2,1,48,4096]{3,2,1,0:T(8,128)(2,1)}, bf16[2,1,48,4096]{3,2,1,0:T(8,128)(2,1)S(1)}, u32[]{:S(2)}, u32[]{:S(2)}) collective-permute-start(bf16[2,1,48,4096]{3,2,1,0:T(8,128)(2,1)} %get-tuple-element.87), channel_id=1, source_target_pairs={{0,8},{8,0},{16,24},{24,16},{1,9},{9,1},{17,25},{25,17},{2,10},{10... | collective-permute-start | bytes 2359304 | tf_op jit(solution)/shard_map/ppermute | solution.py:913
  144.5 34.2 %collective-permute-start.13 = (bf16[2,1,48,4096]{3,2,1,0:T(8,128)(2,1)}, bf16[2,1,48,4096]{3,2,1,0:T(8,128)(2,1)S(1)}, u32[]{:S(2)}, u32[]{:S(2)}) collective-permute-start(bf16[2,1,48,4096]{3,2,1,0:T(8,128)(2,1)} %get-tuple-element.88), channel_id=1, source_target_pairs={{0,16},{8,24},{16,0},{24,8},{1,17},{9,25},{17,1},{25,9},{2,18},{10... | collective-permute-start | bytes 2359304 | tf_op jit(solution)/shard_map/ppermute | solution.py:913
  152.5 11.9 %collective-permute-start.19 = (f32[48,48]{1,0:T(8,128)S(1)}, f32[48,48]{1,0:T(8,128)S(1)}, u32[]{:S(2)}, u32[]{:S(2)}) collective-permute-start(f32[48,48]{1,0:T(8,128)S(1)} %add.171), channel_id=1, source_target_pairs={{0,2},{1,3},{2,0},{3,1},{4,6},{5,7},{6,4},{7,5},{8,10},{9,11},{10,... | collective-permute-start | bytes 27656 | tf_op jit(solution)/shard_map/ppermute | solution.py:913
  (17 other events, 259.4 us)

commit v10 on v9

--- a/solution.py
+++ b/solution.py
@@ -691,7 +691,7 @@
 
 def lin_kernel(ids_ref, inv_ref, *refs):
     x = refs[:4]
-    g_ref, lin_ref, lacc = refs[4:]
+    g_ref, lb_ref, lin_ref, back_ref, lacc = refs[4:]
     samples = x[1].shape[0]
     rows = 4 * C
 
@@ -703,6 +703,7 @@
         fields = jnp.concatenate([x[t][s, 0] for t in range(4)], axis=0)
         g = g_ref[s * rows : (s + 1) * rows]
         lacc[...] += dot(fields, g, ((1,), (1,))) * inv_ref[s]
+        back_ref[s * rows : (s + 1) * rows] = dot(lb_ref[...], g).astype(BF16)
 
     @pl.when(pl.program_id(0) == pl.num_programs(0) - 1)
     def _():
@@ -715,7 +716,7 @@
             lin_ref[k] = total
 
 
-def lin_grads(ids, inv, x, g):
+def lin_grads(ids, inv, x, g, lb):
     rows = g.shape[0]
     samples = rows // (4 * C)
     tile = 2048
@@ -727,18 +728,18 @@
         grid_spec=pltpu.PrefetchScalarGridSpec(
             num_scalar_prefetch=2,
             grid=(NPIX // tile,),
-            in_specs=[mine] + [block] * 3 + [flat],
-            out_specs=whole((4, C, C)),
+            in_specs=[mine] + [block] * 3 + [flat, whole((4 * C, 4 * C))],
+            out_specs=[whole((4, C, C)), flat],
             scratch_shapes=[pltpu.VMEM((4 * C, 4 * C), F32)],
         ),
-        out_shape=slow((4, C, C), F32),
+        out_shape=[slow((4, C, C), F32), slow(g.shape, BF16)],
         compiler_params=params(28),
         cost_estimate=cost(),
         name="lin_grads",
-    )(*stay(ids, inv, *x, g))
-
-
-def inner_kernel(ids_ref, inv_ref, y_ref, g_ref, row_ref, col_ref, lb_ref, cot_ref, mine_ref, *refs):
+    )(*stay(ids, inv, *x, g, lb))
+
+
+def inner_kernel(ids_ref, inv_ref, y_ref, back_ref, row_ref, col_ref, cot_ref, mine_ref, *refs):
     o1, o2, o3, ysc = refs
     samples = cot_ref.shape[0]
     rows = 4 * C
@@ -751,13 +752,13 @@
     spatial = dot(ysc[...], table, ((1,), (1,)))
     for s in range(samples):
         at = slice(s * rows, (s + 1) * rows)
-        total = spatial[at] + dot(lb_ref[...], g_ref[at])
+        total = spatial[at] + back_ref[at].astype(F32)
         mine_ref[s, 0] = (cot_ref[s, 0].astype(F32) + total[:C]) * inv_ref[s]
         for t, out in ((1, o1), (2, o2), (3, o3)):
             out[s, 0] = total[t * C : (t + 1) * C].astype(BF16)
 
 
-def inner_grads(ids, inv, y, g, small, lb, cotangent):
+def inner_grads(ids, inv, y, back, small, cotangent):
     samples = inv.shape[0]
     n = 2 * MODES
     tile = 2048
@@ -773,7 +774,6 @@
                 whole(y.shape),
                 pl.BlockSpec((rows, tile), lambda i, ids, inv: (0, i)),
                 *small_specs(tile),
-                whole((4 * C, 4 * C)),
                 mine,
             ],
             out_specs=[mine] + [block] * 3,
@@ -783,7 +783,7 @@
         compiler_params=params(28),
         cost_estimate=cost(),
         name="inner_grads",
-    )(*stay(ids, inv), y, *stay(g, small, small, lb, cotangent))
+    )(*stay(ids, inv), y, *stay(back, small, small, cotangent))
 
 
 def place_kernel(ids_ref, a_ref, b_ref, c_ref, old_ref, out_ref):
@@ -983,14 +983,14 @@
     out_parts = [swap(parts[t - 1], "blade", 4, t) for t in (1, 2, 3)]
 
     grad_pre, sent, pq = pixel_grads(ids, cot, slope, small, y.shape, pq)
-    lin = lin_grads(ids, inv, x, grad_pre)
+    lin, from_lin = lin_grads(ids, inv, x, grad_pre, lb)
     g = after(to_modes(sent), (out_parts[2], xt, pq, lin))
     mixed = mix_back(ids, g, pq)
     back = to_modes(mixed)
     spec_grads = weight_grads(ids, xt, g, lin)
     spec_grads = [spec_grads[0]] + [swap(spec_grads[t], "blade", 4, t) for t in (1, 2, 3)]
 
-    inner = inner_grads(ids, inv, back, grad_pre, small, lb, cotangent)
+    inner = inner_grads(ids, inv, back, from_lin, small, cotangent)
     inner = after(inner, out_parts)
     grad_parts = [swap(inner[t], "blade", 4, t) for t in (1, 2, 3)]
 

time: 183 us -> 182 us (level)
  no operation moved by 1% of the time
where the time goes in v10:
time: 182 us; the launch traced here: 181 us
  Pallas kernels  79 us (43%)
  starting transfers between devices  58.1 us (32%)
  waiting for transfers between devices  31.1 us (17%)
  local copies, waits for them, and re-layouts  8.6 us (5%)
  other arithmetic  3.45 us (2%)
    ppermute x21, starting transfers between devices, swap(): return lax.ppermute(value, axis, [(i, i ^ x) for i in range(size)])  35.5 us
    all_to_all x5, starting transfers between devices, to_modes(): return lax.all_to_all(value, 'dp', split_axis=0, concat_axis=0, tiled=True)  22.5 us
    ppermute x21, waiting for transfers between devices, swap(): return lax.ppermute(value, axis, [(i, i ^ x) for i in range(size)])  15.7 us
    all_to_all x5, waiting for transfers between devices, to_modes(): return lax.all_to_all(value, 'dp', split_axis=0, concat_axis=0, tiled=True)  15.4 us
    pallas_call x1, Pallas kernels, pixels(): pl.pallas_call(pixel_kernel, grid_spec=pltpu.PrefetchScalarGridSpec(num_s...  11.5 us
    pallas_call x2, Pallas kernels, forward_spectrum(): pl.pallas_call(forward_kernel, grid_spec=pltpu.PrefetchScalarGridSpec(num...  8.63 us
    dynamic_slice x4, local copies, waits for them, and re-layouts, cut(): lax.dynamic_slice_in_dim(array, jnp.bitwise_xor(own, t) * samples, sample...  7.92 us
    pallas_call x1, Pallas kernels, lin_grads(): pl.pallas_call(lin_kernel, grid_spec=pltpu.PrefetchScalarGridSpec(num_sca...  6.32 us
  transfers between devices with their start and end apart: 26, of which 8 were waited for; matrix products, arithmetic and copies ran while one was open for 5% of the time, Pallas kernels for 42%

profile of v10, /device:TPU:0, one launch (start us, length us, event | category | flops | bytes accessed | tf_op | source)
XLA Modules:
  0.0 181.0 jit_solution(10500729332266647607)
XLA Ops:
  2.7 3.9 %collective-permute-start.2 = (bf16[2,1,48,4096]{3,2,1,0:T(8,128)(2,1)}, bf16[2,1,48,4096]{3,2,1,0:T(8,128)(2,1)}, u32[]{:S(2)}, u32[]{:S(2)}) collective-permute-start(bf16[2,1,48,4096]{3,2,1,0:T(8,128)(2,1)} %constant_dynamic-slice_fusion.5), channel_id=1, source_target_pairs={{0,24},{8,16},{16,8},{24,0},{1,25},{9,17},{17,9},{25,1},{2,26},{10... | collective-permute-start | bytes 2359304 | tf_op jit(solution)/shard_map/ppermute | solution.py:913
  13.4 5.9 %turned.1.refs_5_ = bf16[512,4096]{1,0:T(8,128)(2,1)} custom-call(f32[4,64,512]{2,1,0:T(8,128)} %pad_maximum_fusion.row_ref.col_ref.refs_2_.refs_3_.refs_5_.refs_6_, f32[4,64,512]{2,1,0:T(8,128)} %pad_maximum_fusion.row_ref.col_ref.refs_2_.refs_3_.refs_5_.refs_6_), custom_call_target="tpu_custom_call" | custom-call | flops 1 | bytes 1 | tf_op jit(solution)/shard_map/turned/pallas_call | solution.py:125
  21.5 3.9 %collective-permute-done.2.refs_1_.refs_3_ = bf16[2,1,48,4096]{3,2,1,0:T(8,128)(2,1)} collective-permute-done((bf16[2,1,48,4096]{3,2,1,0:T(8,128)(2,1)}, bf16[2,1,48,4096]{3,2,1,0:T(8,128)(2,1)}, u32[]{:S(2)}, u32[]{:S(2)}) %collective-permute-start.2) | collective-permute-done | bytes 786464 | tf_op jit(solution)/shard_map/ppermute | solution.py:913
  25.3 4.3 %forward.2 = bf16[8,32,384]{2,1,0:T(8,128)(2,1)} custom-call(s32[2]{0:T(128)} %pad_add_fusion.ids_ref, f32[2]{0:T(128)} %dynamic_slice.21.inv_ref, bf16[8,1,48,4096]{3,2,1,0:T(8,128)(2,1)} %refs_0_.6, bf16[2,1,48,4096]{3,2,1,0:T(8,128)(2,1)} %collective-permute-done.2.refs_1_.refs_3_, ...), custom_call_target="tpu_custom_call" | custom-call | flops 1 | bytes 1 | tf_op jit(solution)/shard_map/forward/pallas_call | solution.py:281
  29.7 5.4 %all-to-all-start = ((bf16[8,32,384]{2,1,0:T(8,128)(2,1)}), bf16[8,32,384]{2,1,0:T(8,128)(2,1)}, u32[]{:S(2)}, u32[]{:S(2)}) async-start(bf16[8,32,384]{2,1,0:T(8,128)(2,1)} %forward.2), calls=%async_computation | async-start | bytes 393216 | tf_op jit(solution)/shard_map/all_to_all | solution.py:917
  38.6 4.2 %collective-permute-done.refs_0_.refs_1_ = bf16[2,1,48,4096]{3,2,1,0:T(8,128)(2,1)} collective-permute-done((bf16[2,1,48,4096]{3,2,1,0:T(8,128)(2,1)}, bf16[2,1,48,4096]{3,2,1,0:T(8,128)(2,1)}, u32[]{:S(2)}, u32[]{:S(2)}) %collective-permute-start) | collective-permute-done | bytes 786464 | tf_op jit(solution)/shard_map/ppermute | solution.py:913
  42.8 4.3 %forward.3 = bf16[8,32,384]{2,1,0:T(8,128)(2,1)} custom-call(s32[2]{0:T(128)} %pad_add_fusion.ids_ref, f32[2]{0:T(128)} %dynamic_slice.21.inv_ref, bf16[2,1,48,4096]{3,2,1,0:T(8,128)(2,1)} %collective-permute-done.refs_0_.refs_1_, bf16[2,1,48,4096]{3,2,1,0:T(8,128)(2,1)} %collective-permute-done.1.refs_1_.refs_2_, ...), custom_call_target="tpu_custom_call" | custom-call | flops 1 | bytes 1 | tf_op jit(solution)/shard_map/forward/pallas_call | solution.py:281
  47.1 4.9 %all-to-all-start.1 = ((bf16[8,32,384]{2,1,0:T(8,128)(2,1)}), bf16[8,32,384]{2,1,0:T(8,128)(2,1)}, u32[]{:S(2)}, u32[]{:S(2)}) async-start(bf16[8,32,384]{2,1,0:T(8,128)(2,1)} %forward.3), calls=%async_computation.1 | async-start | bytes 393216 | tf_op jit(solution)/shard_map/all_to_all | solution.py:917
  57.1 4.1 %unpack.1.pq_ref = bf16[32,96,512]{2,1,0:T(8,128)(2,1)S(1)} custom-call(s32[2]{0:T(128)} %pad_add_fusion.ids_ref, bf16[48,3200]{1,0:T(8,128)(2,1)} %copy-done.4, bf16[48,3200]{1,0:T(8,128)(2,1)} %collective-permute-done.3.w1.l1, bf16[48,3200]{1,0:T(8,128)(2,1)} %collective-permute-done.4.w2.l2, bf16[48,3200]{1,0:T(8,128)(2,1)} %collective-permute-done.5.w3.l3), custom_call_target="tpu_custom_call" | custom-call | flops 1 | bytes 1 | tf_op jit(solution)/shard_map/unpack/pallas_call | solution.py:214
  63.9 5.1 %all-to-all-start.2 = ((bf16[8,32,768]{2,1,0:T(8,128)(2,1)}), bf16[8,32,768]{2,1,0:T(8,128)(2,1)S(1)}, u32[]{:S(2)}, u32[]{:S(2)}) async-start(bf16[8,32,768]{2,1,0:T(8,128)(2,1)} %mix.1), calls=%async_computation.2 | async-start | bytes 786432 | tf_op jit(solution)/shard_map/all_to_all | solution.py:917
  69.0 5.1 %turn.1 = (bf16[32,96,512]{2,1,0:T(8,128)(2,1)S(1)}, bf16[32,48,128]{2,1,0:T(8,128)(2,1)}, bf16[192,192]{1,0:T(8,128)(2,1)}, bf16[192,192]{1,0:T(8,128)(2,1)}) custom-call(s32[2]{0:T(128)} %pad_add_fusion.ids_ref, bf16[32,96,512]{2,1,0:T(8,128)(2,1)S(1)} %unpack.1.pq_ref, bf16[8,32,384]{2,1,0:T(8,128)(2,1)} %all-to-all-done.xa, ...), custom_call_target="tpu_custom_call", output_to_operand_aliasing={{0}: (1, {})} | custom-call | flops 1 | bytes 1 | tf_op jit(solution)/shard_map/turn/pallas_call | solution.py:466
  74.1 7.4 %all-to-all-done.2.refs_4_ = bf16[8,32,768]{2,1,0:T(8,128)(2,1)S(1)} async-done(((bf16[8,32,768]{2,1,0:T(8,128)(2,1)}), bf16[8,32,768]{2,1,0:T(8,128)(2,1)S(1)}, u32[]{:S(2)}, u32[]{:S(2)}) %all-to-all-start.2) | async-done | bytes 393248 | tf_op jit(solution)/shard_map/all_to_all | solution.py:917
  81.6 11.5 %pixels.1 = (bf16[8,1,48,4096]{3,2,1,0:T(8,128)(2,1)}, bf16[2,1,48,4096]{3,2,1,0:T(8,128)(2,1)}, bf16[2,1,48,4096]{3,2,1,0:T(8,128)(2,1)}, bf16[2,1,48,4096]{3,2...) custom-call(s32[2]{0:T(128)} %pad_add_fusion.ids_ref, ...), custom_call_target="tpu_custom_call", output_to_operand_aliasing={{5}: (9, {})} | custom-call | flops 1 | bytes 1 | tf_op jit(solution)/shard_map/pixels/pallas_call | solution.py:611
  94.6 6.0 %pixel_grads.1 = (bf16[384,4096]{1,0:T(8,128)(2,1)}, bf16[8,32,768]{2,1,0:T(8,128)(2,1)}, bf16[32,96,512]{2,1,0:T(8,128)(2,1)S(1)}) custom-call(s32[2]{0:T(128)} %pad_add_fusion.ids_ref, bf16[8,1,48,4096]{3,2,1,0:T(8,128)(2,1)} %cot_ref.5, bf16[2,1,48,4096]{3,2,1,0:T(8,128)(2,1)} %collective-permute-done.8.refs_1_, ...), custom_call_target="tpu_custom_call", output_to_operand_aliasing={{2}: (8, {})} | custom-call | flops 1 | bytes 1 | tf_op jit(solution)/shard_map/pixel_grads/pallas_call | solution.py:675
  106.1 6.3 %lin_grads.1 = (f32[4,48,48]{2,1,0:T(8,128)}, bf16[384,4096]{1,0:T(8,128)(2,1)}) custom-call(s32[2]{0:T(128)} %pad_add_fusion.ids_ref, f32[2]{0:T(128)} %dynamic_slice.21.inv_ref, bf16[8,1,48,4096]{3,2,1,0:T(8,128)(2,1)} %refs_0_.6, bf16[2,1,48,4096]{3,2,1,0:T(8,128)(2,1)} %collective-permute-done.refs_0_.refs_1_, ...), custom_call_target="tpu_custom_call" | custom-call | flops 1 | bytes 1 | tf_op jit(solution)/shard_map/lin_grads/pallas_call | solution.py:726
  112.5 4.0 %all-to-all-done.3.g_ref = bf16[8,32,768]{2,1,0:T(8,128)(2,1)S(1)} async-done(((bf16[8,32,768]{2,1,0:T(8,128)(2,1)}), bf16[8,32,768]{2,1,0:T(8,128)(2,1)S(1)}, u32[]{:S(2)}, u32[]{:S(2)}) %all-to-all-start.3) | async-done | bytes 393248 | tf_op jit(solution)/shard_map/all_to_all | solution.py:917
  118.9 3.7 %all-to-all-start.4 = ((bf16[8,32,768]{2,1,0:T(8,128)(2,1)}), bf16[8,32,768]{2,1,0:T(8,128)(2,1)S(1)}, u32[]{:S(2)}, u32[]{:S(2)}) async-start(bf16[8,32,768]{2,1,0:T(8,128)(2,1)} %mix_back.1), calls=%async_computation.4 | async-start | bytes 786432 | tf_op jit(solution)/shard_map/all_to_all | solution.py:917
  122.6 4.8 %weight_grads.1 = (bf16[48,3200]{1,0:T(8,128)(2,1)}, bf16[48,3200]{1,0:T(8,128)(2,1)}, bf16[48,3200]{1,0:T(8,128)(2,1)}, bf16[48,3200]{1,0:T(8,128)(2,1)}) custom-call(s32[2]{0:T(128)} %pad_add_fusion.ids_ref, bf16[32,48,128]{2,1,0:T(8,128)(2,1)} %get-tuple-element.80.xt_ref, bf16[8,32,768]{2,1,0:T(8,128)(2,1)S(1)} %all-to-all-done.3.g_ref, ...), custom_call_target="tpu_custom_call" | custom-call | flops 1 | bytes 1 | tf_op jit(solution)/shard_map/weight_grads/pallas_call | solution.py:534
  130.9 3.9 %all-to-all-done.4.y_ref = bf16[8,32,768]{2,1,0:T(8,128)(2,1)S(1)} async-done(((bf16[8,32,768]{2,1,0:T(8,128)(2,1)}), bf16[8,32,768]{2,1,0:T(8,128)(2,1)S(1)}, u32[]{:S(2)}, u32[]{:S(2)}) %all-to-all-start.4) | async-done | bytes 393248 | tf_op jit(solution)/shard_map/all_to_all | solution.py:917
  134.8 6.1 %inner_grads.1 = (f32[8,1,48,4096]{3,2,1,0:T(8,128)}, bf16[2,1,48,4096]{3,2,1,0:T(8,128)(2,1)}, bf16[2,1,48,4096]{3,2,1,0:T(8,128)(2,1)}, bf16[2,1,48,4096]{3,2,1,0:T(8,128)(2,1)}) custom-call(s32[2]{0:T(128)} %pad_add_fusion.ids_ref, f32[2]{0:T(128)} %dynamic_slice.21.inv_ref, bf16[8,32,768]{2,1,0:T(8,128)(2,1)S(1)} %all-to-all-done.4.y_ref, ...), custom_call_target="tpu_custom_call" | custom-call | flops 1 | bytes 1 | tf_op jit(solution)/shard_map/inner_grads/pallas_call | solution.py:768
  144.5 6.1 %place.1 = bf16[8,1,48,4096]{3,2,1,0:T(8,128)(2,1)} custom-call(s32[2]{0:T(128)S(1)} %copy-done.8, bf16[2,1,48,4096]{3,2,1,0:T(8,128)(2,1)} %collective-permute-done.6.a_ref, bf16[2,1,48,4096]{3,2,1,0:T(8,128)(2,1)} %collective-permute-done.7.b_ref, bf16[2,1,48,4096]{3,2,1,0:T(8,128)(2,1)} %collective-permute-done.11.c_ref, ...), custom_call_target="tpu_custom_call", output_to_operand_aliasing={{}: (4, {})} | custom-call | flops 1 | bytes 1 | tf_op jit(solution)/shard_map/place/pallas_call | solution.py:807
  152.0 10.4 %collective-permute-start.19 = (f32[48,48]{1,0:T(8,128)S(1)}, f32[48,48]{1,0:T(8,128)S(1)}, u32[]{:S(2)}, u32[]{:S(2)}) collective-permute-start(f32[48,48]{1,0:T(8,128)S(1)} %add.171), channel_id=1, source_target_pairs={{0,2},{1,3},{2,0},{3,1},{4,6},{5,7},{6,4},{7,5},{8,10},{9,11},{10,... | collective-permute-start | bytes 27656 | tf_op jit(solution)/shard_map/ppermute | solution.py:913
  167.3 3.8 %adam.1 = (f32[1,32,2,48,48]{4,3,2,1,0:T(8,128)}, f32[1,32,2,48,48]{4,3,2,1,0:T(8,128)}, f32[1,32,2,48,48]{4,3,2,1,0:T(8,128)}) custom-call(f32[4]{0:T(128)S(1)} %pad_maximum_fusion.1.flips, bf16[48,3200]{1,0:T(8,128)(2,1)S(1)} %copy-done.7, bf16[48,3200]{1,0:T(8,128)(2,1)S(1)} %collective-permute-done.15.d1, ...), custom_call_target="tpu_custom_call" | custom-call | flops 1 | bytes 1 | tf_op jit(solution)/shard_map/adam/pallas_call | solution.py:900
  173.6 4.6 %collective-permute-done.12.refs_0_ = bf16[2,1,48,4096]{3,2,1,0:T(8,128)(2,1)S(1)} collective-permute-done((bf16[2,1,48,4096]{3,2,1,0:T(8,128)(2,1)}, bf16[2,1,48,4096]{3,2,1,0:T(8,128)(2,1)S(1)}, u32[]{:S(2)}, u32[]{:S(2)}) %collective-permute-start.12) | collective-permute-done | bytes 786464 | tf_op jit(solution)/shard_map/ppermute | solution.py:913
  (93 shorter events, 50.3 us)
Async XLA Ops:
  2.7 22.6 %collective-permute-start.2 = (bf16[2,1,48,4096]{3,2,1,0:T(8,128)(2,1)}, bf16[2,1,48,4096]{3,2,1,0:T(8,128)(2,1)}, u32[]{:S(2)}, u32[]{:S(2)}) collective-permute-start(bf16[2,1,48,4096]{3,2,1,0:T(8,128)(2,1)} %constant_dynamic-slice_fusion.5), channel_id=1, source_target_pairs={{0,24},{8,16},{16,8},{24,0},{1,25},{9,17},{17,9},{25,1},{2,26},{10... | collective-permute-start | bytes 2359304 | tf_op jit(solution)/shard_map/ppermute | solution.py:913
  8.7 34.1 %collective-permute-start = (bf16[2,1,48,4096]{3,2,1,0:T(8,128)(2,1)}, bf16[2,1,48,4096]{3,2,1,0:T(8,128)(2,1)}, u32[]{:S(2)}, u32[]{:S(2)}) collective-permute-start(bf16[2,1,48,4096]{3,2,1,0:T(8,128)(2,1)} %constant_dynamic-slice_fusion.4), channel_id=1, source_target_pairs={{0,8},{8,0},{16,24},{24,16},{1,9},{9,1},{17,25},{25,17},{2,10},{10... | collective-permute-start | bytes 2359304 | tf_op jit(solution)/shard_map/ppermute | solution.py:913
  13.3 29.4 %collective-permute-start.1 = (bf16[2,1,48,4096]{3,2,1,0:T(8,128)(2,1)}, bf16[2,1,48,4096]{3,2,1,0:T(8,128)(2,1)}, u32[]{:S(2)}, u32[]{:S(2)}) collective-permute-start(bf16[2,1,48,4096]{3,2,1,0:T(8,128)(2,1)} %constant_dynamic-slice_fusion.3), channel_id=1, source_target_pairs={{0,16},{8,24},{16,0},{24,8},{1,17},{9,25},{17,1},{25,9},{2,18},{10... | collective-permute-start | bytes 2359304 | tf_op jit(solution)/shard_map/ppermute | solution.py:913
  29.7 17.4 %all-to-all-start = ((bf16[8,32,384]{2,1,0:T(8,128)(2,1)}), bf16[8,32,384]{2,1,0:T(8,128)(2,1)}, u32[]{:S(2)}, u32[]{:S(2)}) async-start(bf16[8,32,384]{2,1,0:T(8,128)(2,1)} %forward.2), calls=%async_computation | async-start | bytes 393216 | tf_op jit(solution)/shard_map/all_to_all | solution.py:917
  35.1 20.5 %collective-permute-start.3 = (bf16[48,3200]{1,0:T(8,128)(2,1)S(1)}, bf16[48,3200]{1,0:T(8,128)(2,1)}, u32[]{:S(2)}, u32[]{:S(2)}) collective-permute-start(bf16[48,3200]{1,0:T(8,128)(2,1)S(1)} %pack.1.w0.l0), channel_id=1, source_target_pairs={{0,8},{8,0},{16,24},{24,16},{1,9},{9,1},{17,25},{25,17},{2,10},{10... | collective-permute-start | bytes 921608 | tf_op jit(solution)/shard_map/ppermute | solution.py:913
  36.5 20.5 %collective-permute-start.4 = (bf16[48,3200]{1,0:T(8,128)(2,1)S(1)}, bf16[48,3200]{1,0:T(8,128)(2,1)}, u32[]{:S(2)}, u32[]{:S(2)}) collective-permute-start(bf16[48,3200]{1,0:T(8,128)(2,1)S(1)} %pack.1.w0.l0), channel_id=1, source_target_pairs={{0,16},{8,24},{16,0},{24,8},{1,17},{9,25},{17,1},{25,9},{2,18},{10... | collective-permute-start | bytes 921608 | tf_op jit(solution)/shard_map/ppermute | solution.py:913
  38.1 19.0 %collective-permute-start.5 = (bf16[48,3200]{1,0:T(8,128)(2,1)S(1)}, bf16[48,3200]{1,0:T(8,128)(2,1)}, u32[]{:S(2)}, u32[]{:S(2)}) collective-permute-start(bf16[48,3200]{1,0:T(8,128)(2,1)S(1)} %pack.1.w0.l0), channel_id=1, source_target_pairs={{0,24},{8,16},{16,8},{24,0},{1,25},{9,17},{17,9},{25,1},{2,26},{10... | collective-permute-start | bytes 921608 | tf_op jit(solution)/shard_map/ppermute | solution.py:913
  47.1 14.1 %all-to-all-start.1 = ((bf16[8,32,384]{2,1,0:T(8,128)(2,1)}), bf16[8,32,384]{2,1,0:T(8,128)(2,1)}, u32[]{:S(2)}, u32[]{:S(2)}) async-start(bf16[8,32,384]{2,1,0:T(8,128)(2,1)} %forward.3), calls=%async_computation.1 | async-start | bytes 393216 | tf_op jit(solution)/shard_map/all_to_all | solution.py:917
  53.6 39.5 %collective-permute-start.8 = (bf16[2,1,48,4096]{3,2,1,0:T(8,128)(2,1)}, bf16[2,1,48,4096]{3,2,1,0:T(8,128)(2,1)}, u32[]{:S(2)}, u32[]{:S(2)}) collective-permute-start(bf16[2,1,48,4096]{3,2,1,0:T(8,128)(2,1)} %get-tuple-element.68), channel_id=1, source_target_pairs={{0,8},{8,0},{16,24},{24,16},{1,9},{9,1},{17,25},{25,17},{2,10},{10... | collective-permute-start | bytes 2359304 | tf_op jit(solution)/shard_map/ppermute | solution.py:913
  55.1 38.0 %collective-permute-start.9 = (bf16[2,1,48,4096]{3,2,1,0:T(8,128)(2,1)}, bf16[2,1,48,4096]{3,2,1,0:T(8,128)(2,1)}, u32[]{:S(2)}, u32[]{:S(2)}) collective-permute-start(bf16[2,1,48,4096]{3,2,1,0:T(8,128)(2,1)} %get-tuple-element.69), channel_id=1, source_target_pairs={{0,16},{8,24},{16,0},{24,8},{1,17},{9,25},{17,1},{25,9},{2,18},{10... | collective-permute-start | bytes 2359304 | tf_op jit(solution)/shard_map/ppermute | solution.py:913
  55.6 37.5 %collective-permute-start.10 = (bf16[2,1,48,4096]{3,2,1,0:T(8,128)(2,1)}, bf16[2,1,48,4096]{3,2,1,0:T(8,128)(2,1)}, u32[]{:S(2)}, u32[]{:S(2)}) collective-permute-start(bf16[2,1,48,4096]{3,2,1,0:T(8,128)(2,1)} %get-tuple-element.70), channel_id=1, source_target_pairs={{0,24},{8,16},{16,8},{24,0},{1,25},{9,17},{17,9},{25,1},{2,26},{10... | collective-permute-start | bytes 2359304 | tf_op jit(solution)/shard_map/ppermute | solution.py:913
  63.9 17.6 %all-to-all-start.2 = ((bf16[8,32,768]{2,1,0:T(8,128)(2,1)}), bf16[8,32,768]{2,1,0:T(8,128)(2,1)S(1)}, u32[]{:S(2)}, u32[]{:S(2)}) async-start(bf16[8,32,768]{2,1,0:T(8,128)(2,1)} %mix.1), calls=%async_computation.2 | async-start | bytes 786432 | tf_op jit(solution)/shard_map/all_to_all | solution.py:917
  93.1 23.4 %collective-permute-start.11 = (bf16[2,1,48,4096]{3,2,1,0:T(8,128)(2,1)}, bf16[2,1,48,4096]{3,2,1,0:T(8,128)(2,1)}, u32[]{:S(2)}, u32[]{:S(2)}) collective-permute-start(bf16[2,1,48,4096]{3,2,1,0:T(8,128)(2,1)} %get-tuple-element.71), channel_id=1, source_target_pairs={{0,24},{8,16},{16,8},{24,0},{1,25},{9,17},{17,9},{25,1},{2,26},{10... | collective-permute-start | bytes 2359304 | tf_op jit(solution)/shard_map/ppermute | solution.py:913
  100.5 15.9 %all-to-all-start.3 = ((bf16[8,32,768]{2,1,0:T(8,128)(2,1)}), bf16[8,32,768]{2,1,0:T(8,128)(2,1)S(1)}, u32[]{:S(2)}, u32[]{:S(2)}) async-start(bf16[8,32,768]{2,1,0:T(8,128)(2,1)} %get-tuple-element.79), calls=%async_computation.3 | async-start | bytes 786432 | tf_op jit(solution)/shard_map/all_to_all | solution.py:917
  104.0 36.9 %collective-permute-start.6 = (bf16[2,1,48,4096]{3,2,1,0:T(8,128)(2,1)}, bf16[2,1,48,4096]{3,2,1,0:T(8,128)(2,1)}, u32[]{:S(2)}, u32[]{:S(2)}) collective-permute-start(bf16[2,1,48,4096]{3,2,1,0:T(8,128)(2,1)} %get-tuple-element.65), channel_id=1, source_target_pairs={{0,8},{8,0},{16,24},{24,16},{1,9},{9,1},{17,25},{25,17},{2,10},{10... | collective-permute-start | bytes 2359304 | tf_op jit(solution)/shard_map/ppermute | solution.py:913
  104.6 36.3 %collective-permute-start.7 = (bf16[2,1,48,4096]{3,2,1,0:T(8,128)(2,1)}, bf16[2,1,48,4096]{3,2,1,0:T(8,128)(2,1)}, u32[]{:S(2)}, u32[]{:S(2)}) collective-permute-start(bf16[2,1,48,4096]{3,2,1,0:T(8,128)(2,1)} %get-tuple-element.66), channel_id=1, source_target_pairs={{0,16},{8,24},{16,0},{24,8},{1,17},{9,25},{17,1},{25,9},{2,18},{10... | collective-permute-start | bytes 2359304 | tf_op jit(solution)/shard_map/ppermute | solution.py:913
  118.9 15.9 %all-to-all-start.4 = ((bf16[8,32,768]{2,1,0:T(8,128)(2,1)}), bf16[8,32,768]{2,1,0:T(8,128)(2,1)S(1)}, u32[]{:S(2)}, u32[]{:S(2)}) async-start(bf16[8,32,768]{2,1,0:T(8,128)(2,1)} %mix_back.1), calls=%async_computation.4 | async-start | bytes 786432 | tf_op jit(solution)/shard_map/all_to_all | solution.py:917
  127.4 16.6 %collective-permute-start.15 = (bf16[48,3200]{1,0:T(8,128)(2,1)}, bf16[48,3200]{1,0:T(8,128)(2,1)S(1)}, u32[]{:S(2)}, u32[]{:S(2)}) collective-permute-start(bf16[48,3200]{1,0:T(8,128)(2,1)} %get-tuple-element.96), channel_id=1, source_target_pairs={{0,8},{8,0},{16,24},{24,16},{1,9},{9,1},{17,25},{25,17},{2,10},{10... | collective-permute-start | bytes 921608 | tf_op jit(solution)/shard_map/ppermute | solution.py:913
  128.1 22.6 %collective-permute-start.16 = (bf16[48,3200]{1,0:T(8,128)(2,1)}, bf16[48,3200]{1,0:T(8,128)(2,1)S(1)}, u32[]{:S(2)}, u32[]{:S(2)}) collective-permute-start(bf16[48,3200]{1,0:T(8,128)(2,1)} %get-tuple-element.97), channel_id=1, source_target_pairs={{0,16},{8,24},{16,0},{24,8},{1,17},{9,25},{17,1},{25,9},{2,18},{10... | collective-permute-start | bytes 921608 | tf_op jit(solution)/shard_map/ppermute | solution.py:913
  129.6 21.1 %collective-permute-start.17 = (bf16[48,3200]{1,0:T(8,128)(2,1)}, bf16[48,3200]{1,0:T(8,128)(2,1)S(1)}, u32[]{:S(2)}, u32[]{:S(2)}) collective-permute-start(bf16[48,3200]{1,0:T(8,128)(2,1)} %get-tuple-element.98), channel_id=1, source_target_pairs={{0,24},{8,16},{16,8},{24,0},{1,25},{9,17},{17,9},{25,1},{2,26},{10... | collective-permute-start | bytes 921608 | tf_op jit(solution)/shard_map/ppermute | solution.py:913
  140.9 30.8 %collective-permute-start.14 = (bf16[2,1,48,4096]{3,2,1,0:T(8,128)(2,1)}, bf16[2,1,48,4096]{3,2,1,0:T(8,128)(2,1)S(1)}, u32[]{:S(2)}, u32[]{:S(2)}) collective-permute-start(bf16[2,1,48,4096]{3,2,1,0:T(8,128)(2,1)} %get-tuple-element.93), channel_id=1, source_target_pairs={{0,24},{8,16},{16,8},{24,0},{1,25},{9,17},{17,9},{25,1},{2,26},{10... | collective-permute-start | bytes 2359304 | tf_op jit(solution)/shard_map/ppermute | solution.py:913
  142.6 35.5 %collective-permute-start.12 = (bf16[2,1,48,4096]{3,2,1,0:T(8,128)(2,1)}, bf16[2,1,48,4096]{3,2,1,0:T(8,128)(2,1)S(1)}, u32[]{:S(2)}, u32[]{:S(2)}) collective-permute-start(bf16[2,1,48,4096]{3,2,1,0:T(8,128)(2,1)} %get-tuple-element.91), channel_id=1, source_target_pairs={{0,8},{8,0},{16,24},{24,16},{1,9},{9,1},{17,25},{25,17},{2,10},{10... | collective-permute-start | bytes 2359304 | tf_op jit(solution)/shard_map/ppermute | solution.py:913
  144.0 34.2 %collective-permute-start.13 = (bf16[2,1,48,4096]{3,2,1,0:T(8,128)(2,1)}, bf16[2,1,48,4096]{3,2,1,0:T(8,128)(2,1)S(1)}, u32[]{:S(2)}, u32[]{:S(2)}) collective-permute-start(bf16[2,1,48,4096]{3,2,1,0:T(8,128)(2,1)} %get-tuple-element.92), channel_id=1, source_target_pairs={{0,16},{8,24},{16,0},{24,8},{1,17},{9,25},{17,1},{25,9},{2,18},{10... | collective-permute-start | bytes 2359304 | tf_op jit(solution)/shard_map/ppermute | solution.py:913
  152.0 12.2 %collective-permute-start.19 = (f32[48,48]{1,0:T(8,128)S(1)}, f32[48,48]{1,0:T(8,128)S(1)}, u32[]{:S(2)}, u32[]{:S(2)}) collective-permute-start(f32[48,48]{1,0:T(8,128)S(1)} %add.171), channel_id=1, source_target_pairs={{0,2},{1,3},{2,0},{3,1},{4,6},{5,7},{6,4},{7,5},{8,10},{9,11},{10,... | collective-permute-start | bytes 27656 | tf_op jit(solution)/shard_map/ppermute | solution.py:913
  (17 other events, 261.8 us)

commit v11 on v10

--- a/solution.py
+++ b/solution.py
@@ -136,9 +136,14 @@
 
 def pack_kernel(w_ref, l_ref, o_ref):
     def step(g, carry):
-        parts = [w_ref[0, g * QUAD + q, r] for q in range(QUAD) for r in range(2)]
-        at = pl.ds(pl.multiple_of(g * QUAD * LANES, PACK), QUAD * LANES)
-        o_ref[:, at] = jnp.concatenate(parts, axis=1).astype(BF16)
+        rest = jnp.zeros((C, PACK - LANES), F32)
+        pieces = []
+        for q in range(QUAD):
+            parts = [w_ref[0, g * QUAD + q, 0], w_ref[0, g * QUAD + q, 1], rest]
+            pieces.append(jnp.concatenate(parts, axis=1))
+        for n, tile in enumerate(join_lanes(*pieces)):
+            at = pl.ds(pl.multiple_of(g * QUAD * LANES + n * PACK, PACK), PACK)
+            o_ref[:, at] = tile.astype(BF16)
         return carry
 
     modes = w_ref.shape[1]
@@ -166,16 +171,15 @@
 
 def split_lanes(a, b, c):
     lane = lanes_of(a.shape)
-    second = jnp.where(lane < 32, pltpu.roll(a, 32, 1), pltpu.roll(b, 32, 1))
-    third = jnp.where(lane < 64, pltpu.roll(b, 64, 1), pltpu.roll(c, 64, 1))
-    return a, second, third, pltpu.roll(c, 96, 1)
+    last = jnp.where(lane < 64, pltpu.roll(b, 64, 1), pltpu.roll(c, 96, 1))
+    return a, b, c, jnp.where(lane < 32, pltpu.roll(a, 32, 1), last)
 
 
 def join_lanes(first, second, third, fourth):
-    lane = lanes_of(first.shape)
-    a = jnp.where(lane < 96, first, pltpu.roll(second, 96, 1))
-    b = jnp.where(lane < 64, pltpu.roll(second, 96, 1), pltpu.roll(third, 64, 1))
-    c = jnp.where(lane < 32, pltpu.roll(third, 64, 1), pltpu.roll(fourth, 32, 1))
+    near = lanes_of(first.shape) < LANES
+    a = jnp.where(near, first, pltpu.roll(fourth, 96, 1))
+    b = jnp.where(near, second, pltpu.roll(fourth, 64, 1))
+    c = jnp.where(near, third, pltpu.roll(fourth, 32, 1))
     return a, b, c
 
 
@@ -223,25 +227,32 @@
 
 
 def spread(acc, out_ref, scales=None):
+    def piece(n):
+        parts = [acc[n * C : (n + 1) * C, r * MODES : (r + 1) * MODES] for r in range(2)]
+        row = jnp.concatenate(parts, axis=0)
+        return row if scales is None else row * scales[n]
+
     rows = []
-    for n in range(acc.shape[0] // C):
-        for r in range(2):
-            row = acc[n * C : (n + 1) * C, r * MODES : (r + 1) * MODES]
-            rows.append(row if scales is None else row * scales[n])
-    extra = out_ref.shape[2] - len(rows) * C
-    if extra:
-        rows.append(jnp.zeros((extra, MODES), F32))
+    third = LANES // 3
+    for n in range(0, acc.shape[0] // C, 4):
+        last = piece(n + 3)
+        for k in range(3):
+            rows += [piece(n + k), last[k * third : (k + 1) * third]]
     turned = jnp.concatenate(rows, axis=0).T
     out_ref[...] = turned.reshape(out_ref.shape).astype(BF16)
 
 
 def collect(block, ysc):
     turned = block[...].astype(F32).reshape(MODES, block.shape[2]).T
-    for n in range(ysc.shape[0] // C):
-        for r in range(2):
-            row = (n * 2 + r) * C
-            piece = turned[row : row + C].astype(BF16)
-            ysc[n * C : (n + 1) * C, r * MODES : (r + 1) * MODES] = piece
+    for n in range(0, ysc.shape[0] // C, 4):
+        tiles = [turned[(n // 4 * 3 + k) * PACK :][:PACK] for k in range(3)]
+        pieces = [tile[:LANES] for tile in tiles]
+        pieces.append(jnp.concatenate([tile[LANES:] for tile in tiles], axis=0))
+        for k, piece in enumerate(pieces):
+            row = (n + k) * C
+            for r in range(2):
+                part = piece[r * C : (r + 1) * C].astype(BF16)
+                ysc[row : row + C, r * MODES : (r + 1) * MODES] = part
 
 
 def forward_kernel(ids_ref, inv_ref, *refs):
@@ -496,13 +507,13 @@
         for q in range(QUAD):
             m = g * QUAD + q
             factor = mode_factor(first_mode + m)
-            plain = [rows * factor for rows in blade_rows(gsc, m, shards, groups)]
+            plain = [(rows * factor).astype(BF16) for rows in blade_rows(gsc, m, shards, groups)]
             turned = [
                 jnp.where(lane < C, pltpu.roll(rows, PACK - C, 1), -pltpu.roll(rows, C, 1))
                 for rows in plain
             ]
-            plus = [rows.astype(BF16) for rows in plain + turned]
-            minus = [(-rows).astype(BF16) for rows in plain + turned]
+            plus = plain + turned
+            minus = [-rows for rows in plus]
             right = []
             for k in range(4):
                 rows = []
@@ -884,12 +895,13 @@
     grad = d0[...].astype(F32) * flips[0]
     for t, d in ((1, d1), (2, d2), (3, d3)):
         grad = grad + d[...].astype(F32) * flips[t]
-    for q in range(w_ref.shape[1]):
-        for r in range(2):
-            lane = q * LANES + r * C
-            at = (0, q, r)
-            new = adamw(w_ref[at], first_ref[at], second_ref[at], grad[:, lane : lane + C])
-            w_out[at], first_out[at], second_out[at] = new
+    for g in range(w_ref.shape[1] // QUAD):
+        tiles = [grad[:, (3 * g + n) * PACK : (3 * g + n + 1) * PACK] for n in range(3)]
+        for q, piece in enumerate(split_lanes(*tiles)):
+            for r in range(2):
+                at = (0, g * QUAD + q, r)
+                new = adamw(w_ref[at], first_ref[at], second_ref[at], piece[:, r * C : (r + 1) * C])
+                w_out[at], first_out[at], second_out[at] = new
 
 
 def adam_spec(flips, grads, weight, first, second):

time: 182 us -> 182 us (level)
  no operation moved by 1% of the time
where the time goes in v11:
time: 182 us; the launch traced here: 181 us
  Pallas kernels  78.4 us (43%)
  starting transfers between devices  58.6 us (32%)
  waiting for transfers between devices  31 us (17%)
  local copies, waits for them, and re-layouts  8.6 us (5%)
  other arithmetic  3.45 us (2%)
    ppermute x21, starting transfers between devices, swap(): return lax.ppermute(value, axis, [(i, i ^ x) for i in range(size)])  36.1 us
    all_to_all x5, starting transfers between devices, to_modes(): return lax.all_to_all(value, 'dp', split_axis=0, concat_axis=0, tiled=True)  22.5 us
    all_to_all x5, waiting for transfers between devices, to_modes(): return lax.all_to_all(value, 'dp', split_axis=0, concat_axis=0, tiled=True)  16.2 us
    ppermute x21, waiting for transfers between devices, swap(): return lax.ppermute(value, axis, [(i, i ^ x) for i in range(size)])  14.8 us
    pallas_call x1, Pallas kernels, pixels(): pl.pallas_call(pixel_kernel, grid_spec=pltpu.PrefetchScalarGridSpec(num_s...  11.5 us
    pallas_call x2, Pallas kernels, forward_spectrum(): pl.pallas_call(forward_kernel, grid_spec=pltpu.PrefetchScalarGridSpec(num...  8.63 us
    dynamic_slice x4, local copies, waits for them, and re-layouts, cut(): lax.dynamic_slice_in_dim(array, jnp.bitwise_xor(own, t) * samples, sample...  7.92 us
    pallas_call x1, Pallas kernels, lin_grads(): pl.pallas_call(lin_kernel, grid_spec=pltpu.PrefetchScalarGridSpec(num_sca...  6.33 us
  transfers between devices with their start and end apart: 26, of which 8 were waited for; matrix products, arithmetic and copies ran while one was open for 5% of the time, Pallas kernels for 42%

profile of v11, /device:TPU:0, one launch (start us, length us, event | category | flops | bytes accessed | tf_op | source)
XLA Modules:
  0.0 180.9 jit_solution(3498195177069648421)
XLA Ops:
  2.7 3.9 %collective-permute-start.2 = (bf16[2,1,48,4096]{3,2,1,0:T(8,128)(2,1)}, bf16[2,1,48,4096]{3,2,1,0:T(8,128)(2,1)}, u32[]{:S(2)}, u32[]{:S(2)}) collective-permute-start(bf16[2,1,48,4096]{3,2,1,0:T(8,128)(2,1)} %constant_dynamic-slice_fusion.5), channel_id=1, source_target_pairs={{0,24},{8,16},{16,8},{24,0},{1,25},{9,17},{17,9},{25,1},{2,26},{10... | collective-permute-start | bytes 2359304 | tf_op jit(solution)/shard_map/ppermute | solution.py:925
  13.4 5.9 %turned.1.refs_5_ = bf16[512,4096]{1,0:T(8,128)(2,1)} custom-call(f32[4,64,512]{2,1,0:T(8,128)} %pad_maximum_fusion.row_ref.col_ref.refs_2_.refs_3_.refs_5_.refs_6_, f32[4,64,512]{2,1,0:T(8,128)} %pad_maximum_fusion.row_ref.col_ref.refs_2_.refs_3_.refs_5_.refs_6_), custom_call_target="tpu_custom_call" | custom-call | flops 1 | bytes 1 | tf_op jit(solution)/shard_map/turned/pallas_call | solution.py:125
  25.3 4.3 %forward.2 = bf16[8,32,384]{2,1,0:T(8,128)(2,1)} custom-call(s32[2]{0:T(128)} %pad_add_fusion.ids_ref, f32[2]{0:T(128)} %dynamic_slice.21.inv_ref, bf16[8,1,48,4096]{3,2,1,0:T(8,128)(2,1)} %refs_0_.6, bf16[2,1,48,4096]{3,2,1,0:T(8,128)(2,1)} %collective-permute-done.2.refs_1_.refs_3_, ...), custom_call_target="tpu_custom_call" | custom-call | flops 1 | bytes 1 | tf_op jit(solution)/shard_map/forward/pallas_call | solution.py:292
  29.7 5.4 %all-to-all-start = ((bf16[8,32,384]{2,1,0:T(8,128)(2,1)}), bf16[8,32,384]{2,1,0:T(8,128)(2,1)}, u32[]{:S(2)}, u32[]{:S(2)}) async-start(bf16[8,32,384]{2,1,0:T(8,128)(2,1)} %forward.2), calls=%async_computation | async-start | bytes 393216 | tf_op jit(solution)/shard_map/all_to_all | solution.py:929
  38.6 4.2 %collective-permute-done.refs_0_.refs_1_ = bf16[2,1,48,4096]{3,2,1,0:T(8,128)(2,1)} collective-permute-done((bf16[2,1,48,4096]{3,2,1,0:T(8,128)(2,1)}, bf16[2,1,48,4096]{3,2,1,0:T(8,128)(2,1)}, u32[]{:S(2)}, u32[]{:S(2)}) %collective-permute-start) | collective-permute-done | bytes 786464 | tf_op jit(solution)/shard_map/ppermute | solution.py:925
  42.8 4.3 %forward.3 = bf16[8,32,384]{2,1,0:T(8,128)(2,1)} custom-call(s32[2]{0:T(128)} %pad_add_fusion.ids_ref, f32[2]{0:T(128)} %dynamic_slice.21.inv_ref, bf16[2,1,48,4096]{3,2,1,0:T(8,128)(2,1)} %collective-permute-done.refs_0_.refs_1_, bf16[2,1,48,4096]{3,2,1,0:T(8,128)(2,1)} %collective-permute-done.1.refs_1_.refs_2_, ...), custom_call_target="tpu_custom_call" | custom-call | flops 1 | bytes 1 | tf_op jit(solution)/shard_map/forward/pallas_call | solution.py:292
  47.1 4.9 %all-to-all-start.1 = ((bf16[8,32,384]{2,1,0:T(8,128)(2,1)}), bf16[8,32,384]{2,1,0:T(8,128)(2,1)}, u32[]{:S(2)}, u32[]{:S(2)}) async-start(bf16[8,32,384]{2,1,0:T(8,128)(2,1)} %forward.3), calls=%async_computation.1 | async-start | bytes 393216 | tf_op jit(solution)/shard_map/all_to_all | solution.py:929
  57.1 3.7 %unpack.1.pq_ref = bf16[32,96,512]{2,1,0:T(8,128)(2,1)S(1)} custom-call(s32[2]{0:T(128)} %pad_add_fusion.ids_ref, bf16[48,3200]{1,0:T(8,128)(2,1)} %copy-done.4, bf16[48,3200]{1,0:T(8,128)(2,1)} %collective-permute-done.3.w1.l1, bf16[48,3200]{1,0:T(8,128)(2,1)} %collective-permute-done.4.w2.l2, bf16[48,3200]{1,0:T(8,128)(2,1)} %collective-permute-done.5.w3.l3), custom_call_target="tpu_custom_call" | custom-call | flops 1 | bytes 1 | tf_op jit(solution)/shard_map/unpack/pallas_call | solution.py:218
  63.6 5.1 %all-to-all-start.2 = ((bf16[8,32,768]{2,1,0:T(8,128)(2,1)}), bf16[8,32,768]{2,1,0:T(8,128)(2,1)S(1)}, u32[]{:S(2)}, u32[]{:S(2)}) async-start(bf16[8,32,768]{2,1,0:T(8,128)(2,1)} %mix.1), calls=%async_computation.2 | async-start | bytes 786432 | tf_op jit(solution)/shard_map/all_to_all | solution.py:929
  68.7 4.7 %turn.1 = (bf16[32,96,512]{2,1,0:T(8,128)(2,1)S(1)}, bf16[32,48,128]{2,1,0:T(8,128)(2,1)}, bf16[192,192]{1,0:T(8,128)(2,1)}, bf16[192,192]{1,0:T(8,128)(2,1)}) custom-call(s32[2]{0:T(128)} %pad_add_fusion.ids_ref, bf16[32,96,512]{2,1,0:T(8,128)(2,1)S(1)} %unpack.1.pq_ref, bf16[8,32,384]{2,1,0:T(8,128)(2,1)} %all-to-all-done.xa, ...), custom_call_target="tpu_custom_call", output_to_operand_aliasing={{0}: (1, {})} | custom-call | flops 1 | bytes 1 | tf_op jit(solution)/shard_map/turn/pallas_call | solution.py:477
  73.3 7.9 %all-to-all-done.2.refs_4_ = bf16[8,32,768]{2,1,0:T(8,128)(2,1)S(1)} async-done(((bf16[8,32,768]{2,1,0:T(8,128)(2,1)}), bf16[8,32,768]{2,1,0:T(8,128)(2,1)S(1)}, u32[]{:S(2)}, u32[]{:S(2)}) %all-to-all-start.2) | async-done | bytes 393248 | tf_op jit(solution)/shard_map/all_to_all | solution.py:929
  81.2 11.5 %pixels.1 = (bf16[8,1,48,4096]{3,2,1,0:T(8,128)(2,1)}, bf16[2,1,48,4096]{3,2,1,0:T(8,128)(2,1)}, bf16[2,1,48,4096]{3,2,1,0:T(8,128)(2,1)}, bf16[2,1,48,4096]{3,2...) custom-call(s32[2]{0:T(128)} %pad_add_fusion.ids_ref, ...), custom_call_target="tpu_custom_call", output_to_operand_aliasing={{5}: (9, {})} | custom-call | flops 1 | bytes 1 | tf_op jit(solution)/shard_map/pixels/pallas_call | solution.py:622
  94.2 6.0 %pixel_grads.1 = (bf16[384,4096]{1,0:T(8,128)(2,1)}, bf16[8,32,768]{2,1,0:T(8,128)(2,1)}, bf16[32,96,512]{2,1,0:T(8,128)(2,1)S(1)}) custom-call(s32[2]{0:T(128)} %pad_add_fusion.ids_ref, bf16[8,1,48,4096]{3,2,1,0:T(8,128)(2,1)} %cot_ref.5, bf16[2,1,48,4096]{3,2,1,0:T(8,128)(2,1)} %collective-permute-done.8.refs_1_, ...), custom_call_target="tpu_custom_call", output_to_operand_aliasing={{2}: (8, {})} | custom-call | flops 1 | bytes 1 | tf_op jit(solution)/shard_map/pixel_grads/pallas_call | solution.py:686
  100.2 3.6 %all-to-all-start.3 = ((bf16[8,32,768]{2,1,0:T(8,128)(2,1)}), bf16[8,32,768]{2,1,0:T(8,128)(2,1)S(1)}, u32[]{:S(2)}, u32[]{:S(2)}) async-start(bf16[8,32,768]{2,1,0:T(8,128)(2,1)} %get-tuple-element.79), calls=%async_computation.3 | async-start | bytes 786432 | tf_op jit(solution)/shard_map/all_to_all | solution.py:929
  106.1 6.3 %lin_grads.1 = (f32[4,48,48]{2,1,0:T(8,128)}, bf16[384,4096]{1,0:T(8,128)(2,1)}) custom-call(s32[2]{0:T(128)} %pad_add_fusion.ids_ref, f32[2]{0:T(128)} %dynamic_slice.21.inv_ref, bf16[8,1,48,4096]{3,2,1,0:T(8,128)(2,1)} %refs_0_.6, bf16[2,1,48,4096]{3,2,1,0:T(8,128)(2,1)} %collective-permute-done.refs_0_.refs_1_, ...), custom_call_target="tpu_custom_call" | custom-call | flops 1 | bytes 1 | tf_op jit(solution)/shard_map/lin_grads/pallas_call | solution.py:737
  112.4 3.9 %all-to-all-done.3.g_ref = bf16[8,32,768]{2,1,0:T(8,128)(2,1)S(1)} async-done(((bf16[8,32,768]{2,1,0:T(8,128)(2,1)}), bf16[8,32,768]{2,1,0:T(8,128)(2,1)S(1)}, u32[]{:S(2)}, u32[]{:S(2)}) %all-to-all-start.3) | async-done | bytes 393248 | tf_op jit(solution)/shard_map/all_to_all | solution.py:929
  118.8 3.5 %all-to-all-start.4 = ((bf16[8,32,768]{2,1,0:T(8,128)(2,1)}), bf16[8,32,768]{2,1,0:T(8,128)(2,1)S(1)}, u32[]{:S(2)}, u32[]{:S(2)}) async-start(bf16[8,32,768]{2,1,0:T(8,128)(2,1)} %mix_back.1), calls=%async_computation.4 | async-start | bytes 786432 | tf_op jit(solution)/shard_map/all_to_all | solution.py:929
  122.3 4.6 %weight_grads.1 = (bf16[48,3200]{1,0:T(8,128)(2,1)}, bf16[48,3200]{1,0:T(8,128)(2,1)}, bf16[48,3200]{1,0:T(8,128)(2,1)}, bf16[48,3200]{1,0:T(8,128)(2,1)}) custom-call(s32[2]{0:T(128)} %pad_add_fusion.ids_ref, bf16[32,48,128]{2,1,0:T(8,128)(2,1)} %get-tuple-element.80.xt_ref, bf16[8,32,768]{2,1,0:T(8,128)(2,1)S(1)} %all-to-all-done.3.g_ref, ...), custom_call_target="tpu_custom_call" | custom-call | flops 1 | bytes 1 | tf_op jit(solution)/shard_map/weight_grads/pallas_call | solution.py:545
  130.3 4.4 %all-to-all-done.4.y_ref = bf16[8,32,768]{2,1,0:T(8,128)(2,1)S(1)} async-done(((bf16[8,32,768]{2,1,0:T(8,128)(2,1)}), bf16[8,32,768]{2,1,0:T(8,128)(2,1)S(1)}, u32[]{:S(2)}, u32[]{:S(2)}) %all-to-all-start.4) | async-done | bytes 393248 | tf_op jit(solution)/shard_map/all_to_all | solution.py:929
  134.7 6.1 %inner_grads.1 = (f32[8,1,48,4096]{3,2,1,0:T(8,128)}, bf16[2,1,48,4096]{3,2,1,0:T(8,128)(2,1)}, bf16[2,1,48,4096]{3,2,1,0:T(8,128)(2,1)}, bf16[2,1,48,4096]{3,2,1,0:T(8,128)(2,1)}) custom-call(s32[2]{0:T(128)} %pad_add_fusion.ids_ref, f32[2]{0:T(128)} %dynamic_slice.21.inv_ref, bf16[8,32,768]{2,1,0:T(8,128)(2,1)S(1)} %all-to-all-done.4.y_ref, ...), custom_call_target="tpu_custom_call" | custom-call | flops 1 | bytes 1 | tf_op jit(solution)/shard_map/inner_grads/pallas_call | solution.py:779
  144.4 6.1 %place.1 = bf16[8,1,48,4096]{3,2,1,0:T(8,128)(2,1)} custom-call(s32[2]{0:T(128)S(1)} %copy-done.8, bf16[2,1,48,4096]{3,2,1,0:T(8,128)(2,1)} %collective-permute-done.6.a_ref, bf16[2,1,48,4096]{3,2,1,0:T(8,128)(2,1)} %collective-permute-done.7.b_ref, bf16[2,1,48,4096]{3,2,1,0:T(8,128)(2,1)} %collective-permute-done.11.c_ref, ...), custom_call_target="tpu_custom_call", output_to_operand_aliasing={{}: (4, {})} | custom-call | flops 1 | bytes 1 | tf_op jit(solution)/shard_map/place/pallas_call | solution.py:818
  151.9 10.9 %collective-permute-start.19 = (f32[48,48]{1,0:T(8,128)S(1)}, f32[48,48]{1,0:T(8,128)S(1)}, u32[]{:S(2)}, u32[]{:S(2)}) collective-permute-start(f32[48,48]{1,0:T(8,128)S(1)} %add.171), channel_id=1, source_target_pairs={{0,2},{1,3},{2,0},{3,1},{4,6},{5,7},{6,4},{7,5},{8,10},{9,11},{10,... | collective-permute-start | bytes 27656 | tf_op jit(solution)/shard_map/ppermute | solution.py:925
  167.6 3.8 %adam.1 = (f32[1,32,2,48,48]{4,3,2,1,0:T(8,128)}, f32[1,32,2,48,48]{4,3,2,1,0:T(8,128)}, f32[1,32,2,48,48]{4,3,2,1,0:T(8,128)}) custom-call(f32[4]{0:T(128)S(1)} %pad_maximum_fusion.1.flips, bf16[48,3200]{1,0:T(8,128)(2,1)S(1)} %copy-done.7, bf16[48,3200]{1,0:T(8,128)(2,1)S(1)} %collective-permute-done.15.d1, ...), custom_call_target="tpu_custom_call" | custom-call | flops 1 | bytes 1 | tf_op jit(solution)/shard_map/adam/pallas_call | solution.py:912
  173.9 4.2 %collective-permute-done.12.refs_0_ = bf16[2,1,48,4096]{3,2,1,0:T(8,128)(2,1)S(1)} collective-permute-done((bf16[2,1,48,4096]{3,2,1,0:T(8,128)(2,1)}, bf16[2,1,48,4096]{3,2,1,0:T(8,128)(2,1)S(1)}, u32[]{:S(2)}, u32[]{:S(2)}) %collective-permute-start.12) | collective-permute-done | bytes 786464 | tf_op jit(solution)/shard_map/ppermute | solution.py:925
  (93 shorter events, 50.9 us)
Async XLA Ops:
  2.7 22.6 %collective-permute-start.2 = (bf16[2,1,48,4096]{3,2,1,0:T(8,128)(2,1)}, bf16[2,1,48,4096]{3,2,1,0:T(8,128)(2,1)}, u32[]{:S(2)}, u32[]{:S(2)}) collective-permute-start(bf16[2,1,48,4096]{3,2,1,0:T(8,128)(2,1)} %constant_dynamic-slice_fusion.5), channel_id=1, source_target_pairs={{0,24},{8,16},{16,8},{24,0},{1,25},{9,17},{17,9},{25,1},{2,26},{10... | collective-permute-start | bytes 2359304 | tf_op jit(solution)/shard_map/ppermute | solution.py:925
  8.7 34.1 %collective-permute-start = (bf16[2,1,48,4096]{3,2,1,0:T(8,128)(2,1)}, bf16[2,1,48,4096]{3,2,1,0:T(8,128)(2,1)}, u32[]{:S(2)}, u32[]{:S(2)}) collective-permute-start(bf16[2,1,48,4096]{3,2,1,0:T(8,128)(2,1)} %constant_dynamic-slice_fusion.4), channel_id=1, source_target_pairs={{0,8},{8,0},{16,24},{24,16},{1,9},{9,1},{17,25},{25,17},{2,10},{10... | collective-permute-start | bytes 2359304 | tf_op jit(solution)/shard_map/ppermute | solution.py:925
  13.3 29.4 %collective-permute-start.1 = (bf16[2,1,48,4096]{3,2,1,0:T(8,128)(2,1)}, bf16[2,1,48,4096]{3,2,1,0:T(8,128)(2,1)}, u32[]{:S(2)}, u32[]{:S(2)}) collective-permute-start(bf16[2,1,48,4096]{3,2,1,0:T(8,128)(2,1)} %constant_dynamic-slice_fusion.3), channel_id=1, source_target_pairs={{0,16},{8,24},{16,0},{24,8},{1,17},{9,25},{17,1},{25,9},{2,18},{10... | collective-permute-start | bytes 2359304 | tf_op jit(solution)/shard_map/ppermute | solution.py:925
  29.7 17.4 %all-to-all-start = ((bf16[8,32,384]{2,1,0:T(8,128)(2,1)}), bf16[8,32,384]{2,1,0:T(8,128)(2,1)}, u32[]{:S(2)}, u32[]{:S(2)}) async-start(bf16[8,32,384]{2,1,0:T(8,128)(2,1)} %forward.2), calls=%async_computation | async-start | bytes 393216 | tf_op jit(solution)/shard_map/all_to_all | solution.py:929
  35.1 20.5 %collective-permute-start.3 = (bf16[48,3200]{1,0:T(8,128)(2,1)S(1)}, bf16[48,3200]{1,0:T(8,128)(2,1)}, u32[]{:S(2)}, u32[]{:S(2)}) collective-permute-start(bf16[48,3200]{1,0:T(8,128)(2,1)S(1)} %pack.1.w0.l0), channel_id=1, source_target_pairs={{0,8},{8,0},{16,24},{24,16},{1,9},{9,1},{17,25},{25,17},{2,10},{10... | collective-permute-start | bytes 921608 | tf_op jit(solution)/shard_map/ppermute | solution.py:925
  36.5 20.5 %collective-permute-start.4 = (bf16[48,3200]{1,0:T(8,128)(2,1)S(1)}, bf16[48,3200]{1,0:T(8,128)(2,1)}, u32[]{:S(2)}, u32[]{:S(2)}) collective-permute-start(bf16[48,3200]{1,0:T(8,128)(2,1)S(1)} %pack.1.w0.l0), channel_id=1, source_target_pairs={{0,16},{8,24},{16,0},{24,8},{1,17},{9,25},{17,1},{25,9},{2,18},{10... | collective-permute-start | bytes 921608 | tf_op jit(solution)/shard_map/ppermute | solution.py:925
  38.1 19.0 %collective-permute-start.5 = (bf16[48,3200]{1,0:T(8,128)(2,1)S(1)}, bf16[48,3200]{1,0:T(8,128)(2,1)}, u32[]{:S(2)}, u32[]{:S(2)}) collective-permute-start(bf16[48,3200]{1,0:T(8,128)(2,1)S(1)} %pack.1.w0.l0), channel_id=1, source_target_pairs={{0,24},{8,16},{16,8},{24,0},{1,25},{9,17},{17,9},{25,1},{2,26},{10... | collective-permute-start | bytes 921608 | tf_op jit(solution)/shard_map/ppermute | solution.py:925
  47.1 13.7 %all-to-all-start.1 = ((bf16[8,32,384]{2,1,0:T(8,128)(2,1)}), bf16[8,32,384]{2,1,0:T(8,128)(2,1)}, u32[]{:S(2)}, u32[]{:S(2)}) async-start(bf16[8,32,384]{2,1,0:T(8,128)(2,1)} %forward.3), calls=%async_computation.1 | async-start | bytes 393216 | tf_op jit(solution)/shard_map/all_to_all | solution.py:929
  53.6 39.1 %collective-permute-start.8 = (bf16[2,1,48,4096]{3,2,1,0:T(8,128)(2,1)}, bf16[2,1,48,4096]{3,2,1,0:T(8,128)(2,1)}, u32[]{:S(2)}, u32[]{:S(2)}) collective-permute-start(bf16[2,1,48,4096]{3,2,1,0:T(8,128)(2,1)} %get-tuple-element.68), channel_id=1, source_target_pairs={{0,8},{8,0},{16,24},{24,16},{1,9},{9,1},{17,25},{25,17},{2,10},{10... | collective-permute-start | bytes 2359304 | tf_op jit(solution)/shard_map/ppermute | solution.py:925
  55.1 37.6 %collective-permute-start.9 = (bf16[2,1,48,4096]{3,2,1,0:T(8,128)(2,1)}, bf16[2,1,48,4096]{3,2,1,0:T(8,128)(2,1)}, u32[]{:S(2)}, u32[]{:S(2)}) collective-permute-start(bf16[2,1,48,4096]{3,2,1,0:T(8,128)(2,1)} %get-tuple-element.69), channel_id=1, source_target_pairs={{0,16},{8,24},{16,0},{24,8},{1,17},{9,25},{17,1},{25,9},{2,18},{10... | collective-permute-start | bytes 2359304 | tf_op jit(solution)/shard_map/ppermute | solution.py:925
  55.6 37.1 %collective-permute-start.10 = (bf16[2,1,48,4096]{3,2,1,0:T(8,128)(2,1)}, bf16[2,1,48,4096]{3,2,1,0:T(8,128)(2,1)}, u32[]{:S(2)}, u32[]{:S(2)}) collective-permute-start(bf16[2,1,48,4096]{3,2,1,0:T(8,128)(2,1)} %get-tuple-element.70), channel_id=1, source_target_pairs={{0,24},{8,16},{16,8},{24,0},{1,25},{9,17},{17,9},{25,1},{2,26},{10... | collective-permute-start | bytes 2359304 | tf_op jit(solution)/shard_map/ppermute | solution.py:925
  63.6 17.6 %all-to-all-start.2 = ((bf16[8,32,768]{2,1,0:T(8,128)(2,1)}), bf16[8,32,768]{2,1,0:T(8,128)(2,1)S(1)}, u32[]{:S(2)}, u32[]{:S(2)}) async-start(bf16[8,32,768]{2,1,0:T(8,128)(2,1)} %mix.1), calls=%async_computation.2 | async-start | bytes 786432 | tf_op jit(solution)/shard_map/all_to_all | solution.py:929
  92.7 23.6 %collective-permute-start.11 = (bf16[2,1,48,4096]{3,2,1,0:T(8,128)(2,1)}, bf16[2,1,48,4096]{3,2,1,0:T(8,128)(2,1)}, u32[]{:S(2)}, u32[]{:S(2)}) collective-permute-start(bf16[2,1,48,4096]{3,2,1,0:T(8,128)(2,1)} %get-tuple-element.71), channel_id=1, source_target_pairs={{0,24},{8,16},{16,8},{24,0},{1,25},{9,17},{17,9},{25,1},{2,26},{10... | collective-permute-start | bytes 2359304 | tf_op jit(solution)/shard_map/ppermute | solution.py:925
  100.2 16.1 %all-to-all-start.3 = ((bf16[8,32,768]{2,1,0:T(8,128)(2,1)}), bf16[8,32,768]{2,1,0:T(8,128)(2,1)S(1)}, u32[]{:S(2)}, u32[]{:S(2)}) async-start(bf16[8,32,768]{2,1,0:T(8,128)(2,1)} %get-tuple-element.79), calls=%async_computation.3 | async-start | bytes 786432 | tf_op jit(solution)/shard_map/all_to_all | solution.py:929
  103.8 37.0 %collective-permute-start.6 = (bf16[2,1,48,4096]{3,2,1,0:T(8,128)(2,1)}, bf16[2,1,48,4096]{3,2,1,0:T(8,128)(2,1)}, u32[]{:S(2)}, u32[]{:S(2)}) collective-permute-start(bf16[2,1,48,4096]{3,2,1,0:T(8,128)(2,1)} %get-tuple-element.65), channel_id=1, source_target_pairs={{0,8},{8,0},{16,24},{24,16},{1,9},{9,1},{17,25},{25,17},{2,10},{10... | collective-permute-start | bytes 2359304 | tf_op jit(solution)/shard_map/ppermute | solution.py:925
  104.6 36.3 %collective-permute-start.7 = (bf16[2,1,48,4096]{3,2,1,0:T(8,128)(2,1)}, bf16[2,1,48,4096]{3,2,1,0:T(8,128)(2,1)}, u32[]{:S(2)}, u32[]{:S(2)}) collective-permute-start(bf16[2,1,48,4096]{3,2,1,0:T(8,128)(2,1)} %get-tuple-element.66), channel_id=1, source_target_pairs={{0,16},{8,24},{16,0},{24,8},{1,17},{9,25},{17,1},{25,9},{2,18},{10... | collective-permute-start | bytes 2359304 | tf_op jit(solution)/shard_map/ppermute | solution.py:925
  118.8 15.9 %all-to-all-start.4 = ((bf16[8,32,768]{2,1,0:T(8,128)(2,1)}), bf16[8,32,768]{2,1,0:T(8,128)(2,1)S(1)}, u32[]{:S(2)}, u32[]{:S(2)}) async-start(bf16[8,32,768]{2,1,0:T(8,128)(2,1)} %mix_back.1), calls=%async_computation.4 | async-start | bytes 786432 | tf_op jit(solution)/shard_map/all_to_all | solution.py:929
  126.8 17.1 %collective-permute-start.15 = (bf16[48,3200]{1,0:T(8,128)(2,1)}, bf16[48,3200]{1,0:T(8,128)(2,1)S(1)}, u32[]{:S(2)}, u32[]{:S(2)}) collective-permute-start(bf16[48,3200]{1,0:T(8,128)(2,1)} %get-tuple-element.96), channel_id=1, source_target_pairs={{0,8},{8,0},{16,24},{24,16},{1,9},{9,1},{17,25},{25,17},{2,10},{10... | collective-permute-start | bytes 921608 | tf_op jit(solution)/shard_map/ppermute | solution.py:925
  127.6 23.0 %collective-permute-start.16 = (bf16[48,3200]{1,0:T(8,128)(2,1)}, bf16[48,3200]{1,0:T(8,128)(2,1)S(1)}, u32[]{:S(2)}, u32[]{:S(2)}) collective-permute-start(bf16[48,3200]{1,0:T(8,128)(2,1)} %get-tuple-element.97), channel_id=1, source_target_pairs={{0,16},{8,24},{16,0},{24,8},{1,17},{9,25},{17,1},{25,9},{2,18},{10... | collective-permute-start | bytes 921608 | tf_op jit(solution)/shard_map/ppermute | solution.py:925
  129.2 21.4 %collective-permute-start.17 = (bf16[48,3200]{1,0:T(8,128)(2,1)}, bf16[48,3200]{1,0:T(8,128)(2,1)S(1)}, u32[]{:S(2)}, u32[]{:S(2)}) collective-permute-start(bf16[48,3200]{1,0:T(8,128)(2,1)} %get-tuple-element.98), channel_id=1, source_target_pairs={{0,24},{8,16},{16,8},{24,0},{1,25},{9,17},{17,9},{25,1},{2,26},{10... | collective-permute-start | bytes 921608 | tf_op jit(solution)/shard_map/ppermute | solution.py:925
  140.9 31.2 %collective-permute-start.14 = (bf16[2,1,48,4096]{3,2,1,0:T(8,128)(2,1)}, bf16[2,1,48,4096]{3,2,1,0:T(8,128)(2,1)S(1)}, u32[]{:S(2)}, u32[]{:S(2)}) collective-permute-start(bf16[2,1,48,4096]{3,2,1,0:T(8,128)(2,1)} %get-tuple-element.93), channel_id=1, source_target_pairs={{0,24},{8,16},{16,8},{24,0},{1,25},{9,17},{17,9},{25,1},{2,26},{10... | collective-permute-start | bytes 2359304 | tf_op jit(solution)/shard_map/ppermute | solution.py:925
  142.7 35.4 %collective-permute-start.12 = (bf16[2,1,48,4096]{3,2,1,0:T(8,128)(2,1)}, bf16[2,1,48,4096]{3,2,1,0:T(8,128)(2,1)S(1)}, u32[]{:S(2)}, u32[]{:S(2)}) collective-permute-start(bf16[2,1,48,4096]{3,2,1,0:T(8,128)(2,1)} %get-tuple-element.91), channel_id=1, source_target_pairs={{0,8},{8,0},{16,24},{24,16},{1,9},{9,1},{17,25},{25,17},{2,10},{10... | collective-permute-start | bytes 2359304 | tf_op jit(solution)/shard_map/ppermute | solution.py:925
  143.9 34.2 %collective-permute-start.13 = (bf16[2,1,48,4096]{3,2,1,0:T(8,128)(2,1)}, bf16[2,1,48,4096]{3,2,1,0:T(8,128)(2,1)S(1)}, u32[]{:S(2)}, u32[]{:S(2)}) collective-permute-start(bf16[2,1,48,4096]{3,2,1,0:T(8,128)(2,1)} %get-tuple-element.92), channel_id=1, source_target_pairs={{0,16},{8,24},{16,0},{24,8},{1,17},{9,25},{17,1},{25,9},{2,18},{10... | collective-permute-start | bytes 2359304 | tf_op jit(solution)/shard_map/ppermute | solution.py:925
  151.9 12.7 %collective-permute-start.19 = (f32[48,48]{1,0:T(8,128)S(1)}, f32[48,48]{1,0:T(8,128)S(1)}, u32[]{:S(2)}, u32[]{:S(2)}) collective-permute-start(f32[48,48]{1,0:T(8,128)S(1)} %add.171), channel_id=1, source_target_pairs={{0,2},{1,3},{2,0},{3,1},{4,6},{5,7},{6,4},{7,5},{8,10},{9,11},{10,... | collective-permute-start | bytes 27656 | tf_op jit(solution)/shard_map/ppermute | solution.py:925
  (17 other events, 264.7 us)

commit v12 on v10

--- a/solution.py
+++ b/solution.py
@@ -823,20 +823,21 @@
 
 
 def final_kernel(count, codes, ids_ref, inv_ref, cot_ref, *refs):
-    samples = pl.num_programs(1)
+    samples = cot_ref.shape[0]
     j = pl.program_id(0)
     for n in range(count):
 
         @pl.when(j == n)
         def _():
-            inv = inv_ref[jnp.bitwise_xor(ids_ref[0], codes[n]) * samples + pl.program_id(1)]
-            refs[-1][...] = (cot_ref[...].astype(F32) + refs[n][...].astype(F32)) * inv
+            for s in range(samples):
+                inv = inv_ref[jnp.bitwise_xor(ids_ref[0], codes[n]) * samples + s]
+                refs[-1][s] = (cot_ref[s].astype(F32) + refs[n][s].astype(F32)) * inv
 
 
 def final_grads(ids, inv, cotangent, parts, codes, result):
     samples = parts[0].shape[0]
     count = len(parts)
-    shape = (1, 1, C, NPIX)
+    shape = (samples, 1, C, NPIX)
 
     def code(j):
         value = codes[0]
@@ -845,19 +846,16 @@
         return value
 
     def spec(n):
-        def at(j, s, ids, inv):
-            return (jnp.where(j == n, s, jnp.where(j < n, 0, samples - 1)), 0, 0, 0)
-
-        return pl.BlockSpec(shape, at)
+        return pl.BlockSpec(shape, lambda j, ids, inv: (0, 0, 0, 0))
 
     place = pl.BlockSpec(
-        shape, lambda j, s, ids, inv: (jnp.bitwise_xor(ids[0], code(j)) * samples + s, 0, 0, 0)
+        shape, lambda j, ids, inv: (jnp.bitwise_xor(ids[0], code(j)), 0, 0, 0)
     )
     return pl.pallas_call(
         partial(final_kernel, count, codes),
         grid_spec=pltpu.PrefetchScalarGridSpec(
             num_scalar_prefetch=2,
-            grid=(count, samples),
+            grid=(count,),
             in_specs=[place]
             + [spec(n) for n in range(count)]
             + [pl.BlockSpec(memory_space=pl.ANY)],

time: 182 us -> 182 us (level)
  no operation moved by 1% of the time
where the time goes in v12:
time: 182 us; the launch traced here: 181 us
  Pallas kernels  78.7 us (43%)
  starting transfers between devices  58.1 us (32%)
  waiting for transfers between devices  31 us (17%)
  local copies, waits for them, and re-layouts  8.6 us (5%)
  other arithmetic  3.45 us (2%)
    ppermute x21, starting transfers between devices, swap(): return lax.ppermute(value, axis, [(i, i ^ x) for i in range(size)])  35.5 us
    all_to_all x5, starting transfers between devices, to_modes(): return lax.all_to_all(value, 'dp', split_axis=0, concat_axis=0, tiled=True)  22.5 us
    ppermute x21, waiting for transfers between devices, swap(): return lax.ppermute(value, axis, [(i, i ^ x) for i in range(size)])  15.6 us
    all_to_all x5, waiting for transfers between devices, to_modes(): return lax.all_to_all(value, 'dp', split_axis=0, concat_axis=0, tiled=True)  15.4 us
    pallas_call x1, Pallas kernels, pixels(): pl.pallas_call(pixel_kernel, grid_spec=pltpu.PrefetchScalarGridSpec(num_s...  11.5 us
    pallas_call x2, Pallas kernels, forward_spectrum(): pl.pallas_call(forward_kernel, grid_spec=pltpu.PrefetchScalarGridSpec(num...  8.63 us
    dynamic_slice x4, local copies, waits for them, and re-layouts, cut(): lax.dynamic_slice_in_dim(array, jnp.bitwise_xor(own, t) * samples, sample...  7.92 us
    pallas_call x1, Pallas kernels, lin_grads(): pl.pallas_call(lin_kernel, grid_spec=pltpu.PrefetchScalarGridSpec(num_sca...  6.32 us
  transfers between devices with their start and end apart: 26, of which 8 were waited for; matrix products, arithmetic and copies ran while one was open for 5% of the time, Pallas kernels for 42%

profile of v12, /device:TPU:0, one launch (start us, length us, event | category | flops | bytes accessed | tf_op | source)
XLA Modules:
  0.0 180.7 jit_solution(9350500306293856128)
XLA Ops:
  2.7 3.9 %collective-permute-start.2 = (bf16[2,1,48,4096]{3,2,1,0:T(8,128)(2,1)}, bf16[2,1,48,4096]{3,2,1,0:T(8,128)(2,1)}, u32[]{:S(2)}, u32[]{:S(2)}) collective-permute-start(bf16[2,1,48,4096]{3,2,1,0:T(8,128)(2,1)} %constant_dynamic-slice_fusion.5), channel_id=1, source_target_pairs={{0,24},{8,16},{16,8},{24,0},{1,25},{9,17},{17,9},{25,1},{2,26},{10... | collective-permute-start | bytes 2359304 | tf_op jit(solution)/shard_map/ppermute | solution.py:911
  13.4 5.9 %turned.1.refs_5_ = bf16[512,4096]{1,0:T(8,128)(2,1)} custom-call(f32[4,64,512]{2,1,0:T(8,128)} %pad_maximum_fusion.row_ref.col_ref.refs_2_.refs_3_.refs_5_.refs_6_, f32[4,64,512]{2,1,0:T(8,128)} %pad_maximum_fusion.row_ref.col_ref.refs_2_.refs_3_.refs_5_.refs_6_), custom_call_target="tpu_custom_call" | custom-call | flops 1 | bytes 1 | tf_op jit(solution)/shard_map/turned/pallas_call | solution.py:125
  21.5 3.9 %collective-permute-done.2.refs_1_.refs_3_ = bf16[2,1,48,4096]{3,2,1,0:T(8,128)(2,1)} collective-permute-done((bf16[2,1,48,4096]{3,2,1,0:T(8,128)(2,1)}, bf16[2,1,48,4096]{3,2,1,0:T(8,128)(2,1)}, u32[]{:S(2)}, u32[]{:S(2)}) %collective-permute-start.2) | collective-permute-done | bytes 786464 | tf_op jit(solution)/shard_map/ppermute | solution.py:911
  25.3 4.3 %forward.2 = bf16[8,32,384]{2,1,0:T(8,128)(2,1)} custom-call(s32[2]{0:T(128)} %pad_add_fusion.ids_ref, f32[2]{0:T(128)} %dynamic_slice.21.inv_ref, bf16[8,1,48,4096]{3,2,1,0:T(8,128)(2,1)} %refs_0_.6, bf16[2,1,48,4096]{3,2,1,0:T(8,128)(2,1)} %collective-permute-done.2.refs_1_.refs_3_, ...), custom_call_target="tpu_custom_call" | custom-call | flops 1 | bytes 1 | tf_op jit(solution)/shard_map/forward/pallas_call | solution.py:281
  29.7 5.4 %all-to-all-start = ((bf16[8,32,384]{2,1,0:T(8,128)(2,1)}), bf16[8,32,384]{2,1,0:T(8,128)(2,1)}, u32[]{:S(2)}, u32[]{:S(2)}) async-start(bf16[8,32,384]{2,1,0:T(8,128)(2,1)} %forward.2), calls=%async_computation | async-start | bytes 393216 | tf_op jit(solution)/shard_map/all_to_all | solution.py:915
  38.6 4.2 %collective-permute-done.refs_0_.refs_1_ = bf16[2,1,48,4096]{3,2,1,0:T(8,128)(2,1)} collective-permute-done((bf16[2,1,48,4096]{3,2,1,0:T(8,128)(2,1)}, bf16[2,1,48,4096]{3,2,1,0:T(8,128)(2,1)}, u32[]{:S(2)}, u32[]{:S(2)}) %collective-permute-start) | collective-permute-done | bytes 786464 | tf_op jit(solution)/shard_map/ppermute | solution.py:911
  42.8 4.3 %forward.3 = bf16[8,32,384]{2,1,0:T(8,128)(2,1)} custom-call(s32[2]{0:T(128)} %pad_add_fusion.ids_ref, f32[2]{0:T(128)} %dynamic_slice.21.inv_ref, bf16[2,1,48,4096]{3,2,1,0:T(8,128)(2,1)} %collective-permute-done.refs_0_.refs_1_, bf16[2,1,48,4096]{3,2,1,0:T(8,128)(2,1)} %collective-permute-done.1.refs_1_.refs_2_, ...), custom_call_target="tpu_custom_call" | custom-call | flops 1 | bytes 1 | tf_op jit(solution)/shard_map/forward/pallas_call | solution.py:281
  47.1 4.9 %all-to-all-start.1 = ((bf16[8,32,384]{2,1,0:T(8,128)(2,1)}), bf16[8,32,384]{2,1,0:T(8,128)(2,1)}, u32[]{:S(2)}, u32[]{:S(2)}) async-start(bf16[8,32,384]{2,1,0:T(8,128)(2,1)} %forward.3), calls=%async_computation.1 | async-start | bytes 393216 | tf_op jit(solution)/shard_map/all_to_all | solution.py:915
  57.1 4.1 %unpack.1.pq_ref = bf16[32,96,512]{2,1,0:T(8,128)(2,1)S(1)} custom-call(s32[2]{0:T(128)} %pad_add_fusion.ids_ref, bf16[48,3200]{1,0:T(8,128)(2,1)} %copy-done.4, bf16[48,3200]{1,0:T(8,128)(2,1)} %collective-permute-done.3.w1.l1, bf16[48,3200]{1,0:T(8,128)(2,1)} %collective-permute-done.4.w2.l2, bf16[48,3200]{1,0:T(8,128)(2,1)} %collective-permute-done.5.w3.l3), custom_call_target="tpu_custom_call" | custom-call | flops 1 | bytes 1 | tf_op jit(solution)/shard_map/unpack/pallas_call | solution.py:214
  63.9 5.1 %all-to-all-start.2 = ((bf16[8,32,768]{2,1,0:T(8,128)(2,1)}), bf16[8,32,768]{2,1,0:T(8,128)(2,1)S(1)}, u32[]{:S(2)}, u32[]{:S(2)}) async-start(bf16[8,32,768]{2,1,0:T(8,128)(2,1)} %mix.1), calls=%async_computation.2 | async-start | bytes 786432 | tf_op jit(solution)/shard_map/all_to_all | solution.py:915
  69.0 5.1 %turn.1 = (bf16[32,96,512]{2,1,0:T(8,128)(2,1)S(1)}, bf16[32,48,128]{2,1,0:T(8,128)(2,1)}, bf16[192,192]{1,0:T(8,128)(2,1)}, bf16[192,192]{1,0:T(8,128)(2,1)}) custom-call(s32[2]{0:T(128)} %pad_add_fusion.ids_ref, bf16[32,96,512]{2,1,0:T(8,128)(2,1)S(1)} %unpack.1.pq_ref, bf16[8,32,384]{2,1,0:T(8,128)(2,1)} %all-to-all-done.xa, ...), custom_call_target="tpu_custom_call", output_to_operand_aliasing={{0}: (1, {})} | custom-call | flops 1 | bytes 1 | tf_op jit(solution)/shard_map/turn/pallas_call | solution.py:466
  74.1 7.4 %all-to-all-done.2.refs_4_ = bf16[8,32,768]{2,1,0:T(8,128)(2,1)S(1)} async-done(((bf16[8,32,768]{2,1,0:T(8,128)(2,1)}), bf16[8,32,768]{2,1,0:T(8,128)(2,1)S(1)}, u32[]{:S(2)}, u32[]{:S(2)}) %all-to-all-start.2) | async-done | bytes 393248 | tf_op jit(solution)/shard_map/all_to_all | solution.py:915
  81.6 11.5 %pixels.1 = (bf16[8,1,48,4096]{3,2,1,0:T(8,128)(2,1)}, bf16[2,1,48,4096]{3,2,1,0:T(8,128)(2,1)}, bf16[2,1,48,4096]{3,2,1,0:T(8,128)(2,1)}, bf16[2,1,48,4096]{3,2...) custom-call(s32[2]{0:T(128)} %pad_add_fusion.ids_ref, ...), custom_call_target="tpu_custom_call", output_to_operand_aliasing={{5}: (9, {})} | custom-call | flops 1 | bytes 1 | tf_op jit(solution)/shard_map/pixels/pallas_call | solution.py:611
  94.6 6.0 %pixel_grads.1 = (bf16[384,4096]{1,0:T(8,128)(2,1)}, bf16[8,32,768]{2,1,0:T(8,128)(2,1)}, bf16[32,96,512]{2,1,0:T(8,128)(2,1)S(1)}) custom-call(s32[2]{0:T(128)} %pad_add_fusion.ids_ref, bf16[8,1,48,4096]{3,2,1,0:T(8,128)(2,1)} %cot_ref.5, bf16[2,1,48,4096]{3,2,1,0:T(8,128)(2,1)} %collective-permute-done.8.refs_1_, ...), custom_call_target="tpu_custom_call", output_to_operand_aliasing={{2}: (8, {})} | custom-call | flops 1 | bytes 1 | tf_op jit(solution)/shard_map/pixel_grads/pallas_call | solution.py:675
  106.1 6.3 %lin_grads.1 = (f32[4,48,48]{2,1,0:T(8,128)}, bf16[384,4096]{1,0:T(8,128)(2,1)}) custom-call(s32[2]{0:T(128)} %pad_add_fusion.ids_ref, f32[2]{0:T(128)} %dynamic_slice.21.inv_ref, bf16[8,1,48,4096]{3,2,1,0:T(8,128)(2,1)} %refs_0_.6, bf16[2,1,48,4096]{3,2,1,0:T(8,128)(2,1)} %collective-permute-done.refs_0_.refs_1_, ...), custom_call_target="tpu_custom_call" | custom-call | flops 1 | bytes 1 | tf_op jit(solution)/shard_map/lin_grads/pallas_call | solution.py:726
  112.5 4.0 %all-to-all-done.3.g_ref = bf16[8,32,768]{2,1,0:T(8,128)(2,1)S(1)} async-done(((bf16[8,32,768]{2,1,0:T(8,128)(2,1)}), bf16[8,32,768]{2,1,0:T(8,128)(2,1)S(1)}, u32[]{:S(2)}, u32[]{:S(2)}) %all-to-all-start.3) | async-done | bytes 393248 | tf_op jit(solution)/shard_map/all_to_all | solution.py:915
  118.9 3.7 %all-to-all-start.4 = ((bf16[8,32,768]{2,1,0:T(8,128)(2,1)}), bf16[8,32,768]{2,1,0:T(8,128)(2,1)S(1)}, u32[]{:S(2)}, u32[]{:S(2)}) async-start(bf16[8,32,768]{2,1,0:T(8,128)(2,1)} %mix_back.1), calls=%async_computation.4 | async-start | bytes 786432 | tf_op jit(solution)/shard_map/all_to_all | solution.py:915
  122.6 4.8 %weight_grads.1 = (bf16[48,3200]{1,0:T(8,128)(2,1)}, bf16[48,3200]{1,0:T(8,128)(2,1)}, bf16[48,3200]{1,0:T(8,128)(2,1)}, bf16[48,3200]{1,0:T(8,128)(2,1)}) custom-call(s32[2]{0:T(128)} %pad_add_fusion.ids_ref, bf16[32,48,128]{2,1,0:T(8,128)(2,1)} %get-tuple-element.80.xt_ref, bf16[8,32,768]{2,1,0:T(8,128)(2,1)S(1)} %all-to-all-done.3.g_ref, ...), custom_call_target="tpu_custom_call" | custom-call | flops 1 | bytes 1 | tf_op jit(solution)/shard_map/weight_grads/pallas_call | solution.py:534
  130.9 3.9 %all-to-all-done.4.y_ref = bf16[8,32,768]{2,1,0:T(8,128)(2,1)S(1)} async-done(((bf16[8,32,768]{2,1,0:T(8,128)(2,1)}), bf16[8,32,768]{2,1,0:T(8,128)(2,1)S(1)}, u32[]{:S(2)}, u32[]{:S(2)}) %all-to-all-start.4) | async-done | bytes 393248 | tf_op jit(solution)/shard_map/all_to_all | solution.py:915
  134.8 6.1 %inner_grads.1 = (f32[8,1,48,4096]{3,2,1,0:T(8,128)}, bf16[2,1,48,4096]{3,2,1,0:T(8,128)(2,1)}, bf16[2,1,48,4096]{3,2,1,0:T(8,128)(2,1)}, bf16[2,1,48,4096]{3,2,1,0:T(8,128)(2,1)}) custom-call(s32[2]{0:T(128)} %pad_add_fusion.ids_ref, f32[2]{0:T(128)} %dynamic_slice.21.inv_ref, bf16[8,32,768]{2,1,0:T(8,128)(2,1)S(1)} %all-to-all-done.4.y_ref, ...), custom_call_target="tpu_custom_call" | custom-call | flops 1 | bytes 1 | tf_op jit(solution)/shard_map/inner_grads/pallas_call | solution.py:768
  144.5 6.1 %place.1 = bf16[8,1,48,4096]{3,2,1,0:T(8,128)(2,1)} custom-call(s32[2]{0:T(128)S(1)} %copy-done.8, bf16[2,1,48,4096]{3,2,1,0:T(8,128)(2,1)} %collective-permute-done.6.a_ref, bf16[2,1,48,4096]{3,2,1,0:T(8,128)(2,1)} %collective-permute-done.7.b_ref, bf16[2,1,48,4096]{3,2,1,0:T(8,128)(2,1)} %collective-permute-done.11.c_ref, ...), custom_call_target="tpu_custom_call", output_to_operand_aliasing={{}: (4, {})} | custom-call | flops 1 | bytes 1 | tf_op jit(solution)/shard_map/place/pallas_call | solution.py:807
  152.0 10.4 %collective-permute-start.19 = (f32[48,48]{1,0:T(8,128)S(1)}, f32[48,48]{1,0:T(8,128)S(1)}, u32[]{:S(2)}, u32[]{:S(2)}) collective-permute-start(f32[48,48]{1,0:T(8,128)S(1)} %add.171), channel_id=1, source_target_pairs={{0,2},{1,3},{2,0},{3,1},{4,6},{5,7},{6,4},{7,5},{8,10},{9,11},{10,... | collective-permute-start | bytes 27656 | tf_op jit(solution)/shard_map/ppermute | solution.py:911
  167.3 3.8 %adam.1 = (f32[1,32,2,48,48]{4,3,2,1,0:T(8,128)}, f32[1,32,2,48,48]{4,3,2,1,0:T(8,128)}, f32[1,32,2,48,48]{4,3,2,1,0:T(8,128)}) custom-call(f32[4]{0:T(128)S(1)} %pad_maximum_fusion.1.flips, bf16[48,3200]{1,0:T(8,128)(2,1)S(1)} %copy-done.7, bf16[48,3200]{1,0:T(8,128)(2,1)S(1)} %collective-permute-done.15.d1, ...), custom_call_target="tpu_custom_call" | custom-call | flops 1 | bytes 1 | tf_op jit(solution)/shard_map/adam/pallas_call | solution.py:898
  173.7 4.5 %collective-permute-done.12.refs_0_ = bf16[2,1,48,4096]{3,2,1,0:T(8,128)(2,1)S(1)} collective-permute-done((bf16[2,1,48,4096]{3,2,1,0:T(8,128)(2,1)}, bf16[2,1,48,4096]{3,2,1,0:T(8,128)(2,1)S(1)}, u32[]{:S(2)}, u32[]{:S(2)}) %collective-permute-start.12) | collective-permute-done | bytes 786464 | tf_op jit(solution)/shard_map/ppermute | solution.py:911
  (93 shorter events, 50.0 us)
Async XLA Ops:
  2.7 22.6 %collective-permute-start.2 = (bf16[2,1,48,4096]{3,2,1,0:T(8,128)(2,1)}, bf16[2,1,48,4096]{3,2,1,0:T(8,128)(2,1)}, u32[]{:S(2)}, u32[]{:S(2)}) collective-permute-start(bf16[2,1,48,4096]{3,2,1,0:T(8,128)(2,1)} %constant_dynamic-slice_fusion.5), channel_id=1, source_target_pairs={{0,24},{8,16},{16,8},{24,0},{1,25},{9,17},{17,9},{25,1},{2,26},{10... | collective-permute-start | bytes 2359304 | tf_op jit(solution)/shard_map/ppermute | solution.py:911
  8.7 34.1 %collective-permute-start = (bf16[2,1,48,4096]{3,2,1,0:T(8,128)(2,1)}, bf16[2,1,48,4096]{3,2,1,0:T(8,128)(2,1)}, u32[]{:S(2)}, u32[]{:S(2)}) collective-permute-start(bf16[2,1,48,4096]{3,2,1,0:T(8,128)(2,1)} %constant_dynamic-slice_fusion.4), channel_id=1, source_target_pairs={{0,8},{8,0},{16,24},{24,16},{1,9},{9,1},{17,25},{25,17},{2,10},{10... | collective-permute-start | bytes 2359304 | tf_op jit(solution)/shard_map/ppermute | solution.py:911
  13.3 29.4 %collective-permute-start.1 = (bf16[2,1,48,4096]{3,2,1,0:T(8,128)(2,1)}, bf16[2,1,48,4096]{3,2,1,0:T(8,128)(2,1)}, u32[]{:S(2)}, u32[]{:S(2)}) collective-permute-start(bf16[2,1,48,4096]{3,2,1,0:T(8,128)(2,1)} %constant_dynamic-slice_fusion.3), channel_id=1, source_target_pairs={{0,16},{8,24},{16,0},{24,8},{1,17},{9,25},{17,1},{25,9},{2,18},{10... | collective-permute-start | bytes 2359304 | tf_op jit(solution)/shard_map/ppermute | solution.py:911
  29.7 17.4 %all-to-all-start = ((bf16[8,32,384]{2,1,0:T(8,128)(2,1)}), bf16[8,32,384]{2,1,0:T(8,128)(2,1)}, u32[]{:S(2)}, u32[]{:S(2)}) async-start(bf16[8,32,384]{2,1,0:T(8,128)(2,1)} %forward.2), calls=%async_computation | async-start | bytes 393216 | tf_op jit(solution)/shard_map/all_to_all | solution.py:915
  35.1 20.5 %collective-permute-start.3 = (bf16[48,3200]{1,0:T(8,128)(2,1)S(1)}, bf16[48,3200]{1,0:T(8,128)(2,1)}, u32[]{:S(2)}, u32[]{:S(2)}) collective-permute-start(bf16[48,3200]{1,0:T(8,128)(2,1)S(1)} %pack.1.w0.l0), channel_id=1, source_target_pairs={{0,8},{8,0},{16,24},{24,16},{1,9},{9,1},{17,25},{25,17},{2,10},{10... | collective-permute-start | bytes 921608 | tf_op jit(solution)/shard_map/ppermute | solution.py:911
  36.5 20.5 %collective-permute-start.4 = (bf16[48,3200]{1,0:T(8,128)(2,1)S(1)}, bf16[48,3200]{1,0:T(8,128)(2,1)}, u32[]{:S(2)}, u32[]{:S(2)}) collective-permute-start(bf16[48,3200]{1,0:T(8,128)(2,1)S(1)} %pack.1.w0.l0), channel_id=1, source_target_pairs={{0,16},{8,24},{16,0},{24,8},{1,17},{9,25},{17,1},{25,9},{2,18},{10... | collective-permute-start | bytes 921608 | tf_op jit(solution)/shard_map/ppermute | solution.py:911
  38.1 19.0 %collective-permute-start.5 = (bf16[48,3200]{1,0:T(8,128)(2,1)S(1)}, bf16[48,3200]{1,0:T(8,128)(2,1)}, u32[]{:S(2)}, u32[]{:S(2)}) collective-permute-start(bf16[48,3200]{1,0:T(8,128)(2,1)S(1)} %pack.1.w0.l0), channel_id=1, source_target_pairs={{0,24},{8,16},{16,8},{24,0},{1,25},{9,17},{17,9},{25,1},{2,26},{10... | collective-permute-start | bytes 921608 | tf_op jit(solution)/shard_map/ppermute | solution.py:911
  47.1 14.1 %all-to-all-start.1 = ((bf16[8,32,384]{2,1,0:T(8,128)(2,1)}), bf16[8,32,384]{2,1,0:T(8,128)(2,1)}, u32[]{:S(2)}, u32[]{:S(2)}) async-start(bf16[8,32,384]{2,1,0:T(8,128)(2,1)} %forward.3), calls=%async_computation.1 | async-start | bytes 393216 | tf_op jit(solution)/shard_map/all_to_all | solution.py:915
  53.6 39.5 %collective-permute-start.8 = (bf16[2,1,48,4096]{3,2,1,0:T(8,128)(2,1)}, bf16[2,1,48,4096]{3,2,1,0:T(8,128)(2,1)}, u32[]{:S(2)}, u32[]{:S(2)}) collective-permute-start(bf16[2,1,48,4096]{3,2,1,0:T(8,128)(2,1)} %get-tuple-element.68), channel_id=1, source_target_pairs={{0,8},{8,0},{16,24},{24,16},{1,9},{9,1},{17,25},{25,17},{2,10},{10... | collective-permute-start | bytes 2359304 | tf_op jit(solution)/shard_map/ppermute | solution.py:911
  55.1 38.0 %collective-permute-start.9 = (bf16[2,1,48,4096]{3,2,1,0:T(8,128)(2,1)}, bf16[2,1,48,4096]{3,2,1,0:T(8,128)(2,1)}, u32[]{:S(2)}, u32[]{:S(2)}) collective-permute-start(bf16[2,1,48,4096]{3,2,1,0:T(8,128)(2,1)} %get-tuple-element.69), channel_id=1, source_target_pairs={{0,16},{8,24},{16,0},{24,8},{1,17},{9,25},{17,1},{25,9},{2,18},{10... | collective-permute-start | bytes 2359304 | tf_op jit(solution)/shard_map/ppermute | solution.py:911
  55.6 37.5 %collective-permute-start.10 = (bf16[2,1,48,4096]{3,2,1,0:T(8,128)(2,1)}, bf16[2,1,48,4096]{3,2,1,0:T(8,128)(2,1)}, u32[]{:S(2)}, u32[]{:S(2)}) collective-permute-start(bf16[2,1,48,4096]{3,2,1,0:T(8,128)(2,1)} %get-tuple-element.70), channel_id=1, source_target_pairs={{0,24},{8,16},{16,8},{24,0},{1,25},{9,17},{17,9},{25,1},{2,26},{10... | collective-permute-start | bytes 2359304 | tf_op jit(solution)/shard_map/ppermute | solution.py:911
  63.9 17.6 %all-to-all-start.2 = ((bf16[8,32,768]{2,1,0:T(8,128)(2,1)}), bf16[8,32,768]{2,1,0:T(8,128)(2,1)S(1)}, u32[]{:S(2)}, u32[]{:S(2)}) async-start(bf16[8,32,768]{2,1,0:T(8,128)(2,1)} %mix.1), calls=%async_computation.2 | async-start | bytes 786432 | tf_op jit(solution)/shard_map/all_to_all | solution.py:915
  93.1 23.4 %collective-permute-start.11 = (bf16[2,1,48,4096]{3,2,1,0:T(8,128)(2,1)}, bf16[2,1,48,4096]{3,2,1,0:T(8,128)(2,1)}, u32[]{:S(2)}, u32[]{:S(2)}) collective-permute-start(bf16[2,1,48,4096]{3,2,1,0:T(8,128)(2,1)} %get-tuple-element.71), channel_id=1, source_target_pairs={{0,24},{8,16},{16,8},{24,0},{1,25},{9,17},{17,9},{25,1},{2,26},{10... | collective-permute-start | bytes 2359304 | tf_op jit(solution)/shard_map/ppermute | solution.py:911
  100.5 15.9 %all-to-all-start.3 = ((bf16[8,32,768]{2,1,0:T(8,128)(2,1)}), bf16[8,32,768]{2,1,0:T(8,128)(2,1)S(1)}, u32[]{:S(2)}, u32[]{:S(2)}) async-start(bf16[8,32,768]{2,1,0:T(8,128)(2,1)} %get-tuple-element.79), calls=%async_computation.3 | async-start | bytes 786432 | tf_op jit(solution)/shard_map/all_to_all | solution.py:915
  104.0 36.9 %collective-permute-start.6 = (bf16[2,1,48,4096]{3,2,1,0:T(8,128)(2,1)}, bf16[2,1,48,4096]{3,2,1,0:T(8,128)(2,1)}, u32[]{:S(2)}, u32[]{:S(2)}) collective-permute-start(bf16[2,1,48,4096]{3,2,1,0:T(8,128)(2,1)} %get-tuple-element.65), channel_id=1, source_target_pairs={{0,8},{8,0},{16,24},{24,16},{1,9},{9,1},{17,25},{25,17},{2,10},{10... | collective-permute-start | bytes 2359304 | tf_op jit(solution)/shard_map/ppermute | solution.py:911
  104.6 36.3 %collective-permute-start.7 = (bf16[2,1,48,4096]{3,2,1,0:T(8,128)(2,1)}, bf16[2,1,48,4096]{3,2,1,0:T(8,128)(2,1)}, u32[]{:S(2)}, u32[]{:S(2)}) collective-permute-start(bf16[2,1,48,4096]{3,2,1,0:T(8,128)(2,1)} %get-tuple-element.66), channel_id=1, source_target_pairs={{0,16},{8,24},{16,0},{24,8},{1,17},{9,25},{17,1},{25,9},{2,18},{10... | collective-permute-start | bytes 2359304 | tf_op jit(solution)/shard_map/ppermute | solution.py:911
  118.9 15.9 %all-to-all-start.4 = ((bf16[8,32,768]{2,1,0:T(8,128)(2,1)}), bf16[8,32,768]{2,1,0:T(8,128)(2,1)S(1)}, u32[]{:S(2)}, u32[]{:S(2)}) async-start(bf16[8,32,768]{2,1,0:T(8,128)(2,1)} %mix_back.1), calls=%async_computation.4 | async-start | bytes 786432 | tf_op jit(solution)/shard_map/all_to_all | solution.py:915
  127.4 16.6 %collective-permute-start.15 = (bf16[48,3200]{1,0:T(8,128)(2,1)}, bf16[48,3200]{1,0:T(8,128)(2,1)S(1)}, u32[]{:S(2)}, u32[]{:S(2)}) collective-permute-start(bf16[48,3200]{1,0:T(8,128)(2,1)} %get-tuple-element.96), channel_id=1, source_target_pairs={{0,8},{8,0},{16,24},{24,16},{1,9},{9,1},{17,25},{25,17},{2,10},{10... | collective-permute-start | bytes 921608 | tf_op jit(solution)/shard_map/ppermute | solution.py:911
  128.1 22.6 %collective-permute-start.16 = (bf16[48,3200]{1,0:T(8,128)(2,1)}, bf16[48,3200]{1,0:T(8,128)(2,1)S(1)}, u32[]{:S(2)}, u32[]{:S(2)}) collective-permute-start(bf16[48,3200]{1,0:T(8,128)(2,1)} %get-tuple-element.97), channel_id=1, source_target_pairs={{0,16},{8,24},{16,0},{24,8},{1,17},{9,25},{17,1},{25,9},{2,18},{10... | collective-permute-start | bytes 921608 | tf_op jit(solution)/shard_map/ppermute | solution.py:911
  129.6 21.1 %collective-permute-start.17 = (bf16[48,3200]{1,0:T(8,128)(2,1)}, bf16[48,3200]{1,0:T(8,128)(2,1)S(1)}, u32[]{:S(2)}, u32[]{:S(2)}) collective-permute-start(bf16[48,3200]{1,0:T(8,128)(2,1)} %get-tuple-element.98), channel_id=1, source_target_pairs={{0,24},{8,16},{16,8},{24,0},{1,25},{9,17},{17,9},{25,1},{2,26},{10... | collective-permute-start | bytes 921608 | tf_op jit(solution)/shard_map/ppermute | solution.py:911
  140.9 30.8 %collective-permute-start.14 = (bf16[2,1,48,4096]{3,2,1,0:T(8,128)(2,1)}, bf16[2,1,48,4096]{3,2,1,0:T(8,128)(2,1)S(1)}, u32[]{:S(2)}, u32[]{:S(2)}) collective-permute-start(bf16[2,1,48,4096]{3,2,1,0:T(8,128)(2,1)} %get-tuple-element.93), channel_id=1, source_target_pairs={{0,24},{8,16},{16,8},{24,0},{1,25},{9,17},{17,9},{25,1},{2,26},{10... | collective-permute-start | bytes 2359304 | tf_op jit(solution)/shard_map/ppermute | solution.py:911
  142.6 35.5 %collective-permute-start.12 = (bf16[2,1,48,4096]{3,2,1,0:T(8,128)(2,1)}, bf16[2,1,48,4096]{3,2,1,0:T(8,128)(2,1)S(1)}, u32[]{:S(2)}, u32[]{:S(2)}) collective-permute-start(bf16[2,1,48,4096]{3,2,1,0:T(8,128)(2,1)} %get-tuple-element.91), channel_id=1, source_target_pairs={{0,8},{8,0},{16,24},{24,16},{1,9},{9,1},{17,25},{25,17},{2,10},{10... | collective-permute-start | bytes 2359304 | tf_op jit(solution)/shard_map/ppermute | solution.py:911
  144.0 34.2 %collective-permute-start.13 = (bf16[2,1,48,4096]{3,2,1,0:T(8,128)(2,1)}, bf16[2,1,48,4096]{3,2,1,0:T(8,128)(2,1)S(1)}, u32[]{:S(2)}, u32[]{:S(2)}) collective-permute-start(bf16[2,1,48,4096]{3,2,1,0:T(8,128)(2,1)} %get-tuple-element.92), channel_id=1, source_target_pairs={{0,16},{8,24},{16,0},{24,8},{1,17},{9,25},{17,1},{25,9},{2,18},{10... | collective-permute-start | bytes 2359304 | tf_op jit(solution)/shard_map/ppermute | solution.py:911
  152.0 12.2 %collective-permute-start.19 = (f32[48,48]{1,0:T(8,128)S(1)}, f32[48,48]{1,0:T(8,128)S(1)}, u32[]{:S(2)}, u32[]{:S(2)}) collective-permute-start(f32[48,48]{1,0:T(8,128)S(1)} %add.171), channel_id=1, source_target_pairs={{0,2},{1,3},{2,0},{3,1},{4,6},{5,7},{6,4},{7,5},{8,10},{9,11},{10,... | collective-permute-start | bytes 27656 | tf_op jit(solution)/shard_map/ppermute | solution.py:911
  (17 other events, 261.8 us)
